TPU v7x, 32 devices: a whole 2x2x4 slice. The times are simulated.
32 devices in a mesh: wide: 8 (over z, y), narrow: 4 (over x, core).
Axes of the slice: x: 2, y: 2, z: 4, core: 2. Of those that a mesh axis runs over, the one named last changes fastest.
Arguments:
- tokens: bfloat16 [16384, 1024], P(('wide', 'narrow')), may hold values from -6 to 6
- cotangent: bfloat16 [16384, 1024], P(('wide', 'narrow')), may hold values from -6 to 6
- segment_ids: int32 [16384], P(('wide', 'narrow')), may hold values from 0 to 2, as said below
- key_keep: int32 [16384], P(('wide', 'narrow')), may hold values from 0 to 1, as said below
- patch_coords: int32 [3, 16384], P(None, ('wide', 'narrow')), may hold values from 0 to 13, as said below
- step_count: int32 [1], replicated, may hold values from 2 to 20
- weight_qkv: float32 [1024, 3072], P('wide'), may hold values from -0.25 to 0.25
- weight_out: float32 [1024, 1024], P('wide'), may hold values from -0.75 to 0.75
- weight_up: float32 [1024, 4096], P('wide'), may hold values from -0.1875 to 0.1875
- weight_down: float32 [1024, 4096], P('wide'), may hold values from -0.09375 to 0.09375
- vectors: float32 [13, 1024], P(None, 'wide'), may hold values from -0.6 to 1.45, as said below
- first_qkv: float32 [1024, 3072], P('wide'), may hold values from -0.00018310547 to 0.00018310547
- first_out: float32 [1024, 1024], P('wide'), may hold values from -0.00018310547 to 0.00018310547
- first_up: float32 [1024, 4096], P('wide'), may hold values from -6.1035156e-05 to 6.1035156e-05
- first_down: float32 [1024, 4096], P('wide'), may hold values from -0.00018310547 to 0.00018310547
- first_vectors: float32 [13, 1024], P(None, 'wide'), may hold values from -0.00018310547 to 0.00018310547
- second_qkv: float32 [1024, 3072], P('wide'), may hold values from 7.938887e-11 to 3.1755548e-10
- second_out: float32 [1024, 1024], P('wide'), may hold values from 7.938887e-11 to 3.1755548e-10
- second_up: float32 [1024, 4096], P('wide'), may hold values from 1.03205534e-11 to 3.9694435e-11
- second_down: float32 [1024, 4096], P('wide'), may hold values from 7.938887e-11 to 3.1755548e-10
- second_vectors: float32 [13, 1024], P(None, 'wide'), may hold values from 7.938887e-11 to 3.1755548e-10
Outputs:
- layer_out: bfloat16 [16384, 1024], P(('wide', 'narrow'))
- grad_tokens: bfloat16 [16384, 1024], P(('wide', 'narrow'))
- updated_qkv: float32 [1024, 3072], P('wide')
- updated_out: float32 [1024, 1024], P('wide')
- updated_up: float32 [1024, 4096], P('wide')
- updated_down: float32 [1024, 4096], P('wide')
- updated_vectors: float32 [13, 1024], P(None, 'wide')
- moment_qkv: float32 [1024, 3072], P('wide')
- moment_out: float32 [1024, 1024], P('wide')
- moment_up: float32 [1024, 4096], P('wide')
- moment_down: float32 [1024, 4096], P('wide')
- moment_vectors: float32 [13, 1024], P(None, 'wide')
- square_qkv: float32 [1024, 3072], P('wide')
- square_out: float32 [1024, 1024], P('wide')
- square_up: float32 [1024, 4096], P('wide')
- square_down: float32 [1024, 4096], P('wide')
- square_vectors: float32 [13, 1024], P(None, 'wide')
- grad_norm: float32 [], replicated
- grad_down_bias: float32 [1024], P('wide')
Inputs may be any that keep to these rules, and one draw needn't show every extreme that they name: `segment_ids`: within each aligned block of 2048 tokens, segment numbers start at 0 and never fall; each segment is a clip of 784 or 1568 tokens, the last one cut at the block's end. `key_keep`: within each clip the tokens with 0 are its last 0 to 195 tokens; a clip's first token is always 1. `patch_coords`: position of a token in its clip as time = index // 196, row = (index // 14) mod 14, column = index mod 14. `vectors`: rows 0 and 6 lie in 0.55 to 1.45, the other rows in -0.6 to 0.6.
All inputs are finite; a program needn't handle non-finite values.
Results may differ from a plain program's by a relative error of at most 0.014.
The roundings to bfloat16 on the way count: a program that leaves them out, or rounds other values in their place, can miss the bound.
Values may be sent and summed in bfloat16 or wider, within the bound.
A program may use at most 256 MiB of HBM per device.

v0:
```python
import jax
import jax.numpy as jnp
from jax import lax
from jax.sharding import PartitionSpec as P

HEADS = 16


def layer_norm(values, gain, shift):
    center = values - jnp.mean(values, axis=-1, keepdims=True)
    spread = jnp.mean(center * center, axis=-1, keepdims=True)
    return center * lax.rsqrt(spread + 1e-06) * gain + shift


def exact_gelu(values):
    return jax.nn.gelu(values, approximate=False)


def rotary(patch, head_dim):
    pairs = head_dim // 2
    index = jnp.arange(pairs)
    which = index % 3
    rates = jnp.power(10000.0, -(index // 3).astype(jnp.float32) / ((pairs + 2) // 3))
    place = patch.astype(jnp.float32)
    chosen = jnp.where(
        which[None, :] == 0,
        place[0][:, None],
        jnp.where(which[None, :] == 1, place[1][:, None], place[2][:, None]),
    )
    angle = chosen * rates[None, :]
    return (jnp.cos(angle), jnp.sin(angle))


def rotate(values, cosine, sine):
    half = values.shape[-1] // 2
    first = values[..., :half]
    second = values[..., half:]
    cosine = cosine[:, None, :]
    sine = sine[:, None, :]
    return jnp.concatenate(
        [first * cosine - second * sine, first * sine + second * cosine], axis=-1
    )


def unrotate(grads, cosine, sine):
    half = grads.shape[-1] // 2
    first = grads[..., :half]
    second = grads[..., half:]
    cosine = cosine[:, None, :]
    sine = sine[:, None, :]
    return jnp.concatenate(
        [first * cosine + second * sine, second * cosine - first * sine], axis=-1
    )


def contract_last(left, right):
    return lax.dot_general(
        left, right, (((1,), (1,)), ((), ())), preferred_element_type=jnp.float32
    )


def contract_first(left, right):
    return lax.dot_general(
        left, right, (((0,), (0,)), ((), ())), preferred_element_type=jnp.float32
    )


def adamw(param, grad, first, second, clip, rate, decay, fix_first, fix_second):
    clipped = grad * clip
    moment = 0.9 * first + 0.1 * clipped
    square = 0.999 * second + 0.001 * clipped * clipped
    direction = moment / fix_first / (jnp.sqrt(square / fix_second) + 1e-08)
    return (param - rate * (direction + decay * param), moment, square)


def on_device(
    tokens,
    cotangent,
    segment_ids,
    key_keep,
    patch_coords,
    step_count,
    weight_qkv,
    weight_out,
    weight_up,
    weight_down,
    vectors,
    first_qkv,
    first_out,
    first_up,
    first_down,
    first_vectors,
    second_qkv,
    second_out,
    second_up,
    second_down,
    second_vectors,
):
    rows, width = tokens.shape
    hidden = weight_up.shape[1]
    head_dim = width // HEADS
    pair_width = 2 * head_dim
    scale = head_dim ** (-0.5)
    shard_rows = width // lax.axis_size("wide")
    qkv_low = weight_qkv.astype(jnp.bfloat16)
    out_low = weight_out.astype(jnp.bfloat16)
    up_low = weight_up.astype(jnp.bfloat16)
    down_low = weight_down.astype(jnp.bfloat16)
    qkv_w, out_w, up_w, down_w, vec_w = (
        lax.all_gather(qkv_low, "wide", axis=0, tiled=True),
        lax.all_gather(out_low, "wide", axis=0, tiled=True),
        lax.all_gather(up_low, "wide", axis=0, tiled=True),
        lax.all_gather(down_low, "wide", axis=0, tiled=True),
        lax.all_gather(vectors.astype(jnp.bfloat16), "wide", axis=1, tiled=True),
    )
    vec = vec_w.astype(jnp.float32)
    xin = tokens.astype(jnp.float32)
    normed1, norm1_pull = jax.vjp(layer_norm, xin, vec[0], vec[1])
    normed1_b = normed1.astype(jnp.bfloat16)
    projected = jnp.dot(normed1_b, qkv_w, preferred_element_type=jnp.float32) + vec[2:5].reshape(-1)
    cosine, sine = rotary(patch_coords, head_dim)
    query_b = (
        rotate(projected[:, :width].reshape(rows, HEADS, head_dim), cosine, sine)
        .reshape(rows, width)
        .astype(jnp.bfloat16)
    )
    keys_b = (
        rotate(projected[:, width : 2 * width].reshape(rows, HEADS, head_dim), cosine, sine)
        .reshape(rows, width)
        .astype(jnp.bfloat16)
    )
    values_b = projected[:, 2 * width :].astype(jnp.bfloat16)
    key_tag = jnp.where(key_keep == 1, segment_ids, -1).astype(jnp.bfloat16)
    keys_all, values_all, tags_all = (
        lax.all_gather(keys_b, "narrow", axis=0, tiled=True),
        lax.all_gather(values_b, "narrow", axis=0, tiled=True),
        lax.all_gather(key_tag, "narrow", axis=0, tiled=True),
    )
    group = keys_all.shape[0]
    query_tags = segment_ids.astype(jnp.float32)
    allowed = query_tags[:, None] == tags_all.astype(jnp.float32)[None, :]
    pair_index = jnp.arange(HEADS // 2)

    def take_pair(source, index, count):
        return lax.dynamic_slice_in_dim(source, index * pair_width, pair_width, 1).reshape(
            count, 2, head_dim
        )

    def masked_scores(query_pair, key_pair, mask):
        raw = (
            jnp.einsum("qhd,khd->hqk", query_pair, key_pair, preferred_element_type=jnp.float32)
            * scale
        )
        return jnp.where(mask[None], raw, -1e30)

    def forward_pair(index):
        query_pair = take_pair(query_b, index, rows)
        key_pair = take_pair(keys_all, index, group)
        value_pair = take_pair(values_all, index, group)
        masked = masked_scores(query_pair, key_pair, allowed)
        peak = jnp.max(masked, axis=-1, keepdims=True)
        expo = jnp.exp(masked - peak)
        total = jnp.sum(expo, axis=-1, keepdims=True)
        probs_b = (expo / total).astype(jnp.bfloat16)
        mixed_pair = jnp.einsum(
            "hqk,khd->qhd", probs_b, value_pair, preferred_element_type=jnp.float32
        )
        return (mixed_pair.reshape(rows, pair_width), (peak + jnp.log(total))[..., 0])

    mixed_parts, logsums = lax.map(forward_pair, pair_index)
    mixed_b = jnp.moveaxis(mixed_parts, 0, 1).reshape(rows, width).astype(jnp.bfloat16)
    branch = jnp.dot(mixed_b, out_w, preferred_element_type=jnp.float32) + vec[5]
    resid = xin + branch
    normed2, norm2_pull = jax.vjp(layer_norm, resid, vec[6], vec[7])
    normed2_b = normed2.astype(jnp.bfloat16)
    up_pre = jnp.dot(normed2_b, up_w, preferred_element_type=jnp.float32) + vec[9:].reshape(-1)
    act, gelu_pull = jax.vjp(exact_gelu, up_pre)
    act_b = act.astype(jnp.bfloat16)
    down = contract_last(act_b, down_w) + vec[8]
    layer_out = (resid + down).astype(jnp.bfloat16)
    qkv_w, out_w, up_w, down_w = (
        lax.all_gather(qkv_low, "wide", axis=0, tiled=True),
        lax.all_gather(out_low, "wide", axis=0, tiled=True),
        lax.all_gather(up_low, "wide", axis=0, tiled=True),
        lax.all_gather(down_low, "wide", axis=0, tiled=True),
    )
    grad_act = jnp.dot(cotangent, down_w, preferred_element_type=jnp.float32)
    grad_up_b = gelu_pull(grad_act)[0].astype(jnp.bfloat16)
    grad_normed2 = contract_last(grad_up_b, up_w)
    resid_part, gain2_grad, shift2_grad = norm2_pull(grad_normed2)
    grad_resid = cotangent.astype(jnp.float32) + resid_part
    grad_branch_b = grad_resid.astype(jnp.bfloat16)
    grad_mixed_b = contract_last(grad_branch_b, out_w).astype(jnp.bfloat16)

    def backward_pair(index):
        query_pair = take_pair(query_b, index, rows)
        key_pair = take_pair(keys_all, index, group)
        value_pair = take_pair(values_all, index, group)
        grad_pair = take_pair(grad_mixed_b, index, rows)
        masked = masked_scores(query_pair, key_pair, allowed)
        probs = jnp.exp(masked - logsums[index][..., None])
        grad_probs = jnp.einsum(
            "qhd,khd->hqk", grad_pair, value_pair, preferred_element_type=jnp.float32
        )
        grad_value_pair = jnp.einsum(
            "hqk,qhd->khd",
            probs.astype(jnp.bfloat16),
            grad_pair,
            preferred_element_type=jnp.float32,
        )
        delta = jnp.sum(probs * grad_probs, axis=-1, keepdims=True)
        grad_scores = (probs * (grad_probs - delta)).astype(jnp.bfloat16)
        grad_query_pair = (
            jnp.einsum("hqk,khd->qhd", grad_scores, key_pair, preferred_element_type=jnp.float32)
            * scale
        )
        grad_key_pair = (
            jnp.einsum("hqk,qhd->khd", grad_scores, query_pair, preferred_element_type=jnp.float32)
            * scale
        )
        return (
            grad_query_pair.reshape(rows, pair_width),
            grad_key_pair.reshape(group, pair_width),
            grad_value_pair.reshape(group, pair_width),
        )

    query_parts, key_parts, value_parts = lax.map(backward_pair, pair_index)
    grad_query = jnp.moveaxis(query_parts, 0, 1).reshape(rows, width)
    grad_keys_all = jnp.moveaxis(key_parts, 0, 1).reshape(group, width)
    grad_values_all = jnp.moveaxis(value_parts, 0, 1).reshape(group, width)
    grad_keys, grad_values = (
        lax.psum_scatter(grad_keys_all, "narrow", scatter_dimension=0, tiled=True),
        lax.psum_scatter(grad_values_all, "narrow", scatter_dimension=0, tiled=True),
    )
    grad_query_pre = unrotate(grad_query.reshape(rows, HEADS, head_dim), cosine, sine).reshape(
        rows, width
    )
    grad_keys_pre = unrotate(grad_keys.reshape(rows, HEADS, head_dim), cosine, sine).reshape(
        rows, width
    )
    grad_proj_b = jnp.concatenate([grad_query_pre, grad_keys_pre, grad_values], axis=1).astype(
        jnp.bfloat16
    )
    grad_normed1 = contract_last(grad_proj_b, qkv_w)
    input_part, gain1_grad, shift1_grad = norm1_pull(grad_normed1)
    grad_tokens = (grad_resid + input_part).astype(jnp.bfloat16)
    vector_part = jnp.concatenate(
        [
            gain1_grad[None],
            shift1_grad[None],
            jnp.sum(grad_proj_b.astype(jnp.float32), axis=0).reshape(3, width),
            jnp.sum(grad_branch_b.astype(jnp.float32), axis=0)[None],
            gain2_grad[None],
            shift2_grad[None],
            jnp.sum(cotangent.astype(jnp.float32), axis=0)[None],
            jnp.sum(grad_up_b.astype(jnp.float32), axis=0).reshape(hidden // width, width),
        ],
        axis=0,
    )

    def part_term(activ, grads_b):
        return contract_first(activ, grads_b)

    matrix_part = lax.psum_scatter(
        jnp.concatenate(
            [
                part_term(normed1_b, grad_proj_b),
                part_term(mixed_b, grad_branch_b),
                part_term(normed2_b, grad_up_b),
                part_term(cotangent, act_b),
            ],
            axis=1,
        ),
        "wide",
        scatter_dimension=0,
        tiled=True,
    )
    matrix_total, vector_group = lax.psum((matrix_part, vector_part), "narrow")
    matrix_squares = jnp.sum(matrix_total * matrix_total)
    vector_total, squares_total = lax.psum((vector_group, matrix_squares), "wide")
    grad_norm = jnp.sqrt(squares_total + jnp.sum(vector_total * vector_total))
    clip = 1.0 / jnp.maximum(grad_norm, 1.0)
    count_float = step_count[0].astype(jnp.float32)
    rate = 0.4 * count_float / (count_float + 4.0)
    decay = 0.04 + 0.018 * count_float
    fix_first = 1.0 - jnp.power(0.9, count_float)
    fix_second = 1.0 - jnp.power(0.999, count_float)
    grad_qkv = matrix_total[:, : 3 * width]
    grad_out = matrix_total[:, 3 * width : 4 * width]
    grad_up = matrix_total[:, 4 * width : 4 * width + hidden]
    grad_down = matrix_total[:, 4 * width + hidden :]
    grad_vectors = lax.dynamic_slice_in_dim(
        vector_total, lax.axis_index("wide") * shard_rows, shard_rows, 1
    )
    new_qkv = adamw(
        weight_qkv, grad_qkv, first_qkv, second_qkv, clip, rate, decay, fix_first, fix_second
    )
    new_out = adamw(
        weight_out, grad_out, first_out, second_out, clip, rate, decay, fix_first, fix_second
    )
    new_up = adamw(
        weight_up, grad_up, first_up, second_up, clip, rate, decay, fix_first, fix_second
    )
    new_down = adamw(
        weight_down, grad_down, first_down, second_down, clip, rate, decay, fix_first, fix_second
    )
    new_vectors = adamw(
        vectors, grad_vectors, first_vectors, second_vectors, clip, rate, 0.0, fix_first, fix_second
    )
    return (
        layer_out,
        grad_tokens,
        new_qkv[0],
        new_out[0],
        new_up[0],
        new_down[0],
        new_vectors[0],
        new_qkv[1],
        new_out[1],
        new_up[1],
        new_down[1],
        new_vectors[1],
        new_qkv[2],
        new_out[2],
        new_up[2],
        new_down[2],
        new_vectors[2],
        grad_norm,
        grad_vectors[8],
    )


def solution(mesh):
    return jax.shard_map(
        on_device,
        mesh=mesh,
        in_specs=(
            P(("wide", "narrow"), None),
            P(("wide", "narrow"), None),
            P(("wide", "narrow")),
            P(("wide", "narrow")),
            P(None, ("wide", "narrow")),
            P(),
            P("wide", None),
            P("wide", None),
            P("wide", None),
            P("wide", None),
            P(None, "wide"),
            P("wide", None),
            P("wide", None),
            P("wide", None),
            P("wide", None),
            P(None, "wide"),
            P("wide", None),
            P("wide", None),
            P("wide", None),
            P("wide", None),
            P(None, "wide"),
        ),
        out_specs=(
            P(("wide", "narrow"), None),
            P(("wide", "narrow"), None),
            P("wide", None),
            P("wide", None),
            P("wide", None),
            P("wide", None),
            P(None, "wide"),
            P("wide", None),
            P("wide", None),
            P("wide", None),
            P("wide", None),
            P(None, "wide"),
            P("wide", None),
            P("wide", None),
            P("wide", None),
            P("wide", None),
            P(None, "wide"),
            P(),
            P("wide"),
        ),
        check_vma=False,
    )
```

profile of v0, /device:TPU:0, one launch (start us, length us, event | category | flops | bytes accessed | tf_op | source)
XLA Modules:
  0.0 1886.7 jit_solution(16548710068729517539)
XLA Ops:
  10.5 28.5 %all_gather.28 = bf16[13,1024]{1,0:T(8,128)(2,1)S(1)} all-gather(bf16[13,128]{1,0:T(8,128)(2,1)S(1)} %convert_element_type.110), channel_id=1, replica_groups=mesh['wide'=8,'narrow'=4] {'wide'}, dimensions={1}, use_global_device_ids=true | all-gather | bytes 29952 | tf_op jit(solution)/shard_map/all_gather | solution.py:114
  42.1 70.4 %all-gather.8.cloned.1.call-done = bf16[1024,3072]{1,0:T(8,128)(2,1)} async-done(((bf16[128,3072]{1,0:T(8,128)(2,1)}), bf16[1024,3072]{1,0:T(8,128)(2,1)}) %all-gather.8.cloned.1.call-update) | async-done | bytes 6291472 | tf_op jit(solution)/shard_map/all_gather | solution.py:110
  112.5 5.8 convolution_add_fusion
  122.6 4.9 fusion.62
  142.9 5.7 all-gather
  149.9 5.1 all-gather.10.cloned.1.call-done
  155.0 6.6 copy.61
  161.5 30.1 %all-gather.12.cloned.1.call-done = bf16[2048,1024]{0,1:T(8,128)(2,1)} async-done(((bf16[512,1024]{0,1:T(8,128)(2,1)}), bf16[2048,1024]{0,1:T(8,128)(2,1)}) %all-gather.12.cloned.1.call-update) | async-done | bytes 4194320 | tf_op jit(solution)/shard_map/all_gather | solution.py:135
  191.6 83.2 %while.30 = (s32[]{:T(128)}, bf16[8,512,128]{1,2,0:T(8,128)(2,1)S(1)}, f32[8,2,512]{2,1,0:T(2,128)S(1)}, s32[8]{0:T(128)S(1)}, bf16[2048,1024]{0,1:T(8,128)(2,1)...) while((s32[]{:T(128)}, ...), condition=%wide.region_5.6_spmd.clone.clone, body=%wide.region_2.5_spmd.clone.sunk.clone | while | flops 563084288 | bytes 33335480 | solution.py:170
  279.8 89.0 %all-gather.16.cloned.1.call-done = bf16[1024,4096]{1,0:T(8,128)(2,1)} async-done(((bf16[128,4096]{1,0:T(8,128)(2,1)}), bf16[1024,4096]{1,0:T(8,128)(2,1)}) %all-gather.16.cloned.1.call-update) | async-done | bytes 8388624 | tf_op jit(solution)/shard_map/all_gather | solution.py:112
  368.8 10.4 fusion.52
  379.2 114.8 %all-gather.18.cloned.1.call-done = bf16[1024,4096]{1,0:T(8,128)(2,1)} async-done(((bf16[128,4096]{1,0:T(8,128)(2,1)}), bf16[1024,4096]{1,0:T(8,128)(2,1)}) %all-gather.18.cloned.1.call-update) | async-done | bytes 8388624 | tf_op jit(solution)/shard_map/all_gather | solution.py:113
  494.1 28.5 %convert_reduce_fusion = (f32[4096]{0:T(1024)}, bf16[512,4096]{1,0:T(8,128)(2,1)S(1)}, f32[512,4096]{1,0:T(8,128)}) fusion(f32[512,4096]{1,0:T(8,128)} %fusion.52, f32[4096]{0:T(1024)S(1)} %bitcast.218, bf16[512,1024]{1,0:T(8,128)(2,1)S(1)} %copy-done.11, bf16[1024,4096]{1,0:T(8,128)(2,1)} %all-gather.18.cloned.1.call-done), kind=kOutput, calls=%fused_computation.39 | convolution fusion | flops 4452249600 | bytes 30441472 | tf_op jit(solution)/shard_map/dot_general | solution.py:187
  522.6 5.5 multiply_reduce_fusion.2
  532.4 175.1 %while.31 = (s32[]{:T(128)}, f32[8,512,128]{1,2,0:T(8,128)}, f32[8,2048,128]{1,2,0:T(8,128)}, f32[8,2048,128]{1,2,0:T(8,128)}, s32[8]{0:T(128)S(1)}, /*index=5*/...) while((s32[]{:T(128)}, f32[8,512,128]{1,2,0:T(8,128)}, ...), condition=%wide.region_12.13_spmd.clone.clone, body=%wide.region_10.12_spmd.clone.sunk.clone | while | flops 1375009792 | bytes 79206648 | solution.py:227
  708.3 4.9 fusion.68
  713.2 10.0 fusion.51
  723.2 10.1 multiply_convert_fusion.1
  733.3 10.5 convolution_bitcast_fusion
  743.8 33.2 %reduce-scatter.4.cloned.1.call-done = f32[512,1024]{0,1:T(8,128)} async-done(((f32[2048,1024]{0,1:T(8,128)}), f32[512,1024]{0,1:T(8,128)}) %reduce-scatter.4.cloned.1.call-update) | async-done | bytes 2097168 | tf_op jit(solution)/shard_map/reduce_scatter | solution.py:232
  782.1 68.8 %reduce-scatter.6.cloned.1.call-done = f32[512,1024]{0,1:T(8,128)} async-done(((f32[2048,1024]{0,1:T(8,128)}), f32[512,1024]{0,1:T(8,128)}) %reduce-scatter.6.cloned.1.call-update) | async-done | bytes 2097168 | tf_op jit(solution)/shard_map/reduce_scatter | solution.py:233
  853.7 9.8 fusion.46
  863.5 33.2 %pad_maximum_fusion = f32[1024,12288]{1,0:T(8,128)} fusion(f32[1024,4096]{1,0:T(8,128)} %convolution_bitcast_fusion, f32[1024,4096]{1,0:T(8,128)} %fusion.51, f32[1024,1024]{1,0:T(8,128)} %fusion.68, f32[1024,3072]{1,0:T(8,128)} %fusion.46), kind=kLoop, calls=%fused_computation.35 | loop fusion | flops 37748736 | bytes 100663296 | tf_op jit(solution)/shard_map/concatenate | solution.py:265
  896.8 786.1 %reduce-scatter.8.cloned.1.call-done = f32[128,12288]{1,0:T(8,128)} async-done(((f32[1024,12288]{1,0:T(8,128)}), f32[128,12288]{1,0:T(8,128)}) %reduce-scatter.8.cloned.1.call-update) | async-done | bytes 6291472 | tf_op jit(solution)/shard_map/reduce_scatter | solution.py:264
  1686.5 7.6 fusion.53
  1697.8 13.9 psum.30
  1711.8 93.2 %all-reduce.3.cloned.1.call-done = f32[128,12288]{1,0:T(8,128)} async-done(((f32[128,12288]{1,0:T(8,128)}), f32[128,12288]{1,0:T(8,128)}) %all-reduce.3.cloned.1.call-update) | async-done | bytes 6291472 | tf_op jit(solution)/shard_map/psum | solution.py:278
  1804.9 5.2 multiply_reduce_fusion.1
  1810.1 9.0 add_convert_fusion.2
  1819.1 39.3 %all-reduce = (f32[]{:T(128)}, f32[13,1024]{1,0:T(8,128)S(1)}) all-reduce(f32[]{:T(128)} %multiply_reduce_fusion.1, f32[13,1024]{1,0:T(8,128)S(1)} %psum.30), channel_id=1, replica_groups=mesh['wide'=8,'narrow'=4] {'wide'}, use_global_device_ids=true, to_apply=%region_20.21 | all-reduce | flops 13313 | bytes 106504 | tf_op jit(solution)/shard_map/psum | solution.py:280
  1864.4 5.6 multiply_subtract_fusion.2
  1871.0 7.6 multiply_subtract_fusion
  (391 shorter events, 288.0 us)
Async XLA Ops:
  7.2 33.3 %copy-start = (bf16[512,1024]{1,0:T(8,128)(2,1)S(1)}, bf16[512,1024]{1,0:T(8,128)(2,1)}, u32[]{:S(2)}) copy-start(bf16[512,1024]{1,0:T(8,128)(2,1)} %param.25) | copy-start | bytes 3145732
  7.2 105.3 %all-gather.8.cloned.1.call-start = ((), (), s32[]{:S(2)}) async-start(), calls=%async_computation.3 | async-start | bytes 7077888 | tf_op jit(solution)/shard_map/all_gather | solution.py:110
  9.7 145.2 %all-gather.10.cloned.1.call-start = ((), (), s32[]{:S(2)}) async-start(), calls=%async_computation.4 | async-start | bytes 5242880 | tf_op jit(solution)/shard_map/all_gather | solution.py:136
  40.5 77.8 %copy-start.27 = (f32[512]{0:T(512)}, f32[512]{0:T(512)S(1)}, u32[]{:S(2)}) copy-start(f32[512]{0:T(512)S(1)} %broadcast_multiply_fusion.1) | copy-start | bytes 6148
  41.5 76.8 %copy-start.31 = (f32[512]{0:T(512)}, f32[512]{0:T(512)S(1)}, u32[]{:S(2)}) copy-start(f32[512]{0:T(512)S(1)} %fusion.40) | copy-start | bytes 6148
  42.1 76.2 %copy-start.24 = (f32[1,1024]{1,0:T(1,128)}, f32[1,1024]{1,0:T(1,128)S(1)}, u32[]{:S(2)}) copy-start(f32[1,1024]{1,0:T(1,128)S(1)} %get-tuple-element.343) | copy-start | bytes 12292
  42.1 76.2 %copy-start.41 = (f32[1,1024]{1,0:T(1,128)}, f32[1,1024]{1,0:T(1,128)S(1)}, u32[]{:S(2)}) copy-start(f32[1,1024]{1,0:T(1,128)S(1)} %get-tuple-element.344) | copy-start | bytes 12292
  42.1 326.7 %copy-start.43 = (f32[1,1024]{1,0:T(1,128)}, f32[1,1024]{1,0:T(1,128)S(1)}, u32[]{:S(2)}) copy-start(f32[1,1024]{1,0:T(1,128)S(1)} %get-tuple-element.341) | copy-start | bytes 12292
  122.1 69.5 %all-gather.12.cloned.1.call-start = ((), (), s32[]{:S(2)}) async-start(), calls=%async_computation.5 | async-start | bytes 5242880 | tf_op jit(solution)/shard_map/all_gather | solution.py:135
  136.8 138.1 %all-gather.14.cloned.1.call-start = ((), (), s32[]{:S(2)}) async-start(), calls=%async_computation.6 | async-start | bytes 2359296 | tf_op jit(solution)/shard_map/all_gather | solution.py:111
  138.7 230.2 %all-gather.16.cloned.1.call-start = ((), (), s32[]{:S(2)}) async-start(), calls=%async_computation.7 | async-start | bytes 9437184 | tf_op jit(solution)/shard_map/all_gather | solution.py:112
  139.9 354.2 %all-gather.18.cloned.1.call-start = ((), (), s32[]{:S(2)}) async-start(), calls=%async_computation.8 | async-start | bytes 9437184 | tf_op jit(solution)/shard_map/all_gather | solution.py:113
  142.7 634.4 %reduce-scatter.4.cloned.1.call-start = ((), (), s32[]{:S(2)}) async-start(), calls=%async_computation.9 | async-start | bytes 10485760 | tf_op jit(solution)/shard_map/reduce_scatter | solution.py:232
  368.8 125.2 %copy-start.11 = (bf16[512,1024]{1,0:T(8,128)(2,1)S(1)}, bf16[512,1024]{1,0:T(8,128)(2,1)}, u32[]{:S(2)}) copy-start(bf16[512,1024]{1,0:T(8,128)(2,1)} %param.26) | copy-start | bytes 3145732
  707.5 143.5 %reduce-scatter.6.cloned.1.call-start = ((), (), s32[]{:S(2)}) async-start(), calls=%async_computation.10 | async-start | bytes 10485760 | tf_op jit(solution)/shard_map/reduce_scatter | solution.py:233
  708.2 974.6 %reduce-scatter.8.cloned.1.call-start = ((), (), s32[]{:S(2)}) async-start(), calls=%async_computation.11 | async-start | bytes 56623104 | tf_op jit(solution)/shard_map/reduce_scatter | solution.py:264
  733.3 43.8 %copy-start.20 = (f32[512,32]{0,1:T(8,128)S(1)}, f32[512,32]{0,1:T(8,128)}, u32[]{:S(2)}) copy-start(f32[512,32]{0,1:T(8,128)} %copy-done.19) | copy-start | bytes 196612
  733.3 43.8 %copy-start.22 = (f32[512,32]{0,1:T(8,128)S(1)}, f32[512,32]{0,1:T(8,128)}, u32[]{:S(2)}) copy-start(f32[512,32]{0,1:T(8,128)} %copy-done.21) | copy-start | bytes 196612
  780.0 73.7 %copy-start.1 = (bf16[512,1024]{1,0:T(8,128)(2,1)S(1)}, bf16[512,1024]{1,0:T(8,128)(2,1)}, u32[]{:S(2)}) copy-start(bf16[512,1024]{1,0:T(8,128)(2,1)} %param.25) | copy-start | bytes 3145732
  780.0 73.7 %copy-start.25 = (f32[1,1024]{1,0:T(1,128)S(1)}, f32[1,1024]{1,0:T(1,128)}, u32[]{:S(2)}) copy-start(f32[1,1024]{1,0:T(1,128)} %copy-done.24) | copy-start | bytes 12292
  780.0 73.7 %copy-start.28 = (f32[512]{0:T(512)S(1)}, f32[512]{0:T(512)}, u32[]{:S(2)}) copy-start(f32[512]{0:T(512)} %copy-done.27) | copy-start | bytes 6148
  780.0 73.7 %copy-start.32 = (f32[512]{0:T(512)S(1)}, f32[512]{0:T(512)}, u32[]{:S(2)}) copy-start(f32[512]{0:T(512)} %copy-done.31) | copy-start | bytes 6148
  780.0 73.7 %copy-start.42 = (f32[1,1024]{1,0:T(1,128)S(1)}, f32[1,1024]{1,0:T(1,128)}, u32[]{:S(2)}) copy-start(f32[1,1024]{1,0:T(1,128)} %copy-done.41) | copy-start | bytes 12292
  896.7 787.0 %copy-start.36 = (f32[4096]{0:T(1024)S(1)}, f32[4096]{0:T(1024)}, u32[]{:S(2)}) copy-start(f32[4096]{0:T(1024)} %get-tuple-element.305) | copy-start | bytes 49156
  896.8 908.2 %all-reduce.3.cloned.1.call-start = ((), (), s32[]{:S(2)}) async-start(), calls=%async_computation.12 | async-start | bytes 12582912 | tf_op jit(solution)/shard_map/psum | solution.py:278
  1697.8 112.3 %copy-start.40 = (f32[1,1024]{1,0:T(1,128)S(1)}, f32[1,1024]{1,0:T(1,128)}, u32[]{:S(2)}) copy-start(f32[1,1024]{1,0:T(1,128)} %get-tuple-element.339) | copy-start | bytes 12292
  1810.1 50.9 %copy-start.26 = (f32[13,128]{1,0:T(8,128)S(1)}, f32[13,128]{1,0:T(8,128)}, u32[]{:S(2)}) copy-start(f32[13,128]{1,0:T(8,128)} %param.35) | copy-start | bytes 19972
  1810.1 50.9 %copy-start.38 = (f32[13,128]{1,0:T(8,128)S(1)}, f32[13,128]{1,0:T(8,128)}, u32[]{:S(2)}) copy-start(f32[13,128]{1,0:T(8,128)} %param.45) | copy-start | bytes 19972
  1810.1 50.9 %copy-start.39 = (f32[13,128]{1,0:T(8,128)S(1)}, f32[13,128]{1,0:T(8,128)}, u32[]{:S(2)}) copy-start(f32[13,128]{1,0:T(8,128)} %param.40) | copy-start | bytes 19972
  1810.1 51.5 %copy-start.15 = (f32[128,1024]{1,0:T(8,128)S(1)}, f32[128,1024]{1,0:T(8,128)}, u32[]{:S(2)}) copy-start(f32[128,1024]{1,0:T(8,128)} %param.32) | copy-start | bytes 1572868
  1810.1 51.5 %copy-start.23 = (f32[128,1024]{1,0:T(8,128)S(1)}, f32[128,1024]{1,0:T(8,128)}, u32[]{:S(2)}) copy-start(f32[128,1024]{1,0:T(8,128)} %param.42) | copy-start | bytes 1572868
  1819.1 45.3 %copy-start.7 = (f32[128,3072]{1,0:T(8,128)S(1)}, f32[128,3072]{1,0:T(8,128)}, u32[]{:S(2)}) copy-start(f32[128,3072]{1,0:T(8,128)} %param.31) | copy-start | bytes 4718596
  (32 other events, 174.2 us)
Sparse Core Ops, SparseCore 0:
  10.8 101.7 all-gather.7
  122.3 32.6 all-gather.9
  157.1 34.4 all-gather.11
  194.2 49.1 all-gather.13
  245.9 122.9 all-gather.15
  371.4 122.6 all-gather.17
  707.6 69.4 reduce-scatter.3
  779.6 71.2 reduce-scatter.5
  896.9 785.9 reduce-scatter.7
  1685.1 119.7 all-reduce.2
where the time goes:
time: 1890 us
  waiting for transfers between devices  1290 us (68%)
  matrix products  217 us (11%)
  other arithmetic  148 us (8%)
  local copies, waits for them, and re-layouts  96.9 us (5%)
  blocking collectives  87.4 us (5%)
  loops' own time  27.1 us (1%)
    reduce_scatter x1, waiting for transfers between devices, on_device(): lax.psum_scatter(jnp.concatenate([part_term(normed1_b, grad_proj_b), part...  786 us
    all_gather x1, waiting for transfers between devices, on_device(): lax.all_gather(down_low, 'wide', axis=0, tiled=True)  115 us
    psum x1, waiting for transfers between devices, on_device(): matrix_total, vector_group = lax.psum((matrix_part, vector_part), 'narrow')  93.2 us
    all_gather x1, waiting for transfers between devices, on_device(): lax.all_gather(up_low, 'wide', axis=0, tiled=True)  89 us
    all_gather x1, waiting for transfers between devices, on_device(): lax.all_gather(qkv_low, 'wide', axis=0, tiled=True)  70.4 us
    reduce_scatter x1, waiting for transfers between devices, on_device(): lax.psum_scatter(grad_values_all, 'narrow', scatter_dimension=0, tiled=True)  68.8 us
    dynamic_slice x56, local copies, waits for them, and re-layouts, take_pair(): lax.dynamic_slice_in_dim(source, index * pair_width, pair_width, 1)  43.4 us
    psum x1, blocking collectives, on_device(): lax.psum((vector_group, matrix_squares), 'wide')  39.3 us
  transfers between devices with their start and end apart: 10, of which 9 were waited for; matrix products, arithmetic and copies ran while one was open for 9% of the time, Pallas kernels for 0%

commit v1 on v0

v1 whole, which is shorter than its diff:
```python
import functools

import jax
import jax.numpy as jnp
from jax import lax
from jax.experimental import pallas as pl
from jax.experimental.pallas import tpu as pltpu
from jax.sharding import PartitionSpec as P

HEADS = 16
BLOCK = 256
BF = jnp.bfloat16
F32 = jnp.float32


def dot(a, b, ca, cb):
    return lax.dot_general(a, b, (((ca,), (cb,)), ((), ())), preferred_element_type=F32)


def swap_halves(x, half):
    lane = lax.broadcasted_iota(jnp.int32, x.shape, 1)
    width = x.shape[1]
    return jnp.where(
        lane % (2 * half) < half, pltpu.roll(x, width - half, 1), pltpu.roll(x, half, 1)
    )


def turn(x, cosine, sine, half, sign):
    parts = []
    for start in range(0, x.shape[1], 128):
        part = x[:, start : start + 128]
        other = swap_halves(part, half) * sine
        parts.append(part * cosine + other if sign > 0 else part * cosine - other)
    return jnp.concatenate(parts, axis=1)


def rotary_table(head_dim):
    half = head_dim // 2
    lane = jnp.arange(128)
    pair = lane % half
    rates = jnp.power(10000.0, -(pair // 3).astype(F32) / ((half + 2) // 3))
    row = jnp.arange(128)
    axis = row // 14
    value = (row % 14).astype(F32)
    live = (axis[:, None] == (pair % 3)[None, :]) & (row[:, None] < 42)
    angle = value[:, None] * rates[None, :]
    signs = jnp.where(lane % head_dim < half, -1.0, 1.0)
    return jnp.concatenate(
        [
            jnp.where(live, jnp.cos(angle), 0.0),
            jnp.where(live, jnp.sin(angle) * signs[None, :], 0.0),
        ],
        axis=1,
    )


def qkv_kernel(half, x_ref, w_ref, bias_ref, onehot_ref, table_ref, q_ref, k_ref, v_ref, turn_ref):
    width = q_ref.shape[1]
    angles = lax.dot_general(
        onehot_ref[...],
        table_ref[...],
        (((1,), (0,)), ((), ())),
        precision=lax.Precision.HIGHEST,
        preferred_element_type=F32,
    )
    turn_ref[...] = angles
    cosine, sine = angles[:, :128], angles[:, 128:]
    proj = dot(x_ref[...], w_ref[...], 1, 0) + bias_ref[...]
    q_ref[...] = turn(proj[:, :width], cosine, sine, half, 1).astype(BF)
    k_ref[...] = turn(proj[:, width : 2 * width], cosine, sine, half, 1).astype(BF)
    v_ref[...] = proj[:, 2 * width :].astype(BF)


def qkv_call(x, w, bias, onehot, table, half):
    rows, depth = x.shape
    width = w.shape[1] // 3
    out = jax.ShapeDtypeStruct((rows, width), BF)
    row_block = lambda cols: pl.BlockSpec((BLOCK, cols), lambda i: (i, 0))
    whole = lambda a: pl.BlockSpec(a.shape, lambda i: (0, 0))
    return pl.pallas_call(
        functools.partial(qkv_kernel, half),
        grid=(rows // BLOCK,),
        in_specs=[row_block(depth), whole(w), whole(bias), row_block(128), whole(table)],
        out_specs=[row_block(width)] * 3 + [row_block(256)],
        out_shape=[out, out, out, jax.ShapeDtypeStruct((rows, 256), F32)],
        cost_estimate=pl.CostEstimate(
            flops=2 * rows * depth * 3 * width, bytes_accessed=rows * depth * 4, transcendentals=0
        ),
        name="qkv",
    )(x, w, bias, onehot, table)


def head_lanes(shape, head, head_dim):
    lane = lax.broadcasted_iota(jnp.int32, shape, 1)
    return lane // head_dim == head


def forward_kernel(
    heads, head_dim, low_ref, high_ref, q_ref, k_ref, v_ref, seg_ref, tag_ref, o_ref, lse_ref, acc, peak, total
):
    step = pl.program_id(0)
    query = q_ref[...] * jnp.asarray(head_dim**-0.5, BF)
    seg = seg_ref[...]
    masked_query = [
        jnp.where(head_lanes(query.shape, h, head_dim), query, jnp.zeros_like(query)) for h in range(heads)
    ]
    acc[...] = jnp.zeros_like(acc)
    peak[...] = jnp.full_like(peak, -1e30)
    total[...] = jnp.zeros_like(total)

    def body(j, carry):
        start = pl.multiple_of(j * BLOCK, BLOCK)
        key = k_ref[pl.ds(start, BLOCK), :]
        value = v_ref[pl.ds(start, BLOCK), :]
        allowed = seg == tag_ref[pl.ds(j, 1), :]
        for h in range(heads):
            scores = jnp.where(allowed, dot(masked_query[h], key, 1, 1), -1e30)
            old = peak[h]
            new = jnp.maximum(old, jnp.max(scores, axis=1, keepdims=True))
            probs = jnp.exp(scores - new[:, :1])
            keep = jnp.exp(old - new)
            peak[h] = new
            total[h] = total[h] * keep + jnp.sum(probs, axis=1, keepdims=True)
            acc[h] = acc[h] * keep[:, :1] + dot(probs.astype(BF), value, 1, 0)
        return carry

    lax.fori_loop(low_ref[step], high_ref[step], body, 0)
    out = jnp.zeros(o_ref.shape, F32)
    stats = jnp.zeros((BLOCK, 128), F32)
    for h in range(heads):
        out = jnp.where(head_lanes(out.shape, h, head_dim), acc[h] / total[h][:, :1], out)
        lane = lax.broadcasted_iota(jnp.int32, stats.shape, 1)
        stats = jnp.where(lane == h, peak[h] + jnp.log(total[h]), stats)
    o_ref[...] = out.astype(BF)
    lse_ref[...] = stats.T[:8, :]


def forward_call(low, high, q, k, v, seg_col, tag_rows, head_dim):
    rows, width = q.shape
    heads = width // head_dim
    whole = lambda a: pl.BlockSpec(a.shape, lambda i, *_: (0, 0))
    grid_spec = pltpu.PrefetchScalarGridSpec(
        num_scalar_prefetch=2,
        grid=(rows // BLOCK,),
        in_specs=[
            pl.BlockSpec((BLOCK, width), lambda i, *_: (i, 0)),
            whole(k),
            whole(v),
            pl.BlockSpec((BLOCK, 1), lambda i, *_: (i, 0)),
            whole(tag_rows),
        ],
        out_specs=[
            pl.BlockSpec((BLOCK, width), lambda i, *_: (i, 0)),
            pl.BlockSpec((8, BLOCK), lambda i, *_: (0, i)),
        ],
        scratch_shapes=[
            pltpu.VMEM((heads, BLOCK, width), F32),
            pltpu.VMEM((heads, BLOCK, 128), F32),
            pltpu.VMEM((heads, BLOCK, 128), F32),
        ],
    )
    return pl.pallas_call(
        functools.partial(forward_kernel, heads, head_dim),
        grid_spec=grid_spec,
        out_shape=[jax.ShapeDtypeStruct((rows, width), BF), jax.ShapeDtypeStruct((8, rows), F32)],
        cost_estimate=pl.CostEstimate(
            flops=heads * rows * rows * width * 3, bytes_accessed=rows * width * 8, transcendentals=heads * rows * rows
        ),
        name="attention_forward",
    )(low, high, q, k, v, seg_col, tag_rows)


def backward_kernel(
    heads, head_dim, low_ref, high_ref, q_ref, k_ref, v_ref, o_ref, g_ref, lse_ref, seg_ref, tag_ref, turn_ref,
    out_ref, q_heads, g_heads, delta, grad_query,
):
    step = pl.program_id(0)
    rows, width = q_ref.shape
    scale = head_dim**-0.5
    half = head_dim // 2

    @pl.when(step == 0)
    def _():
        grad_query[...] = jnp.zeros_like(grad_query)
        row = lax.broadcasted_iota(jnp.int32, (8, width), 0)
        lane = lax.broadcasted_iota(jnp.int32, (8, width), 1)
        pick = jnp.where(lane // head_dim == row, 1.0, 0.0)

        def prepare(i, carry):
            at = pl.ds(pl.multiple_of(i * BLOCK, BLOCK), BLOCK)
            query = q_ref[at, :] * jnp.asarray(scale, BF)
            grad = g_ref[at, :]
            for h in range(heads):
                lanes = head_lanes(query.shape, h, head_dim)
                q_heads[h, at, :] = jnp.where(lanes, query, jnp.zeros_like(query))
                g_heads[h, at, :] = jnp.where(lanes, grad, jnp.zeros_like(grad))
            product = grad.astype(F32) * o_ref[at, :].astype(F32)
            delta[pl.ds(i, 1)] = lax.dot_general(
                pick,
                product,
                (((1,), (1,)), ((), ())),
                precision=lax.Precision.HIGHEST,
                preferred_element_type=F32,
            )[None]
            return carry

        lax.fori_loop(0, rows // BLOCK, prepare, 0)

    key = k_ref[...]
    value = v_ref[...]
    tag = tag_ref[...]
    masked_key = [jnp.where(head_lanes(key.shape, h, head_dim), key, jnp.zeros_like(key)) for h in range(heads)]

    def body(i, carry):
        grad_key, grad_value = carry
        at = pl.ds(pl.multiple_of(i * BLOCK, BLOCK), BLOCK)
        allowed = tag == seg_ref[pl.ds(i, 1), :]
        lse = lse_ref[pl.ds(i, 1)][0]
        dlt = delta[pl.ds(i, 1)][0]
        total = None
        for h in range(heads):
            query = q_heads[h, at, :]
            grad = g_heads[h, at, :]
            scores = dot(key, query, 1, 1)
            probs = jnp.where(allowed, jnp.exp(scores - lse[h : h + 1, :]), 0.0)
            grad_probs = dot(value, grad, 1, 1)
            grad_scores = (probs * (grad_probs - dlt[h : h + 1, :])).astype(BF)
            grad_value = grad_value + dot(probs.astype(BF), grad, 1, 0)
            grad_key = grad_key + dot(grad_scores, query, 1, 0)
            term = dot(grad_scores, masked_key[h], 0, 0)
            total = term if total is None else total + term
        grad_query[at, :] += total
        return grad_key, grad_value

    zero = jnp.zeros((BLOCK, width), F32)
    grad_key, grad_value = lax.fori_loop(low_ref[step], high_ref[step], body, (zero, zero))
    here = pl.ds(pl.multiple_of(step * BLOCK, BLOCK), BLOCK)
    cosine, sine = turn_ref[here, :128], turn_ref[here, 128:]
    out_ref[here, width : 2 * width] = turn(grad_key, cosine, sine, half, -1).astype(BF)
    out_ref[here, 2 * width :] = grad_value.astype(BF)

    @pl.when(step == pl.num_programs(0) - 1)
    def _():
        def finish(i, carry):
            at = pl.ds(pl.multiple_of(i * BLOCK, BLOCK), BLOCK)
            grads = grad_query[at, :] * scale
            out_ref[at, :width] = turn(grads, turn_ref[at, :128], turn_ref[at, 128:], half, -1).astype(BF)
            return carry

        lax.fori_loop(0, rows // BLOCK, finish, 0)


def backward_call(low, high, q, k, v, o, g, lse, seg_rows, tag_col, turns, head_dim):
    rows, width = q.shape
    heads = width // head_dim
    blocks = rows // BLOCK
    lse = jnp.moveaxis(lse.reshape(8, blocks, BLOCK), 1, 0)
    whole = lambda a: pl.BlockSpec(a.shape, lambda i, *_: (0,) * a.ndim)
    block = pl.BlockSpec((BLOCK, width), lambda i, *_: (i, 0))
    grid_spec = pltpu.PrefetchScalarGridSpec(
        num_scalar_prefetch=2,
        grid=(blocks,),
        in_specs=[
            whole(q), block, block, whole(o), whole(g), whole(lse), whole(seg_rows),
            pl.BlockSpec((BLOCK, 1), lambda i, *_: (i, 0)),
            whole(turns),
        ],
        out_specs=pl.BlockSpec((rows, 3 * width), lambda i, *_: (0, 0)),
        scratch_shapes=[
            pltpu.VMEM((heads, rows, width), BF),
            pltpu.VMEM((heads, rows, width), BF),
            pltpu.VMEM((blocks, 8, BLOCK), F32),
            pltpu.VMEM((rows, width), F32),
        ],
    )
    return pl.pallas_call(
        functools.partial(backward_kernel, heads, head_dim),
        grid_spec=grid_spec,
        out_shape=jax.ShapeDtypeStruct((rows, 3 * width), BF),
        cost_estimate=pl.CostEstimate(
            flops=heads * rows * rows * width * 7, bytes_accessed=rows * width * 20, transcendentals=heads * rows * rows
        ),
        name="attention_backward",
    )(low, high, q, k, v, o, g, lse, seg_rows, tag_col, turns)


def norm_parts(values):
    center = values - jnp.mean(values, axis=-1, keepdims=True)
    inverse = lax.rsqrt(jnp.mean(center * center, axis=-1, keepdims=True) + 1e-06)
    return center * inverse, inverse


def norm_back(grads, gain, unit, inverse):
    scaled = grads * gain
    return inverse * (
        scaled - jnp.mean(scaled, axis=-1, keepdims=True) - unit * jnp.mean(scaled * unit, axis=-1, keepdims=True)
    )


def adamw(param, grad, first, second, clip, rate, decay, fix_first, fix_second):
    clipped = grad * clip
    moment = 0.9 * first + 0.1 * clipped
    square = 0.999 * second + 0.001 * clipped * clipped
    direction = moment / fix_first / (jnp.sqrt(square / fix_second) + 1e-08)
    return (param - rate * (direction + decay * param), moment, square)


def on_device(
    tokens, cotangent, segment_ids, key_keep, patch_coords, step_count,
    weight_qkv, weight_out, weight_up, weight_down, vectors,
    first_qkv, first_out, first_up, first_down, first_vectors,
    second_qkv, second_out, second_up, second_down, second_vectors,
):
    rows, width = tokens.shape
    hidden = weight_up.shape[1]
    head_dim = width // HEADS
    narrow = lax.axis_size("narrow")
    wide = lax.axis_size("wide")
    shard_rows = width // wide
    me = lax.axis_index("narrow")
    side = me % 2
    mine = width // narrow
    half_hidden = hidden // 2
    group = rows * narrow

    def mate(value):
        return lax.ppermute(value, "narrow", [(i, i ^ 1) for i in range(narrow)])

    def across(value):
        return lax.ppermute(value, "narrow", [(i, i ^ 2) for i in range(narrow)])

    def take(value, start, size, axis=1):
        return lax.dynamic_slice_in_dim(value, start, size, axis)

    qkv_low = jnp.concatenate([take(weight_qkv, i * width + me * mine, mine) for i in range(3)], axis=1).astype(BF)
    out_low = weight_out.astype(BF)
    up_low = take(weight_up, side * half_hidden, half_hidden).astype(BF)
    down_low = take(weight_down, side * half_hidden, half_hidden).astype(BF)

    vec = lax.all_gather(vectors.astype(BF), "wide", axis=1, tiled=True).astype(F32)
    qkv_w = lax.all_gather(qkv_low, "wide", axis=0, tiled=True)
    out_w = lax.all_gather(out_low, "wide", axis=0, tiled=True)
    up_w = lax.all_gather(up_low, "wide", axis=0, tiled=True)
    down_w = lax.all_gather(down_low, "wide", axis=0, tiled=True)

    xin = tokens.astype(F32)
    unit1, inverse1 = norm_parts(xin)
    normed1 = (unit1 * vec[0] + vec[1]).astype(BF)
    normed1_all = lax.all_gather(normed1, "narrow", axis=0, tiled=True)
    tag = jnp.concatenate([segment_ids[None], key_keep[None], patch_coords], axis=0)
    tag_all = lax.all_gather(tag, "narrow", axis=1, tiled=True)
    cot_pair = jnp.concatenate([cotangent, mate(cotangent)], axis=0)

    seg = tag_all[0]
    seg_float = seg.astype(F32)
    key_tag = jnp.where(tag_all[1] == 1, seg, -1).astype(F32)
    slot = jnp.arange(128)[None, :]
    place = tag_all[2:5]
    onehot = (
        (slot == place[0][:, None]) | (slot == 14 + place[1][:, None]) | (slot == 28 + place[2][:, None])
    ).astype(F32)
    blocks = group // BLOCK
    seg_rows = seg.reshape(blocks, BLOCK)
    low = jnp.sum(seg[None, :] < seg_rows[:, :1], axis=1, dtype=jnp.int32) // BLOCK
    high = (jnp.sum(seg[None, :] <= seg_rows[:, -1:], axis=1, dtype=jnp.int32) + BLOCK - 1) // BLOCK

    bias = jnp.concatenate([take(vec[2 + i : 3 + i], me * mine, mine) for i in range(3)], axis=1)
    query, keys, values, turns = qkv_call(normed1_all, qkv_w, bias, onehot, rotary_table(head_dim), head_dim // 2)
    mixed_mine, lse = forward_call(
        low, high, query, keys, values, seg_float[:, None], key_tag.reshape(blocks, BLOCK), head_dim
    )
    mixed = lax.all_to_all(mixed_mine, "narrow", 0, 1, tiled=True)

    resid = xin + (dot(mixed, out_w, 1, 0) + vec[5])
    unit2, inverse2 = norm_parts(resid)
    normed2 = (unit2 * vec[6] + vec[7]).astype(BF)
    normed2_pair = jnp.concatenate([normed2, mate(normed2)], axis=0)
    up_bias = take(vec[9:].reshape(1, -1), side * half_hidden, half_hidden)
    up_pre = dot(normed2_pair, up_w, 1, 0) + up_bias
    erf_part = 0.5 * (1.0 + lax.erf(up_pre * (0.5**0.5)))
    act = (up_pre * erf_part).astype(BF)
    slope = erf_part + up_pre * (jnp.exp(-0.5 * up_pre * up_pre) * ((2.0 * jnp.pi) ** -0.5))
    down_part = dot(act, down_w, 1, 1)
    down = down_part[:rows] + mate(down_part[rows:])
    layer_out = (resid + (down + vec[8])).astype(BF)

    part_down = dot(cot_pair, act, 0, 0).astype(BF)
    grad_down = lax.psum_scatter(part_down, "wide", scatter_dimension=0, tiled=True)
    grad_up_act = (dot(cot_pair, down_w, 1, 0) * slope).astype(BF)
    part_up = dot(normed2_pair, grad_up_act, 0, 0).astype(BF)
    grad_up = lax.psum_scatter(part_up, "wide", scatter_dimension=0, tiled=True)
    grad_normed2_part = dot(grad_up_act, up_w, 1, 1)
    grad_normed2 = grad_normed2_part[:rows] + mate(grad_normed2_part[rows:])
    cot = cotangent.astype(F32)
    grad_resid = cot + norm_back(grad_normed2, vec[6], unit2, inverse2)
    grad_branch = grad_resid.astype(BF)
    grad_mixed = dot(grad_branch, out_w, 1, 1).astype(BF)
    part_out = dot(mixed, grad_branch, 0, 0)
    own_out = take(part_out, side * (width // 2), width // 2)
    other_out = take(part_out, (1 - side) * (width // 2), width // 2)
    part_out = (own_out + mate(other_out.astype(BF)).astype(F32)).astype(BF)
    grad_out = lax.psum_scatter(part_out, "wide", scatter_dimension=0, tiled=True)

    grad_mixed_mine = lax.all_to_all(grad_mixed, "narrow", 1, 0, tiled=True)
    grad_proj = backward_call(
        low, high, query, keys, values, mixed_mine, grad_mixed_mine, lse, seg_float.reshape(blocks, BLOCK),
        key_tag[:, None], turns, head_dim,
    )
    part_qkv = dot(normed1_all, grad_proj, 0, 0).astype(BF)
    grad_qkv = lax.psum_scatter(part_qkv, "wide", scatter_dimension=0, tiled=True)
    grad_normed1_part = dot(grad_proj, qkv_w, 1, 1)
    grad_normed1 = lax.psum_scatter(grad_normed1_part.astype(BF), "narrow", scatter_dimension=0, tiled=True).astype(F32)
    grad_tokens = (grad_resid + norm_back(grad_normed1, vec[0], unit1, inverse1)).astype(BF)

    proj_sums = jnp.sum(grad_proj.astype(F32), axis=0).reshape(3, mine)
    proj_rows = lax.dynamic_update_slice(jnp.zeros((3, width), F32), proj_sums, (0, me * mine))
    up_sums = jnp.sum(grad_up_act.astype(F32), axis=0)
    up_rows = lax.dynamic_update_slice(jnp.zeros((hidden,), F32), up_sums, (side * half_hidden,))
    vector_part = jnp.concatenate(
        [
            jnp.sum(grad_normed1 * unit1, axis=0)[None],
            jnp.sum(grad_normed1, axis=0)[None],
            proj_rows,
            jnp.sum(grad_branch.astype(F32), axis=0)[None],
            jnp.sum(grad_normed2 * unit2, axis=0)[None],
            jnp.sum(grad_normed2, axis=0)[None],
            jnp.sum(cot, axis=0)[None],
            up_rows.reshape(hidden // width, width),
        ],
        axis=0,
    )

    def join(value):
        value = value.astype(F32)
        value = value + across(value)
        other = mate(value)
        first = jnp.where(side == 0, value, other)
        second = jnp.where(side == 0, other, value)
        return jnp.concatenate([first, second], axis=1)

    total_up = join(grad_up)
    total_down = join(grad_down)
    total_out = join(grad_out)
    quarters = lax.all_gather(grad_qkv, "narrow", axis=0)
    total_qkv = jnp.moveaxis(quarters.reshape(narrow, shard_rows, 3, mine), 0, 2).reshape(shard_rows, 3 * width)
    total_qkv = total_qkv.astype(F32)

    squares = sum(jnp.sum(g * g) for g in (total_qkv, total_out, total_up, total_down))
    vector_total = lax.psum(vector_part, ("wide", "narrow"))
    squares_total = lax.psum(squares, "wide")
    grad_norm = jnp.sqrt(squares_total + jnp.sum(vector_total * vector_total))
    clip = 1.0 / jnp.maximum(grad_norm, 1.0)
    count = step_count[0].astype(F32)
    rate = 0.4 * count / (count + 4.0)
    decay = 0.04 + 0.018 * count
    fix_first = 1.0 - jnp.power(0.9, count)
    fix_second = 1.0 - jnp.power(0.999, count)
    grad_vectors = take(vector_total, lax.axis_index("wide") * shard_rows, shard_rows)

    def update(param, grad, first, second, decay_here):
        return adamw(param, grad, first, second, clip, rate, decay_here, fix_first, fix_second)

    new_qkv = update(weight_qkv, total_qkv, first_qkv, second_qkv, decay)
    new_out = update(weight_out, total_out, first_out, second_out, decay)
    new_up = update(weight_up, total_up, first_up, second_up, decay)
    new_down = update(weight_down, total_down, first_down, second_down, decay)
    new_vectors = update(vectors, grad_vectors, first_vectors, second_vectors, 0.0)
    news = (new_qkv, new_out, new_up, new_down, new_vectors)
    return (layer_out, grad_tokens) + tuple(n[i] for i in range(3) for n in news) + (grad_norm, grad_vectors[8])


def solution(mesh):
    by_token = P(("wide", "narrow"), None)
    ids = P(("wide", "narrow"))
    by_row = P("wide", None)
    by_column = P(None, "wide")
    params = (by_row,) * 4 + (by_column,)
    return jax.shard_map(
        on_device,
        mesh=mesh,
        in_specs=(by_token, by_token, ids, ids, P(None, ("wide", "narrow")), P()) + params * 3,
        out_specs=(by_token, by_token) + params * 3 + (P(), P("wide")),
        check_vma=False,
    )
```

time: 1890 us -> 774 us (0.41)
  waiting for transfers between devices: 1290 us -> 271 us
  Pallas kernels: 0 us -> 152 us
  matrix products: 217 us -> 73.8 us
  other arithmetic: 148 us -> 70.6 us
  local copies, waits for them, and re-layouts: 96.9 us -> 62.7 us
  loops' own time: 27.1 us -> 0 us
    reduce_scatter x3 -> x5, waiting for transfers between devices: 888 us -> 129 us  [the longest x1 84.6 us: on_device(): lax.psum_scatter(part_down, 'wide', scatter_dimension=0, tiled=True)]
    all_gather x6 -> x5, waiting for transfers between devices: 309 us -> 98.6 us  [the longest x1 63.3 us: on_device(): down_w = lax.all_gather(down_low, 'wide', axis=0, tiled=True)]
    pallas_call x0 -> x3, Pallas kernels: none -> 152 us  [the longest x1 82.9 us: forward_call(): pl.pallas_call(functools.partial(forward_kernel, heads, head_dim), grid_s...]
    dot_general x68 -> x11, matrix products: 217 us -> 73.8 us  [dot(): lax.dot_general(a, b, (((ca,), (cb,)), ((), ())), preferred_element_type=...]
    psum x1 -> x0, waiting for transfers between devices: 93.2 us -> none  [on_device(): matrix_total, vector_group = lax.psum((matrix_part, vector_part), 'narrow')]
    dynamic_slice x72 -> x3, local copies, waits for them, and re-layouts: 52.8 us -> 0.01 us  [take(): return lax.dynamic_slice_in_dim(value, start, size, axis)]
    concatenate x5 -> x4, other arithmetic: 37.6 us -> 1.95 us  [the longest x1 0.69 us: on_device(): jnp.concatenate([take(weight_qkv, i * width + me * mine, mine) for i in r...]
    another operation x2 -> x0, loops' own time: 27.1 us -> none  [the longest x1 21.4 us: on_device(): query_parts, key_parts, value_parts = lax.map(backward_pair, pair_index)]
  transfers between devices with their start and end apart: 10 -> 23, of which waited for: 9 -> 11; matrix products, arithmetic and copies ran while one was open for 9% -> 17% of each run, Pallas kernels for 0% -> 20%
where the time goes in v1:
time: 774 us; the launch traced here: 767 us
  waiting for transfers between devices  271 us (35%)
  Pallas kernels  152 us (20%)
  blocking collectives  102 us (13%)
  matrix products  73.8 us (10%)
  other arithmetic  70.6 us (9%)
  local copies, waits for them, and re-layouts  62.7 us (8%)
  between operations  21.3 us (3%)
  starting transfers between devices  13.9 us (2%)
    reduce_scatter x1, waiting for transfers between devices, on_device(): lax.psum_scatter(part_down, 'wide', scatter_dimension=0, tiled=True)  84.6 us
    pallas_call x1, Pallas kernels, forward_call(): pl.pallas_call(functools.partial(forward_kernel, heads, head_dim), grid_s...  82.9 us
    dot_general x11, matrix products, dot(): lax.dot_general(a, b, (((ca,), (cb,)), ((), ())), preferred_element_type=...  73.8 us
    all_gather x1, waiting for transfers between devices, on_device(): down_w = lax.all_gather(down_low, 'wide', axis=0, tiled=True)  63.3 us
    pallas_call x1, Pallas kernels, backward_call(): pl.pallas_call(functools.partial(backward_kernel, heads, head_dim), grid_...  58.3 us
    reduce_scatter x1, waiting for transfers between devices, on_device(): lax.psum_scatter(part_qkv, 'wide', scatter_dimension=0, tiled=True)  39.9 us
    psum x1, blocking collectives, on_device(): vector_total = lax.psum(vector_part, ('wide', 'narrow'))  39.8 us
    unnamed x119, local copies, waits for them, and re-layouts  35.7 us
  transfers between devices with their start and end apart: 23, of which 11 were waited for; matrix products, arithmetic and copies ran while one was open for 17% of the time, Pallas kernels for 20%

profile of v1, /device:TPU:0, one launch (start us, length us, event | category | flops | bytes accessed | tf_op | source)
XLA Modules:
  0.0 766.7 jit_solution(2927642231745594330)
XLA Ops:
  9.9 27.9 %all_gather.28 = bf16[13,1024]{1,0:T(8,128)(2,1)S(1)} all-gather(bf16[13,128]{1,0:T(8,128)(2,1)S(1)} %convert_element_type.163), channel_id=1, replica_groups=mesh['wide'=8,'narrow'=4] {'wide'}, dimensions={1}, use_global_device_ids=true | all-gather | bytes 29952 | tf_op jit(solution)/shard_map/all_gather | solution.py:340
  46.5 5.2 all_gather.27
  58.8 34.0 %all-gather.7.cloned.1.call-done.x_ref = bf16[2048,1024]{1,0:T(8,128)(2,1)} async-done(((bf16[512,1024]{1,0:T(8,128)(2,1)}), bf16[2048,1024]{1,0:T(8,128)(2,1)}) %all-gather.7.cloned.1.call-update) | async-done | bytes 4194320 | tf_op jit(solution)/shard_map/all_gather | solution.py:349
  92.8 10.7 %qkv.1 = (bf16[2048,256]{1,0:T(8,128)(2,1)}, bf16[2048,256]{1,0:T(8,128)(2,1)}, bf16[2048,256]{1,0:T(8,128)(2,1)}, f32[2048,256]{1,0:T(8,128)}) custom-call(bf16[2048,1024]{1,0:T(8,128)(2,1)} %all-gather.7.cloned.1.call-done.x_ref, bf16[1024,768]{1,0:T(8,128)(2,1)} %all-gather.9.cloned.1.call-done.w_ref, f32[1,768]{1,0:T(1,128)} %pad_maximum_fusion.8.bias_ref, ...), custom_call_target="tpu_custom_call" | custom-call | flops 3221225472 | bytes 8388608 | tf_op jit(solution)/shard_map/qkv/pallas_call | solution.py:80
  103.5 82.9 %attention_forward.1 = (bf16[2048,256]{1,0:T(8,128)(2,1)}, f32[8,2048]{1,0:T(8,128)}) custom-call(s32[8]{0:T(128)} %get-tuple-element.143.low_ref, s32[8]{0:T(128)} %get-tuple-element.142.high_ref, bf16[2048,256]{1,0:T(8,128)(2,1)} %get-tuple-element.25.q_ref, bf16[2048,256]{1,0:T(8,128)(2,1)} %get-tuple-element.26.k_ref, ...), custom_call_target="tpu_custom_call" | custom-call | flops 12884901888 | bytes 4194304 | tf_op jit(solution)/shard_map/attention_forward/pallas_call | solution.py:162
  188.6 3.5 all-to-all-start
  192.9 13.6 %all-to-all-done = bf16[4,512,256]{1,2,0:T(8,128)(2,1)S(1)} async-done(((bf16[4,512,256]{1,2,0:T(8,128)(2,1)}), bf16[4,512,256]{1,2,0:T(8,128)(2,1)S(1)}, u32[]{:S(2)}, u32[]{:S(2)}) %all-to-all-start) | async-done | bytes 1048608 | tf_op jit(solution)/shard_map/all_to_all | solution.py:372
  207.5 3.3 fusion.55
  218.5 10.7 %multiply_convert_fusion = (bf16[1024,2048]{1,0:T(8,128)(2,1)}, f32[1024,2048]{1,0:T(8,128)}) fusion(f32[2048]{0:T(1024)S(1)} %bitcast.102, bf16[1024,2048]{1,0:T(8,128)(2,1)} %all-gather.13.cloned.1.call-done, bf16[512,1024]{1,0:T(8,128)(2,1)} %collective-permute-done, bf16[512,1024]{1,0:T(8,128)(2,1)} %add_convert_fusion.1), kind=kOutput, calls=%fused_computation.8 | convolution fusion | flops 4311744512 | bytes 18882560 | tf_op jit(solution)/shard_map/dot_general | solution.py:17
  229.2 63.3 %all-gather.15.cloned.1.call-done = bf16[1024,2048]{1,0:T(8,128)(2,1)} async-done(((bf16[128,2048]{1,0:T(8,128)(2,1)}), bf16[1024,2048]{1,0:T(8,128)(2,1)}) %all-gather.15.cloned.1.call-update) | async-done | bytes 4194320 | tf_op jit(solution)/shard_map/all_gather | solution.py:344
  292.4 10.6 %convert_reduce_fusion = (f32[2048]{0:T(1024)S(1)}, bf16[1024,2048]{1,0:T(8,128)(2,1)S(1)}) fusion(f32[1024,2048]{1,0:T(8,128)} %get-tuple-element.133, f32[2048]{0:T(1024)S(1)} %bitcast.103, bf16[1024,1024]{1,0:T(8,128)(2,1)} %constant_dynamic-update-slice_fusion, bf16[1024,2048]{1,0:T(8,128)(2,1)} %all-gather.15.cloned.1.call-done), kind=kOutput, calls=%fused_computation.7 | convolution fusion | flops 4322228224 | bytes 18890752 | tf_op jit(solution)/shard_map/dot_general | solution.py:17
  305.1 7.8 %convolution_convert_fusion.2 = bf16[1024,2048]{1,0:T(8,128)(2,1)} fusion(bf16[1024,2048]{1,0:T(8,128)(2,1)S(1)} %get-tuple-element.135, bf16[512,1024]{1,0:T(8,128)(2,1)} %collective-permute-done, bf16[512,1024]{1,0:T(8,128)(2,1)} %add_convert_fusion.1), kind=kOutput, calls=%fused_computation.13 | convolution fusion | flops 4301258752 | bytes 10485760 | tf_op jit(solution)/shard_map/dot_general | solution.py:17
  313.3 7.7 %fusion.57 = f32[1024,1024]{1,0:T(8,128)S(1)} fusion(bf16[1024,2048]{1,0:T(8,128)(2,1)} %copy-done.54, bf16[1024,2048]{1,0:T(8,128)(2,1)} %all-gather.13.cloned.1.call-done), kind=kOutput, calls=%fused_computation.179 | convolution fusion | flops 4294967296 | bytes 12582912 | tf_op jit(solution)/shard_map/dot_general | solution.py:17
  325.5 4.5 fusion.56
  332.7 4.0 multiply_reduce_fusion
  337.2 4.2 convert_reduce_fusion.5
  350.8 9.4 %convolution_convert_fusion.1 = bf16[1024,2048]{1,0:T(8,128)(2,1)} fusion(bf16[1024,1024]{1,0:T(8,128)(2,1)} %constant_dynamic-update-slice_fusion, bf16[1024,2048]{1,0:T(8,128)(2,1)} %get-tuple-element.132), kind=kOutput, calls=%fused_computation.12 | convolution fusion | flops 4297064448 | bytes 10485760 | tf_op jit(solution)/shard_map/dot_general | solution.py:17
  365.7 4.2 all-to-all-start.1
  371.4 13.1 %all-to-all-done.1 = bf16[512,4,256]{2,0,1:T(8,128)(2,1)} async-done(((bf16[512,4,256]{2,0,1:T(8,128)(2,1)}), bf16[512,4,256]{2,0,1:T(8,128)(2,1)}, u32[]{:S(2)}, u32[]{:S(2)}) %all-to-all-start.1) | async-done | bytes 1048608 | tf_op jit(solution)/shard_map/all_to_all | solution.py:404
  384.5 58.3 %attention_backward.1 = bf16[2048,768]{1,0:T(8,128)(2,1)} custom-call(s32[8]{0:T(128)} %get-tuple-element.143.low_ref, s32[8]{0:T(128)} %get-tuple-element.142.high_ref, bf16[2048,256]{1,0:T(8,128)(2,1)} %get-tuple-element.25.q_ref, bf16[2048,256]{1,0:T(8,128)(2,1)} %get-tuple-element.26.k_ref, bf16[2048,256]{1,0:T(8,128)(2,1)} %get-tuple-element.27.v_ref, ...), custom_call_target="tpu_custom_call" | custom-call | flops 30064771072 | bytes 10485760 | tf_op jit(solution)/shard_map/attention_backward/pallas_call | solution.py:276
  442.7 7.8 %convolution_convert_fusion.3 = bf16[1024,768]{1,0:T(8,128)(2,1)} fusion(bf16[2048,1024]{1,0:T(8,128)(2,1)} %all-gather.7.cloned.1.call-done.x_ref, bf16[2048,768]{1,0:T(8,128)(2,1)} %attention_backward.1), kind=kOutput, calls=%fused_computation.68 | convolution fusion | flops 3222011904 | bytes 8912896 | tf_op jit(solution)/shard_map/dot_general | solution.py:17
  450.9 7.8 %convolution_convert_fusion = bf16[2048,1024]{1,0:T(8,128)(2,1)} fusion(bf16[2048,768]{1,0:T(8,128)(2,1)} %attention_backward.1, bf16[1024,768]{1,0:T(8,128)(2,1)} %all-gather.9.cloned.1.call-done.w_ref), kind=kOutput, calls=%fused_computation.11 | convolution fusion | flops 3223322624 | bytes 8912896 | tf_op jit(solution)/shard_map/dot_general | solution.py:17
  474.1 84.6 %reduce-scatter.14.cloned.1.call-done = bf16[128,2048]{1,0:T(8,128)(2,1)} async-done(((bf16[1024,2048]{1,0:T(8,128)(2,1)}), bf16[128,2048]{1,0:T(8,128)(2,1)}) %reduce-scatter.14.cloned.1.call-update) | async-done | bytes 524304 | tf_op jit(solution)/shard_map/reduce_scatter | solution.py:388
  572.1 13.6 %collective-permute-done.9 = f32[128,2048]{1,0:T(8,128)} collective-permute-done((f32[128,2048]{1,0:T(8,128)}, f32[128,2048]{1,0:T(8,128)}, u32[]{:S(2)}, u32[]{:S(2)}) %collective-permute-start.9) | collective-permute-done | bytes 1048608 | tf_op jit(solution)/shard_map/ppermute | solution.py:330
  588.0 39.9 %reduce-scatter.8.cloned.1.call-done = bf16[128,768]{1,0:T(8,128)(2,1)} async-done(((bf16[1024,768]{1,0:T(8,128)(2,1)}), bf16[128,768]{1,0:T(8,128)(2,1)}) %reduce-scatter.8.cloned.1.call-update) | async-done | bytes 196624 | tf_op jit(solution)/shard_map/reduce_scatter | solution.py:410
  627.9 8.7 %all-gather = bf16[512,768]{1,0:T(8,128)(2,1)S(1)} all-gather(bf16[128,768]{1,0:T(8,128)(2,1)} %reduce-scatter.8.cloned.1.call-done), channel_id=2, replica_groups=mesh['wide'=8,'narrow'=4] {'narrow'}, dimensions={0}, use_global_device_ids=true | all-gather | bytes 983040 | tf_op jit(solution)/shard_map/all_gather | solution.py:444
  649.6 20.0 %psum.14 = f32[]{:T(128)} all-reduce(f32[]{:T(128)S(6)} %add.385), channel_id=1, replica_groups=mesh['wide'=8,'narrow'=4] {'wide'}, use_global_device_ids=true, to_apply=%region_19.20 | all-reduce | flops 1 | bytes 8 | tf_op jit(solution)/shard_map/psum | solution.py:450
  669.6 4.1 reduce-scatter.6.cloned.1.call-done
  676.6 39.8 %psum.15 = f32[13,1024]{1,0:T(8,128)S(1)} all-reduce(f32[13,1024]{1,0:T(8,128)S(1)} %concatenate.40), channel_id=1, replica_groups=mesh['wide'=8,'narrow'=4] {'wide','narrow'}, use_global_device_ids=true, to_apply=%region_28.29 | all-reduce | flops 13312 | bytes 106496 | tf_op jit(solution)/shard_map/psum | solution.py:449
  728.9 4.5 multiply_subtract_fusion.2
  743.7 7.5 multiply_subtract_fusion
  751.3 3.8 multiply_subtract_fusion.1
  (248 shorter events, 124.4 us)
Async XLA Ops:
  7.2 32.0 %copy-start = (bf16[512,1024]{1,0:T(8,128)(2,1)S(1)}, bf16[512,1024]{1,0:T(8,128)(2,1)}, u32[]{:S(2)}) copy-start(bf16[512,1024]{1,0:T(8,128)(2,1)} %param.21) | copy-start | bytes 3145732
  7.2 51.6 %all-gather.9.cloned.1.call-start = ((), (), s32[]{:S(2)}) async-start(), calls=%async_computation.8 | async-start | bytes 1769472 | tf_op jit(solution)/shard_map/all_gather | solution.py:341
  9.1 83.7 %all-gather.7.cloned.1.call-start = ((), (), s32[]{:S(2)}) async-start(), calls=%async_computation.7 | async-start | bytes 5242880 | tf_op jit(solution)/shard_map/all_gather | solution.py:349
  41.2 151.7 %all-gather.11.cloned.1.call-start = ((), (), s32[]{:S(2)}) async-start(), calls=%async_computation.9 | async-start | bytes 2359296 | tf_op jit(solution)/shard_map/all_gather | solution.py:342
  42.0 176.5 %all-gather.13.cloned.1.call-start = ((), (), s32[]{:S(2)}) async-start(), calls=%async_computation.10 | async-start | bytes 4718592 | tf_op jit(solution)/shard_map/all_gather | solution.py:343
  44.2 248.2 %all-gather.15.cloned.1.call-start = ((), (), s32[]{:S(2)}) async-start(), calls=%async_computation.11 | async-start | bytes 4718592 | tf_op jit(solution)/shard_map/all_gather | solution.py:344
  188.6 17.9 %all-to-all-start = ((bf16[4,512,256]{1,2,0:T(8,128)(2,1)}), bf16[4,512,256]{1,2,0:T(8,128)(2,1)S(1)}, u32[]{:S(2)}, u32[]{:S(2)}) async-start(bf16[4,512,256]{1,2,0:T(8,128)(2,1)} %copy.61), calls=%async_computation | async-start | bytes 2097152 | tf_op jit(solution)/shard_map/all_to_all | solution.py:372
  192.2 266.6 %reduce-scatter.12.cloned.1.call-start = ((), (), s32[]{:S(2)}) async-start(), calls=%async_computation.15 | async-start | bytes 4718592 | tf_op jit(solution)/shard_map/reduce_scatter | solution.py:391
  192.4 22.5 %collective-permute-start.2 = (bf16[512,1024]{1,0:T(8,128)(2,1)}, bf16[512,1024]{1,0:T(8,128)(2,1)}, u32[]{:S(2)}, u32[]{:S(2)}) collective-permute-start(bf16[512,1024]{1,0:T(8,128)(2,1)} %param.22), channel_id=1, source_target_pairs={{0,1},{1,0},{2,3},{3,2},{4,5},{5,4},{6,7},{7,6},{8,9},{9,8},{10,11... | collective-permute-start | bytes 3145736 | tf_op jit(solution)/shard_map/ppermute | solution.py:327
  212.6 5.9 collective-permute-start
  312.9 158.6 %reduce-scatter.10.cloned.1.call-start = ((), (), s32[]{:S(2)}) async-start(), calls=%async_computation.14 | async-start | bytes 1179648 | tf_op jit(solution)/shard_map/reduce_scatter | solution.py:402
  324.2 8.5 %collective-permute-start.3 = (f32[512,1024]{1,0:T(8,128)}, f32[512,1024]{1,0:T(8,128)}, u32[]{:S(2)}, u32[]{:S(2)}) collective-permute-start(f32[512,1024]{1,0:T(8,128)} %slice.114), channel_id=1, source_target_pairs={{0,1},{1,0},{2,3},{3,2},{4,5},{5,4},{6,7},{7,6},{8,9},{9,8},{10,11... | collective-permute-start | bytes 6291464 | tf_op jit(solution)/shard_map/ppermute | solution.py:327
  332.7 4.5 collective-permute-start.1
  344.8 2.7 collective-permute-start.4
  350.5 208.2 %reduce-scatter.14.cloned.1.call-start = ((), (), s32[]{:S(2)}) async-start(), calls=%async_computation.16 | async-start | bytes 4718592 | tf_op jit(solution)/shard_map/reduce_scatter | solution.py:388
  365.7 18.7 %all-to-all-start.1 = ((bf16[512,4,256]{2,0,1:T(8,128)(2,1)}), bf16[512,4,256]{2,0,1:T(8,128)(2,1)}, u32[]{:S(2)}, u32[]{:S(2)}) async-start(bf16[512,4,256]{2,0,1:T(8,128)(2,1)} %bitcast.78), calls=%async_computation.1 | async-start | bytes 2097152 | tf_op jit(solution)/shard_map/all_to_all | solution.py:404
  370.0 257.9 %reduce-scatter.8.cloned.1.call-start = ((), (), s32[]{:S(2)}) async-start(), calls=%async_computation.13 | async-start | bytes 1769472 | tf_op jit(solution)/shard_map/reduce_scatter | solution.py:410
  450.6 223.1 %reduce-scatter.6.cloned.1.call-start = ((), (), s32[]{:S(2)}) async-start(), calls=%async_computation.12 | async-start | bytes 5242880 | tf_op jit(solution)/shard_map/reduce_scatter | solution.py:412
  460.9 106.8 %collective-permute-start.7 = (f32[128,2048]{1,0:T(8,128)}, f32[128,2048]{1,0:T(8,128)}, u32[]{:S(2)}, u32[]{:S(2)}) collective-permute-start(f32[128,2048]{1,0:T(8,128)} %convert_element_type.196), channel_id=1, source_target_pairs={{0,2},{1,3},{2,0},{3,1},{4,6},{5,7},{6,4},{7,5},{8,10},{9,11},{10,... | collective-permute-start | bytes 3145736 | tf_op jit(solution)/shard_map/ppermute | solution.py:330
  472.4 94.1 %copy-start.29 = (bf16[128,512]{1,0:T(8,128)(2,1)S(1)}, bf16[128,512]{1,0:T(8,128)(2,1)}, u32[]{:S(2)}) copy-start(bf16[128,512]{1,0:T(8,128)(2,1)} %reduce-scatter.10.cloned.1.call-done) | copy-start | bytes 393220
  472.5 94.1 %collective-permute-start.5 = (f32[128,512]{1,0:T(8,128)S(1)}, f32[128,512]{1,0:T(8,128)}, u32[]{:S(2)}, u32[]{:S(2)}) collective-permute-start(f32[128,512]{1,0:T(8,128)S(1)} %convert_element_type.194), channel_id=1, source_target_pairs={{0,2},{1,3},{2,0},{3,1},{4,6},{5,7},{6,4},{7,5},{8,10},{9,11},{10,... | collective-permute-start | bytes 786440 | tf_op jit(solution)/shard_map/ppermute | solution.py:330
  560.8 24.8 %collective-permute-start.9 = (f32[128,2048]{1,0:T(8,128)}, f32[128,2048]{1,0:T(8,128)}, u32[]{:S(2)}, u32[]{:S(2)}) collective-permute-start(f32[128,2048]{1,0:T(8,128)} %convert_element_type.198), channel_id=1, source_target_pairs={{0,2},{1,3},{2,0},{3,1},{4,6},{5,7},{6,4},{7,5},{8,10},{9,11},{10,... | collective-permute-start | bytes 3145736 | tf_op jit(solution)/shard_map/ppermute | solution.py:330
  567.6 3.0 collective-permute-start.6
  570.1 69.7 %collective-permute-start.8 = (f32[128,2048]{1,0:T(8,128)}, f32[128,2048]{1,0:T(8,128)}, u32[]{:S(2)}, u32[]{:S(2)}) collective-permute-start(f32[128,2048]{1,0:T(8,128)} %convert_add_fusion.3), channel_id=1, source_target_pairs={{0,1},{1,0},{2,3},{3,2},{4,5},{5,4},{6,7},{7,6},{8,9},{9,8},{10,11... | collective-permute-start | bytes 3145736 | tf_op jit(solution)/shard_map/ppermute | solution.py:327
  588.0 56.7 %collective-permute-start.10 = (f32[128,2048]{1,0:T(8,128)}, f32[128,2048]{1,0:T(8,128)}, u32[]{:S(2)}, u32[]{:S(2)}) collective-permute-start(f32[128,2048]{1,0:T(8,128)} %convert_add_fusion.2), channel_id=1, source_target_pairs={{0,1},{1,0},{2,3},{3,2},{4,5},{5,4},{6,7},{7,6},{8,9},{9,8},{10,11... | collective-permute-start | bytes 3145736 | tf_op jit(solution)/shard_map/ppermute | solution.py:327
  646.4 27.3 %copy-start.31 = (f32[1,1024]{1,0:T(1,128)S(1)}, f32[1,1024]{1,0:T(1,128)}, u32[]{:S(2)}) copy-start(f32[1,1024]{1,0:T(1,128)} %copy-done.30) | copy-start | bytes 12292
  646.4 27.3 %copy-start.34 = (f32[512]{0:T(512)S(1)}, f32[512]{0:T(512)}, u32[]{:S(2)}) copy-start(f32[512]{0:T(512)} %copy-done.33) | copy-start | bytes 6148
  646.5 27.2 %copy-start.38 = (f32[512]{0:T(512)S(1)}, f32[512]{0:T(512)}, u32[]{:S(2)}) copy-start(f32[512]{0:T(512)} %copy-done.37) | copy-start | bytes 6148
  647.7 28.8 %copy-start.40 = (f32[1024]{0:T(1024)S(1)}, f32[1024]{0:T(1024)}, u32[]{:S(2)}) copy-start(f32[1024]{0:T(1024)} %get-tuple-element.69) | copy-start | bytes 12292
  647.7 28.8 %copy-start.41 = (f32[1024]{0:T(1024)S(1)}, f32[1024]{0:T(1024)}, u32[]{:S(2)}) copy-start(f32[1024]{0:T(1024)} %get-tuple-element.74) | copy-start | bytes 12292
  647.7 28.8 %copy-start.42 = (f32[1024]{0:T(1024)S(1)}, f32[1024]{0:T(1024)}, u32[]{:S(2)}) copy-start(f32[1024]{0:T(1024)} %get-tuple-element.96) | copy-start | bytes 12292
  647.7 28.8 %copy-start.43 = (f32[1024]{0:T(1024)S(1)}, f32[1024]{0:T(1024)}, u32[]{:S(2)}) copy-start(f32[1024]{0:T(1024)} %get-tuple-element.107) | copy-start | bytes 12292
  (46 other events, 169.6 us)
Sparse Core Ops, SparseCore 0:
  10.8 46.9 all-gather.8
  59.9 32.8 all-gather.6
  95.5 49.0 all-gather.10
  147.2 71.3 all-gather.12
  221.1 71.3 all-gather.14
  313.0 86.8 reduce-scatter.11
  403.8 63.8 reduce-scatter.9
  471.3 87.3 reduce-scatter.13
  562.7 65.1 reduce-scatter.7
  630.3 43.3 reduce-scatter.5

commit v2 on v1

--- a/solution.py
+++ b/solution.py
@@ -11,6 +11,7 @@
 BLOCK = 256
 BF = jnp.bfloat16
 F32 = jnp.float32
+MESH = pl.DeviceIdType.MESH
 
 
 def dot(a, b, ca, cb):
@@ -54,7 +55,7 @@
     )
 
 
-def qkv_kernel(half, x_ref, w_ref, bias_ref, onehot_ref, table_ref, q_ref, k_ref, v_ref, turn_ref):
+def qkv_kernel(half, x_ref, vec_ref, w_ref, bias_ref, onehot_ref, table_ref, q_ref, k_ref, v_ref, turn_ref, norm_ref):
     width = q_ref.shape[1]
     angles = lax.dot_general(
         onehot_ref[...],
@@ -65,13 +66,16 @@
     )
     turn_ref[...] = angles
     cosine, sine = angles[:, :128], angles[:, 128:]
-    proj = dot(x_ref[...], w_ref[...], 1, 0) + bias_ref[...]
+    unit, _ = norm_parts(x_ref[...].astype(F32))
+    normed = (unit * vec_ref[0:1, :] + vec_ref[1:2, :]).astype(BF)
+    norm_ref[...] = normed
+    proj = dot(normed, w_ref[...], 1, 0) + bias_ref[...]
     q_ref[...] = turn(proj[:, :width], cosine, sine, half, 1).astype(BF)
     k_ref[...] = turn(proj[:, width : 2 * width], cosine, sine, half, 1).astype(BF)
     v_ref[...] = proj[:, 2 * width :].astype(BF)
 
 
-def qkv_call(x, w, bias, onehot, table, half):
+def qkv_call(x, vec, w, bias, onehot, table, half):
     rows, depth = x.shape
     width = w.shape[1] // 3
     out = jax.ShapeDtypeStruct((rows, width), BF)
@@ -80,14 +84,297 @@
     return pl.pallas_call(
         functools.partial(qkv_kernel, half),
         grid=(rows // BLOCK,),
-        in_specs=[row_block(depth), whole(w), whole(bias), row_block(128), whole(table)],
-        out_specs=[row_block(width)] * 3 + [row_block(256)],
-        out_shape=[out, out, out, jax.ShapeDtypeStruct((rows, 256), F32)],
+        in_specs=[row_block(depth), whole(vec), whole(w), whole(bias), row_block(128), whole(table)],
+        out_specs=[row_block(width)] * 3 + [row_block(256), row_block(depth)],
+        out_shape=[
+            out, out, out, jax.ShapeDtypeStruct((rows, 256), F32), jax.ShapeDtypeStruct((rows, depth), BF)
+        ],
         cost_estimate=pl.CostEstimate(
-            flops=2 * rows * depth * 3 * width, bytes_accessed=rows * depth * 4, transcendentals=0
+            flops=2 * rows * depth * 3 * width, bytes_accessed=rows * depth * 6, transcendentals=0
         ),
         name="qkv",
-    )(x, w, bias, onehot, table)
+    )(x, vec, w, bias, onehot, table)
+
+
+def greet(targets):
+    barrier = pltpu.get_barrier_semaphore()
+    for target in targets:
+        pl.semaphore_signal(barrier, inc=1, device_id=target, device_id_type=MESH)
+    pl.semaphore_wait(barrier, len(targets))
+
+
+def others(name, index, size):
+    return [{name: lax.rem(index + d, size)} for d in range(1, size)]
+
+
+class Copies:
+    def __init__(self, send, recv):
+        self.send, self.recv, self.all = send, recv, []
+
+    def start(self, src, dst, **target):
+        i = len(self.all)
+        copy = pltpu.make_async_remote_copy(
+            src_ref=src, dst_ref=dst, send_sem=self.send.at[i], recv_sem=self.recv.at[i],
+            device_id=target, device_id_type=MESH,
+        )
+        copy.start()
+        self.all.append([copy, False])
+        return i
+
+    def arrived(self, i):
+        if not self.all[i][1]:
+            self.all[i][0].wait_recv()
+            self.all[i][1] = True
+
+    def finish(self):
+        for i in range(len(self.all)):
+            self.arrived(i)
+        for copy, _ in self.all:
+            copy.wait_send()
+
+
+def rows_at(index, size):
+    return pl.ds(pl.multiple_of(index * size, size), size)
+
+
+def gather_kernel(
+    wide, narrow, tok, qkv, vec, tag, tok_all, qkv_all, vec_all, tag_all, send, recv, local
+):
+    w, n = lax.axis_index("wide"), lax.axis_index("narrow")
+    column = wide // 2
+    z, y = w // 2, lax.rem(w, 2)
+    near, mate, cross = w + 1 - 2 * y, n + 1 - 2 * lax.rem(n, 2), lax.rem(n + 2, narrow)
+    wide_rows, group_rows = qkv.shape[0], tok.shape[0]
+    pieces = 4
+    piece = group_rows // pieces
+    greet(others("wide", w, wide) + others("narrow", n, narrow))
+    go = Copies(send, recv)
+    for d in range(1, wide):
+        go.start(vec, vec_all.at[w], wide=lax.rem(w + d, wide))
+    for d in range(1, narrow):
+        go.start(tag, tag_all.at[n], narrow=lax.rem(n + d, narrow))
+    own_rows = rows_at(w, wide_rows)
+    token_rows = lambda i, p: rows_at(i * pieces + p, piece)
+    far = [go.start(qkv, qkv_all.at[own_rows], wide=lax.rem(z + d, column) * 2 + y) for d in range(1, column)]
+    over = [
+        go.start(tok.at[pl.ds(p * piece, piece)], tok_all.at[token_rows(n, p)], narrow=cross) for p in range(pieces)
+    ]
+    go.start(qkv, qkv_all.at[own_rows], wide=near)
+    for p in range(pieces):
+        go.start(tok.at[pl.ds(p * piece, piece)], tok_all.at[token_rows(n, p)], narrow=mate)
+    own = [
+        pltpu.make_async_copy(tok, tok_all.at[rows_at(n, group_rows)], local.at[0]),
+        pltpu.make_async_copy(qkv, qkv_all.at[own_rows], local.at[1]),
+        pltpu.make_async_copy(vec, vec_all.at[w], local.at[2]),
+        pltpu.make_async_copy(tag, tag_all.at[n], local.at[3]),
+    ]
+    for copy in own:
+        copy.start()
+    for i in range(max(pieces, column - 1)):
+        if i < column - 1:
+            go.arrived(far[i])
+            block = qkv_all.at[rows_at(lax.rem(z - (i + 1) + column, column) * 2 + y, wide_rows)]
+            go.start(block, block, wide=near)
+        if i < pieces:
+            go.arrived(over[i])
+            block = tok_all.at[token_rows(cross, i)]
+            go.start(block, block, narrow=mate)
+    for copy in own:
+        copy.wait()
+    go.finish()
+
+
+def gather_call(tok, qkv, vec, tag, wide, narrow):
+    copies = (wide - 1) + (narrow - 1) + 2 * (wide // 2 - 1) + 1 + 12
+    vmem = pl.BlockSpec(memory_space=pltpu.VMEM)
+    anywhere = pl.BlockSpec(memory_space=pl.ANY)
+    return pl.pallas_call(
+        functools.partial(gather_kernel, wide, narrow),
+        in_specs=[vmem] * 4,
+        out_specs=[anywhere] * 4,
+        out_shape=[
+            jax.ShapeDtypeStruct((narrow * tok.shape[0], tok.shape[1]), BF),
+            jax.ShapeDtypeStruct((wide * qkv.shape[0], qkv.shape[1]), BF),
+            jax.ShapeDtypeStruct((wide,) + vec.shape, BF),
+            jax.ShapeDtypeStruct((narrow,) + tag.shape, jnp.int32),
+        ],
+        scratch_shapes=[
+            pltpu.SemaphoreType.DMA((copies,)),
+            pltpu.SemaphoreType.DMA((copies,)),
+            pltpu.SemaphoreType.DMA((4,)),
+        ],
+        compiler_params=pltpu.CompilerParams(collective_id=0, has_side_effects=True),
+        name="gather",
+    )(tok, qkv, vec, tag)
+
+
+def tail_kernel(
+    wide, narrow, part, grad_proj, weight, tok, vec_in, normed_out, quarters_out, vec_out,
+    partial, mate_in, cross_out, cross_in, near_in, far_out, far_in, shards, vec_box, sums, send, recv,
+):
+    w, n = lax.axis_index("wide"), lax.axis_index("narrow")
+    column = wide // 2
+    z, y = w // 2, lax.rem(w, 2)
+    x, c = n // 2, lax.rem(n, 2)
+    near, mate, cross = w + 1 - 2 * y, n + 1 - 2 * c, lax.rem(n + 2, narrow)
+    wide_rows, group_rows = part.shape[0] // wide, normed_out.shape[0]
+    towards = [lax.rem(z + d, column) for d in range(1, column + 1)]
+    greet([{"wide": near}] + [{"wide": to * 2 + y} for to in towards[:-1]] + others("narrow", n, narrow))
+    go = Copies(send, recv)
+    first = [
+        go.start(part.at[rows_at(towards[k] * 2 + 1 - y, wide_rows)], near_in.at[k], wide=near) for k in range(column)
+    ]
+
+    sums[...] = jnp.zeros_like(sums)
+    owners = [(1 - x) * 2 + 1 - c, x * 2 + 1 - c, (1 - x) * 2 + c, n]
+    mates = []
+    for slot, owner in enumerate(owners):
+
+        def body(i, carry):
+            at = pl.ds(pl.multiple_of(owner * group_rows + i * BLOCK, BLOCK), BLOCK)
+            here = pl.ds(pl.multiple_of(i * BLOCK, BLOCK), BLOCK)
+            grads = dot(grad_proj[at, :], weight[...], 1, 1)
+            unit, _ = norm_parts(tok[at, :].astype(F32))
+            sums[0:1, :] += jnp.sum(grads * unit, axis=0, keepdims=True)
+            sums[1:2, :] += jnp.sum(grads, axis=0, keepdims=True)
+            if slot < 3:
+                partial[slot, here, :] = grads.astype(BF)
+            else:
+                normed_out[here, :] = grads
+            return carry
+
+        lax.fori_loop(0, group_rows // BLOCK, body, 0)
+        if slot < 2:
+            mates.append(go.start(partial.at[slot], mate_in.at[slot], narrow=mate))
+
+    vec_box[pl.ds(n, 1)] = vec_in[...][None]
+    vec_box[pl.ds(n, 1), 0:2, :] = sums[0:2, :][None]
+    vecs = [go.start(vec_box.at[n], vec_box.at[n], narrow=lax.rem(n + d, narrow)) for d in range(1, narrow)]
+
+    go.arrived(mates[0])
+    half = group_rows // 2
+    overs = []
+    for p in range(2):
+        at = pl.ds(p * half, half)
+        cross_out[at, :] = (partial[2, at, :].astype(F32) + mate_in[0, at, :].astype(F32)).astype(BF)
+        overs.append(go.start(cross_out.at[at], cross_in.at[at], narrow=cross))
+
+    seconds = []
+    total = None
+    for k in range(column):
+        go.arrived(first[k])
+        mine = part[rows_at(towards[k] * 2 + y, wide_rows), :].astype(F32) + near_in[k].astype(F32)
+        if k < column - 1:
+            far_out[k] = mine.astype(BF)
+            seconds.append(go.start(far_out.at[k], far_in.at[k], wide=towards[k] * 2 + y))
+        else:
+            total = mine
+    for k in range(column - 1):
+        go.arrived(seconds[k])
+        total = total + far_in[k].astype(F32)
+    shards[pl.ds(n, 1)] = total.astype(BF)[None]
+    over = go.start(shards.at[n], shards.at[n], narrow=cross)
+    go.start(shards.at[n], shards.at[n], narrow=mate)
+
+    go.arrived(mates[1])
+    for p in range(2):
+        go.arrived(overs[p])
+        at = pl.ds(p * half, half)
+        normed_out[at, :] += mate_in[1, at, :].astype(F32) + cross_in[at, :].astype(F32)
+    for i in vecs:
+        go.arrived(i)
+    group = vec_box[0]
+    for i in range(1, narrow):
+        group = group + vec_box[i]
+    vec_out[...] = group
+
+    go.arrived(over)
+    go.start(shards.at[cross], shards.at[cross], narrow=mate)
+    go.finish()
+    quarters_out[...] = shards[...]
+
+
+def tail_call(part, grad_proj, weight, tok, vec_in, wide, narrow):
+    depth, cols = part.shape
+    rows = tok.shape[0] // narrow
+    wide_rows = depth // wide
+    column = wide // 2
+    copies = 2 * column - 1 + 2 + (narrow - 1) + 2 + 3
+    vmem = pl.BlockSpec(memory_space=pltpu.VMEM)
+    return pl.pallas_call(
+        functools.partial(tail_kernel, wide, narrow),
+        in_specs=[vmem] * 5,
+        out_specs=[vmem] * 3,
+        out_shape=[
+            jax.ShapeDtypeStruct((rows, depth), F32),
+            jax.ShapeDtypeStruct((narrow, wide_rows, cols), BF),
+            jax.ShapeDtypeStruct(vec_in.shape, F32),
+        ],
+        scratch_shapes=[
+            pltpu.VMEM((3, rows, depth), BF),
+            pltpu.VMEM((2, rows, depth), BF),
+            pltpu.VMEM((rows, depth), BF),
+            pltpu.VMEM((rows, depth), BF),
+            pltpu.VMEM((column, wide_rows, cols), BF),
+            pltpu.VMEM((column - 1, wide_rows, cols), BF),
+            pltpu.VMEM((column - 1, wide_rows, cols), BF),
+            pltpu.VMEM((narrow, wide_rows, cols), BF),
+            pltpu.VMEM((narrow,) + vec_in.shape, F32),
+            pltpu.VMEM((8, depth), F32),
+            pltpu.SemaphoreType.DMA((copies,)),
+            pltpu.SemaphoreType.DMA((copies,)),
+        ],
+        compiler_params=pltpu.CompilerParams(
+            collective_id=1, has_side_effects=True, vmem_limit_bytes=56 * 1024 * 1024
+        ),
+        name="tail",
+    )(part, grad_proj, weight, tok, vec_in)
+
+
+def norm_kernel(wide, slices, total_out, square_out, box, squares, send, recv):
+    w = lax.axis_index("wide")
+    greet(others("wide", w, wide))
+    go = Copies(send, recv)
+    peers = [lax.rem(w + d, wide) for d in range(1, wide)]
+    for peer in peers:
+        go.start(slices.at[peer], box.at[w], wide=peer)
+    box[pl.ds(w, 1)] = slices[pl.ds(w, 1)]
+    for i in range(wide - 1):
+        go.arrived(i)
+    total = box[0]
+    for i in range(1, wide):
+        total = total + box[i]
+    total_out[...] = total
+    row = lax.broadcasted_iota(jnp.int32, total.shape, 0)
+    entries = jnp.where(row == 15, 0.0, total)
+    entries = entries * entries
+    squares[pl.ds(w, 1)] = (entries[:8] + entries[8:])[None]
+    for peer in peers:
+        go.start(squares.at[w], squares.at[w], wide=peer)
+    go.finish()
+    all_squares = squares[0]
+    for i in range(1, wide):
+        all_squares = all_squares + squares[i]
+    square_out[...] = all_squares
+
+
+def norm_call(slices, wide):
+    vmem = pl.BlockSpec(memory_space=pltpu.VMEM)
+    copies = 2 * (wide - 1)
+    return pl.pallas_call(
+        functools.partial(norm_kernel, wide),
+        in_specs=[vmem],
+        out_specs=[vmem] * 2,
+        out_shape=[jax.ShapeDtypeStruct((16, 128), F32), jax.ShapeDtypeStruct((8, 128), F32)],
+        scratch_shapes=[
+            pltpu.VMEM((wide, 16, 128), F32),
+            pltpu.VMEM((wide, 8, 128), F32),
+            pltpu.SemaphoreType.DMA((copies,)),
+            pltpu.SemaphoreType.DMA((copies,)),
+        ],
+        compiler_params=pltpu.CompilerParams(collective_id=2, has_side_effects=True),
+        name="norm",
+    )(slices)
 
 
 def head_lanes(shape, head, head_dim):
@@ -96,11 +383,18 @@
 
 
 def forward_kernel(
-    heads, head_dim, low_ref, high_ref, q_ref, k_ref, v_ref, seg_ref, tag_ref, o_ref, lse_ref, acc, peak, total
+    heads, head_dim, low_ref, high_ref, q_ref, k_ref, v_ref, seg_ref, tag_ref, o_ref, lse_ref,
+    values_turned, acc, peak, total,
 ):
     step = pl.program_id(0)
+    width = q_ref.shape[1]
+
+    @pl.when(step == 0)
+    def _():
+        values_turned[...] = v_ref[...].T
+
     query = q_ref[...] * jnp.asarray(head_dim**-0.5, BF)
-    seg = seg_ref[...]
+    seg = seg_ref[0]
     masked_query = [
         jnp.where(head_lanes(query.shape, h, head_dim), query, jnp.zeros_like(query)) for h in range(heads)
     ]
@@ -111,63 +405,61 @@
     def body(j, carry):
         start = pl.multiple_of(j * BLOCK, BLOCK)
         key = k_ref[pl.ds(start, BLOCK), :]
-        value = v_ref[pl.ds(start, BLOCK), :]
-        allowed = seg == tag_ref[pl.ds(j, 1), :]
+        allowed = tag_ref[pl.ds(start, BLOCK), :] == seg
+        scores = [jnp.where(allowed, dot(key, masked_query[h], 1, 1), -1e30) for h in range(heads)]
         for h in range(heads):
-            scores = jnp.where(allowed, dot(masked_query[h], key, 1, 1), -1e30)
-            old = peak[h]
-            new = jnp.maximum(old, jnp.max(scores, axis=1, keepdims=True))
-            probs = jnp.exp(scores - new[:, :1])
+            rows = slice(h * head_dim, (h + 1) * head_dim)
+            old = peak[h : h + 1, :]
+            new = jnp.maximum(old, jnp.max(scores[h], axis=0, keepdims=True))
+            probs = jnp.exp(scores[h] - new)
             keep = jnp.exp(old - new)
-            peak[h] = new
-            total[h] = total[h] * keep + jnp.sum(probs, axis=1, keepdims=True)
-            acc[h] = acc[h] * keep[:, :1] + dot(probs.astype(BF), value, 1, 0)
+            peak[h : h + 1, :] = new
+            total[h : h + 1, :] = total[h : h + 1, :] * keep + jnp.sum(probs, axis=0, keepdims=True)
+            value = values_turned[rows, pl.ds(start, BLOCK)]
+            acc[rows, :] = acc[rows, :] * keep + dot(value, probs.astype(BF), 1, 0)
         return carry
 
     lax.fori_loop(low_ref[step], high_ref[step], body, 0)
-    out = jnp.zeros(o_ref.shape, F32)
-    stats = jnp.zeros((BLOCK, 128), F32)
-    for h in range(heads):
-        out = jnp.where(head_lanes(out.shape, h, head_dim), acc[h] / total[h][:, :1], out)
-        lane = lax.broadcasted_iota(jnp.int32, stats.shape, 1)
-        stats = jnp.where(lane == h, peak[h] + jnp.log(total[h]), stats)
-    o_ref[...] = out.astype(BF)
-    lse_ref[...] = stats.T[:8, :]
-
-
-def forward_call(low, high, q, k, v, seg_col, tag_rows, head_dim):
+    parts = [acc[h * head_dim : (h + 1) * head_dim, :] / total[h : h + 1, :] for h in range(heads)]
+    o_ref[...] = jnp.concatenate(parts, axis=0).T.astype(BF)
+    lse_ref[0] = peak[...] + jnp.log(jnp.maximum(total[...], 1e-30))
+
+
+def forward_call(low, high, q, k, v, seg_rows, tag_col, head_dim):
     rows, width = q.shape
     heads = width // head_dim
-    whole = lambda a: pl.BlockSpec(a.shape, lambda i, *_: (0, 0))
+    blocks = rows // BLOCK
+    whole = lambda a: pl.BlockSpec(a.shape, lambda i, *_: (0,) * a.ndim)
     grid_spec = pltpu.PrefetchScalarGridSpec(
         num_scalar_prefetch=2,
-        grid=(rows // BLOCK,),
+        grid=(blocks,),
         in_specs=[
             pl.BlockSpec((BLOCK, width), lambda i, *_: (i, 0)),
             whole(k),
             whole(v),
-            pl.BlockSpec((BLOCK, 1), lambda i, *_: (i, 0)),
-            whole(tag_rows),
+            pl.BlockSpec((1, 1, BLOCK), lambda i, *_: (i, 0, 0)),
+            whole(tag_col),
         ],
         out_specs=[
             pl.BlockSpec((BLOCK, width), lambda i, *_: (i, 0)),
-            pl.BlockSpec((8, BLOCK), lambda i, *_: (0, i)),
+            pl.BlockSpec((1, 8, BLOCK), lambda i, *_: (i, 0, 0)),
         ],
         scratch_shapes=[
-            pltpu.VMEM((heads, BLOCK, width), F32),
-            pltpu.VMEM((heads, BLOCK, 128), F32),
-            pltpu.VMEM((heads, BLOCK, 128), F32),
+            pltpu.VMEM((width, rows), BF),
+            pltpu.VMEM((width, BLOCK), F32),
+            pltpu.VMEM((8, BLOCK), F32),
+            pltpu.VMEM((8, BLOCK), F32),
         ],
     )
     return pl.pallas_call(
         functools.partial(forward_kernel, heads, head_dim),
         grid_spec=grid_spec,
-        out_shape=[jax.ShapeDtypeStruct((rows, width), BF), jax.ShapeDtypeStruct((8, rows), F32)],
+        out_shape=[jax.ShapeDtypeStruct((rows, width), BF), jax.ShapeDtypeStruct((blocks, 8, BLOCK), F32)],
         cost_estimate=pl.CostEstimate(
             flops=heads * rows * rows * width * 3, bytes_accessed=rows * width * 8, transcendentals=heads * rows * rows
         ),
         name="attention_forward",
-    )(low, high, q, k, v, seg_col, tag_rows)
+    )(low, high, q, k, v, seg_rows[:, None, :], tag_col)
 
 
 def backward_kernel(
@@ -254,7 +546,6 @@
     rows, width = q.shape
     heads = width // head_dim
     blocks = rows // BLOCK
-    lse = jnp.moveaxis(lse.reshape(8, blocks, BLOCK), 1, 0)
     whole = lambda a: pl.BlockSpec(a.shape, lambda i, *_: (0,) * a.ndim)
     block = pl.BlockSpec((BLOCK, width), lambda i, *_: (i, 0))
     grid_spec = pltpu.PrefetchScalarGridSpec(
@@ -329,6 +620,20 @@
     def across(value):
         return lax.ppermute(value, "narrow", [(i, i ^ 2) for i in range(narrow)])
 
+    def scatter(part):
+        w = lax.axis_index("wide")
+        z, y = w // 2, w % 2
+        column = wide // 2
+        blocks = part.reshape(column, 2, shard_rows, part.shape[1])
+        pick = lambda value, at, axis: lax.dynamic_index_in_dim(value, at, axis, keepdims=False)
+        came = lax.ppermute(pick(blocks, 1 - y, 1), "wide", [(i, i ^ 1) for i in range(wide)])
+        both = (pick(blocks, y, 1).astype(F32) + came.astype(F32)).astype(BF)
+        total = pick(both, z, 0).astype(F32)
+        for d in range(1, column):
+            pairs = [(i, (i // 2 + d) % column * 2 + i % 2) for i in range(wide)]
+            total = total + lax.ppermute(pick(both, (z + d) % column, 0), "wide", pairs).astype(F32)
+        return total.astype(BF)
+
     def take(value, start, size, axis=1):
         return lax.dynamic_slice_in_dim(value, start, size, axis)
 
@@ -337,18 +642,19 @@
     up_low = take(weight_up, side * half_hidden, half_hidden).astype(BF)
     down_low = take(weight_down, side * half_hidden, half_hidden).astype(BF)
 
-    vec = lax.all_gather(vectors.astype(BF), "wide", axis=1, tiled=True).astype(F32)
-    qkv_w = lax.all_gather(qkv_low, "wide", axis=0, tiled=True)
+    shard_cols = vectors.shape[1]
+    vec_shard = jnp.pad(vectors.astype(BF), ((0, 16 - vectors.shape[0]), (0, -shard_cols % 128)))
+    tag = jnp.concatenate([segment_ids[None], key_keep[None], patch_coords, patch_coords], axis=0)
+    tokens_all, qkv_w, vec_all, tag_all = gather_call(tokens, qkv_low, vec_shard, tag, wide, narrow)
+    vec_all = vec_all[:, :, :shard_cols]
+    vec = jnp.moveaxis(vec_all, 0, 1).reshape(16, width).astype(F32)[: vectors.shape[0]]
+    tag_all = jnp.moveaxis(tag_all, 0, 1).reshape(8, group)
     out_w = lax.all_gather(out_low, "wide", axis=0, tiled=True)
     up_w = lax.all_gather(up_low, "wide", axis=0, tiled=True)
     down_w = lax.all_gather(down_low, "wide", axis=0, tiled=True)
 
     xin = tokens.astype(F32)
     unit1, inverse1 = norm_parts(xin)
-    normed1 = (unit1 * vec[0] + vec[1]).astype(BF)
-    normed1_all = lax.all_gather(normed1, "narrow", axis=0, tiled=True)
-    tag = jnp.concatenate([segment_ids[None], key_keep[None], patch_coords], axis=0)
-    tag_all = lax.all_gather(tag, "narrow", axis=1, tiled=True)
     cot_pair = jnp.concatenate([cotangent, mate(cotangent)], axis=0)
 
     seg = tag_all[0]
@@ -365,9 +671,9 @@
     high = (jnp.sum(seg[None, :] <= seg_rows[:, -1:], axis=1, dtype=jnp.int32) + BLOCK - 1) // BLOCK
 
     bias = jnp.concatenate([take(vec[2 + i : 3 + i], me * mine, mine) for i in range(3)], axis=1)
-    query, keys, values, turns = qkv_call(normed1_all, qkv_w, bias, onehot, rotary_table(head_dim), head_dim // 2)
+    query, keys, values, turns, normed1_all = qkv_call(tokens_all, vec[:2], qkv_w, bias, onehot, rotary_table(head_dim), head_dim // 2)
     mixed_mine, lse = forward_call(
-        low, high, query, keys, values, seg_float[:, None], key_tag.reshape(blocks, BLOCK), head_dim
+        low, high, query, keys, values, seg_float.reshape(blocks, BLOCK), key_tag[:, None], head_dim
     )
     mixed = lax.all_to_all(mixed_mine, "narrow", 0, 1, tiled=True)
 
@@ -399,7 +705,7 @@
     own_out = take(part_out, side * (width // 2), width // 2)
     other_out = take(part_out, (1 - side) * (width // 2), width // 2)
     part_out = (own_out + mate(other_out.astype(BF)).astype(F32)).astype(BF)
-    grad_out = lax.psum_scatter(part_out, "wide", scatter_dimension=0, tiled=True)
+    grad_out = scatter(part_out)
 
     grad_mixed_mine = lax.all_to_all(grad_mixed, "narrow", 1, 0, tiled=True)
     grad_proj = backward_call(
@@ -407,10 +713,6 @@
         key_tag[:, None], turns, head_dim,
     )
     part_qkv = dot(normed1_all, grad_proj, 0, 0).astype(BF)
-    grad_qkv = lax.psum_scatter(part_qkv, "wide", scatter_dimension=0, tiled=True)
-    grad_normed1_part = dot(grad_proj, qkv_w, 1, 1)
-    grad_normed1 = lax.psum_scatter(grad_normed1_part.astype(BF), "narrow", scatter_dimension=0, tiled=True).astype(F32)
-    grad_tokens = (grad_resid + norm_back(grad_normed1, vec[0], unit1, inverse1)).astype(BF)
 
     proj_sums = jnp.sum(grad_proj.astype(F32), axis=0).reshape(3, mine)
     proj_rows = lax.dynamic_update_slice(jnp.zeros((3, width), F32), proj_sums, (0, me * mine))
@@ -418,44 +720,51 @@
     up_rows = lax.dynamic_update_slice(jnp.zeros((hidden,), F32), up_sums, (side * half_hidden,))
     vector_part = jnp.concatenate(
         [
-            jnp.sum(grad_normed1 * unit1, axis=0)[None],
-            jnp.sum(grad_normed1, axis=0)[None],
+            jnp.zeros((2, width), F32),
             proj_rows,
             jnp.sum(grad_branch.astype(F32), axis=0)[None],
             jnp.sum(grad_normed2 * unit2, axis=0)[None],
             jnp.sum(grad_normed2, axis=0)[None],
             jnp.sum(cot, axis=0)[None],
             up_rows.reshape(hidden // width, width),
+            jnp.zeros((16 - vectors.shape[0], width), F32),
         ],
         axis=0,
     )
+    grad_normed1, quarters, vector_group = tail_call(
+        part_qkv, grad_proj, qkv_w, tokens_all, vector_part, wide, narrow
+    )
+    grad_tokens = (grad_resid + norm_back(grad_normed1, vec[0], unit1, inverse1)).astype(BF)
 
     def join(value):
-        value = value.astype(F32)
-        value = value + across(value)
-        other = mate(value)
-        first = jnp.where(side == 0, value, other)
-        second = jnp.where(side == 0, other, value)
+        other = across(value)
+        mine = value.astype(F32) + other.astype(F32)
+        theirs = mate(value).astype(F32) + mate(other).astype(F32)
+        first = jnp.where(side == 0, mine, theirs)
+        second = jnp.where(side == 0, theirs, mine)
         return jnp.concatenate([first, second], axis=1)
 
     total_up = join(grad_up)
     total_down = join(grad_down)
     total_out = join(grad_out)
-    quarters = lax.all_gather(grad_qkv, "narrow", axis=0)
-    total_qkv = jnp.moveaxis(quarters.reshape(narrow, shard_rows, 3, mine), 0, 2).reshape(shard_rows, 3 * width)
-    total_qkv = total_qkv.astype(F32)
+    total_qkv = jnp.concatenate(
+        [quarters[i, :, j * mine : (j + 1) * mine] for j in range(3) for i in range(narrow)], axis=1
+    ).astype(F32)
 
     squares = sum(jnp.sum(g * g) for g in (total_qkv, total_out, total_up, total_down))
-    vector_total = lax.psum(vector_part, ("wide", "narrow"))
-    squares_total = lax.psum(squares, "wide")
-    grad_norm = jnp.sqrt(squares_total + jnp.sum(vector_total * vector_total))
+    slices = jnp.moveaxis(vector_group.reshape(16, wide, shard_rows), 1, 0)
+    slices = jnp.pad(slices, ((0, 0), (0, 0), (0, -shard_rows % 128)))
+    place = (jnp.arange(16)[:, None] == 15) & (jnp.arange(slices.shape[2])[None, :] == 0)
+    slices = jnp.where(place[None], squares, slices)
+    vector_total, vector_squares = norm_call(slices, wide)
+    grad_norm = jnp.sqrt(vector_total[15, 0] + jnp.sum(vector_squares))
     clip = 1.0 / jnp.maximum(grad_norm, 1.0)
     count = step_count[0].astype(F32)
     rate = 0.4 * count / (count + 4.0)
     decay = 0.04 + 0.018 * count
     fix_first = 1.0 - jnp.power(0.9, count)
     fix_second = 1.0 - jnp.power(0.999, count)
-    grad_vectors = take(vector_total, lax.axis_index("wide") * shard_rows, shard_rows)
+    grad_vectors = vector_total[: vectors.shape[0], :shard_rows]
 
     def update(param, grad, first, second, decay_here):
         return adamw(param, grad, first, second, clip, rate, decay_here, fix_first, fix_second)

time: 774 us -> 564 us (0.73)
  waiting for transfers between devices: 271 us -> 123 us
  blocking collectives: 102 us -> 0 us
  Pallas kernels: 152 us -> 229 us
  other arithmetic: 70.6 us -> 51.6 us
  local copies, waits for them, and re-layouts: 62.7 us -> 46.1 us
  starting transfers between devices: 13.9 us -> 22.5 us
  matrix products: 73.8 us -> 65.7 us
    pallas_call x0 -> x3, Pallas kernels: none -> 129 us  [the longest x1 72.8 us: tail_call(): pl.pallas_call(functools.partial(tail_kernel, wide, narrow), in_specs=[vm...]
    reduce_scatter x1, waiting for transfers between devices: 84.6 us -> 0.01 us  [on_device(): lax.psum_scatter(part_down, 'wide', scatter_dimension=0, tiled=True)]
    psum x2 -> x0, blocking collectives: 59.9 us -> none  [the longest x1 39.8 us: on_device(): vector_total = lax.psum(vector_part, ('wide', 'narrow'))]
    pallas_call x1, Pallas kernels: 82.9 us -> 29.2 us  [forward_call(): pl.pallas_call(functools.partial(forward_kernel, heads, head_dim), grid_s...]
    reduce_scatter x3 -> x0, waiting for transfers between devices: 44 us -> none  [the longest x1 39.9 us: on_device(): lax.psum_scatter(part_qkv, 'wide', scatter_dimension=0, tiled=True)]
    all_gather x3 -> x0, blocking collectives: 41.9 us -> none  [the longest x1 27.9 us: on_device(): lax.all_gather(vectors.astype(BF), 'wide', axis=1, tiled=True).astype(F32)]
    all_gather x2 -> x0, waiting for transfers between devices: 34 us -> none  [the longest x1 34 us: on_device(): normed1_all = lax.all_gather(normed1, 'narrow', axis=0, tiled=True)]
    ppermute x0 -> x4, waiting for transfers between devices: none -> 21.8 us  [the longest x1 12.5 us: scatter(): lax.ppermute(pick(blocks, 1 - y, 1), 'wide', [(i, i ^ 1) for i in range(w...]
  transfers between devices with their start and end apart: 23 -> 25, of which waited for: 11 -> 10; matrix products, arithmetic and copies ran while one was open for 17% -> 19% of each run, Pallas kernels for 20% -> 39%
where the time goes in v2:
time: 564 us; the launch traced here: 559 us
  Pallas kernels  229 us (41%)
  waiting for transfers between devices  123 us (22%)
  matrix products  65.7 us (12%)
  other arithmetic  51.6 us (9%)
  local copies, waits for them, and re-layouts  46.1 us (8%)
  starting transfers between devices  22.5 us (4%)
  between operations  20.8 us (4%)
    pallas_call x1, Pallas kernels, tail_call(): pl.pallas_call(functools.partial(tail_kernel, wide, narrow), in_specs=[vm...  72.8 us
    dot_general x10, matrix products, dot(): lax.dot_general(a, b, (((ca,), (cb,)), ((), ())), preferred_element_type=...  65.7 us
    all_gather x1, waiting for transfers between devices, on_device(): down_w = lax.all_gather(down_low, 'wide', axis=0, tiled=True)  63.4 us
    pallas_call x1, Pallas kernels, backward_call(): pl.pallas_call(functools.partial(backward_kernel, heads, head_dim), grid_...  58.4 us
    pallas_call x1, Pallas kernels, gather_call(): pl.pallas_call(functools.partial(gather_kernel, wide, narrow), in_specs=[...  43.4 us
    pallas_call x1, Pallas kernels, forward_call(): pl.pallas_call(functools.partial(forward_kernel, heads, head_dim), grid_s...  29.2 us
    unnamed x98, local copies, waits for them, and re-layouts  25.7 us
    sub x5, other arithmetic, adamw(): return (param - rate * (direction + decay * param), moment, square)  15.4 us
  transfers between devices with their start and end apart: 25, of which 10 were waited for; matrix products, arithmetic and copies ran while one was open for 19% of the time, Pallas kernels for 39%

profile of v2, /device:TPU:0, one launch (start us, length us, event | category | flops | bytes accessed | tf_op | source)
XLA Modules:
  0.0 558.6 jit_solution(5006175818376286467)
XLA Ops:
  16.5 43.4 %gather.1 = (bf16[2048,1024]{1,0:T(8,128)(2,1)}, bf16[1024,768]{1,0:T(8,128)(2,1)}, bf16[8,16,128]{2,1,0:T(8,128)(2,1)}, s32[4,8,512]{2,1,0:T(8,128)}) custom-call(bf16[512,1024]{1,0:T(8,128)(2,1)} %tok.1, bf16[128,768]{1,0:T(8,128)(2,1)} %pad_maximum_fusion.6.qkv, bf16[16,128]{1,0:T(8,128)(2,1)} %pad.4.vec, s32[8,512]{1,0:T(8,128)} %pad_add_fusion.tag), custom_call_target="tpu_custom_call" | custom-call | tf_op jit(solution)/shard_map/gather/pallas_call | solution.py:191
  66.9 2.5 fusion.29.onehot_ref
  69.4 12.3 %qkv.1 = (bf16[2048,256]{1,0:T(8,128)(2,1)}, bf16[2048,256]{1,0:T(8,128)(2,1)}, bf16[2048,256]{1,0:T(8,128)(2,1)}, f32[2048,256]{1,0:T(8,128)}, bf16[2048,1024]{1,0:T(8,128)(2,1)}) custom-call(bf16[2048,1024]{1,0:T(8,128)(2,1)} %get-tuple-element.36.x_ref.tok, f32[2,1024]{1,0:T(2,128)} %slice_bitcast_fusion.vec_ref, ...), custom_call_target="tpu_custom_call" | custom-call | flops 3221225472 | bytes 12582912 | tf_op jit(solution)/shard_map/qkv/pallas_call | solution.py:84
  81.7 29.2 %attention_forward.1 = (bf16[2048,256]{1,0:T(8,128)(2,1)}, f32[8,8,256]{2,1,0:T(8,128)}) custom-call(s32[8]{0:T(128)} %get-tuple-element.121.low_ref, s32[8]{0:T(128)} %get-tuple-element.120.high_ref, bf16[2048,256]{1,0:T(8,128)(2,1)} %get-tuple-element.39.q_ref, bf16[2048,256]{1,0:T(8,128)(2,1)} %get-tuple-element.40.k_ref, ...), custom_call_target="tpu_custom_call" | custom-call | flops 12884901888 | bytes 4194304 | tf_op jit(solution)/shard_map/attention_forward/pallas_call | solution.py:454
  113.3 3.6 all-to-all-start
  117.9 13.4 %all-to-all-done = bf16[4,512,256]{1,2,0:T(8,128)(2,1)S(1)} async-done(((bf16[4,512,256]{1,2,0:T(8,128)(2,1)}), bf16[4,512,256]{1,2,0:T(8,128)(2,1)S(1)}, u32[]{:S(2)}, u32[]{:S(2)}) %all-to-all-start) | async-done | bytes 1048608 | tf_op jit(solution)/shard_map/all_to_all | solution.py:678
  132.3 3.3 fusion.59
  136.4 2.5 constant_dynamic-update-slice_fusion.1
  141.3 13.6 %all-gather.6.cloned.1.call-done = bf16[1024,2048]{1,0:T(8,128)(2,1)} async-done(((bf16[128,2048]{1,0:T(8,128)(2,1)}), bf16[1024,2048]{1,0:T(8,128)(2,1)}) %all-gather.6.cloned.1.call-update) | async-done | bytes 4194320 | tf_op jit(solution)/shard_map/all_gather | solution.py:653
  154.8 10.7 %multiply_convert_fusion = (bf16[1024,2048]{1,0:T(8,128)(2,1)}, f32[1024,2048]{1,0:T(8,128)}) fusion(f32[2048]{0:T(1024)S(1)} %bitcast.140, bf16[1024,2048]{1,0:T(8,128)(2,1)} %all-gather.6.cloned.1.call-done, bf16[512,1024]{1,0:T(8,128)(2,1)} %collective-permute-done, bf16[512,1024]{1,0:T(8,128)(2,1)} %copy-done.22), kind=kOutput, calls=%fused_computation.8 | convolution fusion | flops 4311744512 | bytes 18882560 | tf_op jit(solution)/shard_map/dot_general | solution.py:18
  165.5 63.4 %all-gather.8.cloned.1.call-done = bf16[1024,2048]{1,0:T(8,128)(2,1)} async-done(((bf16[128,2048]{1,0:T(8,128)(2,1)}), bf16[1024,2048]{1,0:T(8,128)(2,1)}) %all-gather.8.cloned.1.call-update) | async-done | bytes 4194320 | tf_op jit(solution)/shard_map/all_gather | solution.py:654
  228.9 10.7 %convert_reduce_fusion = (f32[2048]{0:T(1024)S(1)}, bf16[1024,2048]{1,0:T(8,128)(2,1)S(1)}) fusion(f32[1024,2048]{1,0:T(8,128)} %get-tuple-element.113, f32[2048]{0:T(1024)S(1)} %bitcast.141, bf16[1024,1024]{1,0:T(8,128)(2,1)} %constant_dynamic-update-slice_fusion, bf16[1024,2048]{1,0:T(8,128)(2,1)} %all-gather.8.cloned.1.call-done), kind=kOutput, calls=%fused_computation.7 | convolution fusion | flops 4322228224 | bytes 18890752 | tf_op jit(solution)/shard_map/dot_general | solution.py:18
  241.6 7.4 %convolution_convert_fusion.1 = bf16[1024,2048]{1,0:T(8,128)(2,1)} fusion(bf16[1024,2048]{1,0:T(8,128)(2,1)S(1)} %get-tuple-element.115, bf16[512,1024]{1,0:T(8,128)(2,1)} %collective-permute-done, bf16[512,1024]{1,0:T(8,128)(2,1)S(1)} %copy-done.23), kind=kOutput, calls=%fused_computation.12 | convolution fusion | flops 4301258752 | bytes 10485760 | tf_op jit(solution)/shard_map/dot_general | solution.py:18
  250.5 7.9 %fusion.61 = f32[1024,1024]{1,0:T(8,128)S(1)} fusion(bf16[1024,2048]{1,0:T(8,128)(2,1)} %copy-done.42, bf16[1024,2048]{1,0:T(8,128)(2,1)} %all-gather.6.cloned.1.call-done), kind=kOutput, calls=%fused_computation.199 | convolution fusion | flops 4294967296 | bytes 12582912 | tf_op jit(solution)/shard_map/dot_general | solution.py:18
  260.6 4.5 fusion.60
  269.6 3.4 convert_reduce_fusion.4
  275.4 4.3 all-to-all-start.1
  279.7 9.4 %convolution_convert_fusion = bf16[1024,2048]{1,0:T(8,128)(2,1)} fusion(bf16[1024,1024]{1,0:T(8,128)(2,1)} %constant_dynamic-update-slice_fusion, bf16[1024,2048]{1,0:T(8,128)(2,1)} %get-tuple-element.112), kind=kOutput, calls=%fused_computation.11 | convolution fusion | flops 4297064448 | bytes 10485760 | tf_op jit(solution)/shard_map/dot_general | solution.py:18
  291.3 2.5 fusion.49
  297.2 58.4 %attention_backward.1.grad_proj = bf16[2048,768]{1,0:T(8,128)(2,1)} custom-call(s32[8]{0:T(128)} %get-tuple-element.121.low_ref, s32[8]{0:T(128)} %get-tuple-element.120.high_ref, bf16[2048,256]{1,0:T(8,128)(2,1)} %get-tuple-element.39.q_ref, bf16[2048,256]{1,0:T(8,128)(2,1)} %get-tuple-element.40.k_ref, bf16[2048,256]{1,0:T(8,128)(2,1)} %get-tuple-element.41.v_ref, ...), custom_call_target="tpu_custom_call" | custom-call | flops 30064771072 | bytes 10485760 | tf_op jit(solution)/shard_map/attention_backward/pallas_call | solution.py:567
  355.6 2.4 convert_reduce_fusion.1
  359.4 7.9 %convolution_convert_fusion.2.part = bf16[1024,768]{1,0:T(8,128)(2,1)} fusion(bf16[2048,1024]{1,0:T(8,128)(2,1)} %get-tuple-element.43, bf16[2048,768]{1,0:T(8,128)(2,1)} %attention_backward.1.grad_proj), kind=kOutput, calls=%fused_computation.60 | convolution fusion | flops 3222011904 | bytes 8912896 | tf_op jit(solution)/shard_map/dot_general | solution.py:18
  367.3 72.8 %tail.1 = (f32[512,1024]{1,0:T(8,128)}, bf16[4,128,768]{2,1,0:T(8,128)(2,1)}, f32[16,1024]{1,0:T(8,128)}) custom-call(bf16[1024,768]{1,0:T(8,128)(2,1)} %convolution_convert_fusion.2.part, bf16[2048,768]{1,0:T(8,128)(2,1)} %attention_backward.1.grad_proj, bf16[1024,768]{1,0:T(8,128)(2,1)} %get-tuple-element.38.w_ref.weight, ...), custom_call_target="tpu_custom_call" | custom-call | tf_op jit(solution)/shard_map/tail/pallas_call | solution.py:304
  455.8 12.5 %collective-permute-done.5 = bf16[4,128,512]{2,1,0:T(8,128)(2,1)S(1)} collective-permute-done((bf16[4,128,512]{2,1,0:T(8,128)(2,1)S(1)}, bf16[4,128,512]{2,1,0:T(8,128)(2,1)S(1)}, u32[]{:S(2)}, u32[]{:S(2)}) %collective-permute-start.5) | collective-permute-done | bytes 524320 | tf_op jit(solution)/shard_map/ppermute | solution.py:629
  468.6 9.2 %collective-permute-start.8 = (bf16[128,512]{1,0:T(8,128)(2,1)S(1)}, bf16[128,512]{1,0:T(8,128)(2,1)S(1)}, u32[]{:S(2)}, u32[]{:S(2)}) collective-permute-start(bf16[128,512]{1,0:T(8,128)(2,1)S(1)} %get-tuple-element.91), channel_id=1, source_target_pairs={{0,24},{4,28},{8,0},{12,4},{16,8},{20,12},{24,16},{28,20},{1,25},{... | collective-permute-start | bytes 393224 | tf_op jit(solution)/shard_map/ppermute | solution.py:634
  479.3 2.4 collective-permute-done.8
  481.7 6.9 %collective-permute-done.7 = bf16[128,512]{1,0:T(8,128)(2,1)S(1)} collective-permute-done((bf16[128,512]{1,0:T(8,128)(2,1)S(1)}, bf16[128,512]{1,0:T(8,128)(2,1)S(1)}, u32[]{:S(2)}, u32[]{:S(2)}) %collective-permute-start.7) | collective-permute-done | bytes 131104 | tf_op jit(solution)/shard_map/ppermute | solution.py:634
  498.7 6.4 %collective-permute-done.15 = bf16[128,2048]{1,0:T(8,128)(2,1)} collective-permute-done((bf16[128,2048]{1,0:T(8,128)(2,1)}, bf16[128,2048]{1,0:T(8,128)(2,1)}, u32[]{:S(2)}, u32[]{:S(2)}) %collective-permute-start.15) | collective-permute-done | bytes 524320 | tf_op jit(solution)/shard_map/ppermute | solution.py:621
  514.8 12.8 %norm.1 = (f32[16,128]{1,0:T(8,128)}, f32[8,128]{1,0:T(8,128)}) custom-call(f32[8,16,128]{2,1,0:T(8,128)} %fusion.43.slices), custom_call_target="tpu_custom_call" | custom-call | tf_op jit(solution)/shard_map/norm/pallas_call | solution.py:364
  532.7 5.7 %multiply_subtract_fusion.2 = (f32[128,3072]{1,0:T(8,128)}, f32[128,3072]{1,0:T(8,128)}, f32[128,3072]{1,0:T(8,128)}) fusion(f32[128,3072]{1,0:T(8,128)} %param.27, f32[]{:T(128)} %bitcast.55, f32[]{:T(128)} %bitcast.54, f32[]{:T(128)} %bitcast.53, f32[]{:T(128)} %bitcast.30, f32[]{:T(128)S(6)} %div.176, bf16[128,3072]{1,0:T(8,128)(2,1)} %copy-done.11, ...), kind=kLoop, calls=%fused_computation.64 | loop fusion | flops 6684672 | bytes 10223636 | tf_op jit(solution)/shard_map/sub | solution.py:596
  540.7 3.9 multiply_subtract_fusion.1
  546.1 3.8 multiply_subtract_fusion
  (225 shorter events, 84.6 us)
Async XLA Ops:
  7.2 124.1 %all-gather.4.cloned.1.call-start = ((), (), s32[]{:S(2)}) async-start(), calls=%async_computation.4 | async-start | bytes 2359296 | tf_op jit(solution)/shard_map/all_gather | solution.py:652
  9.1 145.8 %all-gather.6.cloned.1.call-start = ((), (), s32[]{:S(2)}) async-start(), calls=%async_computation.5 | async-start | bytes 4718592 | tf_op jit(solution)/shard_map/all_gather | solution.py:653
  11.2 217.7 %all-gather.8.cloned.1.call-start = ((), (), s32[]{:S(2)}) async-start(), calls=%async_computation.6 | async-start | bytes 4718592 | tf_op jit(solution)/shard_map/all_gather | solution.py:654
  110.9 21.3 %copy-start = (bf16[512,1024]{1,0:T(8,128)(2,1)S(1)}, bf16[512,1024]{1,0:T(8,128)(2,1)}, u32[]{:S(2)}) copy-start(bf16[512,1024]{1,0:T(8,128)(2,1)} %tok.1) | copy-start | bytes 3145732
  113.3 18.0 %all-to-all-start = ((bf16[4,512,256]{1,2,0:T(8,128)(2,1)}), bf16[4,512,256]{1,2,0:T(8,128)(2,1)S(1)}, u32[]{:S(2)}, u32[]{:S(2)}) async-start(bf16[4,512,256]{1,2,0:T(8,128)(2,1)} %copy.50), calls=%async_computation | async-start | bytes 2097152 | tf_op jit(solution)/shard_map/all_to_all | solution.py:678
  116.9 351.6 %reduce-scatter.3.cloned.1.call-start = ((), (), s32[]{:S(2)}) async-start(), calls=%async_computation.7 | async-start | bytes 4718592 | tf_op jit(solution)/shard_map/reduce_scatter | solution.py:697
  117.4 21.6 %collective-permute-start.2 = (bf16[512,1024]{1,0:T(8,128)(2,1)}, bf16[512,1024]{1,0:T(8,128)(2,1)}, u32[]{:S(2)}, u32[]{:S(2)}) collective-permute-start(bf16[512,1024]{1,0:T(8,128)(2,1)} %param.22), channel_id=1, source_target_pairs={{0,1},{1,0},{2,3},{3,2},{4,5},{5,4},{6,7},{7,6},{8,9},{9,8},{10,11... | collective-permute-start | bytes 3145736 | tf_op jit(solution)/shard_map/ppermute | solution.py:618
  136.3 4.9 collective-permute-start
  228.9 12.7 %copy-start.23 = (bf16[512,1024]{1,0:T(8,128)(2,1)S(1)}, bf16[512,1024]{1,0:T(8,128)(2,1)}, u32[]{:S(2)}) copy-start(bf16[512,1024]{1,0:T(8,128)(2,1)} %copy-done.22) | copy-start | bytes 3145732
  258.7 7.5 %collective-permute-start.3 = (f32[512,1024]{1,0:T(8,128)S(1)}, f32[512,1024]{1,0:T(8,128)S(1)}, u32[]{:S(2)}, u32[]{:S(2)}) collective-permute-start(f32[512,1024]{1,0:T(8,128)S(1)} %slice.208), channel_id=1, source_target_pairs={{0,1},{1,0},{2,3},{3,2},{4,5},{5,4},{6,7},{7,6},{8,9},{9,8},{10,11... | collective-permute-start | bytes 6291464 | tf_op jit(solution)/shard_map/ppermute | solution.py:618
  265.4 4.2 collective-permute-start.1
  275.4 21.9 %all-to-all-start.1 = ((bf16[512,4,256]{2,0,1:T(8,128)(2,1)}), bf16[512,4,256]{2,0,1:T(8,128)(2,1)}, u32[]{:S(2)}, u32[]{:S(2)}) async-start(bf16[512,4,256]{2,0,1:T(8,128)(2,1)} %bitcast.113), calls=%async_computation.1 | async-start | bytes 2097152 | tf_op jit(solution)/shard_map/all_to_all | solution.py:710
  279.6 210.8 %reduce-scatter.5.cloned.1.call-start = ((), (), s32[]{:S(2)}) async-start(), calls=%async_computation.8 | async-start | bytes 4718592 | tf_op jit(solution)/shard_map/reduce_scatter | solution.py:694
  296.9 155.3 %collective-permute-start.4 = (bf16[1024,512]{1,0:T(8,128)(2,1)}, bf16[1024,512]{1,0:T(8,128)(2,1)}, u32[]{:S(2)}, u32[]{:S(2)}) collective-permute-start(bf16[1024,512]{1,0:T(8,128)(2,1)} %dynamic-slice_convert_fusion), channel_id=1, source_target_pairs={{0,1},{1,0},{2,3},{3,2},{4,5},{5,4},{6,7},{7,6},{8,9},{9,8},{10,11... | collective-permute-start | bytes 3145736 | tf_op jit(solution)/shard_map/ppermute | solution.py:618
  441.8 10.4 %copy-start.2 = (f32[1024,1024]{1,0:T(8,128)S(1)}, f32[1024,1024]{1,0:T(8,128)}, u32[]{:S(2)}) copy-start(f32[1024,1024]{1,0:T(8,128)} %copy-done.1) | copy-start | bytes 12582916
  454.0 14.3 %collective-permute-start.5 = (bf16[4,128,512]{2,1,0:T(8,128)(2,1)S(1)}, bf16[4,128,512]{2,1,0:T(8,128)(2,1)S(1)}, u32[]{:S(2)}, u32[]{:S(2)}) collective-permute-start(bf16[4,128,512]{2,1,0:T(8,128)(2,1)S(1)} %dynamic-slice_bitcast_fusion), channel_id=1, source_target_pairs={{0,4},{4,0},{8,12},{12,8},{16,20},{20,16},{24,28},{28,24},{1,5},{5... | collective-permute-start | bytes 1572872 | tf_op jit(solution)/shard_map/ppermute | solution.py:629
  455.8 22.7 %copy-start.10 = (bf16[128,3072]{1,0:T(8,128)(2,1)S(1)}, bf16[128,3072]{1,0:T(8,128)(2,1)}, u32[]{:S(2)}) copy-start(bf16[128,3072]{1,0:T(8,128)(2,1)} %copy-done.9) | copy-start | bytes 2359300
  468.5 37.5 %copy-start.26 = (bf16[128,2048]{1,0:T(8,128)(2,1)S(1)}, bf16[128,2048]{1,0:T(8,128)(2,1)}, u32[]{:S(2)}) copy-start(bf16[128,2048]{1,0:T(8,128)(2,1)} %reduce-scatter.3.cloned.1.call-done) | copy-start | bytes 1572868
  468.5 22.4 %collective-permute-start.12 = (bf16[128,2048]{1,0:T(8,128)(2,1)}, bf16[128,2048]{1,0:T(8,128)(2,1)S(1)}, u32[]{:S(2)}, u32[]{:S(2)}) collective-permute-start(bf16[128,2048]{1,0:T(8,128)(2,1)} %reduce-scatter.3.cloned.1.call-done), channel_id=1, source_target_pairs={{0,2},{1,3},{2,0},{3,1},{4,6},{5,7},{6,4},{7,5},{8,10},{9,11},{10,... | collective-permute-start | bytes 1572872 | tf_op jit(solution)/shard_map/ppermute | solution.py:621
  468.6 13.1 %collective-permute-start.8 = (bf16[128,512]{1,0:T(8,128)(2,1)S(1)}, bf16[128,512]{1,0:T(8,128)(2,1)S(1)}, u32[]{:S(2)}, u32[]{:S(2)}) collective-permute-start(bf16[128,512]{1,0:T(8,128)(2,1)S(1)} %get-tuple-element.91), channel_id=1, source_target_pairs={{0,24},{4,28},{8,0},{12,4},{16,8},{20,12},{24,16},{28,20},{1,25},{... | collective-permute-start | bytes 393224 | tf_op jit(solution)/shard_map/ppermute | solution.py:634
  477.8 10.8 %collective-permute-start.7 = (bf16[128,512]{1,0:T(8,128)(2,1)S(1)}, bf16[128,512]{1,0:T(8,128)(2,1)S(1)}, u32[]{:S(2)}, u32[]{:S(2)}) collective-permute-start(bf16[128,512]{1,0:T(8,128)(2,1)S(1)} %get-tuple-element.92), channel_id=1, source_target_pairs={{0,16},{4,20},{8,24},{12,28},{16,0},{20,4},{24,8},{28,12},{1,17},{... | collective-permute-start | bytes 393224 | tf_op jit(solution)/shard_map/ppermute | solution.py:634
  477.8 10.8 %collective-permute-start.6 = (bf16[128,512]{1,0:T(8,128)(2,1)S(1)}, bf16[128,512]{1,0:T(8,128)(2,1)S(1)}, u32[]{:S(2)}, u32[]{:S(2)}) collective-permute-start(bf16[128,512]{1,0:T(8,128)(2,1)S(1)} %get-tuple-element.90), channel_id=1, source_target_pairs={{0,8},{4,12},{8,16},{12,20},{16,24},{20,28},{24,0},{28,4},{1,9},{5... | collective-permute-start | bytes 393224 | tf_op jit(solution)/shard_map/ppermute | solution.py:634
  488.8 5.3 collective-permute-start.9
  490.4 14.7 %collective-permute-start.13 = (bf16[128,2048]{1,0:T(8,128)(2,1)}, bf16[128,2048]{1,0:T(8,128)(2,1)S(1)}, u32[]{:S(2)}, u32[]{:S(2)}) collective-permute-start(bf16[128,2048]{1,0:T(8,128)(2,1)} %reduce-scatter.3.cloned.1.call-done), channel_id=1, source_target_pairs={{0,1},{1,0},{2,3},{3,2},{4,5},{5,4},{6,7},{7,6},{8,9},{9,8},{10,11... | collective-permute-start | bytes 1572872 | tf_op jit(solution)/shard_map/ppermute | solution.py:618
  490.4 14.7 %collective-permute-start.15 = (bf16[128,2048]{1,0:T(8,128)(2,1)}, bf16[128,2048]{1,0:T(8,128)(2,1)}, u32[]{:S(2)}, u32[]{:S(2)}) collective-permute-start(bf16[128,2048]{1,0:T(8,128)(2,1)} %reduce-scatter.5.cloned.1.call-done), channel_id=1, source_target_pairs={{0,2},{1,3},{2,0},{3,1},{4,6},{5,7},{6,4},{7,5},{8,10},{9,11},{10,... | collective-permute-start | bytes 1572872 | tf_op jit(solution)/shard_map/ppermute | solution.py:621
  490.9 14.3 %copy-start.28 = (bf16[128,2048]{1,0:T(8,128)(2,1)}, bf16[128,2048]{1,0:T(8,128)(2,1)S(1)}, u32[]{:S(2)}) copy-start(bf16[128,2048]{1,0:T(8,128)(2,1)S(1)} %collective-permute-done.12) | copy-start | bytes 1572868
  490.9 15.1 %collective-permute-start.14 = (bf16[128,2048]{1,0:T(8,128)(2,1)S(1)}, bf16[128,2048]{1,0:T(8,128)(2,1)}, u32[]{:S(2)}, u32[]{:S(2)}) collective-permute-start(bf16[128,2048]{1,0:T(8,128)(2,1)S(1)} %collective-permute-done.12), channel_id=1, source_target_pairs={{0,1},{1,0},{2,3},{3,2},{4,5},{5,4},{6,7},{7,6},{8,9},{9,8},{10,11... | collective-permute-start | bytes 1572872 | tf_op jit(solution)/shard_map/ppermute | solution.py:618
  491.9 13.2 %copy-start.11 = (bf16[128,3072]{1,0:T(8,128)(2,1)}, bf16[128,3072]{1,0:T(8,128)(2,1)S(1)}, u32[]{:S(2)}) copy-start(bf16[128,3072]{1,0:T(8,128)(2,1)S(1)} %bitcast_dynamic-update-slice_fusion) | copy-start | bytes 2359300
  491.9 3.2 collective-permute-start.10
  494.1 1.3 collective-permute-start.11
  498.5 11.0 %collective-permute-start.16 = (bf16[128,2048]{1,0:T(8,128)(2,1)S(1)}, bf16[128,2048]{1,0:T(8,128)(2,1)}, u32[]{:S(2)}, u32[]{:S(2)}) collective-permute-start(bf16[128,2048]{1,0:T(8,128)(2,1)S(1)} %copy-done.27), channel_id=1, source_target_pairs={{0,1},{1,0},{2,3},{3,2},{4,5},{5,4},{6,7},{7,6},{8,9},{9,8},{10,11... | collective-permute-start | bytes 1572872 | tf_op jit(solution)/shard_map/ppermute | solution.py:618
  505.1 4.4 collective-permute-start.17
  (36 other events, 151.1 us)
Sparse Core Ops, SparseCore 0:
  10.7 66.9 all-gather.3
  80.4 74.4 all-gather.5
  157.5 71.3 all-gather.7
  249.2 86.8 reduce-scatter.2
  339.5 100.2 reduce-scatter.4

commit v3 on v2

--- a/solution.py
+++ b/solution.py
@@ -111,14 +111,22 @@
     def __init__(self, send, recv):
         self.send, self.recv, self.all = send, recv, []
 
-    def start(self, src, dst, **target):
+    def make(self, src, dst, **target):
         i = len(self.all)
         copy = pltpu.make_async_remote_copy(
             src_ref=src, dst_ref=dst, send_sem=self.send.at[i], recv_sem=self.recv.at[i],
             device_id=target, device_id_type=MESH,
         )
-        copy.start()
         self.all.append([copy, False])
+        return i
+
+    def launch(self, *indices):
+        for i in indices:
+            self.all[i][0].start()
+
+    def start(self, src, dst, **target):
+        i = self.make(src, dst, **target)
+        self.launch(i)
         return i
 
     def arrived(self, i):
@@ -377,24 +385,115 @@
     )(slices)
 
 
+CLIP = 784
+
+
 def head_lanes(shape, head, head_dim):
     lane = lax.broadcasted_iota(jnp.int32, shape, 1)
     return lane // head_dim == head
 
 
+def meeting(block, blocks):
+    before, after = CLIP // BLOCK, -(-2 * CLIP // BLOCK)
+    low = before * (block // after)
+    high = blocks - (blocks - after) * (1 - jnp.minimum(block // before, 1))
+    return low, high
+
+
 def forward_kernel(
-    heads, head_dim, low_ref, high_ref, q_ref, k_ref, v_ref, seg_ref, tag_ref, o_ref, lse_ref,
-    values_turned, acc, peak, total,
+    heads, head_dim, wide, narrow,
+    q_ref, k_ref, v_ref, seg_ref, tag_ref, up_ref, out_ref,
+    o_ref, lse_ref, mixed_ref, up_all, out_all,
+    values_turned, acc, peak, total, o_box, send, recv, mix_send, mix_recv, local,
 ):
     step = pl.program_id(0)
-    width = q_ref.shape[1]
+    rows, width = q_ref.shape
+    blocks = rows // BLOCK
+    per = blocks // narrow
+    last = blocks - 1
+    w, n = lax.axis_index("wide"), lax.axis_index("narrow")
+    column = wide // 2
+    z, y, side = w // 2, lax.rem(w, 2), lax.rem(n, 2)
+    near, mate = w + 1 - 2 * y, n + 1 - 2 * side
+    block = lax.rem((n + 1) * per + step, blocks)
+
+    go = Copies(send, recv)
+    wide_rows, half = out_ref.shape
+    out_cols = pl.ds(pl.multiple_of(side * half, half), half)
+    pieces = 2
+    piece = up_ref.shape[1] // pieces
+    up_at = lambda i, p: up_all.at[rows_at(i, wide_rows), pl.ds(p * piece, piece)]
+    out_at = lambda i: out_all.at[rows_at(i, wide_rows), out_cols]
+    source = lambda d: lax.rem(z - d + column, column) * 2 + y
+    target = lambda d: lax.rem(z + d, column) * 2 + y
+    starts, early, late = [], [], []
+    out_near = [go.make(out_ref, out_at(w), wide=near)]
+    out_mate = [go.make(out_ref, out_at(w), narrow=mate)]
+    starts += out_near + out_mate
+    for d in range(1, column):
+        far = go.make(out_ref, out_at(w), wide=target(d))
+        block_ref = out_at(source(d))
+        out_near.append(go.make(block_ref, block_ref, wide=near))
+        starts.append(far)
+        early.append((far, [out_near[-1], go.make(block_ref, block_ref, narrow=mate)]))
+    for d in range(column):
+        block_ref = out_at(lax.rem(z - d + column, column) * 2 + 1 - y)
+        late.append((out_near[d], [go.make(block_ref, block_ref, narrow=mate)]))
+    for p in range(pieces):
+        cols = pl.ds(p * piece, piece)
+        starts.append(go.make(up_ref.at[:, cols], up_at(w, p), wide=near))
+        for d in range(1, column):
+            far = go.make(up_ref.at[:, cols], up_at(w, p), wide=target(d))
+            block_ref = up_at(source(d), p)
+            starts.append(far)
+            early.append((far, [go.make(block_ref, block_ref, wide=near)]))
+    actions = early + late
+    own = [
+        pltpu.make_async_copy(up_ref, up_all.at[rows_at(w, wide_rows)], local.at[0]),
+        pltpu.make_async_copy(out_ref, out_at(w), local.at[1]),
+    ]
+
+    mine = pl.ds(pl.multiple_of(n * width, width), width)
+
+    def result(s):
+        at = lax.rem((n + 1) * per + s, blocks)
+        return pltpu.make_async_remote_copy(
+            src_ref=o_box.at[rows_at(at, BLOCK)],
+            dst_ref=mixed_ref.at[rows_at(lax.rem(s, per), BLOCK), mine],
+            send_sem=mix_send.at[s],
+            recv_sem=mix_recv.at[s],
+            device_id={"narrow": lax.rem(n + 1 + s // per, narrow)},
+            device_id_type=MESH,
+        )
+
+    def result_here(s):
+        return pltpu.make_async_copy(
+            o_box.at[rows_at(n * per + s, BLOCK)], mixed_ref.at[rows_at(s, BLOCK), mine], local.at[2 + s]
+        )
 
     @pl.when(step == 0)
     def _():
+        greet(
+            [{"wide": near}] + [{"wide": target(d)} for d in range(1, column)] + others("narrow", n, narrow)
+        )
+        go.launch(*starts)
+        for copy in own:
+            copy.start()
         values_turned[...] = v_ref[...].T
 
-    query = q_ref[...] * jnp.asarray(head_dim**-0.5, BF)
-    seg = seg_ref[0]
+    share = -(-len(actions) // last)
+    for i in range(last):
+        some = actions[i * share : (i + 1) * share]
+
+        @pl.when(step == i + 1)
+        def _():
+            for arrival, follow in some:
+                go.arrived(arrival)
+                go.launch(*follow)
+
+    at = rows_at(block, BLOCK)
+    query = q_ref[at, :] * jnp.asarray(head_dim**-0.5, BF)
+    seg = seg_ref[pl.ds(block, 1)][0]
     masked_query = [
         jnp.where(head_lanes(query.shape, h, head_dim), query, jnp.zeros_like(query)) for h in range(heads)
     ]
@@ -408,58 +507,82 @@
         allowed = tag_ref[pl.ds(start, BLOCK), :] == seg
         scores = [jnp.where(allowed, dot(key, masked_query[h], 1, 1), -1e30) for h in range(heads)]
         for h in range(heads):
-            rows = slice(h * head_dim, (h + 1) * head_dim)
+            lines = slice(h * head_dim, (h + 1) * head_dim)
             old = peak[h : h + 1, :]
             new = jnp.maximum(old, jnp.max(scores[h], axis=0, keepdims=True))
             probs = jnp.exp(scores[h] - new)
             keep = jnp.exp(old - new)
             peak[h : h + 1, :] = new
             total[h : h + 1, :] = total[h : h + 1, :] * keep + jnp.sum(probs, axis=0, keepdims=True)
-            value = values_turned[rows, pl.ds(start, BLOCK)]
-            acc[rows, :] = acc[rows, :] * keep + dot(value, probs.astype(BF), 1, 0)
+            value = values_turned[lines, pl.ds(start, BLOCK)]
+            acc[lines, :] = acc[lines, :] * keep + dot(value, probs.astype(BF), 1, 0)
         return carry
 
-    lax.fori_loop(low_ref[step], high_ref[step], body, 0)
+    low, high = meeting(block, blocks)
+    lax.fori_loop(low, high, body, 0)
     parts = [acc[h * head_dim : (h + 1) * head_dim, :] / total[h : h + 1, :] for h in range(heads)]
-    o_ref[...] = jnp.concatenate(parts, axis=0).T.astype(BF)
-    lse_ref[0] = peak[...] + jnp.log(jnp.maximum(total[...], 1e-30))
-
-
-def forward_call(low, high, q, k, v, seg_rows, tag_col, head_dim):
+    out = jnp.concatenate(parts, axis=0).T.astype(BF)
+    o_ref[at, :] = out
+    o_box[at, :] = out
+    lse_ref[pl.ds(block, 1)] = (peak[...] + jnp.log(jnp.maximum(total[...], 1e-30)))[None]
+
+    @pl.when(step < blocks - per)
+    def _():
+        result(step).start()
+
+    @pl.when(step == last)
+    def _():
+        for s in range(per):
+            result_here(s).start()
+        for copy in own:
+            copy.wait()
+        for s in range(blocks - per):
+            result(s).wait()
+        for s in range(per):
+            result_here(s).wait()
+        go.finish()
+
+
+def forward_call(q, k, v, seg_rows, tag_col, up_low, out_half, head_dim, wide, narrow):
     rows, width = q.shape
     heads = width // head_dim
     blocks = rows // BLOCK
-    whole = lambda a: pl.BlockSpec(a.shape, lambda i, *_: (0,) * a.ndim)
-    grid_spec = pltpu.PrefetchScalarGridSpec(
-        num_scalar_prefetch=2,
+    column = wide // 2
+    copies = 2 + 3 * (column - 1) + column + 2 * (2 * column - 1)
+    whole = lambda a: pl.BlockSpec(a.shape, lambda i: (0,) * a.ndim)
+    anywhere = pl.BlockSpec(memory_space=pl.ANY)
+    lse = jax.ShapeDtypeStruct((blocks, 8, BLOCK), F32)
+    seg_rows = seg_rows[:, None, :]
+    return pl.pallas_call(
+        functools.partial(forward_kernel, heads, head_dim, wide, narrow),
         grid=(blocks,),
-        in_specs=[
-            pl.BlockSpec((BLOCK, width), lambda i, *_: (i, 0)),
-            whole(k),
-            whole(v),
-            pl.BlockSpec((1, 1, BLOCK), lambda i, *_: (i, 0, 0)),
-            whole(tag_col),
-        ],
-        out_specs=[
-            pl.BlockSpec((BLOCK, width), lambda i, *_: (i, 0)),
-            pl.BlockSpec((1, 8, BLOCK), lambda i, *_: (i, 0, 0)),
+        in_specs=[whole(a) for a in (q, k, v, seg_rows, tag_col, up_low, out_half)],
+        out_specs=[whole(q), whole(lse), anywhere, anywhere, anywhere],
+        out_shape=[
+            jax.ShapeDtypeStruct((rows, width), BF),
+            lse,
+            jax.ShapeDtypeStruct((rows // narrow, width * narrow), BF),
+            jax.ShapeDtypeStruct((up_low.shape[0] * wide, up_low.shape[1]), BF),
+            jax.ShapeDtypeStruct((out_half.shape[0] * wide, 2 * out_half.shape[1]), BF),
         ],
         scratch_shapes=[
             pltpu.VMEM((width, rows), BF),
             pltpu.VMEM((width, BLOCK), F32),
             pltpu.VMEM((8, BLOCK), F32),
             pltpu.VMEM((8, BLOCK), F32),
-        ],
-    )
-    return pl.pallas_call(
-        functools.partial(forward_kernel, heads, head_dim),
-        grid_spec=grid_spec,
-        out_shape=[jax.ShapeDtypeStruct((rows, width), BF), jax.ShapeDtypeStruct((blocks, 8, BLOCK), F32)],
+            pltpu.VMEM((rows, width), BF),
+            pltpu.SemaphoreType.DMA((copies,)),
+            pltpu.SemaphoreType.DMA((copies,)),
+            pltpu.SemaphoreType.DMA((blocks,)),
+            pltpu.SemaphoreType.DMA((blocks,)),
+            pltpu.SemaphoreType.DMA((2 + blocks // narrow,)),
+        ],
+        compiler_params=pltpu.CompilerParams(collective_id=3, has_side_effects=True),
         cost_estimate=pl.CostEstimate(
-            flops=heads * rows * rows * width * 3, bytes_accessed=rows * width * 8, transcendentals=heads * rows * rows
+            flops=heads * rows * rows * width * 4, bytes_accessed=rows * width * 8, transcendentals=heads * rows * rows
         ),
         name="attention_forward",
-    )(low, high, q, k, v, seg_rows[:, None, :], tag_col)
+    )(q, k, v, seg_rows, tag_col, up_low, out_half)
 
 
 def backward_kernel(
@@ -638,7 +761,7 @@
         return lax.dynamic_slice_in_dim(value, start, size, axis)
 
     qkv_low = jnp.concatenate([take(weight_qkv, i * width + me * mine, mine) for i in range(3)], axis=1).astype(BF)
-    out_low = weight_out.astype(BF)
+    out_low = take(weight_out, side * (width // 2), width // 2).astype(BF)
     up_low = take(weight_up, side * half_hidden, half_hidden).astype(BF)
     down_low = take(weight_down, side * half_hidden, half_hidden).astype(BF)
 
@@ -649,8 +772,6 @@
     vec_all = vec_all[:, :, :shard_cols]
     vec = jnp.moveaxis(vec_all, 0, 1).reshape(16, width).astype(F32)[: vectors.shape[0]]
     tag_all = jnp.moveaxis(tag_all, 0, 1).reshape(8, group)
-    out_w = lax.all_gather(out_low, "wide", axis=0, tiled=True)
-    up_w = lax.all_gather(up_low, "wide", axis=0, tiled=True)
     down_w = lax.all_gather(down_low, "wide", axis=0, tiled=True)
 
     xin = tokens.astype(F32)
@@ -672,10 +793,9 @@
 
     bias = jnp.concatenate([take(vec[2 + i : 3 + i], me * mine, mine) for i in range(3)], axis=1)
     query, keys, values, turns, normed1_all = qkv_call(tokens_all, vec[:2], qkv_w, bias, onehot, rotary_table(head_dim), head_dim // 2)
-    mixed_mine, lse = forward_call(
-        low, high, query, keys, values, seg_float.reshape(blocks, BLOCK), key_tag[:, None], head_dim
+    mixed_mine, lse, mixed, up_w, out_w = forward_call(
+        query, keys, values, seg_float.reshape(blocks, BLOCK), key_tag[:, None], up_low, out_low, head_dim, wide, narrow
     )
-    mixed = lax.all_to_all(mixed_mine, "narrow", 0, 1, tiled=True)
 
     resid = xin + (dot(mixed, out_w, 1, 0) + vec[5])
     unit2, inverse2 = norm_parts(resid)

time: 564 us -> 567 us (level)
  waiting for transfers between devices: 123 us -> 55.6 us
  Pallas kernels: 229 us -> 291 us
  local copies, waits for them, and re-layouts: 46.1 us -> 53.3 us
  starting transfers between devices: 22.5 us -> 16.2 us
    pallas_call x1, Pallas kernels: 29.2 us -> 95.6 us  [forward_call(): pl.pallas_call(functools.partial(forward_kernel, heads, head_dim, wide, n...]
    all_gather x1, waiting for transfers between devices: 63.4 us -> 0.02 us  [on_device(): down_w = lax.all_gather(down_low, 'wide', axis=0, tiled=True)]
    reduce_scatter x1, waiting for transfers between devices: 0.01 us -> 27.3 us  [on_device(): lax.psum_scatter(part_down, 'wide', scatter_dimension=0, tiled=True)]
    all_gather x2 -> x0, waiting for transfers between devices: 13.6 us -> none  [the longest x1 13.6 us: on_device(): up_w = lax.all_gather(up_low, 'wide', axis=0, tiled=True)]
    all_to_all x1 -> x0, waiting for transfers between devices: 13.4 us -> none  [on_device(): mixed = lax.all_to_all(mixed_mine, 'narrow', 0, 1, tiled=True)]
    ppermute x3, starting transfers between devices: 9.87 us -> 3.56 us  [scatter(): lax.ppermute(pick(both, (z + d) % column, 0), 'wide', pairs).astype(F32)]
    unnamed x98 -> x104, local copies, waits for them, and re-layouts: 25.7 us -> 31.1 us
  transfers between devices with their start and end apart: 25 -> 22, of which waited for: 10 -> 7; matrix products, arithmetic and copies ran while one was open for 19% -> 25% of each run, Pallas kernels for 39% -> 50%
where the time goes in v3:
time: 567 us; the launch traced here: 558 us
  Pallas kernels  291 us (51%)
  matrix products  68.8 us (12%)
  waiting for transfers between devices  55.6 us (10%)
  local copies, waits for them, and re-layouts  53.3 us (9%)
  other arithmetic  52.8 us (9%)
  between operations  20.5 us (4%)
  starting transfers between devices  16.2 us (3%)
    pallas_call x1, Pallas kernels, forward_call(): pl.pallas_call(functools.partial(forward_kernel, heads, head_dim, wide, n...  95.6 us
    pallas_call x1, Pallas kernels, tail_call(): pl.pallas_call(functools.partial(tail_kernel, wide, narrow), in_specs=[vm...  70.1 us
    dot_general x10, matrix products, dot(): lax.dot_general(a, b, (((ca,), (cb,)), ((), ())), preferred_element_type=...  68.8 us
    pallas_call x1, Pallas kernels, backward_call(): pl.pallas_call(functools.partial(backward_kernel, heads, head_dim), grid_...  58.2 us
    pallas_call x1, Pallas kernels, gather_call(): pl.pallas_call(functools.partial(gather_kernel, wide, narrow), in_specs=[...  40.9 us
    unnamed x104, local copies, waits for them, and re-layouts  31.1 us
    reduce_scatter x1, waiting for transfers between devices, on_device(): lax.psum_scatter(part_down, 'wide', scatter_dimension=0, tiled=True)  27.3 us
    sub x5, other arithmetic, adamw(): return (param - rate * (direction + decay * param), moment, square)  15.4 us
  transfers between devices with their start and end apart: 22, of which 7 were waited for; matrix products, arithmetic and copies ran while one was open for 25% of the time, Pallas kernels for 50%

profile of v3, /device:TPU:0, one launch (start us, length us, event | category | flops | bytes accessed | tf_op | source)
XLA Modules:
  0.0 558.2 jit_solution(17955537993010131838)
XLA Ops:
  7.8 2.1 dynamic-slice_convert_fusion.1
  13.7 40.9 %gather.1 = (bf16[2048,1024]{1,0:T(8,128)(2,1)}, bf16[1024,768]{1,0:T(8,128)(2,1)}, bf16[8,16,128]{2,1,0:T(8,128)(2,1)}, s32[4,8,512]{2,1,0:T(8,128)}) custom-call(bf16[512,1024]{1,0:T(8,128)(2,1)} %tok.1, bf16[128,768]{1,0:T(8,128)(2,1)} %pad_maximum_fusion.6.qkv, bf16[16,128]{1,0:T(8,128)(2,1)} %pad.4.vec, s32[8,512]{1,0:T(8,128)} %pad_add_fusion.tag), custom_call_target="tpu_custom_call" | custom-call | tf_op jit(solution)/shard_map/gather/pallas_call | solution.py:199
  64.4 2.5 fusion.29.onehot_ref
  66.8 12.4 %qkv.1 = (bf16[2048,256]{1,0:T(8,128)(2,1)}, bf16[2048,256]{1,0:T(8,128)(2,1)}, bf16[2048,256]{1,0:T(8,128)(2,1)}, f32[2048,256]{1,0:T(8,128)}, bf16[2048,1024]{1,0:T(8,128)(2,1)}) custom-call(bf16[2048,1024]{1,0:T(8,128)(2,1)} %get-tuple-element.38.x_ref.tok, f32[2,1024]{1,0:T(2,128)} %slice_bitcast_fusion.vec_ref, ...), custom_call_target="tpu_custom_call" | custom-call | flops 3221225472 | bytes 12582912 | tf_op jit(solution)/shard_map/qkv/pallas_call | solution.py:84
  79.2 95.6 %attention_forward.1 = (bf16[2048,256]{1,0:T(8,128)(2,1)}, f32[8,8,256]{2,1,0:T(8,128)}, bf16[512,1024]{1,0:T(8,128)(2,1)}, bf16[1024,2048]{1,0:T(8,128)(2,1)}, bf16[1024,1024]{1,0:T(8,128)(2,1)}) custom-call(bf16[2048,256]{1,0:T(8,128)(2,1)} %get-tuple-element.42.q_ref, bf16[2048,256]{1,0:T(8,128)(2,1)} %get-tuple-element.43.k_ref, ...), custom_call_target="tpu_custom_call" | custom-call | flops 17179869184 | bytes 4194304 | tf_op jit(solution)/shard_map/attention_forward/pallas_call | solution.py:556
  174.9 3.3 fusion.59
  182.2 8.3 %multiply_convert_fusion = (bf16[1024,2048]{1,0:T(8,128)(2,1)S(1)}, f32[1024,2048]{1,0:T(8,128)}) fusion(f32[2048]{0:T(1024)S(1)} %bitcast.132, bf16[1024,2048]{1,0:T(8,128)(2,1)S(1)} %copy-done.44, bf16[512,1024]{1,0:T(8,128)(2,1)S(1)} %collective-permute-done, bf16[512,1024]{1,0:T(8,128)(2,1)S(1)} %add_convert_fusion.1), kind=kOutput, calls=%fused_computation.8 | convolution fusion | flops 4311744512 | bytes 18882560 | tf_op jit(solution)/shard_map/dot_general | solution.py:18
  192.5 6.2 %convolution_convert_fusion = bf16[1024,2048]{1,0:T(8,128)(2,1)} fusion(bf16[1024,1024]{1,0:T(8,128)(2,1)S(1)} %constant_dynamic-update-slice_fusion, bf16[1024,2048]{1,0:T(8,128)(2,1)S(1)} %get-tuple-element.118), kind=kOutput, calls=%fused_computation.11 | convolution fusion | flops 4297064448 | bytes 10485760 | tf_op jit(solution)/shard_map/dot_general | solution.py:18
  199.3 21.5 %convert_reduce_fusion = (f32[2048]{0:T(1024)S(1)}, bf16[1024,2048]{1,0:T(8,128)(2,1)S(1)}) fusion(f32[1024,2048]{1,0:T(8,128)} %get-tuple-element.119, f32[2048]{0:T(1024)S(1)} %bitcast.133, bf16[1024,1024]{1,0:T(8,128)(2,1)} %copy-done.28, bf16[1024,2048]{1,0:T(8,128)(2,1)} %all-gather.2.cloned.1.call-done), kind=kOutput, calls=%fused_computation.7 | convolution fusion | flops 4322228224 | bytes 18890752 | tf_op jit(solution)/shard_map/dot_general | solution.py:18
  222.8 4.5 fusion.61
  231.8 4.5 fusion.60
  241.7 3.4 multiply_reduce_fusion.2
  245.5 3.4 convert_reduce_fusion.4
  251.3 5.3 all-to-all-start
  256.6 8.8 %convolution_convert_fusion.1 = bf16[1024,2048]{1,0:T(8,128)(2,1)} fusion(bf16[1024,2048]{1,0:T(8,128)(2,1)} %copy-done.43, bf16[512,1024]{1,0:T(8,128)(2,1)S(1)} %copy-done.39, bf16[512,1024]{1,0:T(8,128)(2,1)S(1)} %copy-done.22), kind=kOutput, calls=%fused_computation.12 | convolution fusion | flops 4301258752 | bytes 10485760 | tf_op jit(solution)/shard_map/dot_general | solution.py:18
  265.8 27.3 %reduce-scatter.5.cloned.1.call-done = bf16[128,2048]{1,0:T(8,128)(2,1)} async-done(((bf16[1024,2048]{1,0:T(8,128)(2,1)}), bf16[128,2048]{1,0:T(8,128)(2,1)}) %reduce-scatter.5.cloned.1.call-update) | async-done | bytes 524304 | tf_op jit(solution)/shard_map/reduce_scatter | solution.py:814
  294.5 2.5 fusion.49
  300.7 6.0 %collective-permute-done.15 = bf16[128,2048]{1,0:T(8,128)(2,1)} collective-permute-done((bf16[128,2048]{1,0:T(8,128)(2,1)}, bf16[128,2048]{1,0:T(8,128)(2,1)}, u32[]{:S(2)}, u32[]{:S(2)}) %collective-permute-start.15) | collective-permute-done | bytes 524320 | tf_op jit(solution)/shard_map/ppermute | solution.py:744
  306.7 58.2 %attention_backward.1.grad_proj = bf16[2048,768]{1,0:T(8,128)(2,1)} custom-call(s32[8]{0:T(128)} %get-tuple-element.123.low_ref, s32[8]{0:T(128)} %get-tuple-element.122.high_ref, bf16[2048,256]{1,0:T(8,128)(2,1)} %get-tuple-element.42.q_ref, bf16[2048,256]{1,0:T(8,128)(2,1)} %get-tuple-element.43.k_ref, bf16[2048,256]{1,0:T(8,128)(2,1)} %get-tuple-element.44.v_ref, ...), custom_call_target="tpu_custom_call" | custom-call | flops 30064771072 | bytes 10485760 | tf_op jit(solution)/shard_map/attention_backward/pallas_call | solution.py:690
  364.9 2.4 convert_reduce_fusion.1
  368.7 7.9 %convolution_convert_fusion.2.part = bf16[1024,768]{1,0:T(8,128)(2,1)} fusion(bf16[2048,1024]{1,0:T(8,128)(2,1)} %get-tuple-element.48, bf16[2048,768]{1,0:T(8,128)(2,1)} %attention_backward.1.grad_proj), kind=kOutput, calls=%fused_computation.60 | convolution fusion | flops 3222011904 | bytes 8912896 | tf_op jit(solution)/shard_map/dot_general | solution.py:18
  376.5 70.1 %tail.1 = (f32[512,1024]{1,0:T(8,128)}, bf16[4,128,768]{2,1,0:T(8,128)(2,1)}, f32[16,1024]{1,0:T(8,128)}) custom-call(bf16[1024,768]{1,0:T(8,128)(2,1)} %convolution_convert_fusion.2.part, bf16[2048,768]{1,0:T(8,128)(2,1)} %attention_backward.1.grad_proj, bf16[1024,768]{1,0:T(8,128)(2,1)} %get-tuple-element.40.w_ref.weight, ...), custom_call_target="tpu_custom_call" | custom-call | tf_op jit(solution)/shard_map/tail/pallas_call | solution.py:312
  455.6 2.3 multiply_reduce_fusion.5
  465.6 2.7 collective-permute-start.5
  470.1 10.8 %collective-permute-done.5 = bf16[4,128,512]{2,1,0:T(8,128)(2,1)S(1)} collective-permute-done((bf16[4,128,512]{2,1,0:T(8,128)(2,1)S(1)}, bf16[4,128,512]{2,1,0:T(8,128)(2,1)S(1)}, u32[]{:S(2)}, u32[]{:S(2)}) %collective-permute-start.5) | collective-permute-done | bytes 524320 | tf_op jit(solution)/shard_map/ppermute | solution.py:752
  488.5 6.9 %collective-permute-done.7 = bf16[128,512]{1,0:T(8,128)(2,1)S(1)} collective-permute-done((bf16[128,512]{1,0:T(8,128)(2,1)S(1)}, bf16[128,512]{1,0:T(8,128)(2,1)S(1)}, u32[]{:S(2)}, u32[]{:S(2)}) %collective-permute-start.7) | collective-permute-done | bytes 131104 | tf_op jit(solution)/shard_map/ppermute | solution.py:757
  496.2 2.1 fusion.23
  498.3 3.8 collective-permute-done.9
  513.8 13.7 %norm.1 = (f32[16,128]{1,0:T(8,128)}, f32[8,128]{1,0:T(8,128)}) custom-call(f32[8,16,128]{2,1,0:T(8,128)} %fusion.43.slices), custom_call_target="tpu_custom_call" | custom-call | tf_op jit(solution)/shard_map/norm/pallas_call | solution.py:372
  532.6 5.7 %multiply_subtract_fusion.2 = (f32[128,3072]{1,0:T(8,128)}, f32[128,3072]{1,0:T(8,128)}, f32[128,3072]{1,0:T(8,128)}) fusion(f32[128,3072]{1,0:T(8,128)} %param.27, f32[]{:T(128)} %bitcast.51, f32[]{:T(128)} %bitcast.50, f32[]{:T(128)} %bitcast.49, f32[]{:T(128)} %bitcast.27, f32[]{:T(128)S(6)} %div.176, ...), kind=kLoop, calls=%fused_computation.64 | loop fusion | flops 6684672 | bytes 10223636 | tf_op jit(solution)/shard_map/sub | solution.py:719
  540.9 3.9 multiply_subtract_fusion.1
  545.9 3.8 multiply_subtract_fusion
  (222 shorter events, 85.0 us)
Async XLA Ops:
  7.2 192.0 %all-gather.2.cloned.1.call-start = ((), (), s32[]{:S(2)}) async-start(), calls=%async_computation.3 | async-start | bytes 4718592 | tf_op jit(solution)/shard_map/all_gather | solution.py:775
  7.3 172.5 %collective-permute-start.2 = (bf16[512,1024]{1,0:T(8,128)(2,1)}, bf16[512,1024]{1,0:T(8,128)(2,1)}, u32[]{:S(2)}, u32[]{:S(2)}) collective-permute-start(bf16[512,1024]{1,0:T(8,128)(2,1)} %param.22), channel_id=1, source_target_pairs={{0,1},{1,0},{2,3},{3,2},{4,5},{5,4},{6,7},{7,6},{8,9},{9,8},{10,11... | collective-permute-start | bytes 3145736 | tf_op jit(solution)/shard_map/ppermute | solution.py:741
  9.9 283.1 %reduce-scatter.5.cloned.1.call-start = ((), (), s32[]{:S(2)}) async-start(), calls=%async_computation.5 | async-start | bytes 4718592 | tf_op jit(solution)/shard_map/reduce_scatter | solution.py:814
  79.2 95.6 %copy-start = (bf16[512,1024]{1,0:T(8,128)(2,1)S(1)}, bf16[512,1024]{1,0:T(8,128)(2,1)}, u32[]{:S(2)}) copy-start(bf16[512,1024]{1,0:T(8,128)(2,1)} %tok.1) | copy-start | bytes 3145732
  178.9 2.7 collective-permute-start
  181.3 9.3 %copy-start.28 = (bf16[1024,1024]{1,0:T(8,128)(2,1)}, bf16[1024,1024]{1,0:T(8,128)(2,1)S(1)}, u32[]{:S(2)}) copy-start(bf16[1024,1024]{1,0:T(8,128)(2,1)S(1)} %constant_dynamic-update-slice_fusion) | copy-start | bytes 6291460
  181.7 8.9 %copy-start.38 = (bf16[512,1024]{1,0:T(8,128)(2,1)}, bf16[512,1024]{1,0:T(8,128)(2,1)S(1)}, u32[]{:S(2)}) copy-start(bf16[512,1024]{1,0:T(8,128)(2,1)S(1)} %collective-permute-done) | copy-start | bytes 3145732
  199.3 23.5 %copy-start.45 = (bf16[1024,2048]{1,0:T(8,128)(2,1)S(1)}, bf16[1024,2048]{1,0:T(8,128)(2,1)}, u32[]{:S(2)}) copy-start(bf16[1024,2048]{1,0:T(8,128)(2,1)} %get-tuple-element.47) | copy-start | bytes 12582916
  222.8 7.8 %copy-start.42 = (bf16[1024,2048]{1,0:T(8,128)(2,1)S(1)}, bf16[1024,2048]{1,0:T(8,128)(2,1)}, u32[]{:S(2)}) copy-start(bf16[1024,2048]{1,0:T(8,128)(2,1)} %copy-done.41) | copy-start | bytes 12582916
  230.5 11.2 %collective-permute-start.3 = (f32[512,1024]{1,0:T(8,128)}, f32[512,1024]{1,0:T(8,128)}, u32[]{:S(2)}, u32[]{:S(2)}) collective-permute-start(f32[512,1024]{1,0:T(8,128)} %slice.206), channel_id=1, source_target_pairs={{0,1},{1,0},{2,3},{3,2},{4,5},{5,4},{6,7},{7,6},{8,9},{9,8},{10,11... | collective-permute-start | bytes 6291464 | tf_op jit(solution)/shard_map/ppermute | solution.py:741
  238.9 6.2 %collective-permute-start.1 = (f32[512,1024]{1,0:T(8,128)}, f32[512,1024]{1,0:T(8,128)}, u32[]{:S(2)}, u32[]{:S(2)}) collective-permute-start(f32[512,1024]{1,0:T(8,128)} %slice.203), channel_id=1, source_target_pairs={{0,1},{1,0},{2,3},{3,2},{4,5},{5,4},{6,7},{7,6},{8,9},{9,8},{10,11... | collective-permute-start | bytes 6291464 | tf_op jit(solution)/shard_map/ppermute | solution.py:741
  251.3 55.3 %all-to-all-start = ((bf16[512,4,256]{2,0,1:T(8,128)(2,1)}), bf16[512,4,256]{2,0,1:T(8,128)(2,1)}, u32[]{:S(2)}, u32[]{:S(2)}) async-start(bf16[512,4,256]{2,0,1:T(8,128)(2,1)} %bitcast.109), calls=%async_computation | async-start | bytes 2097152 | tf_op jit(solution)/shard_map/all_to_all | solution.py:830
  256.6 229.9 %reduce-scatter.3.cloned.1.call-start = ((), (), s32[]{:S(2)}) async-start(), calls=%async_computation.4 | async-start | bytes 4718592 | tf_op jit(solution)/shard_map/reduce_scatter | solution.py:817
  265.7 28.8 %copy-start.4 = (f32[512,1024]{1,0:T(8,128)S(1)}, f32[512,1024]{1,0:T(8,128)}, u32[]{:S(2)}) copy-start(f32[512,1024]{1,0:T(8,128)} %copy-done.3) | copy-start | bytes 6291460
  293.0 13.6 %collective-permute-start.15 = (bf16[128,2048]{1,0:T(8,128)(2,1)}, bf16[128,2048]{1,0:T(8,128)(2,1)}, u32[]{:S(2)}, u32[]{:S(2)}) collective-permute-start(bf16[128,2048]{1,0:T(8,128)(2,1)} %reduce-scatter.5.cloned.1.call-done), channel_id=1, source_target_pairs={{0,2},{1,3},{2,0},{3,1},{4,6},{5,7},{6,4},{7,5},{8,10},{9,11},{10,... | collective-permute-start | bytes 1572872 | tf_op jit(solution)/shard_map/ppermute | solution.py:744
  294.5 207.6 %collective-permute-start.16 = (bf16[128,2048]{1,0:T(8,128)(2,1)}, bf16[128,2048]{1,0:T(8,128)(2,1)}, u32[]{:S(2)}, u32[]{:S(2)}) collective-permute-start(bf16[128,2048]{1,0:T(8,128)(2,1)} %reduce-scatter.5.cloned.1.call-done), channel_id=1, source_target_pairs={{0,1},{1,0},{2,3},{3,2},{4,5},{5,4},{6,7},{7,6},{8,9},{9,8},{10,11... | collective-permute-start | bytes 1572872 | tf_op jit(solution)/shard_map/ppermute | solution.py:741
  300.2 163.6 %collective-permute-start.4 = (bf16[1024,512]{1,0:T(8,128)(2,1)}, bf16[1024,512]{1,0:T(8,128)(2,1)}, u32[]{:S(2)}, u32[]{:S(2)}) collective-permute-start(bf16[1024,512]{1,0:T(8,128)(2,1)} %dynamic-slice_convert_fusion), channel_id=1, source_target_pairs={{0,1},{1,0},{2,3},{3,2},{4,5},{5,4},{6,7},{7,6},{8,9},{9,8},{10,11... | collective-permute-start | bytes 3145736 | tf_op jit(solution)/shard_map/ppermute | solution.py:741
  306.7 196.1 %collective-permute-start.17 = (bf16[128,2048]{1,0:T(8,128)(2,1)}, bf16[128,2048]{1,0:T(8,128)(2,1)}, u32[]{:S(2)}, u32[]{:S(2)}) collective-permute-start(bf16[128,2048]{1,0:T(8,128)(2,1)} %collective-permute-done.15), channel_id=1, source_target_pairs={{0,1},{1,0},{2,3},{3,2},{4,5},{5,4},{6,7},{7,6},{8,9},{9,8},{10,11... | collective-permute-start | bytes 1572872 | tf_op jit(solution)/shard_map/ppermute | solution.py:741
  449.6 14.3 %copy-start.2 = (f32[1024,1024]{1,0:T(8,128)S(1)}, f32[1024,1024]{1,0:T(8,128)}, u32[]{:S(2)}) copy-start(f32[1024,1024]{1,0:T(8,128)} %copy-done.1) | copy-start | bytes 12582916
  465.6 15.2 %collective-permute-start.5 = (bf16[4,128,512]{2,1,0:T(8,128)(2,1)S(1)}, bf16[4,128,512]{2,1,0:T(8,128)(2,1)S(1)}, u32[]{:S(2)}, u32[]{:S(2)}) collective-permute-start(bf16[4,128,512]{2,1,0:T(8,128)(2,1)S(1)} %dynamic-slice_bitcast_fusion), channel_id=1, source_target_pairs={{0,4},{4,0},{8,12},{12,8},{16,20},{20,16},{24,28},{28,24},{1,5},{5... | collective-permute-start | bytes 1572872 | tf_op jit(solution)/shard_map/ppermute | solution.py:752
  470.1 32.6 %copy-start.26 = (bf16[128,2048]{1,0:T(8,128)(2,1)S(1)}, bf16[128,2048]{1,0:T(8,128)(2,1)}, u32[]{:S(2)}) copy-start(bf16[128,2048]{1,0:T(8,128)(2,1)} %reduce-scatter.5.cloned.1.call-done) | copy-start | bytes 1572868
  481.0 5.5 collective-permute-start.8
  484.3 11.2 %collective-permute-start.7 = (bf16[128,512]{1,0:T(8,128)(2,1)S(1)}, bf16[128,512]{1,0:T(8,128)(2,1)S(1)}, u32[]{:S(2)}, u32[]{:S(2)}) collective-permute-start(bf16[128,512]{1,0:T(8,128)(2,1)S(1)} %get-tuple-element.98), channel_id=1, source_target_pairs={{0,16},{4,20},{8,24},{12,28},{16,0},{20,4},{24,8},{28,12},{1,17},{... | collective-permute-start | bytes 393224 | tf_op jit(solution)/shard_map/ppermute | solution.py:757
  484.8 10.7 %collective-permute-start.6 = (bf16[128,512]{1,0:T(8,128)(2,1)S(1)}, bf16[128,512]{1,0:T(8,128)(2,1)S(1)}, u32[]{:S(2)}, u32[]{:S(2)}) collective-permute-start(bf16[128,512]{1,0:T(8,128)(2,1)S(1)} %get-tuple-element.96), channel_id=1, source_target_pairs={{0,8},{4,12},{8,16},{12,20},{16,24},{20,28},{24,0},{28,4},{1,9},{5... | collective-permute-start | bytes 393224 | tf_op jit(solution)/shard_map/ppermute | solution.py:757
  486.5 16.1 %collective-permute-start.12 = (bf16[128,2048]{1,0:T(8,128)(2,1)}, bf16[128,2048]{1,0:T(8,128)(2,1)S(1)}, u32[]{:S(2)}, u32[]{:S(2)}) collective-permute-start(bf16[128,2048]{1,0:T(8,128)(2,1)} %reduce-scatter.3.cloned.1.call-done), channel_id=1, source_target_pairs={{0,2},{1,3},{2,0},{3,1},{4,6},{5,7},{6,4},{7,5},{8,10},{9,11},{10,... | collective-permute-start | bytes 1572872 | tf_op jit(solution)/shard_map/ppermute | solution.py:744
  495.6 6.6 %collective-permute-start.9 = (bf16[128,512]{1,0:T(8,128)(2,1)S(1)}, bf16[128,512]{1,0:T(8,128)(2,1)S(1)}, u32[]{:S(2)}, u32[]{:S(2)}) collective-permute-start(bf16[128,512]{1,0:T(8,128)(2,1)S(1)} %fusion.37), channel_id=1, source_target_pairs={{0,2},{1,3},{2,0},{3,1},{4,6},{5,7},{6,4},{7,5},{8,10},{9,11},{10,... | collective-permute-start | bytes 393224 | tf_op jit(solution)/shard_map/ppermute | solution.py:744
  498.3 7.4 %collective-permute-start.10 = (bf16[128,512]{1,0:T(8,128)(2,1)S(1)}, bf16[128,512]{1,0:T(8,128)(2,1)S(1)}, u32[]{:S(2)}, u32[]{:S(2)}) collective-permute-start(bf16[128,512]{1,0:T(8,128)(2,1)S(1)} %fusion.37), channel_id=1, source_target_pairs={{0,1},{1,0},{2,3},{3,2},{4,5},{5,4},{6,7},{7,6},{8,9},{9,8},{10,11... | collective-permute-start | bytes 393224 | tf_op jit(solution)/shard_map/ppermute | solution.py:741
  502.1 3.6 collective-permute-start.11
  502.1 5.7 %collective-permute-start.13 = (bf16[128,2048]{1,0:T(8,128)(2,1)}, bf16[128,2048]{1,0:T(8,128)(2,1)}, u32[]{:S(2)}, u32[]{:S(2)}) collective-permute-start(bf16[128,2048]{1,0:T(8,128)(2,1)} %reduce-scatter.3.cloned.1.call-done), channel_id=1, source_target_pairs={{0,1},{1,0},{2,3},{3,2},{4,5},{5,4},{6,7},{7,6},{8,9},{9,8},{10,11... | collective-permute-start | bytes 1572872 | tf_op jit(solution)/shard_map/ppermute | solution.py:741
  502.6 5.2 collective-permute-start.14
  532.6 7.2 %copy-start.17 = (f32[128,4096]{1,0:T(8,128)S(1)}, f32[128,4096]{1,0:T(8,128)}, u32[]{:S(2)}) copy-start(f32[128,4096]{1,0:T(8,128)} %param.39) | copy-start | bytes 6291460
  532.6 7.2 %copy-start.18 = (f32[128,4096]{1,0:T(8,128)S(1)}, f32[128,4096]{1,0:T(8,128)}, u32[]{:S(2)}) copy-start(f32[128,4096]{1,0:T(8,128)} %param.34) | copy-start | bytes 6291460
  (36 other events, 133.2 us)
Sparse Core Ops, SparseCore 0:
  10.7 110.5 all-gather.1
  198.9 94.0 reduce-scatter.4
  296.7 87.9 reduce-scatter.2

commit v4 on v3

--- a/solution.py
+++ b/solution.py
@@ -217,8 +217,8 @@
 
 
 def tail_kernel(
-    wide, narrow, part, grad_proj, weight, tok, vec_in, normed_out, quarters_out, vec_out,
-    partial, mate_in, cross_out, cross_in, near_in, far_out, far_in, shards, vec_box, sums, send, recv,
+    wide, narrow, part, grad_proj, weight, tok, vec_in, down, normed_out, quarters_out, vec_out, down_out,
+    partial, mate_in, cross_out, cross_in, near_in, far_out, far_in, shards, vec_box, sums, down_box, send, recv,
 ):
     w, n = lax.axis_index("wide"), lax.axis_index("narrow")
     column = wide // 2
@@ -233,6 +233,10 @@
         go.start(part.at[rows_at(towards[k] * 2 + 1 - y, wide_rows)], near_in.at[k], wide=near) for k in range(column)
     ]
 
+    down_over = go.start(down, down_box.at[n], narrow=cross)
+    go.start(down, down_box.at[n], narrow=mate)
+    down_box[pl.ds(n, 1)] = down[...][None]
+
     sums[...] = jnp.zeros_like(sums)
     owners = [(1 - x) * 2 + 1 - c, x * 2 + 1 - c, (1 - x) * 2 + c, n]
     mates = []
@@ -259,6 +263,8 @@
     vec_box[pl.ds(n, 1), 0:2, :] = sums[0:2, :][None]
     vecs = [go.start(vec_box.at[n], vec_box.at[n], narrow=lax.rem(n + d, narrow)) for d in range(1, narrow)]
 
+    go.arrived(down_over)
+    go.start(down_box.at[cross], down_box.at[cross], narrow=mate)
     go.arrived(mates[0])
     half = group_rows // 2
     overs = []
@@ -300,23 +306,25 @@
     go.start(shards.at[cross], shards.at[cross], narrow=mate)
     go.finish()
     quarters_out[...] = shards[...]
-
-
-def tail_call(part, grad_proj, weight, tok, vec_in, wide, narrow):
+    down_out[...] = down_box[...]
+
+
+def tail_call(part, grad_proj, weight, tok, vec_in, down, wide, narrow):
     depth, cols = part.shape
     rows = tok.shape[0] // narrow
     wide_rows = depth // wide
     column = wide // 2
-    copies = 2 * column - 1 + 2 + (narrow - 1) + 2 + 3
+    copies = 2 * column - 1 + 2 + (narrow - 1) + 2 + 3 + 3
     vmem = pl.BlockSpec(memory_space=pltpu.VMEM)
     return pl.pallas_call(
         functools.partial(tail_kernel, wide, narrow),
-        in_specs=[vmem] * 5,
-        out_specs=[vmem] * 3,
+        in_specs=[vmem] * 6,
+        out_specs=[vmem] * 4,
         out_shape=[
             jax.ShapeDtypeStruct((rows, depth), F32),
             jax.ShapeDtypeStruct((narrow, wide_rows, cols), BF),
             jax.ShapeDtypeStruct(vec_in.shape, F32),
+            jax.ShapeDtypeStruct((narrow,) + down.shape, BF),
         ],
         scratch_shapes=[
             pltpu.VMEM((3, rows, depth), BF),
@@ -329,6 +337,7 @@
             pltpu.VMEM((narrow, wide_rows, cols), BF),
             pltpu.VMEM((narrow,) + vec_in.shape, F32),
             pltpu.VMEM((8, depth), F32),
+            pltpu.VMEM((narrow,) + down.shape, BF),
             pltpu.SemaphoreType.DMA((copies,)),
             pltpu.SemaphoreType.DMA((copies,)),
         ],
@@ -336,7 +345,7 @@
             collective_id=1, has_side_effects=True, vmem_limit_bytes=56 * 1024 * 1024
         ),
         name="tail",
-    )(part, grad_proj, weight, tok, vec_in)
+    )(part, grad_proj, weight, tok, vec_in, down)
 
 
 def norm_kernel(wide, slices, total_out, square_out, box, squares, send, recv):
@@ -420,9 +429,11 @@
     go = Copies(send, recv)
     wide_rows, half = out_ref.shape
     out_cols = pl.ds(pl.multiple_of(side * half, half), half)
-    pieces = 2
-    piece = up_ref.shape[1] // pieces
-    up_at = lambda i, p: up_all.at[rows_at(i, wide_rows), pl.ds(p * piece, piece)]
+    quarter = up_ref.shape[1] // 4
+    cross = lax.rem(n + 2, narrow)
+    shared = pl.ds(pl.multiple_of(n // 2 * quarter, quarter), quarter)
+    both = pl.ds(2 * quarter, 2 * quarter)
+    up_at = lambda i, cols: up_all.at[rows_at(i, wide_rows), cols]
     out_at = lambda i: out_all.at[rows_at(i, wide_rows), out_cols]
     source = lambda d: lax.rem(z - d + column, column) * 2 + y
     target = lambda d: lax.rem(z + d, column) * 2 + y
@@ -439,18 +450,26 @@
     for d in range(column):
         block_ref = out_at(lax.rem(z - d + column, column) * 2 + 1 - y)
         late.append((out_near[d], [go.make(block_ref, block_ref, narrow=mate)]))
-    for p in range(pieces):
-        cols = pl.ds(p * piece, piece)
-        starts.append(go.make(up_ref.at[:, cols], up_at(w, p), wide=near))
+    for cols in (shared, both):
+        passes = lambda i: [] if cols is both else [go.make(up_at(i, cols), up_at(i, cols), narrow=cross)]
+        up_near = [go.make(up_ref.at[:, cols], up_at(w, cols), wide=near)]
+        starts += up_near
+        if cols is shared:
+            starts.append(go.make(up_ref.at[:, cols], up_at(w, cols), narrow=cross))
         for d in range(1, column):
-            far = go.make(up_ref.at[:, cols], up_at(w, p), wide=target(d))
-            block_ref = up_at(source(d), p)
+            far = go.make(up_ref.at[:, cols], up_at(w, cols), wide=target(d))
+            block_ref = up_at(source(d), cols)
             starts.append(far)
-            early.append((far, [go.make(block_ref, block_ref, wide=near)]))
+            up_near.append(go.make(block_ref, block_ref, wide=near))
+            early.append((far, [up_near[-1]] + passes(source(d))))
+        if cols is shared:
+            for d in range(column):
+                early.append((up_near[d], passes(lax.rem(z - d + column, column) * 2 + 1 - y)))
     actions = early + late
     own = [
-        pltpu.make_async_copy(up_ref, up_all.at[rows_at(w, wide_rows)], local.at[0]),
+        pltpu.make_async_copy(up_ref.at[:, shared], up_at(w, shared), local.at[0]),
         pltpu.make_async_copy(out_ref, out_at(w), local.at[1]),
+        pltpu.make_async_copy(up_ref.at[:, both], up_at(w, both), local.at[2 + per]),
     ]
 
     mine = pl.ds(pl.multiple_of(n * width, width), width)
@@ -548,7 +567,7 @@
     heads = width // head_dim
     blocks = rows // BLOCK
     column = wide // 2
-    copies = 2 + 3 * (column - 1) + column + 2 * (2 * column - 1)
+    copies = 2 + 3 * (column - 1) + column + 2 * (2 * column - 1) + 2 * column
     whole = lambda a: pl.BlockSpec(a.shape, lambda i: (0,) * a.ndim)
     anywhere = pl.BlockSpec(memory_space=pl.ANY)
     lse = jax.ShapeDtypeStruct((blocks, 8, BLOCK), F32)
@@ -575,7 +594,7 @@
             pltpu.SemaphoreType.DMA((copies,)),
             pltpu.SemaphoreType.DMA((blocks,)),
             pltpu.SemaphoreType.DMA((blocks,)),
-            pltpu.SemaphoreType.DMA((2 + blocks // narrow,)),
+            pltpu.SemaphoreType.DMA((3 + blocks // narrow,)),
         ],
         compiler_params=pltpu.CompilerParams(collective_id=3, has_side_effects=True),
         cost_estimate=pl.CostEstimate(
@@ -585,14 +604,106 @@
     )(q, k, v, seg_rows, tag_col, up_low, out_half)
 
 
+class Scatter:
+    def __init__(self, go, wide, narrow, part, near_in, own, far_out, far_in, box, local):
+        w, self.n = lax.axis_index("wide"), lax.axis_index("narrow")
+        self.go, self.column = go, wide // 2
+        self.near_in, self.own, self.far_out, self.far_in, self.box = near_in, own, far_out, far_in, box
+        z, y = w // 2, lax.rem(w, 2)
+        near, mate, cross = w + 1 - 2 * y, self.n + 1 - 2 * lax.rem(self.n, 2), lax.rem(self.n + 2, narrow)
+        size = part.shape[0] // wide
+        towards = [lax.rem(z + d, self.column) for d in range(1, self.column + 1)]
+        self.first = [
+            go.make(part.at[rows_at(to * 2 + 1 - y, size)], near_in.at[k], wide=near) for k, to in enumerate(towards)
+        ]
+        self.loads = [
+            pltpu.make_async_copy(part.at[rows_at(to * 2 + y, size)], own.at[k], local.at[k])
+            for k, to in enumerate(towards)
+        ]
+        self.second = [
+            go.make(far_out.at[k], far_in.at[k], wide=to * 2 + y) for k, to in enumerate(towards[:-1])
+        ]
+        self.over = go.make(box.at[self.n], box.at[self.n], narrow=cross)
+        self.beside = go.make(box.at[self.n], box.at[self.n], narrow=mate)
+        self.passed = go.make(box.at[cross], box.at[cross], narrow=mate)
+
+    def begin(self):
+        self.go.launch(*self.first)
+        for copy in self.loads:
+            copy.start()
+
+    def relay(self, k):
+        self.go.arrived(self.first[k])
+        self.loads[k].wait()
+        if k < self.column - 1:
+            self.far_out[k] = (self.own[k].astype(F32) + self.near_in[k].astype(F32)).astype(BF)
+            self.go.launch(self.second[k])
+
+    def total(self):
+        value = self.own[self.column - 1].astype(F32) + self.near_in[self.column - 1].astype(F32)
+        for k in range(self.column - 1):
+            self.go.arrived(self.second[k])
+            value = value + self.far_in[k].astype(F32)
+        self.box[pl.ds(self.n, 1)] = value.astype(BF)[None]
+        self.go.launch(self.over, self.beside)
+
+    def share(self):
+        self.go.arrived(self.over)
+        self.go.launch(self.passed)
+
+    @staticmethod
+    def copies(wide):
+        return 2 * (wide // 2) - 1 + 3
+
+    @staticmethod
+    def scratch(wide, narrow, rows, cols):
+        column, size = wide // 2, rows // wide
+        sizes = [column, column, column - 1, column - 1, narrow]
+        return [pltpu.VMEM((count, size, cols), BF) for count in sizes] + [pltpu.SemaphoreType.DMA((column,))]
+
+
 def backward_kernel(
-    heads, head_dim, low_ref, high_ref, q_ref, k_ref, v_ref, o_ref, g_ref, lse_ref, seg_ref, tag_ref, turn_ref,
-    out_ref, q_heads, g_heads, delta, grad_query,
+    heads, head_dim, wide, narrow,
+    q_ref, k_ref, v_ref, o_ref, g_ref, lse_ref, seg_ref, tag_ref, turn_ref, part_out, part_up,
+    grads_out, shards_out, shards_up,
+    q_heads, g_heads, delta, grad_query, send, recv, *boxes,
 ):
     step = pl.program_id(0)
     rows, width = q_ref.shape
+    blocks = rows // BLOCK
+    last = blocks - 1
     scale = head_dim**-0.5
     half = head_dim // 2
+    go = Copies(send, recv)
+    column = wide // 2
+    outs = Scatter(go, wide, narrow, part_out, *boxes[:6])
+    ups = Scatter(go, wide, narrow, part_up, *boxes[6:])
+
+    @pl.when(step == 0)
+    def _():
+        w, n = lax.axis_index("wide"), lax.axis_index("narrow")
+        z, y = w // 2, lax.rem(w, 2)
+        greet(
+            [{"wide": w + 1 - 2 * y}]
+            + [{"wide": lax.rem(z + d, column) * 2 + y} for d in range(1, column)]
+            + [{"narrow": n + 1 - 2 * lax.rem(n, 2)}, {"narrow": lax.rem(n + 2, narrow)}]
+        )
+        outs.begin()
+        ups.begin()
+
+    actions = [[] for _ in range(last)]
+    for k in range(column):
+        actions[1 + 2 * k // column].append(functools.partial(outs.relay, k))
+        actions[2 + 4 * k // column].append(functools.partial(ups.relay, k))
+    actions[last - 3].append(outs.total)
+    actions[last - 2].append(outs.share)
+    for i in range(last):
+        if actions[i]:
+
+            @pl.when(step == i + 1)
+            def _():
+                for action in actions[i]:
+                    action()
 
     @pl.when(step == 0)
     def _():
@@ -619,7 +730,7 @@
             )[None]
             return carry
 
-        lax.fori_loop(0, rows // BLOCK, prepare, 0)
+        lax.fori_loop(0, blocks, prepare, 0)
 
     key = k_ref[...]
     value = v_ref[...]
@@ -648,54 +759,72 @@
         return grad_key, grad_value
 
     zero = jnp.zeros((BLOCK, width), F32)
-    grad_key, grad_value = lax.fori_loop(low_ref[step], high_ref[step], body, (zero, zero))
+    low, high = meeting(step, blocks)
+    grad_key, grad_value = lax.fori_loop(low, high, body, (zero, zero))
     here = pl.ds(pl.multiple_of(step * BLOCK, BLOCK), BLOCK)
     cosine, sine = turn_ref[here, :128], turn_ref[here, 128:]
-    out_ref[here, width : 2 * width] = turn(grad_key, cosine, sine, half, -1).astype(BF)
-    out_ref[here, 2 * width :] = grad_value.astype(BF)
-
-    @pl.when(step == pl.num_programs(0) - 1)
+    grads_out[here, width : 2 * width] = turn(grad_key, cosine, sine, half, -1).astype(BF)
+    grads_out[here, 2 * width :] = grad_value.astype(BF)
+
+    @pl.when(step == last)
     def _():
+        ups.total()
+
         def finish(i, carry):
             at = pl.ds(pl.multiple_of(i * BLOCK, BLOCK), BLOCK)
             grads = grad_query[at, :] * scale
-            out_ref[at, :width] = turn(grads, turn_ref[at, :128], turn_ref[at, 128:], half, -1).astype(BF)
+            grads_out[at, :width] = turn(grads, turn_ref[at, :128], turn_ref[at, 128:], half, -1).astype(BF)
             return carry
 
-        lax.fori_loop(0, rows // BLOCK, finish, 0)
-
-
-def backward_call(low, high, q, k, v, o, g, lse, seg_rows, tag_col, turns, head_dim):
+        lax.fori_loop(0, blocks, finish, 0)
+        ups.share()
+        go.finish()
+        shards_out[...] = outs.box[...]
+        shards_up[...] = ups.box[...]
+
+
+def backward_call(q, k, v, o, g, lse, seg_rows, tag_col, turns, part_out, part_up, head_dim, wide, narrow):
     rows, width = q.shape
     heads = width // head_dim
     blocks = rows // BLOCK
-    whole = lambda a: pl.BlockSpec(a.shape, lambda i, *_: (0,) * a.ndim)
-    block = pl.BlockSpec((BLOCK, width), lambda i, *_: (i, 0))
-    grid_spec = pltpu.PrefetchScalarGridSpec(
-        num_scalar_prefetch=2,
+    whole = lambda a: pl.BlockSpec(a.shape, lambda i: (0,) * len(a.shape), pipeline_mode=pl.Buffered(1))
+    block = pl.BlockSpec((BLOCK, width), lambda i: (i, 0))
+    anywhere = pl.BlockSpec(memory_space=pl.ANY)
+    depth = part_up.shape[0]
+    results = [
+        jax.ShapeDtypeStruct((rows, 3 * width), BF),
+        jax.ShapeDtypeStruct((narrow, depth // wide, part_out.shape[1]), BF),
+        jax.ShapeDtypeStruct((narrow, depth // wide, part_up.shape[1]), BF),
+    ]
+    copies = 2 * Scatter.copies(wide)
+    return pl.pallas_call(
+        functools.partial(backward_kernel, heads, head_dim, wide, narrow),
         grid=(blocks,),
         in_specs=[
             whole(q), block, block, whole(o), whole(g), whole(lse), whole(seg_rows),
-            pl.BlockSpec((BLOCK, 1), lambda i, *_: (i, 0)),
-            whole(turns),
+            pl.BlockSpec((BLOCK, 1), lambda i: (i, 0)),
+            whole(turns), anywhere, anywhere,
         ],
-        out_specs=pl.BlockSpec((rows, 3 * width), lambda i, *_: (0, 0)),
+        out_specs=[whole(a) for a in results],
+        out_shape=results,
         scratch_shapes=[
             pltpu.VMEM((heads, rows, width), BF),
             pltpu.VMEM((heads, rows, width), BF),
             pltpu.VMEM((blocks, 8, BLOCK), F32),
             pltpu.VMEM((rows, width), F32),
-        ],
-    )
-    return pl.pallas_call(
-        functools.partial(backward_kernel, heads, head_dim),
-        grid_spec=grid_spec,
-        out_shape=jax.ShapeDtypeStruct((rows, 3 * width), BF),
+            pltpu.SemaphoreType.DMA((copies,)),
+            pltpu.SemaphoreType.DMA((copies,)),
+        ]
+        + Scatter.scratch(wide, narrow, depth, part_out.shape[1])
+        + Scatter.scratch(wide, narrow, depth, part_up.shape[1]),
+        compiler_params=pltpu.CompilerParams(
+            collective_id=4, has_side_effects=True, vmem_limit_bytes=60 * 1024 * 1024
+        ),
         cost_estimate=pl.CostEstimate(
             flops=heads * rows * rows * width * 7, bytes_accessed=rows * width * 20, transcendentals=heads * rows * rows
         ),
         name="attention_backward",
-    )(low, high, q, k, v, o, g, lse, seg_rows, tag_col, turns)
+    )(q, k, v, o, g, lse, seg_rows, tag_col, turns, part_out, part_up)
 
 
 def norm_parts(values):
@@ -743,20 +872,6 @@
     def across(value):
         return lax.ppermute(value, "narrow", [(i, i ^ 2) for i in range(narrow)])
 
-    def scatter(part):
-        w = lax.axis_index("wide")
-        z, y = w // 2, w % 2
-        column = wide // 2
-        blocks = part.reshape(column, 2, shard_rows, part.shape[1])
-        pick = lambda value, at, axis: lax.dynamic_index_in_dim(value, at, axis, keepdims=False)
-        came = lax.ppermute(pick(blocks, 1 - y, 1), "wide", [(i, i ^ 1) for i in range(wide)])
-        both = (pick(blocks, y, 1).astype(F32) + came.astype(F32)).astype(BF)
-        total = pick(both, z, 0).astype(F32)
-        for d in range(1, column):
-            pairs = [(i, (i // 2 + d) % column * 2 + i % 2) for i in range(wide)]
-            total = total + lax.ppermute(pick(both, (z + d) % column, 0), "wide", pairs).astype(F32)
-        return total.astype(BF)
-
     def take(value, start, size, axis=1):
         return lax.dynamic_slice_in_dim(value, start, size, axis)
 
@@ -787,10 +902,6 @@
         (slot == place[0][:, None]) | (slot == 14 + place[1][:, None]) | (slot == 28 + place[2][:, None])
     ).astype(F32)
     blocks = group // BLOCK
-    seg_rows = seg.reshape(blocks, BLOCK)
-    low = jnp.sum(seg[None, :] < seg_rows[:, :1], axis=1, dtype=jnp.int32) // BLOCK
-    high = (jnp.sum(seg[None, :] <= seg_rows[:, -1:], axis=1, dtype=jnp.int32) + BLOCK - 1) // BLOCK
-
     bias = jnp.concatenate([take(vec[2 + i : 3 + i], me * mine, mine) for i in range(3)], axis=1)
     query, keys, values, turns, normed1_all = qkv_call(tokens_all, vec[:2], qkv_w, bias, onehot, rotary_table(head_dim), head_dim // 2)
     mixed_mine, lse, mixed, up_w, out_w = forward_call(
@@ -814,7 +925,6 @@
     grad_down = lax.psum_scatter(part_down, "wide", scatter_dimension=0, tiled=True)
     grad_up_act = (dot(cot_pair, down_w, 1, 0) * slope).astype(BF)
     part_up = dot(normed2_pair, grad_up_act, 0, 0).astype(BF)
-    grad_up = lax.psum_scatter(part_up, "wide", scatter_dimension=0, tiled=True)
     grad_normed2_part = dot(grad_up_act, up_w, 1, 1)
     grad_normed2 = grad_normed2_part[:rows] + mate(grad_normed2_part[rows:])
     cot = cotangent.astype(F32)
@@ -825,12 +935,11 @@
     own_out = take(part_out, side * (width // 2), width // 2)
     other_out = take(part_out, (1 - side) * (width // 2), width // 2)
     part_out = (own_out + mate(other_out.astype(BF)).astype(F32)).astype(BF)
-    grad_out = scatter(part_out)
 
     grad_mixed_mine = lax.all_to_all(grad_mixed, "narrow", 1, 0, tiled=True)
-    grad_proj = backward_call(
-        low, high, query, keys, values, mixed_mine, grad_mixed_mine, lse, seg_float.reshape(blocks, BLOCK),
-        key_tag[:, None], turns, head_dim,
+    grad_proj, shards_out, shards_up = backward_call(
+        query, keys, values, mixed_mine, grad_mixed_mine, lse, seg_float.reshape(blocks, BLOCK),
+        key_tag[:, None], turns, part_out, part_up, head_dim, wide, narrow,
     )
     part_qkv = dot(normed1_all, grad_proj, 0, 0).astype(BF)
 
@@ -851,22 +960,18 @@
         ],
         axis=0,
     )
-    grad_normed1, quarters, vector_group = tail_call(
-        part_qkv, grad_proj, qkv_w, tokens_all, vector_part, wide, narrow
+    grad_normed1, quarters, vector_group, shards_down = tail_call(
+        part_qkv, grad_proj, qkv_w, tokens_all, vector_part, grad_down, wide, narrow
     )
     grad_tokens = (grad_resid + norm_back(grad_normed1, vec[0], unit1, inverse1)).astype(BF)
 
-    def join(value):
-        other = across(value)
-        mine = value.astype(F32) + other.astype(F32)
-        theirs = mate(value).astype(F32) + mate(other).astype(F32)
-        first = jnp.where(side == 0, mine, theirs)
-        second = jnp.where(side == 0, theirs, mine)
-        return jnp.concatenate([first, second], axis=1)
-
-    total_up = join(grad_up)
-    total_down = join(grad_down)
-    total_out = join(grad_out)
+    def join(shards):
+        shards = shards.astype(F32)
+        return jnp.concatenate([shards[0] + shards[2], shards[1] + shards[3]], axis=1)
+
+    total_up = join(shards_up)
+    total_down = join(shards_down)
+    total_out = join(shards_out)
     total_qkv = jnp.concatenate(
         [quarters[i, :, j * mine : (j + 1) * mine] for j in range(3) for i in range(narrow)], axis=1
     ).astype(F32)

time: 567 us -> 521 us (0.919)
  waiting for transfers between devices: 55.6 us -> 4.31 us
  Pallas kernels: 291 us -> 330 us
  local copies, waits for them, and re-layouts: 53.3 us -> 37.9 us
  starting transfers between devices: 16.2 us -> 6 us
  matrix products: 68.8 us -> 60.5 us
    pallas_call x1, Pallas kernels: 58.2 us -> 117 us  [backward_call(): pl.pallas_call(functools.partial(backward_kernel, heads, head_dim, wide,...]
    ppermute x7 -> x0, waiting for transfers between devices: 27.9 us -> none  [the longest x1 10.8 us: scatter(): lax.ppermute(pick(blocks, 1 - y, 1), 'wide', [(i, i ^ 1) for i in range(w...]
    reduce_scatter x1, waiting for transfers between devices: 27.3 us -> 0.01 us  [on_device(): lax.psum_scatter(part_down, 'wide', scatter_dimension=0, tiled=True)]
    unnamed x104, local copies, waits for them, and re-layouts: 31.1 us -> 17 us
    pallas_call x1, Pallas kernels: 70.1 us -> 58.8 us  [tail_call(): pl.pallas_call(functools.partial(tail_kernel, wide, narrow), in_specs=[vm...]
    ppermute x7 -> x0, starting transfers between devices: 8.96 us -> none  [the longest x3 3.56 us: scatter(): lax.ppermute(pick(both, (z + d) % column, 0), 'wide', pairs).astype(F32)]
    dot_general x10, matrix products: 68.8 us -> 60.5 us  [dot(): lax.dot_general(a, b, (((ca,), (cb,)), ((), ())), preferred_element_type=...]
    pallas_call x1, Pallas kernels: 95.6 us -> 88.5 us  [forward_call(): pl.pallas_call(functools.partial(forward_kernel, heads, head_dim, wide, n...]
  transfers between devices with their start and end apart: 22 -> 8, of which waited for: 7 -> 1; matrix products, arithmetic and copies ran while one was open for 25% -> 17% of each run, Pallas kernels for 50% -> 51%
where the time goes in v4:
time: 521 us; the launch traced here: 511 us
  Pallas kernels  330 us (63%)
  matrix products  60.5 us (12%)
  other arithmetic  51.1 us (10%)
  local copies, waits for them, and re-layouts  37.9 us (7%)
  between operations  20.9 us (4%)
  starting transfers between devices  6 us (1%)
    pallas_call x1, Pallas kernels, backward_call(): pl.pallas_call(functools.partial(backward_kernel, heads, head_dim, wide,...  117 us
    pallas_call x1, Pallas kernels, forward_call(): pl.pallas_call(functools.partial(forward_kernel, heads, head_dim, wide, n...  88.5 us
    dot_general x10, matrix products, dot(): lax.dot_general(a, b, (((ca,), (cb,)), ((), ())), preferred_element_type=...  60.5 us
    pallas_call x1, Pallas kernels, tail_call(): pl.pallas_call(functools.partial(tail_kernel, wide, narrow), in_specs=[vm...  58.8 us
    pallas_call x1, Pallas kernels, gather_call(): pl.pallas_call(functools.partial(gather_kernel, wide, narrow), in_specs=[...  40.9 us
    unnamed x104, local copies, waits for them, and re-layouts  17 us
    sub x5, other arithmetic, adamw(): return (param - rate * (direction + decay * param), moment, square)  15 us
    pallas_call x1, Pallas kernels, norm_call(): pl.pallas_call(functools.partial(norm_kernel, wide), in_specs=[vmem], out...  12.4 us
  transfers between devices with their start and end apart: 8, of which 1 were waited for; matrix products, arithmetic and copies ran while one was open for 17% of the time, Pallas kernels for 51%

profile of v4, /device:TPU:0, one launch (start us, length us, event | category | flops | bytes accessed | tf_op | source)
XLA Modules:
  0.0 510.6 jit_solution(15414680205790858231)
XLA Ops:
  7.3 2.1 dynamic-slice_convert_fusion.1
  13.7 40.9 %gather.1 = (bf16[2048,1024]{1,0:T(8,128)(2,1)}, bf16[1024,768]{1,0:T(8,128)(2,1)}, bf16[8,16,128]{2,1,0:T(8,128)(2,1)}, s32[4,8,512]{2,1,0:T(8,128)}) custom-call(bf16[512,1024]{1,0:T(8,128)(2,1)} %tok.1, bf16[128,768]{1,0:T(8,128)(2,1)} %pad_maximum_fusion.6.qkv, bf16[16,128]{1,0:T(8,128)(2,1)} %pad.4.vec, s32[8,512]{1,0:T(8,128)} %pad_add_fusion.tag), custom_call_target="tpu_custom_call" | custom-call | tf_op jit(solution)/shard_map/gather/pallas_call | solution.py:199
  62.2 2.1 dynamic-slice_convert_fusion.2.up_ref
  64.3 2.5 fusion.32.onehot_ref
  66.8 12.3 %qkv.1 = (bf16[2048,256]{1,0:T(8,128)(2,1)}, bf16[2048,256]{1,0:T(8,128)(2,1)}, bf16[2048,256]{1,0:T(8,128)(2,1)}, f32[2048,256]{1,0:T(8,128)}, bf16[2048,1024]{1,0:T(8,128)(2,1)}) custom-call(bf16[2048,1024]{1,0:T(8,128)(2,1)} %get-tuple-element.42.x_ref.tok, f32[2,1024]{1,0:T(2,128)} %slice_bitcast_fusion.vec_ref, ...), custom_call_target="tpu_custom_call" | custom-call | flops 3221225472 | bytes 12582912 | tf_op jit(solution)/shard_map/qkv/pallas_call | solution.py:84
  79.2 88.5 %attention_forward.1 = (bf16[2048,256]{1,0:T(8,128)(2,1)}, f32[8,8,256]{2,1,0:T(8,128)}, bf16[512,1024]{1,0:T(8,128)(2,1)}, bf16[1024,2048]{1,0:T(8,128)(2,1)}, bf16[1024,1024]{1,0:T(8,128)(2,1)}) custom-call(bf16[2048,256]{1,0:T(8,128)(2,1)} %get-tuple-element.46.q_ref, bf16[2048,256]{1,0:T(8,128)(2,1)} %get-tuple-element.47.k_ref, ...), custom_call_target="tpu_custom_call" | custom-call | flops 17179869184 | bytes 4194304 | tf_op jit(solution)/shard_map/attention_forward/pallas_call | solution.py:575
  167.7 3.3 fusion.56
  175.0 2.4 constant_dynamic-update-slice_fusion.1
  177.6 2.3 constant_dynamic-update-slice_fusion
  179.9 9.4 %multiply_convert_fusion = (bf16[1024,2048]{1,0:T(8,128)(2,1)}, f32[1024,2048]{1,0:T(8,128)}) fusion(f32[2048]{0:T(1024)S(1)} %bitcast.124, bf16[1024,2048]{1,0:T(8,128)(2,1)S(1)} %copy-done.44, bf16[512,1024]{1,0:T(8,128)(2,1)} %collective-permute-done, bf16[512,1024]{1,0:T(8,128)(2,1)} %add_convert_fusion.1), kind=kOutput, calls=%fused_computation.8 | convolution fusion | flops 4311744512 | bytes 18882560 | tf_op jit(solution)/shard_map/dot_general | solution.py:18
  189.3 11.0 %convert_reduce_fusion = (f32[2048]{0:T(1024)S(1)}, bf16[1024,2048]{1,0:T(8,128)(2,1)S(1)}) fusion(f32[1024,2048]{1,0:T(8,128)} %get-tuple-element.118, f32[2048]{0:T(1024)S(1)} %bitcast.125, bf16[1024,1024]{1,0:T(8,128)(2,1)} %constant_dynamic-update-slice_fusion, bf16[1024,2048]{1,0:T(8,128)(2,1)} %all-gather.2.cloned.1.call-done), kind=kOutput, calls=%fused_computation.7 | convolution fusion | flops 4322228224 | bytes 18890752 | tf_op jit(solution)/shard_map/dot_general | solution.py:18
  200.3 2.0 copy-done.43
  202.3 4.5 fusion.58
  211.2 4.5 fusion.57
  215.8 1.7 slice.243
  218.9 7.9 %convolution_convert_fusion = bf16[1024,2048]{1,0:T(8,128)(2,1)} fusion(bf16[1024,1024]{1,0:T(8,128)(2,1)} %constant_dynamic-update-slice_fusion, bf16[1024,2048]{1,0:T(8,128)(2,1)S(1)} %copy-done.42), kind=kOutput, calls=%fused_computation.11 | convolution fusion | flops 4297064448 | bytes 10485760 | tf_op jit(solution)/shard_map/dot_general | solution.py:18
  227.8 3.3 multiply_reduce_fusion.2
  231.5 3.7 convert_reduce_fusion.4
  236.5 2.0 copy-done.1
  242.4 4.2 all-to-all-start
  246.7 9.6 %convolution_convert_fusion.1.part_up = bf16[1024,2048]{1,0:T(8,128)(2,1)} fusion(bf16[1024,2048]{1,0:T(8,128)(2,1)} %copy-done.43, bf16[512,1024]{1,0:T(8,128)(2,1)} %collective-permute-done, bf16[512,1024]{1,0:T(8,128)(2,1)} %add_convert_fusion.1), kind=kOutput, calls=%fused_computation.12 | convolution fusion | flops 4301258752 | bytes 10485760 | tf_op jit(solution)/shard_map/dot_general | solution.py:18
  257.6 4.3 all-to-all-done
  261.8 116.9 %attention_backward.1 = (bf16[2048,768]{1,0:T(8,128)(2,1)}, bf16[4,128,512]{2,1,0:T(8,128)(2,1)}, bf16[4,128,2048]{2,1,0:T(8,128)(2,1)}) custom-call(bf16[2048,256]{1,0:T(8,128)(2,1)} %get-tuple-element.46.q_ref, bf16[2048,256]{1,0:T(8,128)(2,1)} %get-tuple-element.47.k_ref, bf16[2048,256]{1,0:T(8,128)(2,1)} %get-tuple-element.48.v_ref, ...), custom_call_target="tpu_custom_call" | custom-call | flops 30064771072 | bytes 10485760 | tf_op jit(solution)/shard_map/attention_backward/pallas_call | solution.py:800
  378.7 2.4 convert_reduce_fusion.1
  382.5 7.8 %convolution_convert_fusion.2.part = bf16[1024,768]{1,0:T(8,128)(2,1)} fusion(bf16[2048,1024]{1,0:T(8,128)(2,1)} %get-tuple-element.52, bf16[2048,768]{1,0:T(8,128)(2,1)} %get-tuple-element.56.grad_proj), kind=kOutput, calls=%fused_computation.60 | convolution fusion | flops 3222011904 | bytes 8912896 | tf_op jit(solution)/shard_map/dot_general | solution.py:18
  390.3 58.8 %tail.1 = (f32[512,1024]{1,0:T(8,128)}, bf16[4,128,768]{2,1,0:T(8,128)(2,1)}, f32[16,1024]{1,0:T(8,128)}, bf16[4,128,2048]{2,1,0:T(8,128)(2,1)}) custom-call(bf16[1024,768]{1,0:T(8,128)(2,1)} %convolution_convert_fusion.2.part, bf16[2048,768]{1,0:T(8,128)(2,1)} %get-tuple-element.56.grad_proj, bf16[1024,768]{1,0:T(8,128)(2,1)} %get-tuple-element.44.w_ref.weight, ...), custom_call_target="tpu_custom_call" | custom-call | tf_op jit(solution)/shard_map/tail/pallas_call | solution.py:319
  449.1 2.1 convert_element_type.179
  463.7 12.4 %norm.1 = (f32[16,128]{1,0:T(8,128)}, f32[8,128]{1,0:T(8,128)}) custom-call(f32[8,16,128]{2,1,0:T(8,128)} %fusion.39.slices), custom_call_target="tpu_custom_call" | custom-call | tf_op jit(solution)/shard_map/norm/pallas_call | solution.py:381
  481.3 2.5 multiply_reduce_fusion.5
  484.5 6.2 %multiply_subtract_fusion = (f32[128,4096]{1,0:T(8,128)}, f32[128,4096]{1,0:T(8,128)}, f32[128,4096]{1,0:T(8,128)}) fusion(f32[128,4096]{1,0:T(8,128)S(1)} %copy-done.16, f32[]{:T(128)} %bitcast.49, f32[]{:T(128)} %bitcast.48, f32[]{:T(128)} %bitcast.47, f32[]{:T(128)} %bitcast.26, f32[]{:T(128)S(6)} %div.138, f32[128,2048]{1,0:T(8,128)S(1)} %get-tuple-element.90, ...), kind=kLoop, calls=%fused_computation.41 | loop fusion | flops 8912896 | bytes 14680084 | tf_op jit(solution)/shard_map/sub | solution.py:848
  490.7 3.8 multiply_subtract_fusion.1
  496.8 3.0 multiply_subtract_fusion.2
  (189 shorter events, 49.5 us)
Async XLA Ops:
  7.2 5.9 %copy-start.39 = (s32[512]{0:T(512)S(1)}, s32[512]{0:T(512)}, u32[]{:S(2)}) copy-start(s32[512]{0:T(512)} %param.23) | copy-start | bytes 6148
  7.2 5.9 %copy-start.38 = (s32[512]{0:T(512)S(1)}, s32[512]{0:T(512)}, u32[]{:S(2)}) copy-start(s32[512]{0:T(512)} %param.24) | copy-start | bytes 6148
  7.2 5.9 %copy-start.34 = (s32[3,512]{1,0:T(4,128)S(1)}, s32[3,512]{1,0:T(4,128)}, u32[]{:S(2)}) copy-start(s32[3,512]{1,0:T(4,128)} %param.25) | copy-start | bytes 18436
  7.2 182.1 %all-gather.2.cloned.1.call-start = ((), (), s32[]{:S(2)}) async-start(), calls=%async_computation.2 | async-start | bytes 4718592 | tf_op jit(solution)/shard_map/all_gather | solution.py:890
  9.4 380.9 %reduce-scatter.2.cloned.1.call-start = ((), (), s32[]{:S(2)}) async-start(), calls=%async_computation.3 | async-start | bytes 4718592 | tf_op jit(solution)/shard_map/reduce_scatter | solution.py:925
  9.4 168.2 %collective-permute-start.2 = (bf16[512,1024]{1,0:T(8,128)(2,1)}, bf16[512,1024]{1,0:T(8,128)(2,1)}, u32[]{:S(2)}, u32[]{:S(2)}) collective-permute-start(bf16[512,1024]{1,0:T(8,128)(2,1)} %param.22), channel_id=1, source_target_pairs={{0,1},{1,0},{2,3},{3,2},{4,5},{5,4},{6,7},{7,6},{8,9},{9,8},{10,11... | collective-permute-start | bytes 3145736 | tf_op jit(solution)/shard_map/ppermute | solution.py:870
  79.1 88.6 %copy-start = (bf16[512,1024]{1,0:T(8,128)(2,1)S(1)}, bf16[512,1024]{1,0:T(8,128)(2,1)}, u32[]{:S(2)}) copy-start(bf16[512,1024]{1,0:T(8,128)(2,1)} %tok.1) | copy-start | bytes 3145732
  172.7 7.2 %collective-permute-start = (bf16[512,1024]{1,0:T(8,128)(2,1)}, bf16[512,1024]{1,0:T(8,128)(2,1)}, u32[]{:S(2)}, u32[]{:S(2)}) collective-permute-start(bf16[512,1024]{1,0:T(8,128)(2,1)} %add_convert_fusion.1), channel_id=1, source_target_pairs={{0,1},{1,0},{2,3},{3,2},{4,5},{5,4},{6,7},{7,6},{8,9},{9,8},{10,11... | collective-permute-start | bytes 3145736 | tf_op jit(solution)/shard_map/ppermute | solution.py:870
  175.0 4.9 copy-start.44
  189.3 13.0 %copy-start.45 = (bf16[1024,2048]{1,0:T(8,128)(2,1)S(1)}, bf16[1024,2048]{1,0:T(8,128)(2,1)}, u32[]{:S(2)}) copy-start(bf16[1024,2048]{1,0:T(8,128)(2,1)} %get-tuple-element.51) | copy-start | bytes 12582916
  202.3 8.2 %copy-start.42 = (bf16[1024,2048]{1,0:T(8,128)(2,1)S(1)}, bf16[1024,2048]{1,0:T(8,128)(2,1)}, u32[]{:S(2)}) copy-start(bf16[1024,2048]{1,0:T(8,128)(2,1)} %get-tuple-element.117) | copy-start | bytes 12582916
  206.8 4.4 copy-start.40
  210.0 17.8 %collective-permute-start.3 = (f32[512,1024]{1,0:T(8,128)}, f32[512,1024]{1,0:T(8,128)}, u32[]{:S(2)}, u32[]{:S(2)}) collective-permute-start(f32[512,1024]{1,0:T(8,128)} %slice.246), channel_id=1, source_target_pairs={{0,1},{1,0},{2,3},{3,2},{4,5},{5,4},{6,7},{7,6},{8,9},{9,8},{10,11... | collective-permute-start | bytes 6291464 | tf_op jit(solution)/shard_map/ppermute | solution.py:870
  218.4 12.7 %collective-permute-start.1 = (f32[512,1024]{1,0:T(8,128)}, f32[512,1024]{1,0:T(8,128)}, u32[]{:S(2)}, u32[]{:S(2)}) collective-permute-start(f32[512,1024]{1,0:T(8,128)} %slice.243), channel_id=1, source_target_pairs={{0,1},{1,0},{2,3},{3,2},{4,5},{5,4},{6,7},{7,6},{8,9},{9,8},{10,11... | collective-permute-start | bytes 6291464 | tf_op jit(solution)/shard_map/ppermute | solution.py:870
  238.6 17.6 %collective-permute-start.4 = (bf16[1024,512]{1,0:T(8,128)(2,1)S(1)}, bf16[1024,512]{1,0:T(8,128)(2,1)S(1)}, u32[]{:S(2)}, u32[]{:S(2)}) collective-permute-start(bf16[1024,512]{1,0:T(8,128)(2,1)S(1)} %dynamic-slice_convert_fusion), channel_id=1, source_target_pairs={{0,1},{1,0},{2,3},{3,2},{4,5},{5,4},{6,7},{7,6},{8,9},{9,8},{10,11... | collective-permute-start | bytes 3145736 | tf_op jit(solution)/shard_map/ppermute | solution.py:870
  242.4 19.4 %all-to-all-start = ((bf16[512,4,256]{2,0,1:T(8,128)(2,1)}), bf16[512,4,256]{2,0,1:T(8,128)(2,1)}, u32[]{:S(2)}, u32[]{:S(2)}) async-start(bf16[512,4,256]{2,0,1:T(8,128)(2,1)} %bitcast.103), calls=%async_computation | async-start | bytes 2097152 | tf_op jit(solution)/shard_map/all_to_all | solution.py:939
  246.7 9.6 %copy-start.2 = (f32[1024,1024]{1,0:T(8,128)S(1)}, f32[1024,1024]{1,0:T(8,128)}, u32[]{:S(2)}) copy-start(f32[1024,1024]{1,0:T(8,128)} %copy-done.1) | copy-start | bytes 12582916
  453.6 5.0 copy-start.5
  453.6 5.0 copy-start.7
  454.5 5.2 %copy-start.19 = (f32[128,512]{1,0:T(8,128)}, f32[128,512]{1,0:T(8,128)S(1)}, u32[]{:S(2)}) copy-start(f32[128,512]{1,0:T(8,128)S(1)} %get-tuple-element.98) | copy-start | bytes 786436
  457.5 5.6 %copy-start.32 = (f32[16,1024]{1,0:T(8,128)S(1)}, f32[16,1024]{1,0:T(8,128)}, u32[]{:S(2)}) copy-start(f32[16,1024]{1,0:T(8,128)} %get-tuple-element.62) | copy-start | bytes 196612
  459.8 24.0 %copy-start.33 = (f32[13,128]{1,0:T(8,128)S(1)}, f32[13,128]{1,0:T(8,128)}, u32[]{:S(2)}) copy-start(f32[13,128]{1,0:T(8,128)} %param.31) | copy-start | bytes 19972
  459.8 24.0 %copy-start.35 = (f32[13,128]{1,0:T(8,128)S(1)}, f32[13,128]{1,0:T(8,128)}, u32[]{:S(2)}) copy-start(f32[13,128]{1,0:T(8,128)} %param.41) | copy-start | bytes 19972
  459.8 24.0 %copy-start.36 = (f32[13,128]{1,0:T(8,128)S(1)}, f32[13,128]{1,0:T(8,128)}, u32[]{:S(2)}) copy-start(f32[13,128]{1,0:T(8,128)} %param.36) | copy-start | bytes 19972
  476.1 7.7 %copy-start.37 = (f32[16,128]{1,0:T(8,128)S(1)}, f32[16,128]{1,0:T(8,128)}, u32[]{:S(2)}) copy-start(f32[16,128]{1,0:T(8,128)} %get-tuple-element.63) | copy-start | bytes 24580
  484.5 6.2 %copy-start.6 = (f32[128,2048]{1,0:T(8,128)S(1)}, f32[128,2048]{1,0:T(8,128)}, u32[]{:S(2)}) copy-start(f32[128,2048]{1,0:T(8,128)} %copy-done.5) | copy-start | bytes 3145732
  484.5 6.2 %copy-start.8 = (f32[128,2048]{1,0:T(8,128)S(1)}, f32[128,2048]{1,0:T(8,128)}, u32[]{:S(2)}) copy-start(f32[128,2048]{1,0:T(8,128)} %copy-done.7) | copy-start | bytes 3145732
  484.5 6.2 %copy-start.17 = (f32[128,4096]{1,0:T(8,128)S(1)}, f32[128,4096]{1,0:T(8,128)}, u32[]{:S(2)}) copy-start(f32[128,4096]{1,0:T(8,128)} %param.29) | copy-start | bytes 6291460
  484.5 6.2 %copy-start.21 = (f32[128,4096]{1,0:T(8,128)S(1)}, f32[128,4096]{1,0:T(8,128)}, u32[]{:S(2)}) copy-start(f32[128,4096]{1,0:T(8,128)} %param.39) | copy-start | bytes 6291460
  484.5 6.2 %copy-start.22 = (f32[128,4096]{1,0:T(8,128)S(1)}, f32[128,4096]{1,0:T(8,128)}, u32[]{:S(2)}) copy-start(f32[128,4096]{1,0:T(8,128)} %param.34) | copy-start | bytes 6291460
  490.7 5.3 %copy-start.25 = (f32[128,3072]{1,0:T(8,128)S(1)}, f32[128,3072]{1,0:T(8,128)}, u32[]{:S(2)}) copy-start(f32[128,3072]{1,0:T(8,128)} %param.37) | copy-start | bytes 4718596
  490.7 5.3 %copy-start.26 = (f32[128,3072]{1,0:T(8,128)S(1)}, f32[128,3072]{1,0:T(8,128)}, u32[]{:S(2)}) copy-start(f32[128,3072]{1,0:T(8,128)} %param.32) | copy-start | bytes 4718596
  (22 other events, 60.3 us)
Sparse Core Ops, SparseCore 0:
  10.7 104.8 all-gather.1
  226.9 127.7 reduce-scatter.1

commit v5 on v4

v5 whole, which is shorter than its diff:
```python
import functools

import jax
import jax.numpy as jnp
from jax import lax
from jax.experimental import pallas as pl
from jax.experimental.pallas import tpu as pltpu
from jax.sharding import PartitionSpec as P

HEADS = 16
BLOCK = 256
BF = jnp.bfloat16
F32 = jnp.float32
MESH = pl.DeviceIdType.MESH


def dot(a, b, ca, cb):
    return lax.dot_general(a, b, (((ca,), (cb,)), ((), ())), preferred_element_type=F32)


def swap_halves(x, half):
    lane = lax.broadcasted_iota(jnp.int32, x.shape, 1)
    width = x.shape[1]
    return jnp.where(
        lane % (2 * half) < half, pltpu.roll(x, width - half, 1), pltpu.roll(x, half, 1)
    )


def turn(x, cosine, sine, half, sign):
    parts = []
    for start in range(0, x.shape[1], 128):
        part = x[:, start : start + 128]
        other = swap_halves(part, half) * sine
        parts.append(part * cosine + other if sign > 0 else part * cosine - other)
    return jnp.concatenate(parts, axis=1)


def rotary_table(head_dim):
    half = head_dim // 2
    lane = jnp.arange(128)
    pair = lane % half
    rates = jnp.power(10000.0, -(pair // 3).astype(F32) / ((half + 2) // 3))
    row = jnp.arange(128)
    axis = row // 14
    value = (row % 14).astype(F32)
    live = (axis[:, None] == (pair % 3)[None, :]) & (row[:, None] < 42)
    angle = value[:, None] * rates[None, :]
    signs = jnp.where(lane % head_dim < half, -1.0, 1.0)
    return jnp.concatenate(
        [
            jnp.where(live, jnp.cos(angle), 0.0),
            jnp.where(live, jnp.sin(angle) * signs[None, :], 0.0),
        ],
        axis=1,
    )


def greet(targets):
    barrier = pltpu.get_barrier_semaphore()
    for target in targets:
        pl.semaphore_signal(barrier, inc=1, device_id=target, device_id_type=MESH)
    pl.semaphore_wait(barrier, len(targets))


def others(name, index, size):
    return [{name: lax.rem(index + d, size)} for d in range(1, size)]


class Copies:
    def __init__(self, send, recv):
        self.send, self.recv, self.all = send, recv, []

    def make(self, src, dst, **target):
        i = len(self.all)
        copy = pltpu.make_async_remote_copy(
            src_ref=src, dst_ref=dst, send_sem=self.send.at[i], recv_sem=self.recv.at[i],
            device_id=target, device_id_type=MESH,
        )
        self.all.append([copy, False])
        return i

    def launch(self, *indices):
        for i in indices:
            self.all[i][0].start()

    def start(self, src, dst, **target):
        i = self.make(src, dst, **target)
        self.launch(i)
        return i

    def arrived(self, i):
        if not self.all[i][1]:
            self.all[i][0].wait_recv()
            self.all[i][1] = True

    def finish(self):
        for i in range(len(self.all)):
            self.arrived(i)
        for copy, _ in self.all:
            copy.wait_send()


def rows_at(index, size):
    return pl.ds(pl.multiple_of(index * size, size), size)


def tail_kernel(
    wide, narrow, part, grad_proj, weight, tok, vec_in, normed_out, quarters_out, vec_out,
    partial, mate_in, cross_out, cross_in, near_in, far_out, far_in, shards, vec_box, sums, send, recv,
):
    w, n = lax.axis_index("wide"), lax.axis_index("narrow")
    column = wide // 2
    z, y = w // 2, lax.rem(w, 2)
    x, c = n // 2, lax.rem(n, 2)
    near, mate, cross = w + 1 - 2 * y, n + 1 - 2 * c, lax.rem(n + 2, narrow)
    wide_rows, group_rows = part.shape[0] // wide, normed_out.shape[0]
    towards = [lax.rem(z + d, column) for d in range(1, column + 1)]
    greet([{"wide": near}] + [{"wide": to * 2 + y} for to in towards[:-1]] + others("narrow", n, narrow))
    go = Copies(send, recv)
    first = [
        go.start(part.at[rows_at(towards[k] * 2 + 1 - y, wide_rows)], near_in.at[k], wide=near) for k in range(column)
    ]

    seconds, kept = [], []

    def relay(k):
        go.arrived(first[k])
        value = part[rows_at(towards[k] * 2 + y, wide_rows), :].astype(F32) + near_in[k].astype(F32)
        if k < column - 1:
            far_out[k] = value.astype(BF)
            seconds.append(go.start(far_out.at[k], far_in.at[k], wide=towards[k] * 2 + y))
        else:
            kept.append(value)

    sums[...] = jnp.zeros_like(sums)
    owners = [(1 - x) * 2 + 1 - c, (1 - x) * 2 + c, x * 2 + 1 - c, n]
    half = group_rows // 2
    mates, overs = [], []
    for slot, owner in enumerate(owners):

        def body(i, carry):
            at = pl.ds(pl.multiple_of(owner * group_rows + i * BLOCK, BLOCK), BLOCK)
            here = pl.ds(pl.multiple_of(i * BLOCK, BLOCK), BLOCK)
            grads = dot(grad_proj[at, :], weight[...], 1, 1)
            unit, _ = norm_parts(tok[at, :].astype(F32))
            sums[0:1, :] += jnp.sum(grads * unit, axis=0, keepdims=True)
            sums[1:2, :] += jnp.sum(grads, axis=0, keepdims=True)
            if slot < 3:
                partial[slot, here, :] = grads.astype(BF)
            else:
                normed_out[here, :] = grads
            return carry

        lax.fori_loop(0, group_rows // BLOCK, body, 0)
        if slot == 0:
            mates.append(go.start(partial.at[0], mate_in.at[0], narrow=mate))
        if slot == 2:
            mates.append(go.start(partial.at[2], mate_in.at[1], narrow=mate))
        if slot == 1:
            go.arrived(mates[0])
            for p in range(2):
                at = pl.ds(p * half, half)
                cross_out[at, :] = (partial[1, at, :].astype(F32) + mate_in[0, at, :].astype(F32)).astype(BF)
                overs.append(go.start(cross_out.at[at], cross_in.at[at], narrow=cross))
        for k in range(column * slot // 4, column * (slot + 1) // 4):
            if k < column - 1:
                relay(k)

    vec_box[pl.ds(n, 1)] = vec_in[...][None]
    vec_box[pl.ds(n, 1), 0:2, :] = sums[0:2, :][None]
    vecs = [go.start(vec_box.at[n], vec_box.at[n], narrow=lax.rem(n + d, narrow)) for d in range(1, narrow)]
    relay(column - 1)
    total = kept[0]
    for k in range(column - 1):
        go.arrived(seconds[k])
        total = total + far_in[k].astype(F32)
    shards[pl.ds(n, 1)] = total.astype(BF)[None]
    over = go.start(shards.at[n], shards.at[n], narrow=cross)
    go.start(shards.at[n], shards.at[n], narrow=mate)

    go.arrived(mates[1])
    for p in range(2):
        go.arrived(overs[p])
        at = pl.ds(p * half, half)
        normed_out[at, :] += mate_in[1, at, :].astype(F32) + cross_in[at, :].astype(F32)
    for i in vecs:
        go.arrived(i)
    group = vec_box[0]
    for i in range(1, narrow):
        group = group + vec_box[i]
    vec_out[...] = group

    go.arrived(over)
    go.start(shards.at[cross], shards.at[cross], narrow=mate)
    go.finish()
    quarters_out[...] = shards[...]


def tail_call(part, grad_proj, weight, tok, vec_in, wide, narrow):
    depth, cols = part.shape
    rows = tok.shape[0] // narrow
    wide_rows = depth // wide
    column = wide // 2
    copies = 2 * column - 1 + 2 + (narrow - 1) + 2 + 3
    vmem = pl.BlockSpec(memory_space=pltpu.VMEM)
    return pl.pallas_call(
        functools.partial(tail_kernel, wide, narrow),
        in_specs=[vmem] * 5,
        out_specs=[vmem] * 3,
        out_shape=[
            jax.ShapeDtypeStruct((rows, depth), F32),
            jax.ShapeDtypeStruct((narrow, wide_rows, cols), BF),
            jax.ShapeDtypeStruct(vec_in.shape, F32),
        ],
        scratch_shapes=[
            pltpu.VMEM((3, rows, depth), BF),
            pltpu.VMEM((2, rows, depth), BF),
            pltpu.VMEM((rows, depth), BF),
            pltpu.VMEM((rows, depth), BF),
            pltpu.VMEM((column, wide_rows, cols), BF),
            pltpu.VMEM((column - 1, wide_rows, cols), BF),
            pltpu.VMEM((column - 1, wide_rows, cols), BF),
            pltpu.VMEM((narrow, wide_rows, cols), BF),
            pltpu.VMEM((narrow,) + vec_in.shape, F32),
            pltpu.VMEM((8, depth), F32),
            pltpu.SemaphoreType.DMA((copies,)),
            pltpu.SemaphoreType.DMA((copies,)),
        ],
        compiler_params=pltpu.CompilerParams(
            collective_id=1, has_side_effects=True, vmem_limit_bytes=56 * 1024 * 1024
        ),
        name="tail",
    )(part, grad_proj, weight, tok, vec_in)


def norm_kernel(wide, slices, total_out, square_out, box, squares, send, recv):
    w = lax.axis_index("wide")
    greet(others("wide", w, wide))
    go = Copies(send, recv)
    peers = [lax.rem(w + d, wide) for d in range(1, wide)]
    for peer in peers:
        go.start(slices.at[peer], box.at[w], wide=peer)
    box[pl.ds(w, 1)] = slices[pl.ds(w, 1)]
    for i in range(wide - 1):
        go.arrived(i)
    total = box[0]
    for i in range(1, wide):
        total = total + box[i]
    total_out[...] = total
    row = lax.broadcasted_iota(jnp.int32, total.shape, 0)
    entries = jnp.where(row == 15, 0.0, total)
    entries = entries * entries
    squares[pl.ds(w, 1)] = (entries[:8] + entries[8:])[None]
    for peer in peers:
        go.start(squares.at[w], squares.at[w], wide=peer)
    go.finish()
    all_squares = squares[0]
    for i in range(1, wide):
        all_squares = all_squares + squares[i]
    square_out[...] = all_squares


def norm_call(slices, wide):
    vmem = pl.BlockSpec(memory_space=pltpu.VMEM)
    copies = 2 * (wide - 1)
    return pl.pallas_call(
        functools.partial(norm_kernel, wide),
        in_specs=[vmem],
        out_specs=[vmem] * 2,
        out_shape=[jax.ShapeDtypeStruct((16, 128), F32), jax.ShapeDtypeStruct((8, 128), F32)],
        scratch_shapes=[
            pltpu.VMEM((wide, 16, 128), F32),
            pltpu.VMEM((wide, 8, 128), F32),
            pltpu.SemaphoreType.DMA((copies,)),
            pltpu.SemaphoreType.DMA((copies,)),
        ],
        compiler_params=pltpu.CompilerParams(collective_id=2, has_side_effects=True),
        name="norm",
    )(slices)


CLIP = 784


def head_lanes(shape, head, head_dim):
    lane = lax.broadcasted_iota(jnp.int32, shape, 1)
    return lane // head_dim == head


def meeting(block, blocks):
    before, after = CLIP // BLOCK, -(-2 * CLIP // BLOCK)
    low = before * (block // after)
    high = blocks - (blocks - after) * (1 - jnp.minimum(block // before, 1))
    return low, high


def forward_kernel(
    heads, head_dim, wide, narrow,
    tok, vec, tag, table, qkv_f32, out_f32, up_f32, down_f32,
    q_ref, k_ref, v_ref, turn_ref, norm_ref, vec_ref, seg_ref, tag_ref, o_ref, lse_ref,
    tok_all, qkv_all, mixed_ref, out_all, up_all, down_all,
    vec_box, tag_box, tok_box, qkv_box, qkv_own, out_own, up_own, down_own, stage_qkv, stage_out, stage_up, stage_down,
    values_turned, acc, peak, total, o_box, send, recv, mix_send, mix_recv, local, leave,
):
    step = pl.program_id(0)
    rows, width = q_ref.shape
    depth = tok.shape[1]
    blocks = rows // BLOCK
    per = blocks // narrow
    final = 2 * blocks
    w, n = lax.axis_index("wide"), lax.axis_index("narrow")
    column = wide // 2
    z, y, side = w // 2, lax.rem(w, 2), lax.rem(n, 2)
    near, mate, cross = w + 1 - 2 * y, n + 1 - 2 * side, lax.rem(n + 2, narrow)
    source = lambda d: lax.rem(z - d + column, column) * 2 + y
    target = lambda d: lax.rem(z + d, column) * 2 + y
    beside = lambda d: lax.rem(z - d + column, column) * 2 + 1 - y
    wide_rows, out_half = out_own.shape
    half = up_own.shape[1]
    group_rows = tok.shape[0]

    loads = [
        pltpu.make_async_copy(
            qkv_f32.at[:, pl.ds(pl.multiple_of(i * depth + n * width, width), width)],
            stage_qkv.at[:, pl.ds(i * width, width)],
            local.at[i],
        )
        for i in range(3)
    ] + [
        pltpu.make_async_copy(
            whole.at[:, pl.ds(pl.multiple_of(side * size, size), size)], stage, local.at[3 + i]
        )
        for i, (whole, stage, size) in enumerate(
            [(out_f32, stage_out, out_half), (up_f32, stage_up, half), (down_f32, stage_down, half)]
        )
    ]

    go = Copies(send, recv)
    small = [go.make(vec, vec_box.at[w], wide=lax.rem(w + d, wide)) for d in range(1, wide)]
    small += [go.make(tag, tag_box.at[n], narrow=lax.rem(n + d, narrow)) for d in range(1, narrow)]
    pieces = 4
    piece = group_rows // pieces
    token_rows = lambda i, p: tok_box.at[rows_at(i * pieces + p, piece)]
    own_piece = lambda p: tok.at[pl.ds(p * piece, piece)]
    over = [go.make(own_piece(p), token_rows(n, p), narrow=cross) for p in range(pieces)]
    to_mate = [go.make(own_piece(p), token_rows(n, p), narrow=mate) for p in range(pieces)]
    passed = [go.make(token_rows(cross, p), token_rows(cross, p), narrow=mate) for p in range(pieces)]
    qkv_at = lambda i: qkv_box.at[rows_at(i, wide_rows)]
    qkv_far = [go.make(qkv_own, qkv_at(w), wide=target(d)) for d in range(1, column)]
    qkv_near = [go.make(qkv_own, qkv_at(w), wide=near)]
    qkv_near += [go.make(qkv_at(source(d)), qkv_at(source(d)), wide=near) for d in range(1, column)]

    at_step = [[] for _ in range(final + 2)]
    out_cols = pl.ds(pl.multiple_of(side * out_half, out_half), out_half)
    out_at = lambda i: out_all.at[rows_at(i, wide_rows), out_cols]
    out_near = [go.make(out_own, out_at(w), wide=near)]
    out_starts = [out_near[0], go.make(out_own, out_at(w), narrow=mate)]
    for d in range(1, column):
        out_starts.append(go.make(out_own, out_at(w), wide=target(d)))
        ref = out_at(source(d))
        out_near.append(go.make(ref, ref, wide=near))
        at_step[5].append((out_starts[-1], [out_near[-1], go.make(ref, ref, narrow=mate)]))
    for d in range(column):
        ref = out_at(beside(d))
        at_step[blocks + 2].append((out_near[d], [go.make(ref, ref, narrow=mate)]))

    quarter = half // 4
    shared = pl.ds(pl.multiple_of(n // 2 * quarter, quarter), quarter)
    both = pl.ds(2 * quarter, 2 * quarter)
    own_out = [pltpu.make_async_copy(out_own, out_at(w), leave.at[0])]

    def spread(own, result, steps, slot):
        starts = []
        for cols in (shared, both):
            piece_at = lambda i: result.at[rows_at(i, wide_rows), cols]
            passes = lambda i: [go.make(piece_at(i), piece_at(i), narrow=cross)] if cols is shared else []
            nears = [go.make(own.at[:, cols], piece_at(w), wide=near)]
            starts += nears
            if cols is shared:
                starts.append(go.make(own.at[:, cols], piece_at(w), narrow=cross))
            for d in range(1, column):
                starts.append(go.make(own.at[:, cols], piece_at(w), wide=target(d)))
                ref = piece_at(source(d))
                nears.append(go.make(ref, ref, wide=near))
                turn_at = steps[0] if cols is shared else steps[2] + (d - 1) * 2 // column
                at_step[min(turn_at, final + 1)].append((starts[-1], [nears[-1]] + passes(source(d))))
            if cols is shared:
                for d in range(column):
                    at_step[steps[1]].append((nears[d], passes(beside(d))))
            own_out.append(pltpu.make_async_copy(own.at[:, cols], piece_at(w), leave.at[slot + (cols is both)]))
        return starts

    up_starts = spread(up_own, up_all, (blocks + 1, blocks + 3, blocks + 4), 1)
    down_starts = spread(down_own, down_all, (final - 1, final + 1, final + 1), 3)

    mine = pl.ds(pl.multiple_of(n * width, width), width)

    def result(s):
        at = lax.rem((n + 1) * per + s, blocks)
        return pltpu.make_async_remote_copy(
            src_ref=o_box.at[rows_at(at, BLOCK)],
            dst_ref=mixed_ref.at[rows_at(lax.rem(s, per), BLOCK), mine],
            send_sem=mix_send.at[s],
            recv_sem=mix_recv.at[s],
            device_id={"narrow": lax.rem(n + 1 + s // per, narrow)},
            device_id_type=MESH,
        )

    def result_here(s):
        return pltpu.make_async_copy(
            o_box.at[rows_at(n * per + s, BLOCK)], mixed_ref.at[rows_at(s, BLOCK), mine], leave.at[7 + s]
        )

    kept = [
        pltpu.make_async_copy(tok_box, tok_all, leave.at[5]),
        pltpu.make_async_copy(qkv_box, qkv_all, leave.at[6]),
    ]

    @pl.when(step == 0)
    def _():
        for copy in loads:
            copy.start()
        greet(others("wide", w, wide) + others("narrow", n, narrow))
        go.launch(*small, *over)
        for copy in loads[:3]:
            copy.wait()
        qkv_own[...] = stage_qkv[...].astype(BF)
        go.launch(*qkv_far, qkv_near[0], *to_mate)
        for copy, stage, own, starts in zip(
            loads[3:],
            (stage_out, stage_up, stage_down),
            (out_own, up_own, down_own),
            (out_starts, up_starts, down_starts),
        ):
            copy.wait()
            own[...] = stage[...].astype(BF)
            go.launch(*starts)
        tok_box[rows_at(n, group_rows), :] = tok[...]
        qkv_box[rows_at(w, wide_rows), :] = qkv_own[...]
        vec_box[pl.ds(w, 1)] = vec[...][None]
        tag_box[pl.ds(n, 1)] = tag[...][None]
        for copy in own_out:
            copy.start()
        for i in small:
            go.arrived(i)
        cols = depth // wide
        for i in range(wide):
            vec_ref[:, i * cols : (i + 1) * cols] = vec_box[i].astype(F32)[:, :cols]
        for i in range(max(pieces, column - 1)):
            if i < column - 1:
                go.arrived(qkv_far[i])
                go.launch(qkv_near[i + 1])
            if i < pieces:
                go.arrived(over[i])
                go.launch(passed[i])
        for i in qkv_near + to_mate + passed:
            go.arrived(i)
        for copy in kept:
            copy.start()

    for i in range(1, final + 1):
        if at_step[i]:

            @pl.when(step == i)
            def _():
                for arrival, follow in at_step[i]:
                    go.arrived(arrival)
                    go.launch(*follow)

    @pl.when((step > 0) & (step <= blocks))
    def _():
        block = step - 1
        at = rows_at(block, BLOCK)
        marks = tag_box[pl.ds(block // per, 1), :, pl.ds(pl.multiple_of(lax.rem(block, per) * BLOCK, BLOCK), BLOCK)]
        marks = marks[0].astype(F32)
        seg_ref[pl.ds(block, 1)] = marks[0:1][None]
        marks = marks.T
        tag_ref[at, :] = jnp.where(marks[:, 1:2] == 1.0, marks[:, 0:1], -1.0)
        slot = lax.broadcasted_iota(jnp.int32, (BLOCK, 128), 1).astype(F32)
        spot = (slot == marks[:, 2:3]) | (slot == 14 + marks[:, 3:4]) | (slot == 28 + marks[:, 4:5])
        angles = lax.dot_general(
            jnp.where(spot, 1.0, 0.0),
            table[...],
            (((1,), (0,)), ((), ())),
            precision=lax.Precision.HIGHEST,
            preferred_element_type=F32,
        )
        turn_ref[at, :] = angles
        cosine, sine = angles[:, :128], angles[:, 128:]
        unit, _ = norm_parts(tok_box[at, :].astype(F32))
        normed = (unit * vec_ref[0:1, :] + vec_ref[1:2, :]).astype(BF)
        norm_ref[...] = normed
        proj = dot(normed, qkv_box[...], 1, 0)
        parts = [proj[:, i * width : (i + 1) * width] + vec_ref[2 + i : 3 + i, mine] for i in range(3)]
        q_ref[at, :] = turn(parts[0], cosine, sine, head_dim // 2, 1).astype(BF)
        k_ref[at, :] = turn(parts[1], cosine, sine, head_dim // 2, 1).astype(BF)
        v_ref[at, :] = parts[2].astype(BF)
        values_turned[:, at] = parts[2].T.astype(BF)

    @pl.when(step > blocks)
    def _():
        place = step - blocks - 1
        block = lax.rem((n + 1) * per + place, blocks)
        at = rows_at(block, BLOCK)
        query = q_ref[at, :] * jnp.asarray(head_dim**-0.5, BF)
        seg = seg_ref[pl.ds(block, 1)][0]
        masked_query = [
            jnp.where(head_lanes(query.shape, h, head_dim), query, jnp.zeros_like(query)) for h in range(heads)
        ]
        acc[...] = jnp.zeros_like(acc)
        peak[...] = jnp.full_like(peak, -1e30)
        total[...] = jnp.zeros_like(total)

        def body(j, carry):
            start = pl.multiple_of(j * BLOCK, BLOCK)
            key = k_ref[pl.ds(start, BLOCK), :]
            allowed = tag_ref[pl.ds(start, BLOCK), :] == seg
            scores = [jnp.where(allowed, dot(key, masked_query[h], 1, 1), -1e30) for h in range(heads)]
            for h in range(heads):
                lines = slice(h * head_dim, (h + 1) * head_dim)
                old = peak[h : h + 1, :]
                new = jnp.maximum(old, jnp.max(scores[h], axis=0, keepdims=True))
                probs = jnp.exp(scores[h] - new)
                keep = jnp.exp(old - new)
                peak[h : h + 1, :] = new
                total[h : h + 1, :] = total[h : h + 1, :] * keep + jnp.sum(probs, axis=0, keepdims=True)
                value = values_turned[lines, pl.ds(start, BLOCK)]
                acc[lines, :] = acc[lines, :] * keep + dot(value, probs.astype(BF), 1, 0)
            return carry

        low, high = meeting(block, blocks)
        lax.fori_loop(low, high, body, 0)
        parts = [acc[h * head_dim : (h + 1) * head_dim, :] / total[h : h + 1, :] for h in range(heads)]
        out = jnp.concatenate(parts, axis=0).T.astype(BF)
        o_ref[at, :] = out
        o_box[at, :] = out
        lse_ref[pl.ds(block, 1)] = (peak[...] + jnp.log(jnp.maximum(total[...], 1e-30)))[None]

        @pl.when(place < blocks - per)
        def _():
            result(place).start()

    @pl.when(step == final)
    def _():
        for s in range(per):
            result_here(s).start()
        for arrival, follow in at_step[final + 1]:
            go.arrived(arrival)
            go.launch(*follow)
        for copy in own_out + kept:
            copy.wait()
        for s in range(blocks - per):
            result(s).wait()
        for s in range(per):
            result_here(s).wait()
        go.finish()


def forward_call(tok, vec, tag, table, weights, head_dim, wide, narrow):
    qkv, out, up, down = weights
    group_rows, depth = tok.shape
    rows = group_rows * narrow
    width = depth // narrow
    heads = width // head_dim
    blocks = rows // BLOCK
    column = wide // 2
    size = qkv.shape[0]
    half = up.shape[1] // 2
    copies = (wide - 1) + (narrow - 1) + 12 + (2 * column - 1)
    copies += 2 + 3 * (column - 1) + column + 2 * (2 * (2 * column - 1) + 2 * column)
    whole = lambda a: pl.BlockSpec(a.shape, lambda i: (0,) * len(a.shape), pipeline_mode=pl.Buffered(1))
    anywhere = pl.BlockSpec(memory_space=pl.ANY)
    shaped = jax.ShapeDtypeStruct
    head_rows = shaped((rows, width), BF)
    inside = [
        head_rows, head_rows, head_rows, shaped((rows, 256), F32), shaped((rows, depth), BF), shaped((16, depth), F32),
        shaped((blocks, 1, BLOCK), F32), shaped((rows, 1), F32), head_rows, shaped((blocks, 8, BLOCK), F32),
    ]
    inside_specs = [whole(a) for a in inside]
    inside_specs[4] = pl.BlockSpec((BLOCK, depth), lambda i: (jnp.minimum(jnp.maximum(i - 1, 0), blocks - 1), 0))
    outside = [
        shaped((rows, depth), BF), shaped((depth, 3 * width), BF), shaped((group_rows, depth), BF),
        shaped((depth, depth), BF), shaped((depth, half), BF), shaped((depth, half), BF),
    ]
    small = [(size, 3 * width), (size, depth // 2), (size, half), (size, half)]
    return pl.pallas_call(
        functools.partial(forward_kernel, heads, head_dim, wide, narrow),
        grid=(2 * blocks + 1,),
        in_specs=[whole(a) for a in (tok, vec, tag, table)] + [anywhere] * 4,
        out_specs=inside_specs + [anywhere] * 6,
        out_shape=inside + outside,
        scratch_shapes=[
            pltpu.VMEM((wide,) + vec.shape, BF),
            pltpu.VMEM((narrow,) + tag.shape, jnp.int32),
            pltpu.VMEM((rows, depth), BF),
            pltpu.VMEM((depth, 3 * width), BF),
        ]
        + [pltpu.VMEM(shape, BF) for shape in small]
        + [pltpu.VMEM(shape, F32) for shape in small]
        + [
            pltpu.VMEM((width, rows), BF),
            pltpu.VMEM((width, BLOCK), F32),
            pltpu.VMEM((8, BLOCK), F32),
            pltpu.VMEM((8, BLOCK), F32),
            pltpu.VMEM((rows, width), BF),
            pltpu.SemaphoreType.DMA((copies,)),
            pltpu.SemaphoreType.DMA((copies,)),
            pltpu.SemaphoreType.DMA((blocks,)),
            pltpu.SemaphoreType.DMA((blocks,)),
            pltpu.SemaphoreType.DMA((6,)),
            pltpu.SemaphoreType.DMA((7 + blocks // narrow,)),
        ],
        compiler_params=pltpu.CompilerParams(
            collective_id=3, has_side_effects=True, vmem_limit_bytes=48 * 1024 * 1024
        ),
        cost_estimate=pl.CostEstimate(
            flops=heads * rows * rows * width * 4, bytes_accessed=rows * width * 8, transcendentals=heads * rows * rows
        ),
        name="attention_forward",
    )(tok, vec, tag, table, qkv, out, up, down)


class Scatter:
    def __init__(self, go, wide, narrow, split, part, near_in, own, far_out, far_in, box, local, *extra):
        w, self.n = lax.axis_index("wide"), lax.axis_index("narrow")
        self.go, self.column, self.split = go, wide // 2, split
        self.near_in, self.own, self.far_out, self.far_in, self.box = near_in, own, far_out, far_in, box
        z, y, x = w // 2, lax.rem(w, 2), self.n // 2
        near, mate, cross = w + 1 - 2 * y, self.n + 1 - 2 * lax.rem(self.n, 2), lax.rem(self.n + 2, narrow)
        size, cols = part.shape[0] // wide, box.shape[2]
        towards = [lax.rem(z + d, self.column) for d in range(1, self.column + 1)]
        theirs, ours = [to * 2 + 1 - y for to in towards], [to * 2 + y for to in towards]
        here = pl.ds(pl.multiple_of(x * cols, cols), cols) if split else pl.ds(0, cols)
        self.loads = [
            pltpu.make_async_copy(part.at[rows_at(i, size), here], own.at[k], local.at[k])
            for k, i in enumerate(ours + theirs if split else ours)
        ]
        self.zero = []
        if split:
            self.cross_in, self.out = extra
            there = pl.ds(pl.multiple_of((1 - x) * cols, cols), cols)
            order = list(enumerate(ours + theirs))
            order = order[self.column :] + order[: self.column]
            self.zero = {
                k: go.make(part.at[rows_at(i, size), there], self.cross_in.at[k], narrow=cross) for k, i in order
            }
        self.first = [
            go.make(self.out.at[k] if split else part.at[rows_at(i, size)], near_in.at[k], wide=near)
            for k, i in enumerate(theirs)
        ]
        self.second = [go.make(far_out.at[k], far_in.at[k], wide=i) for k, i in enumerate(ours[:-1])]
        self.over = go.make(box.at[self.n], box.at[self.n], narrow=cross)
        self.beside = go.make(box.at[self.n], box.at[self.n], narrow=mate)
        self.passed = go.make(box.at[cross], box.at[cross], narrow=mate)

    def load(self):
        for copy in self.loads:
            copy.start()
        if self.split:
            self.go.launch(*self.zero.values())

    def summed(self, k):
        self.loads[k].wait()
        value = self.own[k].astype(F32)
        if self.split:
            self.go.arrived(self.zero[k])
            value = value + self.cross_in[k].astype(F32)
        return value

    def send(self, k):
        if self.split:
            self.out[k] = self.summed(self.column + k).astype(BF)
        self.go.launch(self.first[k])

    def relay(self, k):
        self.go.arrived(self.first[k])
        if k < self.column - 1:
            self.far_out[k] = (self.summed(k) + self.near_in[k].astype(F32)).astype(BF)
            self.go.launch(self.second[k])

    def total(self):
        value = self.summed(self.column - 1) + self.near_in[self.column - 1].astype(F32)
        for k in range(self.column - 1):
            self.go.arrived(self.second[k])
            value = value + self.far_in[k].astype(F32)
        self.box[pl.ds(self.n, 1)] = value.astype(BF)[None]
        self.go.launch(self.over, self.beside)

    def share(self):
        self.go.arrived(self.over)
        self.go.launch(self.passed)

    @staticmethod
    def copies(wide, split):
        return 2 * (wide // 2) - 1 + 3 + (wide if split else 0)

    @staticmethod
    def scratch(wide, narrow, rows, cols, split):
        column, size = wide // 2, rows // wide
        cols = cols // 2 if split else cols
        many = wide if split else column
        sizes = [column, many, column - 1, column - 1, narrow]
        first = [pltpu.VMEM((count, size, cols), BF) for count in sizes] + [pltpu.SemaphoreType.DMA((many,))]
        return first + ([pltpu.VMEM((count, size, cols), BF) for count in (wide, column)] if split else [])


def backward_kernel(
    heads, head_dim, wide, narrow,
    q_ref, k_ref, v_ref, o_ref, g_ref, lse_ref, seg_ref, tag_ref, turn_ref, part_out, part_down, part_up,
    grads_out, shards_out, shards_down, shards_up,
    q_heads, g_heads, delta, grad_query, send, recv, *boxes,
):
    step = pl.program_id(0)
    rows, width = q_ref.shape
    blocks = rows // BLOCK
    last = blocks - 1
    scale = head_dim**-0.5
    half = head_dim // 2
    go = Copies(send, recv)
    column = wide // 2
    outs = Scatter(go, wide, narrow, False, part_out, *boxes[:6])
    ups = Scatter(go, wide, narrow, False, part_up, *boxes[6:12])
    downs = Scatter(go, wide, narrow, True, part_down, *boxes[12:])

    @pl.when(step == 0)
    def _():
        w, n = lax.axis_index("wide"), lax.axis_index("narrow")
        z, y = w // 2, lax.rem(w, 2)
        greet(
            [{"wide": w + 1 - 2 * y}]
            + [{"wide": lax.rem(z + d, column) * 2 + y} for d in range(1, column)]
            + [{"narrow": n + 1 - 2 * lax.rem(n, 2)}, {"narrow": lax.rem(n + 2, narrow)}]
        )
        downs.load()
        outs.load()
        ups.load()
        for k in range(column):
            outs.send(k)
        for k in range(column // 4):
            ups.send(k)

    quarter = lambda i: range(column * i // 4, column * (i + 1) // 4)
    plan = [
        [(outs.relay, range(column)), (ups.send, quarter(1))],
        [(ups.relay, quarter(0)), (downs.send, range(column // 2)), (ups.send, quarter(2))],
        [(ups.relay, quarter(1)), (downs.send, range(column // 2, column)), (ups.send, quarter(3))],
        [(ups.relay, quarter(2)), (outs.total, None)],
        [(ups.relay, quarter(3)), (downs.relay, range(column // 2)), (outs.share, None)],
        [(downs.relay, range(column // 2, column))],
        [(ups.total, None)],
    ]
    actions = [[] for _ in range(last)]
    for i, entries in enumerate(plan):
        for action, ks in entries:
            actions[min(i, last - 1)] += [action] if ks is None else [functools.partial(action, k) for k in ks]
    for i in range(last):
        if actions[i]:

            @pl.when(step == i + 1)
            def _():
                for action in actions[i]:
                    action()

    @pl.when(step == 0)
    def _():
        grad_query[...] = jnp.zeros_like(grad_query)
        row = lax.broadcasted_iota(jnp.int32, (8, width), 0)
        lane = lax.broadcasted_iota(jnp.int32, (8, width), 1)
        pick = jnp.where(lane // head_dim == row, 1.0, 0.0)

        def prepare(i, carry):
            at = pl.ds(pl.multiple_of(i * BLOCK, BLOCK), BLOCK)
            query = q_ref[at, :] * jnp.asarray(scale, BF)
            grad = g_ref[at, :]
            for h in range(heads):
                lanes = head_lanes(query.shape, h, head_dim)
                q_heads[h, at, :] = jnp.where(lanes, query, jnp.zeros_like(query))
                g_heads[h, at, :] = jnp.where(lanes, grad, jnp.zeros_like(grad))
            product = grad.astype(F32) * o_ref[at, :].astype(F32)
            delta[pl.ds(i, 1)] = lax.dot_general(
                pick,
                product,
                (((1,), (1,)), ((), ())),
                precision=lax.Precision.HIGHEST,
                preferred_element_type=F32,
            )[None]
            return carry

        lax.fori_loop(0, blocks, prepare, 0)

    key = k_ref[...]
    value = v_ref[...]
    tag = tag_ref[...]
    masked_key = [jnp.where(head_lanes(key.shape, h, head_dim), key, jnp.zeros_like(key)) for h in range(heads)]

    def body(i, carry):
        grad_key, grad_value = carry
        at = pl.ds(pl.multiple_of(i * BLOCK, BLOCK), BLOCK)
        allowed = tag == seg_ref[pl.ds(i, 1), :]
        lse = lse_ref[pl.ds(i, 1)][0]
        dlt = delta[pl.ds(i, 1)][0]
        total = None
        for h in range(heads):
            query = q_heads[h, at, :]
            grad = g_heads[h, at, :]
            scores = dot(key, query, 1, 1)
            probs = jnp.where(allowed, jnp.exp(scores - lse[h : h + 1, :]), 0.0)
            grad_probs = dot(value, grad, 1, 1)
            grad_scores = (probs * (grad_probs - dlt[h : h + 1, :])).astype(BF)
            grad_value = grad_value + dot(probs.astype(BF), grad, 1, 0)
            grad_key = grad_key + dot(grad_scores, query, 1, 0)
            term = dot(grad_scores, masked_key[h], 0, 0)
            total = term if total is None else total + term
        grad_query[at, :] += total
        return grad_key, grad_value

    zero = jnp.zeros((BLOCK, width), F32)
    low, high = meeting(step, blocks)
    grad_key, grad_value = lax.fori_loop(low, high, body, (zero, zero))
    here = pl.ds(pl.multiple_of(step * BLOCK, BLOCK), BLOCK)
    cosine, sine = turn_ref[here, :128], turn_ref[here, 128:]
    grads_out[here, width : 2 * width] = turn(grad_key, cosine, sine, half, -1).astype(BF)
    grads_out[here, 2 * width :] = grad_value.astype(BF)

    @pl.when(step == last)
    def _():
        ups.share()
        downs.total()

        def finish(i, carry):
            at = pl.ds(pl.multiple_of(i * BLOCK, BLOCK), BLOCK)
            grads = grad_query[at, :] * scale
            grads_out[at, :width] = turn(grads, turn_ref[at, :128], turn_ref[at, 128:], half, -1).astype(BF)
            return carry

        lax.fori_loop(0, blocks, finish, 0)
        downs.share()
        go.finish()
        shards_out[...] = outs.box[...]
        shards_down[...] = downs.box[...]
        shards_up[...] = ups.box[...]


def backward_call(q, k, v, o, g, lse, seg_rows, tag_col, turns, part_out, part_down, part_up, head_dim, wide, narrow):
    rows, width = q.shape
    heads = width // head_dim
    blocks = rows // BLOCK
    whole = lambda a: pl.BlockSpec(a.shape, lambda i: (0,) * len(a.shape), pipeline_mode=pl.Buffered(1))
    block = pl.BlockSpec((BLOCK, width), lambda i: (i, 0))
    anywhere = pl.BlockSpec(memory_space=pl.ANY)
    depth = part_up.shape[0]
    results = [
        jax.ShapeDtypeStruct((rows, 3 * width), BF),
        jax.ShapeDtypeStruct((narrow, depth // wide, part_out.shape[1]), BF),
        jax.ShapeDtypeStruct((narrow, depth // wide, part_down.shape[1] // 2), BF),
        jax.ShapeDtypeStruct((narrow, depth // wide, part_up.shape[1]), BF),
    ]
    copies = 2 * Scatter.copies(wide, False) + Scatter.copies(wide, True)
    return pl.pallas_call(
        functools.partial(backward_kernel, heads, head_dim, wide, narrow),
        grid=(blocks,),
        in_specs=[
            whole(q), block, block, whole(o), whole(g), whole(lse), whole(seg_rows),
            pl.BlockSpec((BLOCK, 1), lambda i: (i, 0)),
            whole(turns), anywhere, anywhere, anywhere,
        ],
        out_specs=[whole(a) for a in results],
        out_shape=results,
        scratch_shapes=[
            pltpu.VMEM((heads, rows, width), BF),
            pltpu.VMEM((heads, rows, width), BF),
            pltpu.VMEM((blocks, 8, BLOCK), F32),
            pltpu.VMEM((rows, width), F32),
            pltpu.SemaphoreType.DMA((copies,)),
            pltpu.SemaphoreType.DMA((copies,)),
        ]
        + Scatter.scratch(wide, narrow, depth, part_out.shape[1], False)
        + Scatter.scratch(wide, narrow, depth, part_up.shape[1], False)
        + Scatter.scratch(wide, narrow, depth, part_down.shape[1], True),
        compiler_params=pltpu.CompilerParams(
            collective_id=4, has_side_effects=True, vmem_limit_bytes=60 * 1024 * 1024
        ),
        cost_estimate=pl.CostEstimate(
            flops=heads * rows * rows * width * 7, bytes_accessed=rows * width * 20, transcendentals=heads * rows * rows
        ),
        name="attention_backward",
    )(q, k, v, o, g, lse, seg_rows, tag_col, turns, part_out, part_down, part_up)


def norm_parts(values):
    center = values - jnp.mean(values, axis=-1, keepdims=True)
    inverse = lax.rsqrt(jnp.mean(center * center, axis=-1, keepdims=True) + 1e-06)
    return center * inverse, inverse


def norm_back(grads, gain, unit, inverse):
    scaled = grads * gain
    return inverse * (
        scaled - jnp.mean(scaled, axis=-1, keepdims=True) - unit * jnp.mean(scaled * unit, axis=-1, keepdims=True)
    )


def adamw(param, grad, first, second, clip, rate, decay, fix_first, fix_second):
    clipped = grad * clip
    moment = 0.9 * first + 0.1 * clipped
    square = 0.999 * second + 0.001 * clipped * clipped
    direction = moment / fix_first / (jnp.sqrt(square / fix_second) + 1e-08)
    return (param - rate * (direction + decay * param), moment, square)


def on_device(
    tokens, cotangent, segment_ids, key_keep, patch_coords, step_count,
    weight_qkv, weight_out, weight_up, weight_down, vectors,
    first_qkv, first_out, first_up, first_down, first_vectors,
    second_qkv, second_out, second_up, second_down, second_vectors,
):
    rows, width = tokens.shape
    hidden = weight_up.shape[1]
    head_dim = width // HEADS
    narrow = lax.axis_size("narrow")
    wide = lax.axis_size("wide")
    shard_rows = width // wide
    me = lax.axis_index("narrow")
    side = me % 2
    mine = width // narrow
    half_hidden = hidden // 2
    group = rows * narrow

    def mate(value):
        return lax.ppermute(value, "narrow", [(i, i ^ 1) for i in range(narrow)])

    def across(value):
        return lax.ppermute(value, "narrow", [(i, i ^ 2) for i in range(narrow)])

    def take(value, start, size, axis=1):
        return lax.dynamic_slice_in_dim(value, start, size, axis)

    shard_cols = vectors.shape[1]
    vec_shard = jnp.pad(vectors.astype(BF), ((0, 16 - vectors.shape[0]), (0, -shard_cols % 128)))
    tag = jnp.concatenate([segment_ids[None], key_keep[None], patch_coords, patch_coords], axis=0)
    (
        query, keys, values, turns, normed1_all, vec, seg_rows, tag_col, mixed_mine, lse,
        tokens_all, qkv_w, mixed, out_w, up_w, down_w,
    ) = forward_call(
        tokens, vec_shard, tag, rotary_table(head_dim), (weight_qkv, weight_out, weight_up, weight_down),
        head_dim, wide, narrow,
    )
    vec = vec[: vectors.shape[0]]
    xin = tokens.astype(F32)
    unit1, inverse1 = norm_parts(xin)
    cot_pair = jnp.concatenate([cotangent, mate(cotangent)], axis=0)

    resid = xin + (dot(mixed, out_w, 1, 0) + vec[5])
    unit2, inverse2 = norm_parts(resid)
    normed2 = (unit2 * vec[6] + vec[7]).astype(BF)
    normed2_pair = jnp.concatenate([normed2, mate(normed2)], axis=0)
    up_bias = take(vec[9:].reshape(1, -1), side * half_hidden, half_hidden)
    up_pre = dot(normed2_pair, up_w, 1, 0) + up_bias
    erf_part = 0.5 * (1.0 + lax.erf(up_pre * (0.5**0.5)))
    act = (up_pre * erf_part).astype(BF)
    slope = erf_part + up_pre * (jnp.exp(-0.5 * up_pre * up_pre) * ((2.0 * jnp.pi) ** -0.5))
    down_part = dot(act, down_w, 1, 1)
    down = down_part[:rows] + mate(down_part[rows:])
    layer_out = (resid + (down + vec[8])).astype(BF)

    part_down = dot(cot_pair, act, 0, 0).astype(BF)
    grad_up_act = (dot(cot_pair, down_w, 1, 0) * slope).astype(BF)
    part_up = dot(normed2_pair, grad_up_act, 0, 0).astype(BF)
    grad_normed2_part = dot(grad_up_act, up_w, 1, 1)
    grad_normed2 = grad_normed2_part[:rows] + mate(grad_normed2_part[rows:])
    cot = cotangent.astype(F32)
    grad_resid = cot + norm_back(grad_normed2, vec[6], unit2, inverse2)
    grad_branch = grad_resid.astype(BF)
    grad_mixed = dot(grad_branch, out_w, 1, 1).astype(BF)
    part_out = dot(mixed, grad_branch, 0, 0)
    own_out = take(part_out, side * (width // 2), width // 2)
    other_out = take(part_out, (1 - side) * (width // 2), width // 2)
    part_out = (own_out + mate(other_out.astype(BF)).astype(F32)).astype(BF)

    grad_mixed_mine = lax.all_to_all(grad_mixed, "narrow", 1, 0, tiled=True)
    grad_proj, shards_out, shards_down, shards_up = backward_call(
        query, keys, values, mixed_mine, grad_mixed_mine, lse, seg_rows[:, 0], tag_col, turns, part_out, part_down, part_up, head_dim, wide, narrow,
    )
    part_qkv = dot(normed1_all, grad_proj, 0, 0).astype(BF)

    proj_sums = jnp.sum(grad_proj.astype(F32), axis=0).reshape(3, mine)
    proj_rows = lax.dynamic_update_slice(jnp.zeros((3, width), F32), proj_sums, (0, me * mine))
    up_sums = jnp.sum(grad_up_act.astype(F32), axis=0)
    up_rows = lax.dynamic_update_slice(jnp.zeros((hidden,), F32), up_sums, (side * half_hidden,))
    vector_part = jnp.concatenate(
        [
            jnp.zeros((2, width), F32),
            proj_rows,
            jnp.sum(grad_branch.astype(F32), axis=0)[None],
            jnp.sum(grad_normed2 * unit2, axis=0)[None],
            jnp.sum(grad_normed2, axis=0)[None],
            jnp.sum(cot, axis=0)[None],
            up_rows.reshape(hidden // width, width),
            jnp.zeros((16 - vectors.shape[0], width), F32),
        ],
        axis=0,
    )
    grad_normed1, quarters, vector_group = tail_call(
        part_qkv, grad_proj, qkv_w, tokens_all, vector_part, wide, narrow
    )
    grad_tokens = (grad_resid + norm_back(grad_normed1, vec[0], unit1, inverse1)).astype(BF)

    def join(shards):
        shards = shards.astype(F32)
        return jnp.concatenate([shards[0] + shards[2], shards[1] + shards[3]], axis=1)

    total_up = join(shards_up)
    total_down = jnp.concatenate([shards_down[i] for i in (0, 2, 1, 3)], axis=1).astype(F32)
    total_out = join(shards_out)
    total_qkv = jnp.concatenate(
        [quarters[i, :, j * mine : (j + 1) * mine] for j in range(3) for i in range(narrow)], axis=1
    ).astype(F32)

    squares = sum(jnp.sum(g * g) for g in (total_qkv, total_out, total_up, total_down))
    slices = jnp.moveaxis(vector_group.reshape(16, wide, shard_rows), 1, 0)
    slices = jnp.pad(slices, ((0, 0), (0, 0), (0, -shard_rows % 128)))
    place = (jnp.arange(16)[:, None] == 15) & (jnp.arange(slices.shape[2])[None, :] == 0)
    slices = jnp.where(place[None], squares, slices)
    vector_total, vector_squares = norm_call(slices, wide)
    grad_norm = jnp.sqrt(vector_total[15, 0] + jnp.sum(vector_squares))
    clip = 1.0 / jnp.maximum(grad_norm, 1.0)
    count = step_count[0].astype(F32)
    rate = 0.4 * count / (count + 4.0)
    decay = 0.04 + 0.018 * count
    fix_first = 1.0 - jnp.power(0.9, count)
    fix_second = 1.0 - jnp.power(0.999, count)
    grad_vectors = vector_total[: vectors.shape[0], :shard_rows]

    def update(param, grad, first, second, decay_here):
        return adamw(param, grad, first, second, clip, rate, decay_here, fix_first, fix_second)

    new_qkv = update(weight_qkv, total_qkv, first_qkv, second_qkv, decay)
    new_out = update(weight_out, total_out, first_out, second_out, decay)
    new_up = update(weight_up, total_up, first_up, second_up, decay)
    new_down = update(weight_down, total_down, first_down, second_down, decay)
    new_vectors = update(vectors, grad_vectors, first_vectors, second_vectors, 0.0)
    news = (new_qkv, new_out, new_up, new_down, new_vectors)
    return (layer_out, grad_tokens) + tuple(n[i] for i in range(3) for n in news) + (grad_norm, grad_vectors[8])


def solution(mesh):
    by_token = P(("wide", "narrow"), None)
    ids = P(("wide", "narrow"))
    by_row = P("wide", None)
    by_column = P(None, "wide")
    params = (by_row,) * 4 + (by_column,)
    return jax.shard_map(
        on_device,
        mesh=mesh,
        in_specs=(by_token, by_token, ids, ids, P(None, ("wide", "narrow")), P()) + params * 3,
        out_specs=(by_token, by_token) + params * 3 + (P(), P("wide")),
        check_vma=False,
    )
```

time: 521 us -> 497 us (0.954)
  between operations: 20.9 us -> 7.77 us
  other arithmetic: 51.1 us -> 39.7 us
    pallas_call x2 -> x0, Pallas kernels: 53.2 us -> none  [the longest x1 40.9 us: gather_call(): pl.pallas_call(functools.partial(gather_kernel, wide, narrow), in_specs=[...]
    pallas_call x1, Pallas kernels: 88.5 us -> 130 us  [forward_call(): pl.pallas_call(functools.partial(forward_kernel, heads, head_dim, wide, n...]
    pallas_call x1, Pallas kernels: 117 us -> 140 us  [backward_call(): pl.pallas_call(functools.partial(backward_kernel, heads, head_dim, wide,...]
    pallas_call x1, Pallas kernels: 58.8 us -> 48.6 us  [tail_call(): pl.pallas_call(functools.partial(tail_kernel, wide, narrow), in_specs=[vm...]
    convert_element_type x5 -> x0, local copies, waits for them, and re-layouts: 7.75 us -> none  [the longest x1 2.09 us: on_device(): down_low = take(weight_down, side * half_hidden, half_hidden).astype(BF)]
    unnamed x104 -> x115, local copies, waits for them, and re-layouts: 17 us -> 23.1 us
    convert_element_type x4 -> x0, other arithmetic: 5.76 us -> none  [the longest x1 2.46 us: on_device(): onehot = ((slot == place[0][:, None]) | (slot == 14 + place[1][:, None])...]
  transfers between devices with their start and end apart: 8 -> 6, of which waited for: 1 -> 2; matrix products, arithmetic and copies ran while one was open for 17% -> 8% of each run, Pallas kernels for 51% -> 0%
where the time goes in v5:
time: 497 us; the launch traced here: 488 us
  Pallas kernels  330 us (66%)
  matrix products  59.5 us (12%)
  other arithmetic  39.7 us (8%)
  local copies, waits for them, and re-layouts  37.7 us (8%)
  between operations  7.77 us (2%)
  starting transfers between devices  6.69 us (1%)
  waiting for transfers between devices  5.98 us (1%)
    pallas_call x1, Pallas kernels, backward_call(): pl.pallas_call(functools.partial(backward_kernel, heads, head_dim, wide,...  140 us
    pallas_call x1, Pallas kernels, forward_call(): pl.pallas_call(functools.partial(forward_kernel, heads, head_dim, wide, n...  130 us
    dot_general x10, matrix products, dot(): lax.dot_general(a, b, (((ca,), (cb,)), ((), ())), preferred_element_type=...  59.5 us
    pallas_call x1, Pallas kernels, tail_call(): pl.pallas_call(functools.partial(tail_kernel, wide, narrow), in_specs=[vm...  48.6 us
    unnamed x115, local copies, waits for them, and re-layouts  23.1 us
    sub x5, other arithmetic, adamw(): return (param - rate * (direction + decay * param), moment, square)  14.2 us
    pallas_call x1, Pallas kernels, norm_call(): pl.pallas_call(functools.partial(norm_kernel, wide), in_specs=[vmem], out...  11.7 us
  transfers between devices with their start and end apart: 6, of which 2 were waited for; matrix products, arithmetic and copies ran while one was open for 8% of the time, Pallas kernels for 0%

profile of v5, /device:TPU:0, one launch (start us, length us, event | category | flops | bytes accessed | tf_op | source)
XLA Modules:
  0.0 487.8 jit_solution(11184236847879064483)
XLA Ops:
  3.6 130.2 %attention_forward.1 = (bf16[2048,256]{1,0:T(8,128)(2,1)S(1)}, bf16[2048,256]{1,0:T(8,128)(2,1)S(1)}, bf16[2048,256]{1,0:T(8,128)(2,1)S(1)}, f32[2048,256]{1,0:T...) custom-call(bf16[512,1024]{1,0:T(8,128)(2,1)} %tok.1, ...), custom_call_target="tpu_custom_call" | custom-call | flops 17179869184 | bytes 4194304 | tf_op jit(solution)/shard_map/attention_forward/pallas_call | solution.py:586
  134.0 5.1 %fusion.53 = (f32[512]{0:T(512)S(1)}, f32[512,1024]{1,0:T(8,128)S(1)}) fusion(f32[1024]{0:T(1024)S(1)} %bitcast.114, bf16[512,1024]{1,0:T(8,128)(2,1)} %get-tuple-element.44, bf16[1024,1024]{1,0:T(8,128)(2,1)} %get-tuple-element.45, bf16[512,1024]{1,0:T(8,128)(2,1)S(1)} %copy-done.12), kind=kOutput, calls=%fused_computation.153 | convolution fusion | flops 1075838464 | bytes 6297600 | tf_op jit(solution)/shard_map/dot_general | solution.py:18
  139.4 1.4 add_convert_fusion.1
  141.3 2.3 constant_dynamic-update-slice_fusion.1
  143.9 1.4 collective-permute-done.2
  145.3 2.3 constant_dynamic-update-slice_fusion
  147.6 8.1 %multiply_convert_fusion = (bf16[1024,2048]{1,0:T(8,128)(2,1)S(1)}, f32[1024,2048]{1,0:T(8,128)S(1)}) fusion(f32[2048]{0:T(1024)S(1)} %bitcast.112, bf16[1024,2048]{1,0:T(8,128)(2,1)} %get-tuple-element.47, bf16[512,1024]{1,0:T(8,128)(2,1)} %collective-permute-done, bf16[512,1024]{1,0:T(8,128)(2,1)} %add_convert_fusion.1), kind=kOutput, calls=%fused_computation.8 | convolution fusion | flops 4311744512 | bytes 18882560 | tf_op jit(solution)/shard_map/dot_general | solution.py:18
  155.7 7.9 %convert_reduce_fusion = (f32[2048]{0:T(1024)S(1)}, bf16[1024,2048]{1,0:T(8,128)(2,1)S(1)}) fusion(f32[1024,2048]{1,0:T(8,128)S(1)} %get-tuple-element.113, f32[2048]{0:T(1024)S(1)} %bitcast.113, bf16[1024,1024]{1,0:T(8,128)(2,1)S(1)} %copy-done.39, bf16[1024,2048]{1,0:T(8,128)(2,1)S(1)} %copy-done.48), kind=kOutput, calls=%fused_computation.7 | convolution fusion | flops 4322228224 | bytes 18890752 | tf_op jit(solution)/shard_map/dot_general | solution.py:18
  163.7 4.5 fusion.55
  168.2 1.7 slice.160
  171.0 4.5 fusion.54
  175.6 1.7 slice.158
  181.1 9.5 %convolution_convert_fusion.1.part_down = bf16[1024,2048]{1,0:T(8,128)(2,1)} fusion(bf16[1024,1024]{1,0:T(8,128)(2,1)} %constant_dynamic-update-slice_fusion, bf16[1024,2048]{1,0:T(8,128)(2,1)} %copy-done.46), kind=kOutput, calls=%fused_computation.12 | convolution fusion | flops 4297064448 | bytes 10485760 | tf_op jit(solution)/shard_map/dot_general | solution.py:18
  190.6 2.7 multiply_reduce_fusion.1
  193.4 3.5 convert_reduce_fusion.4
  198.3 2.0 copy-done.8
  204.2 5.5 %all-to-all-start = ((bf16[512,4,256]{2,0,1:T(8,128)(2,1)}), bf16[512,4,256]{2,0,1:T(8,128)(2,1)}, u32[]{:S(2)}, u32[]{:S(2)}) async-start(bf16[512,4,256]{2,0,1:T(8,128)(2,1)} %bitcast.96), calls=%async_computation | async-start | bytes 2097152 | tf_op jit(solution)/shard_map/all_to_all | solution.py:980
  209.7 9.5 %convolution_convert_fusion.part_up = bf16[1024,2048]{1,0:T(8,128)(2,1)} fusion(bf16[1024,2048]{1,0:T(8,128)(2,1)} %copy-done.47, bf16[512,1024]{1,0:T(8,128)(2,1)} %collective-permute-done, bf16[512,1024]{1,0:T(8,128)(2,1)} %add_convert_fusion.1), kind=kOutput, calls=%fused_computation.11 | convolution fusion | flops 4301258752 | bytes 10485760 | tf_op jit(solution)/shard_map/dot_general | solution.py:18
  219.2 1.3 add_convert_fusion.part_out
  220.5 4.6 all-to-all-done
  225.1 140.0 %attention_backward.1 = (bf16[2048,768]{1,0:T(8,128)(2,1)}, bf16[4,128,512]{2,1,0:T(8,128)(2,1)}, bf16[4,128,1024]{2,1,0:T(8,128)(2,1)}, bf16[4,128,2048]{2,1,0:T(8,128)(2,1)}) custom-call(bf16[2048,256]{1,0:T(8,128)(2,1)} %copy-done.2, bf16[2048,256]{1,0:T(8,128)(2,1)} %copy-done.3, bf16[2048,256]{1,0:T(8,128)(2,1)} %copy-done.4, ...), custom_call_target="tpu_custom_call" | custom-call | flops 30064771072 | bytes 10485760 | tf_op jit(solution)/shard_map/attention_backward/pallas_call | solution.py:859
  365.1 2.3 slice_bitcast_fusion.3
  370.7 7.8 %convolution_convert_fusion.2.part = bf16[1024,768]{1,0:T(8,128)(2,1)} fusion(bf16[2048,1024]{1,0:T(8,128)(2,1)} %get-tuple-element.49, bf16[2048,768]{1,0:T(8,128)(2,1)} %get-tuple-element.58.grad_proj), kind=kOutput, calls=%fused_computation.62 | convolution fusion | flops 3222011904 | bytes 8912896 | tf_op jit(solution)/shard_map/dot_general | solution.py:18
  379.8 48.6 %tail.1 = (f32[512,1024]{1,0:T(8,128)}, bf16[4,128,768]{2,1,0:T(8,128)(2,1)}, f32[16,1024]{1,0:T(8,128)}) custom-call(bf16[1024,768]{1,0:T(8,128)(2,1)} %convolution_convert_fusion.2.part, bf16[2048,768]{1,0:T(8,128)(2,1)} %get-tuple-element.58.grad_proj, bf16[1024,768]{1,0:T(8,128)(2,1)} %get-tuple-element.59.weight, ...), custom_call_target="tpu_custom_call" | custom-call | tf_op jit(solution)/shard_map/tail/pallas_call | solution.py:206
  444.3 2.3 fusion.18
  448.0 11.7 %norm.1 = (f32[16,128]{1,0:T(8,128)}, f32[8,128]{1,0:T(8,128)}) custom-call(f32[8,16,128]{2,1,0:T(8,128)} %fusion.37.slices), custom_call_target="tpu_custom_call" | custom-call | tf_op jit(solution)/shard_map/norm/pallas_call | solution.py:266
  464.9 2.5 multiply_reduce_fusion.4
  468.1 5.4 %multiply_subtract_fusion = (f32[128,4096]{1,0:T(8,128)}, f32[128,4096]{1,0:T(8,128)}, f32[128,4096]{1,0:T(8,128)}) fusion(f32[128,4096]{1,0:T(8,128)S(1)} %copy-done.32, f32[]{:T(128)} %bitcast.39, f32[]{:T(128)} %bitcast.38, f32[]{:T(128)} %bitcast.37, f32[]{:T(128)} %bitcast.14, f32[]{:T(128)S(6)} %div.138, bf16[128,1024]{1,0:T(8,128)(2,1)S(1)} %copy-done.25, ...), kind=kLoop, calls=%fused_computation.45 | loop fusion | flops 12582912 | bytes 13631508 | tf_op jit(solution)/shard_map/sub | solution.py:908
  474.5 3.8 multiply_subtract_fusion.1
  478.3 1.4 multiply_subtract_fusion.3
  480.6 3.0 multiply_subtract_fusion.2
  484.5 1.7 fusion.15
  (174 shorter events, 39.7 us)
Async XLA Ops:
  3.6 130.3 %copy-start.12 = (bf16[512,1024]{1,0:T(8,128)(2,1)S(1)}, bf16[512,1024]{1,0:T(8,128)(2,1)}, u32[]{:S(2)}) copy-start(bf16[512,1024]{1,0:T(8,128)(2,1)} %tok.1) | copy-start | bytes 3145732
  133.8 5.2 %copy-start.2 = (bf16[2048,256]{1,0:T(8,128)(2,1)}, bf16[2048,256]{1,0:T(8,128)(2,1)S(1)}, u32[]{:S(2)}) copy-start(bf16[2048,256]{1,0:T(8,128)(2,1)S(1)} %get-tuple-element.50.q_ref) | copy-start | bytes 3145732
  133.9 5.2 %copy-start.3 = (bf16[2048,256]{1,0:T(8,128)(2,1)}, bf16[2048,256]{1,0:T(8,128)(2,1)S(1)}, u32[]{:S(2)}) copy-start(bf16[2048,256]{1,0:T(8,128)(2,1)S(1)} %get-tuple-element.51.k_ref) | copy-start | bytes 3145732
  133.9 5.2 %copy-start.4 = (bf16[2048,256]{1,0:T(8,128)(2,1)}, bf16[2048,256]{1,0:T(8,128)(2,1)S(1)}, u32[]{:S(2)}) copy-start(bf16[2048,256]{1,0:T(8,128)(2,1)S(1)} %get-tuple-element.52.v_ref) | copy-start | bytes 3145732
  133.9 5.2 %copy-start.5 = (f32[2048,1]{1,0:T(8,128)}, f32[2048,1]{1,0:T(8,128)S(1)}, u32[]{:S(2)}) copy-start(f32[2048,1]{1,0:T(8,128)S(1)} %get-tuple-element.56.tag_ref) | copy-start | bytes 24580
  133.9 5.2 %copy-start.6 = (bf16[2048,256]{1,0:T(8,128)(2,1)}, bf16[2048,256]{1,0:T(8,128)(2,1)S(1)}, u32[]{:S(2)}) copy-start(bf16[2048,256]{1,0:T(8,128)(2,1)S(1)} %get-tuple-element.53.o_ref) | copy-start | bytes 3145732
  133.9 5.2 %copy-start.7 = (f32[8,8,256]{2,1,0:T(8,128)}, f32[8,8,256]{2,1,0:T(8,128)S(1)}, u32[]{:S(2)}) copy-start(f32[8,8,256]{2,1,0:T(8,128)S(1)} %get-tuple-element.54.lse_ref) | copy-start | bytes 196612
  140.8 6.8 %collective-permute-start = (bf16[512,1024]{1,0:T(8,128)(2,1)}, bf16[512,1024]{1,0:T(8,128)(2,1)}, u32[]{:S(2)}, u32[]{:S(2)}) collective-permute-start(bf16[512,1024]{1,0:T(8,128)(2,1)} %add_convert_fusion.1), channel_id=1, source_target_pairs={{0,1},{1,0},{2,3},{3,2},{4,5},{5,4},{6,7},{7,6},{8,9},{9,8},{10,11... | collective-permute-start | bytes 3145736 | tf_op jit(solution)/shard_map/ppermute | solution.py:930
  140.8 4.5 collective-permute-start.2
  147.6 8.1 %copy-start.39 = (bf16[1024,1024]{1,0:T(8,128)(2,1)S(1)}, bf16[1024,1024]{1,0:T(8,128)(2,1)}, u32[]{:S(2)}) copy-start(bf16[1024,1024]{1,0:T(8,128)(2,1)} %constant_dynamic-update-slice_fusion) | copy-start | bytes 6291460
  147.6 8.1 %copy-start.48 = (bf16[1024,2048]{1,0:T(8,128)(2,1)S(1)}, bf16[1024,2048]{1,0:T(8,128)(2,1)}, u32[]{:S(2)}) copy-start(bf16[1024,2048]{1,0:T(8,128)(2,1)} %get-tuple-element.48) | copy-start | bytes 12582916
  155.7 15.3 %copy-start.46 = (bf16[1024,2048]{1,0:T(8,128)(2,1)}, bf16[1024,2048]{1,0:T(8,128)(2,1)S(1)}, u32[]{:S(2)}) copy-start(bf16[1024,2048]{1,0:T(8,128)(2,1)S(1)} %get-tuple-element.112) | copy-start | bytes 12582916
  155.7 8.0 %copy-start.49 = (bf16[1024,2048]{1,0:T(8,128)(2,1)S(1)}, bf16[1024,2048]{1,0:T(8,128)(2,1)}, u32[]{:S(2)}) copy-start(bf16[1024,2048]{1,0:T(8,128)(2,1)} %get-tuple-element.47) | copy-start | bytes 12582916
  163.7 4.6 copy-start.47
  170.9 19.7 %collective-permute-start.3 = (f32[512,1024]{1,0:T(8,128)}, f32[512,1024]{1,0:T(8,128)}, u32[]{:S(2)}, u32[]{:S(2)}) collective-permute-start(f32[512,1024]{1,0:T(8,128)} %slice.160), channel_id=1, source_target_pairs={{0,1},{1,0},{2,3},{3,2},{4,5},{5,4},{6,7},{7,6},{8,9},{9,8},{10,11... | collective-permute-start | bytes 6291464 | tf_op jit(solution)/shard_map/ppermute | solution.py:930
  178.2 15.2 %collective-permute-start.1 = (f32[512,1024]{1,0:T(8,128)}, f32[512,1024]{1,0:T(8,128)}, u32[]{:S(2)}, u32[]{:S(2)}) collective-permute-start(f32[512,1024]{1,0:T(8,128)} %slice.158), channel_id=1, source_target_pairs={{0,1},{1,0},{2,3},{3,2},{4,5},{5,4},{6,7},{7,6},{8,9},{9,8},{10,11... | collective-permute-start | bytes 6291464 | tf_op jit(solution)/shard_map/ppermute | solution.py:930
  181.1 9.5 %copy-start.18 = (f32[1024,1024]{1,0:T(8,128)S(1)}, f32[1024,1024]{1,0:T(8,128)}, u32[]{:S(2)}) copy-start(f32[1024,1024]{1,0:T(8,128)} %copy-done.17) | copy-start | bytes 12582916
  200.4 18.8 %collective-permute-start.4 = (bf16[1024,512]{1,0:T(8,128)(2,1)S(1)}, bf16[1024,512]{1,0:T(8,128)(2,1)S(1)}, u32[]{:S(2)}, u32[]{:S(2)}) collective-permute-start(bf16[1024,512]{1,0:T(8,128)(2,1)S(1)} %dynamic-slice_convert_fusion), channel_id=1, source_target_pairs={{0,1},{1,0},{2,3},{3,2},{4,5},{5,4},{6,7},{7,6},{8,9},{9,8},{10,11... | collective-permute-start | bytes 3145736 | tf_op jit(solution)/shard_map/ppermute | solution.py:930
  204.2 20.9 %all-to-all-start = ((bf16[512,4,256]{2,0,1:T(8,128)(2,1)}), bf16[512,4,256]{2,0,1:T(8,128)(2,1)}, u32[]{:S(2)}, u32[]{:S(2)}) async-start(bf16[512,4,256]{2,0,1:T(8,128)(2,1)} %bitcast.96), calls=%async_computation | async-start | bytes 2097152 | tf_op jit(solution)/shard_map/all_to_all | solution.py:980
  209.7 9.5 %copy-start.9 = (f32[1024,1024]{1,0:T(8,128)S(1)}, f32[1024,1024]{1,0:T(8,128)}, u32[]{:S(2)}) copy-start(f32[1024,1024]{1,0:T(8,128)} %copy-done.8) | copy-start | bytes 12582916
  430.1 11.5 %copy-start.22 = (f32[128,512]{1,0:T(8,128)S(1)}, f32[128,512]{1,0:T(8,128)}, u32[]{:S(2)}) copy-start(f32[128,512]{1,0:T(8,128)} %get-tuple-element.101) | copy-start | bytes 786436
  439.5 7.9 %copy-start.40 = (f32[16,1024]{1,0:T(8,128)S(1)}, f32[16,1024]{1,0:T(8,128)}, u32[]{:S(2)}) copy-start(f32[16,1024]{1,0:T(8,128)} %get-tuple-element.66) | copy-start | bytes 196612
  444.3 23.1 %copy-start.41 = (f32[13,128]{1,0:T(8,128)S(1)}, f32[13,128]{1,0:T(8,128)}, u32[]{:S(2)}) copy-start(f32[13,128]{1,0:T(8,128)} %param.31) | copy-start | bytes 19972
  444.3 23.1 %copy-start.42 = (f32[13,128]{1,0:T(8,128)S(1)}, f32[13,128]{1,0:T(8,128)}, u32[]{:S(2)}) copy-start(f32[13,128]{1,0:T(8,128)} %param.41) | copy-start | bytes 19972
  444.3 23.1 %copy-start.43 = (f32[13,128]{1,0:T(8,128)S(1)}, f32[13,128]{1,0:T(8,128)}, u32[]{:S(2)}) copy-start(f32[13,128]{1,0:T(8,128)} %param.36) | copy-start | bytes 19972
  459.7 7.7 %copy-start.44 = (f32[16,128]{1,0:T(8,128)S(1)}, f32[16,128]{1,0:T(8,128)}, u32[]{:S(2)}) copy-start(f32[16,128]{1,0:T(8,128)} %get-tuple-element.67) | copy-start | bytes 24580
  468.1 5.5 %copy-start.28 = (f32[128,4096]{1,0:T(8,128)S(1)}, f32[128,4096]{1,0:T(8,128)}, u32[]{:S(2)}) copy-start(f32[128,4096]{1,0:T(8,128)} %up_f32.1) | copy-start | bytes 6291460
  468.1 5.5 %copy-start.29 = (f32[128,4096]{1,0:T(8,128)S(1)}, f32[128,4096]{1,0:T(8,128)}, u32[]{:S(2)}) copy-start(f32[128,4096]{1,0:T(8,128)} %param.39) | copy-start | bytes 6291460
  468.1 6.3 %copy-start.30 = (f32[128,4096]{1,0:T(8,128)S(1)}, f32[128,4096]{1,0:T(8,128)}, u32[]{:S(2)}) copy-start(f32[128,4096]{1,0:T(8,128)} %param.34) | copy-start | bytes 6291460
  474.5 5.3 %copy-start.34 = (f32[128,3072]{1,0:T(8,128)S(1)}, f32[128,3072]{1,0:T(8,128)}, u32[]{:S(2)}) copy-start(f32[128,3072]{1,0:T(8,128)} %param.37) | copy-start | bytes 4718596
  474.5 5.3 %copy-start.35 = (f32[128,3072]{1,0:T(8,128)S(1)}, f32[128,3072]{1,0:T(8,128)}, u32[]{:S(2)}) copy-start(f32[128,3072]{1,0:T(8,128)} %param.32) | copy-start | bytes 4718596
  480.6 3.9 copy-start.14
  (24 other events, 64.2 us)

commit v6 on v5

--- a/solution.py
+++ b/solution.py
@@ -105,8 +105,9 @@
 
 
 def tail_kernel(
-    wide, narrow, part, grad_proj, weight, tok, vec_in, normed_out, quarters_out, vec_out,
-    partial, mate_in, cross_out, cross_in, near_in, far_out, far_in, shards, vec_box, sums, send, recv,
+    wide, narrow, part, grad_proj, weight, tok, vec_in, squares_in, normed_out, qkv_out, vec_out, square_out,
+    partial, mate_in, cross_out, cross_in, near_in, far_out, far_in, shards, vec_box, sums,
+    slices, slice_box, square_box, send, recv,
 ):
     w, n = lax.axis_index("wide"), lax.axis_index("narrow")
     column = wide // 2
@@ -115,7 +116,7 @@
     near, mate, cross = w + 1 - 2 * y, n + 1 - 2 * c, lax.rem(n + 2, narrow)
     wide_rows, group_rows = part.shape[0] // wide, normed_out.shape[0]
     towards = [lax.rem(z + d, column) for d in range(1, column + 1)]
-    greet([{"wide": near}] + [{"wide": to * 2 + y} for to in towards[:-1]] + others("narrow", n, narrow))
+    greet(others("wide", w, wide) + others("narrow", n, narrow))
     go = Copies(send, recv)
     first = [
         go.start(part.at[rows_at(towards[k] * 2 + 1 - y, wide_rows)], near_in.at[k], wide=near) for k in range(column)
@@ -169,6 +170,18 @@
     vec_box[pl.ds(n, 1)] = vec_in[...][None]
     vec_box[pl.ds(n, 1), 0:2, :] = sums[0:2, :][None]
     vecs = [go.start(vec_box.at[n], vec_box.at[n], narrow=lax.rem(n + d, narrow)) for d in range(1, narrow)]
+    for i in vecs:
+        go.arrived(i)
+    group = vec_box[0]
+    for i in range(1, narrow):
+        group = group + vec_box[i]
+    cols = group.shape[1] // wide
+    slices[...] = jnp.zeros_like(slices)
+    for i in range(wide):
+        slices[i, :, :cols] = group[:, i * cols : (i + 1) * cols]
+    peers = [lax.rem(w + d, wide) for d in range(1, wide)]
+    pieces = [go.start(slices.at[peer], slice_box.at[w], wide=peer) for peer in peers]
+    slice_box[pl.ds(w, 1)] = slices[pl.ds(w, 1)]
     relay(column - 1)
     total = kept[0]
     for k in range(column - 1):
@@ -176,41 +189,57 @@
         total = total + far_in[k].astype(F32)
     shards[pl.ds(n, 1)] = total.astype(BF)[None]
     over = go.start(shards.at[n], shards.at[n], narrow=cross)
-    go.start(shards.at[n], shards.at[n], narrow=mate)
+    beside = go.start(shards.at[n], shards.at[n], narrow=mate)
 
     go.arrived(mates[1])
     for p in range(2):
         go.arrived(overs[p])
         at = pl.ds(p * half, half)
         normed_out[at, :] += mate_in[1, at, :].astype(F32) + cross_in[at, :].astype(F32)
-    for i in vecs:
+    for i in pieces:
         go.arrived(i)
-    group = vec_box[0]
-    for i in range(1, narrow):
-        group = group + vec_box[i]
-    vec_out[...] = group
+    vectors = slice_box[0]
+    for i in range(1, wide):
+        vectors = vectors + slice_box[i]
+    vec_out[...] = vectors
 
     go.arrived(over)
-    go.start(shards.at[cross], shards.at[cross], narrow=mate)
+    passed = go.start(shards.at[cross], shards.at[cross], narrow=mate)
+    for i in (beside, passed):
+        go.arrived(i)
+    squares = square_sum(vectors)
+    width = part.shape[1] // 3
+    for i in range(narrow):
+        shard = shards[i]
+        squares += square_sum(shard.astype(F32))
+        for j in range(3):
+            qkv_out[:, (j * narrow + i) * width : (j * narrow + i + 1) * width] = shard[:, j * width : (j + 1) * width]
+    square_box[pl.ds(w, 1)] = (squares_in[...] + squares)[None]
+    for peer in peers:
+        go.start(square_box.at[w], square_box.at[w], wide=peer)
     go.finish()
-    quarters_out[...] = shards[...]
-
-
-def tail_call(part, grad_proj, weight, tok, vec_in, wide, narrow):
+    total = square_box[0]
+    for i in range(1, wide):
+        total = total + square_box[i]
+    square_out[...] = total
+
+
+def tail_call(part, grad_proj, weight, tok, vec_in, squares_in, wide, narrow):
     depth, cols = part.shape
     rows = tok.shape[0] // narrow
     wide_rows = depth // wide
     column = wide // 2
-    copies = 2 * column - 1 + 2 + (narrow - 1) + 2 + 3
+    copies = 2 * column - 1 + 2 + (narrow - 1) + 2 + 3 + 2 * (wide - 1)
     vmem = pl.BlockSpec(memory_space=pltpu.VMEM)
     return pl.pallas_call(
         functools.partial(tail_kernel, wide, narrow),
-        in_specs=[vmem] * 5,
-        out_specs=[vmem] * 3,
+        in_specs=[vmem] * 6,
+        out_specs=[vmem] * 4,
         out_shape=[
             jax.ShapeDtypeStruct((rows, depth), F32),
-            jax.ShapeDtypeStruct((narrow, wide_rows, cols), BF),
-            jax.ShapeDtypeStruct(vec_in.shape, F32),
+            jax.ShapeDtypeStruct((wide_rows, narrow * cols), BF),
+            jax.ShapeDtypeStruct((16, 128), F32),
+            jax.ShapeDtypeStruct((8, 128), F32),
         ],
         scratch_shapes=[
             pltpu.VMEM((3, rows, depth), BF),
@@ -223,6 +252,9 @@
             pltpu.VMEM((narrow, wide_rows, cols), BF),
             pltpu.VMEM((narrow,) + vec_in.shape, F32),
             pltpu.VMEM((8, depth), F32),
+            pltpu.VMEM((wide, 16, 128), F32),
+            pltpu.VMEM((wide, 16, 128), F32),
+            pltpu.VMEM((wide, 8, 128), F32),
             pltpu.SemaphoreType.DMA((copies,)),
             pltpu.SemaphoreType.DMA((copies,)),
         ],
@@ -230,53 +262,7 @@
             collective_id=1, has_side_effects=True, vmem_limit_bytes=56 * 1024 * 1024
         ),
         name="tail",
-    )(part, grad_proj, weight, tok, vec_in)
-
-
-def norm_kernel(wide, slices, total_out, square_out, box, squares, send, recv):
-    w = lax.axis_index("wide")
-    greet(others("wide", w, wide))
-    go = Copies(send, recv)
-    peers = [lax.rem(w + d, wide) for d in range(1, wide)]
-    for peer in peers:
-        go.start(slices.at[peer], box.at[w], wide=peer)
-    box[pl.ds(w, 1)] = slices[pl.ds(w, 1)]
-    for i in range(wide - 1):
-        go.arrived(i)
-    total = box[0]
-    for i in range(1, wide):
-        total = total + box[i]
-    total_out[...] = total
-    row = lax.broadcasted_iota(jnp.int32, total.shape, 0)
-    entries = jnp.where(row == 15, 0.0, total)
-    entries = entries * entries
-    squares[pl.ds(w, 1)] = (entries[:8] + entries[8:])[None]
-    for peer in peers:
-        go.start(squares.at[w], squares.at[w], wide=peer)
-    go.finish()
-    all_squares = squares[0]
-    for i in range(1, wide):
-        all_squares = all_squares + squares[i]
-    square_out[...] = all_squares
-
-
-def norm_call(slices, wide):
-    vmem = pl.BlockSpec(memory_space=pltpu.VMEM)
-    copies = 2 * (wide - 1)
-    return pl.pallas_call(
-        functools.partial(norm_kernel, wide),
-        in_specs=[vmem],
-        out_specs=[vmem] * 2,
-        out_shape=[jax.ShapeDtypeStruct((16, 128), F32), jax.ShapeDtypeStruct((8, 128), F32)],
-        scratch_shapes=[
-            pltpu.VMEM((wide, 16, 128), F32),
-            pltpu.VMEM((wide, 8, 128), F32),
-            pltpu.SemaphoreType.DMA((copies,)),
-            pltpu.SemaphoreType.DMA((copies,)),
-        ],
-        compiler_params=pltpu.CompilerParams(collective_id=2, has_side_effects=True),
-        name="norm",
-    )(slices)
+    )(part, grad_proj, weight, tok, vec_in, squares_in)
 
 
 CLIP = 784
@@ -354,7 +340,8 @@
     out_cols = pl.ds(pl.multiple_of(side * out_half, out_half), out_half)
     out_at = lambda i: out_all.at[rows_at(i, wide_rows), out_cols]
     out_near = [go.make(out_own, out_at(w), wide=near)]
-    out_starts = [out_near[0], go.make(out_own, out_at(w), narrow=mate)]
+    out_starts = [go.make(out_own, out_at(w), narrow=mate)]
+    at_step[1].append((None, [out_near[0]]))
     for d in range(1, column):
         out_starts.append(go.make(out_own, out_at(w), wide=target(d)))
         ref = out_at(source(d))
@@ -375,7 +362,7 @@
             piece_at = lambda i: result.at[rows_at(i, wide_rows), cols]
             passes = lambda i: [go.make(piece_at(i), piece_at(i), narrow=cross)] if cols is shared else []
             nears = [go.make(own.at[:, cols], piece_at(w), wide=near)]
-            starts += nears
+            at_step[1].append((None, [nears[0]]))
             if cols is shared:
                 starts.append(go.make(own.at[:, cols], piece_at(w), narrow=cross))
             for d in range(1, column):
@@ -464,7 +451,8 @@
             @pl.when(step == i)
             def _():
                 for arrival, follow in at_step[i]:
-                    go.arrived(arrival)
+                    if arrival is not None:
+                        go.arrived(arrival)
                     go.launch(*follow)
 
     @pl.when((step > 0) & (step <= blocks))
@@ -621,65 +609,42 @@
 
 
 class Scatter:
-    def __init__(self, go, wide, narrow, split, part, near_in, own, far_out, far_in, box, local, *extra):
+    def __init__(self, go, wide, narrow, part, near_in, own, far_out, far_in, box, local):
         w, self.n = lax.axis_index("wide"), lax.axis_index("narrow")
-        self.go, self.column, self.split = go, wide // 2, split
+        self.go, self.column = go, wide // 2
         self.near_in, self.own, self.far_out, self.far_in, self.box = near_in, own, far_out, far_in, box
-        z, y, x = w // 2, lax.rem(w, 2), self.n // 2
+        z, y = w // 2, lax.rem(w, 2)
         near, mate, cross = w + 1 - 2 * y, self.n + 1 - 2 * lax.rem(self.n, 2), lax.rem(self.n + 2, narrow)
-        size, cols = part.shape[0] // wide, box.shape[2]
+        size = part.shape[0] // wide
         towards = [lax.rem(z + d, self.column) for d in range(1, self.column + 1)]
-        theirs, ours = [to * 2 + 1 - y for to in towards], [to * 2 + y for to in towards]
-        here = pl.ds(pl.multiple_of(x * cols, cols), cols) if split else pl.ds(0, cols)
+        self.first = [
+            go.make(part.at[rows_at(to * 2 + 1 - y, size)], near_in.at[k], wide=near) for k, to in enumerate(towards)
+        ]
         self.loads = [
-            pltpu.make_async_copy(part.at[rows_at(i, size), here], own.at[k], local.at[k])
-            for k, i in enumerate(ours + theirs if split else ours)
+            pltpu.make_async_copy(part.at[rows_at(to * 2 + y, size)], own.at[k], local.at[k])
+            for k, to in enumerate(towards)
         ]
-        self.zero = []
-        if split:
-            self.cross_in, self.out = extra
-            there = pl.ds(pl.multiple_of((1 - x) * cols, cols), cols)
-            order = list(enumerate(ours + theirs))
-            order = order[self.column :] + order[: self.column]
-            self.zero = {
-                k: go.make(part.at[rows_at(i, size), there], self.cross_in.at[k], narrow=cross) for k, i in order
-            }
-        self.first = [
-            go.make(self.out.at[k] if split else part.at[rows_at(i, size)], near_in.at[k], wide=near)
-            for k, i in enumerate(theirs)
+        self.second = [
+            go.make(far_out.at[k], far_in.at[k], wide=to * 2 + y) for k, to in enumerate(towards[:-1])
         ]
-        self.second = [go.make(far_out.at[k], far_in.at[k], wide=i) for k, i in enumerate(ours[:-1])]
         self.over = go.make(box.at[self.n], box.at[self.n], narrow=cross)
         self.beside = go.make(box.at[self.n], box.at[self.n], narrow=mate)
         self.passed = go.make(box.at[cross], box.at[cross], narrow=mate)
 
-    def load(self):
+    def begin(self):
+        self.go.launch(*self.first)
         for copy in self.loads:
             copy.start()
-        if self.split:
-            self.go.launch(*self.zero.values())
-
-    def summed(self, k):
-        self.loads[k].wait()
-        value = self.own[k].astype(F32)
-        if self.split:
-            self.go.arrived(self.zero[k])
-            value = value + self.cross_in[k].astype(F32)
-        return value
-
-    def send(self, k):
-        if self.split:
-            self.out[k] = self.summed(self.column + k).astype(BF)
-        self.go.launch(self.first[k])
 
     def relay(self, k):
         self.go.arrived(self.first[k])
+        self.loads[k].wait()
         if k < self.column - 1:
-            self.far_out[k] = (self.summed(k) + self.near_in[k].astype(F32)).astype(BF)
+            self.far_out[k] = (self.own[k].astype(F32) + self.near_in[k].astype(F32)).astype(BF)
             self.go.launch(self.second[k])
 
     def total(self):
-        value = self.summed(self.column - 1) + self.near_in[self.column - 1].astype(F32)
+        value = self.own[self.column - 1].astype(F32) + self.near_in[self.column - 1].astype(F32)
         for k in range(self.column - 1):
             self.go.arrived(self.second[k])
             value = value + self.far_in[k].astype(F32)
@@ -691,23 +656,24 @@
         self.go.launch(self.passed)
 
     @staticmethod
-    def copies(wide, split):
-        return 2 * (wide // 2) - 1 + 3 + (wide if split else 0)
+    def copies(wide):
+        return 2 * (wide // 2) - 1 + 3
 
     @staticmethod
-    def scratch(wide, narrow, rows, cols, split):
+    def scratch(wide, narrow, rows, cols):
         column, size = wide // 2, rows // wide
-        cols = cols // 2 if split else cols
-        many = wide if split else column
-        sizes = [column, many, column - 1, column - 1, narrow]
-        first = [pltpu.VMEM((count, size, cols), BF) for count in sizes] + [pltpu.SemaphoreType.DMA((many,))]
-        return first + ([pltpu.VMEM((count, size, cols), BF) for count in (wide, column)] if split else [])
+        sizes = [column, column, column - 1, column - 1, narrow]
+        return [pltpu.VMEM((count, size, cols), BF) for count in sizes] + [pltpu.SemaphoreType.DMA((column,))]
+
+
+def square_sum(value):
+    return jnp.sum(jnp.sum(value * value, axis=0, keepdims=True), axis=1, keepdims=True)
 
 
 def backward_kernel(
     heads, head_dim, wide, narrow,
     q_ref, k_ref, v_ref, o_ref, g_ref, lse_ref, seg_ref, tag_ref, turn_ref, part_out, part_down, part_up,
-    grads_out, shards_out, shards_down, shards_up,
+    grads_out, shards_out, shards_down, shards_up, squares_out,
     q_heads, g_heads, delta, grad_query, send, recv, *boxes,
 ):
     step = pl.program_id(0)
@@ -718,9 +684,9 @@
     half = head_dim // 2
     go = Copies(send, recv)
     column = wide // 2
-    outs = Scatter(go, wide, narrow, False, part_out, *boxes[:6])
-    ups = Scatter(go, wide, narrow, False, part_up, *boxes[6:12])
-    downs = Scatter(go, wide, narrow, True, part_down, *boxes[12:])
+    outs = Scatter(go, wide, narrow, part_out, *boxes[:6])
+    ups = Scatter(go, wide, narrow, part_up, *boxes[6:12])
+    downs = Scatter(go, wide, narrow, part_down, *boxes[12:])
 
     @pl.when(step == 0)
     def _():
@@ -731,23 +697,19 @@
             + [{"wide": lax.rem(z + d, column) * 2 + y} for d in range(1, column)]
             + [{"narrow": n + 1 - 2 * lax.rem(n, 2)}, {"narrow": lax.rem(n + 2, narrow)}]
         )
-        downs.load()
-        outs.load()
-        ups.load()
-        for k in range(column):
-            outs.send(k)
-        for k in range(column // 4):
-            ups.send(k)
-
-    quarter = lambda i: range(column * i // 4, column * (i + 1) // 4)
+        outs.begin()
+        ups.begin()
+        downs.begin()
+
+    part = lambda i: range(column * i // 4, column * (i + 1) // 4)
     plan = [
-        [(outs.relay, range(column)), (ups.send, quarter(1))],
-        [(ups.relay, quarter(0)), (downs.send, range(column // 2)), (ups.send, quarter(2))],
-        [(ups.relay, quarter(1)), (downs.send, range(column // 2, column)), (ups.send, quarter(3))],
-        [(ups.relay, quarter(2)), (outs.total, None)],
-        [(ups.relay, quarter(3)), (downs.relay, range(column // 2)), (outs.share, None)],
-        [(downs.relay, range(column // 2, column))],
-        [(ups.total, None)],
+        [],
+        [(outs.relay, range(column))],
+        [(ups.relay, part(0))],
+        [(ups.relay, part(1)), (outs.total, None)],
+        [(ups.relay, part(2)), (outs.share, None)],
+        [(ups.relay, part(3))],
+        [(downs.relay, part(0)), (ups.total, None)],
     ]
     actions = [[] for _ in range(last)]
     for i, entries in enumerate(plan):
@@ -824,8 +786,9 @@
 
     @pl.when(step == last)
     def _():
+        for k in range(column // 4, column):
+            downs.relay(k)
         ups.share()
-        downs.total()
 
         def finish(i, carry):
             at = pl.ds(pl.multiple_of(i * BLOCK, BLOCK), BLOCK)
@@ -834,8 +797,16 @@
             return carry
 
         lax.fori_loop(0, blocks, finish, 0)
+        downs.total()
         downs.share()
         go.finish()
+        squares = jnp.zeros((1, 1), F32)
+        for box in (outs.box, ups.box):
+            for i in range(2):
+                squares += square_sum(box[i].astype(F32) + box[i + 2].astype(F32))
+        for i in range(narrow):
+            squares += square_sum(downs.box[i].astype(F32))
+        squares_out[...] = jnp.broadcast_to(squares, squares_out.shape)
         shards_out[...] = outs.box[...]
         shards_down[...] = downs.box[...]
         shards_up[...] = ups.box[...]
@@ -852,10 +823,11 @@
     results = [
         jax.ShapeDtypeStruct((rows, 3 * width), BF),
         jax.ShapeDtypeStruct((narrow, depth // wide, part_out.shape[1]), BF),
-        jax.ShapeDtypeStruct((narrow, depth // wide, part_down.shape[1] // 2), BF),
+        jax.ShapeDtypeStruct((narrow, depth // wide, part_down.shape[1]), BF),
         jax.ShapeDtypeStruct((narrow, depth // wide, part_up.shape[1]), BF),
+        jax.ShapeDtypeStruct((8, 128), F32),
     ]
-    copies = 2 * Scatter.copies(wide, False) + Scatter.copies(wide, True)
+    copies = 3 * Scatter.copies(wide)
     return pl.pallas_call(
         functools.partial(backward_kernel, heads, head_dim, wide, narrow),
         grid=(blocks,),
@@ -874,9 +846,9 @@
             pltpu.SemaphoreType.DMA((copies,)),
             pltpu.SemaphoreType.DMA((copies,)),
         ]
-        + Scatter.scratch(wide, narrow, depth, part_out.shape[1], False)
-        + Scatter.scratch(wide, narrow, depth, part_up.shape[1], False)
-        + Scatter.scratch(wide, narrow, depth, part_down.shape[1], True),
+        + Scatter.scratch(wide, narrow, depth, part_out.shape[1])
+        + Scatter.scratch(wide, narrow, depth, part_up.shape[1])
+        + Scatter.scratch(wide, narrow, depth, part_down.shape[1]),
         compiler_params=pltpu.CompilerParams(
             collective_id=4, has_side_effects=True, vmem_limit_bytes=60 * 1024 * 1024
         ),
@@ -959,11 +931,17 @@
     erf_part = 0.5 * (1.0 + lax.erf(up_pre * (0.5**0.5)))
     act = (up_pre * erf_part).astype(BF)
     slope = erf_part + up_pre * (jnp.exp(-0.5 * up_pre * up_pre) * ((2.0 * jnp.pi) ** -0.5))
+    part_down = dot(cot_pair, act, 0, 0).astype(BF)
+    far_side = me // 2
+    quarter_hidden = half_hidden // 2
+    leaving = take(part_down, (1 - far_side) * quarter_hidden, quarter_hidden)
+    act, leaving = lax.optimization_barrier((act, leaving))
+    came = across(leaving)
+    part_down = take(part_down, far_side * quarter_hidden, quarter_hidden)
     down_part = dot(act, down_w, 1, 1)
     down = down_part[:rows] + mate(down_part[rows:])
     layer_out = (resid + (down + vec[8])).astype(BF)
 
-    part_down = dot(cot_pair, act, 0, 0).astype(BF)
     grad_up_act = (dot(cot_pair, down_w, 1, 0) * slope).astype(BF)
     part_up = dot(normed2_pair, grad_up_act, 0, 0).astype(BF)
     grad_normed2_part = dot(grad_up_act, up_w, 1, 1)
@@ -977,8 +955,10 @@
     other_out = take(part_out, (1 - side) * (width // 2), width // 2)
     part_out = (own_out + mate(other_out.astype(BF)).astype(F32)).astype(BF)
 
+    part_down = (part_down.astype(F32) + came.astype(F32)).astype(BF)
+
     grad_mixed_mine = lax.all_to_all(grad_mixed, "narrow", 1, 0, tiled=True)
-    grad_proj, shards_out, shards_down, shards_up = backward_call(
+    grad_proj, shards_out, shards_down, shards_up, squares = backward_call(
         query, keys, values, mixed_mine, grad_mixed_mine, lse, seg_rows[:, 0], tag_col, turns, part_out, part_down, part_up, head_dim, wide, narrow,
     )
     part_qkv = dot(normed1_all, grad_proj, 0, 0).astype(BF)
@@ -1000,8 +980,8 @@
         ],
         axis=0,
     )
-    grad_normed1, quarters, vector_group = tail_call(
-        part_qkv, grad_proj, qkv_w, tokens_all, vector_part, wide, narrow
+    grad_normed1, total_qkv, vector_total, square_total = tail_call(
+        part_qkv, grad_proj, qkv_w, tokens_all, vector_part, squares, wide, narrow
     )
     grad_tokens = (grad_resid + norm_back(grad_normed1, vec[0], unit1, inverse1)).astype(BF)
 
@@ -1012,17 +992,8 @@
     total_up = join(shards_up)
     total_down = jnp.concatenate([shards_down[i] for i in (0, 2, 1, 3)], axis=1).astype(F32)
     total_out = join(shards_out)
-    total_qkv = jnp.concatenate(
-        [quarters[i, :, j * mine : (j + 1) * mine] for j in range(3) for i in range(narrow)], axis=1
-    ).astype(F32)
-
-    squares = sum(jnp.sum(g * g) for g in (total_qkv, total_out, total_up, total_down))
-    slices = jnp.moveaxis(vector_group.reshape(16, wide, shard_rows), 1, 0)
-    slices = jnp.pad(slices, ((0, 0), (0, 0), (0, -shard_rows % 128)))
-    place = (jnp.arange(16)[:, None] == 15) & (jnp.arange(slices.shape[2])[None, :] == 0)
-    slices = jnp.where(place[None], squares, slices)
-    vector_total, vector_squares = norm_call(slices, wide)
-    grad_norm = jnp.sqrt(vector_total[15, 0] + jnp.sum(vector_squares))
+    total_qkv = total_qkv.astype(F32)
+    grad_norm = jnp.sqrt(square_total[0, 0])
     clip = 1.0 / jnp.maximum(grad_norm, 1.0)
     count = step_count[0].astype(F32)
     rate = 0.4 * count / (count + 4.0)

time: 497 us -> 481 us (0.968)
  waiting for transfers between devices: 5.98 us -> 24.1 us
  Pallas kernels: 330 us -> 317 us
  local copies, waits for them, and re-layouts: 37.7 us -> 27.8 us
  matrix products: 59.5 us -> 54.4 us
  other arithmetic: 39.7 us -> 34.7 us
    ppermute x0 -> x1, waiting for transfers between devices: none -> 18.8 us  [across(): return lax.ppermute(value, 'narrow', [(i, i ^ 2) for i in range(narrow)])]
    pallas_call x1 -> x0, Pallas kernels: 11.7 us -> none  [norm_call(): pl.pallas_call(functools.partial(norm_kernel, wide), in_specs=[vmem], out...]
    pallas_call x1, Pallas kernels: 140 us -> 131 us  [backward_call(): pl.pallas_call(functools.partial(backward_kernel, heads, head_dim, wide,...]
    unnamed x115 -> x88, local copies, waits for them, and re-layouts: 23.1 us -> 15.4 us
    pallas_call x1, Pallas kernels: 48.6 us -> 55.7 us  [tail_call(): pl.pallas_call(functools.partial(tail_kernel, wide, narrow), in_specs=[vm...]
    reduce_sum x5 -> x0, other arithmetic: 6.49 us -> none  [the longest x4 5.21 us: on_device(): jnp.sum(g * g)]
    dot_general x10, matrix products: 59.5 us -> 54.4 us  [dot(): lax.dot_general(a, b, (((ca,), (cb,)), ((), ())), preferred_element_type=...]
  transfers between devices with their start and end apart: 6 -> 7, of which waited for: 2 -> 3; matrix products, arithmetic and copies ran while one was open for 8% -> 10% of each run, Pallas kernels for 0% -> 28%
where the time goes in v6:
time: 481 us; the launch traced here: 473 us
  Pallas kernels  317 us (66%)
  matrix products  54.4 us (11%)
  other arithmetic  34.7 us (7%)
  local copies, waits for them, and re-layouts  27.8 us (6%)
  waiting for transfers between devices  24.1 us (5%)
  starting transfers between devices  10.3 us (2%)
    pallas_call x1, Pallas kernels, backward_call(): pl.pallas_call(functools.partial(backward_kernel, heads, head_dim, wide,...  131 us
    pallas_call x1, Pallas kernels, forward_call(): pl.pallas_call(functools.partial(forward_kernel, heads, head_dim, wide, n...  130 us
    pallas_call x1, Pallas kernels, tail_call(): pl.pallas_call(functools.partial(tail_kernel, wide, narrow), in_specs=[vm...  55.7 us
    dot_general x10, matrix products, dot(): lax.dot_general(a, b, (((ca,), (cb,)), ((), ())), preferred_element_type=...  54.4 us
    ppermute x1, waiting for transfers between devices, across(): return lax.ppermute(value, 'narrow', [(i, i ^ 2) for i in range(narrow)])  18.8 us
    unnamed x88, local copies, waits for them, and re-layouts  15.4 us
    sub x5, other arithmetic, adamw(): return (param - rate * (direction + decay * param), moment, square)  12.1 us
  transfers between devices with their start and end apart: 7, of which 3 were waited for; matrix products, arithmetic and copies ran while one was open for 10% of the time, Pallas kernels for 28%

profile of v6, /device:TPU:0, one launch (start us, length us, event | category | flops | bytes accessed | tf_op | source)
XLA Modules:
  0.0 472.7 jit_solution(2585504128383594185)
XLA Ops:
  4.2 130.2 %attention_forward.1 = (bf16[2048,256]{1,0:T(8,128)(2,1)S(1)}, bf16[2048,256]{1,0:T(8,128)(2,1)S(1)}, bf16[2048,256]{1,0:T(8,128)(2,1)S(1)}, f32[2048,256]{1,0:T...) custom-call(bf16[512,1024]{1,0:T(8,128)(2,1)} %tok.1, ...), custom_call_target="tpu_custom_call" | custom-call | flops 17179869184 | bytes 4194304 | tf_op jit(solution)/shard_map/attention_forward/pallas_call | solution.py:574
  134.4 5.1 %fusion.44 = (f32[512]{0:T(512)S(1)}, f32[512,1024]{1,0:T(8,128)S(1)}) fusion(f32[1024]{0:T(1024)S(1)} %bitcast.81, bf16[512,1024]{1,0:T(8,128)(2,1)} %get-tuple-element.46, bf16[1024,1024]{1,0:T(8,128)(2,1)} %get-tuple-element.47, bf16[512,1024]{1,0:T(8,128)(2,1)S(1)} %copy-done.12), kind=kOutput, calls=%fused_computation.130 | convolution fusion | flops 1075838464 | bytes 6297600 | tf_op jit(solution)/shard_map/dot_general | solution.py:18
  139.9 1.4 add_convert_fusion.2
  141.4 1.4 constant_dynamic-update-slice_fusion.1
  142.8 1.4 constant_dynamic-update-slice_fusion
  144.3 7.4 %multiply_convert_fusion = (bf16[1024,2048]{1,0:T(8,128)(2,1)S(1)}, f32[1024,2048]{1,0:T(8,128)S(1)}) fusion(f32[2048]{0:T(1024)S(1)} %bitcast.79, bf16[1024,2048]{1,0:T(8,128)(2,1)S(1)} %copy-done.41, bf16[512,1024]{1,0:T(8,128)(2,1)} %collective-permute-done, bf16[512,1024]{1,0:T(8,128)(2,1)} %add_convert_fusion.2), kind=kOutput, calls=%fused_computation.8 | convolution fusion | flops 4311744512 | bytes 18882560 | tf_op jit(solution)/shard_map/dot_general | solution.py:18
  151.7 4.9 %convolution_convert_fusion.1 = bf16[1024,2048]{1,0:T(8,128)(2,1)S(1)} fusion(bf16[1024,1024]{1,0:T(8,128)(2,1)S(1)} %constant_dynamic-update-slice_fusion, bf16[1024,2048]{1,0:T(8,128)(2,1)S(1)} %get-tuple-element.50), kind=kOutput, calls=%fused_computation.13 | convolution fusion | flops 4297064448 | bytes 10485760 | tf_op jit(solution)/shard_map/dot_general | solution.py:18
  156.6 1.5 constant_dynamic-slice_fusion
  158.2 1.6 copy-done.14
  161.0 8.2 %convert_reduce_fusion = (f32[2048]{0:T(1024)S(1)}, bf16[1024,2048]{1,0:T(8,128)(2,1)S(1)}) fusion(f32[1024,2048]{1,0:T(8,128)S(1)} %get-tuple-element.117, f32[2048]{0:T(1024)S(1)} %bitcast.80, bf16[1024,1024]{1,0:T(8,128)(2,1)S(1)} %constant_dynamic-update-slice_fusion, bf16[1024,2048]{1,0:T(8,128)(2,1)S(1)} %copy-done.40), kind=kOutput, calls=%fused_computation.7 | convolution fusion | flops 4322228224 | bytes 18890752 | tf_op jit(solution)/shard_map/dot_general | solution.py:18
  169.2 4.5 fusion.46
  173.8 1.7 slice.112
  176.8 4.5 fusion.45
  181.4 1.8 slice.110
  186.1 4.5 collective-permute-start.5
  190.7 3.2 multiply_reduce_fusion
  193.9 3.4 convert_reduce_fusion.4
  198.7 2.0 copy-done.8
  204.6 4.4 all-to-all-start
  209.0 9.4 %convolution_convert_fusion.part_up = bf16[1024,2048]{1,0:T(8,128)(2,1)} fusion(bf16[1024,2048]{1,0:T(8,128)(2,1)} %copy-done.39, bf16[512,1024]{1,0:T(8,128)(2,1)} %collective-permute-done, bf16[512,1024]{1,0:T(8,128)(2,1)} %add_convert_fusion.2), kind=kOutput, calls=%fused_computation.12 | convolution fusion | flops 4301258752 | bytes 10485760 | tf_op jit(solution)/shard_map/dot_general | solution.py:18
  218.7 18.8 %collective-permute-done.5 = bf16[1024,1024]{1,0:T(8,128)(2,1)} collective-permute-done((bf16[1024,1024]{1,0:T(8,128)(2,1)}, bf16[1024,1024]{1,0:T(8,128)(2,1)}, u32[]{:S(2)}, u32[]{:S(2)}) %collective-permute-start.5) | collective-permute-done | bytes 2097184 | tf_op jit(solution)/shard_map/ppermute | solution.py:905
  237.5 4.5 add_convert_fusion.part_down
  243.3 5.2 %all-to-all-done = bf16[512,4,256]{2,0,1:T(8,128)(2,1)} async-done(((bf16[512,4,256]{2,0,1:T(8,128)(2,1)}), bf16[512,4,256]{2,0,1:T(8,128)(2,1)}, u32[]{:S(2)}, u32[]{:S(2)}) %all-to-all-start) | async-done | bytes 1048608 | tf_op jit(solution)/shard_map/all_to_all | solution.py:960
  248.5 131.2 %attention_backward.1 = (bf16[2048,768]{1,0:T(8,128)(2,1)}, bf16[4,128,512]{2,1,0:T(8,128)(2,1)}, bf16[4,128,1024]{2,1,0:T(8,128)(2,1)}, bf16[4,128,2048]{2,1,0:T(8,128)(2,1)}, f32[8,128]{1,0:T(8,128)}) custom-call(bf16[2048,256]{1,0:T(8,128)(2,1)} %copy-done.2, bf16[2048,256]{1,0:T(8,128)(2,1)} %copy-done.3, bf16[2048,256]{1,0:T(8,128)(2,1)} %copy-done.4, ...), custom_call_target="tpu_custom_call" | custom-call | flops 30064771072 | bytes 10485760 | tf_op jit(solution)/shard_map/attention_backward/pallas_call | solution.py:831
  379.7 2.4 convert_reduce_fusion.1
  382.2 7.8 %convolution_convert_fusion.2.part = bf16[1024,768]{1,0:T(8,128)(2,1)} fusion(bf16[2048,1024]{1,0:T(8,128)(2,1)} %get-tuple-element.52, bf16[2048,768]{1,0:T(8,128)(2,1)} %get-tuple-element.62.grad_proj), kind=kOutput, calls=%fused_computation.56 | convolution fusion | flops 3222011904 | bytes 8912896 | tf_op jit(solution)/shard_map/dot_general | solution.py:18
  391.3 55.7 %tail.1 = (f32[512,1024]{1,0:T(8,128)}, bf16[128,3072]{1,0:T(8,128)(2,1)}, f32[16,128]{1,0:T(8,128)}, f32[8,128]{1,0:T(8,128)}) custom-call(bf16[1024,768]{1,0:T(8,128)(2,1)} %convolution_convert_fusion.2.part, bf16[2048,768]{1,0:T(8,128)(2,1)} %get-tuple-element.62.grad_proj, bf16[1024,768]{1,0:T(8,128)(2,1)} %get-tuple-element.63.weight, ...), custom_call_target="tpu_custom_call" | custom-call | tf_op jit(solution)/shard_map/tail/pallas_call | solution.py:234
  454.2 1.7 fusion.14
  457.1 3.0 multiply_subtract_fusion.2
  461.7 3.9 multiply_subtract_fusion.1
  465.6 1.4 multiply_subtract_fusion.3
  467.9 3.2 multiply_subtract_fusion
  (140 shorter events, 26.9 us)
Async XLA Ops:
  0.7 142.2 %collective-permute-start.1 = (bf16[512,1024]{1,0:T(8,128)(2,1)}, bf16[512,1024]{1,0:T(8,128)(2,1)}, u32[]{:S(2)}, u32[]{:S(2)}) collective-permute-start(bf16[512,1024]{1,0:T(8,128)(2,1)} %param.22), channel_id=1, source_target_pairs={{0,1},{1,0},{2,3},{3,2},{4,5},{5,4},{6,7},{7,6},{8,9},{9,8},{10,11... | collective-permute-start | bytes 3145736 | tf_op jit(solution)/shard_map/ppermute | solution.py:902
  4.2 130.3 %copy-start.12 = (bf16[512,1024]{1,0:T(8,128)(2,1)S(1)}, bf16[512,1024]{1,0:T(8,128)(2,1)}, u32[]{:S(2)}) copy-start(bf16[512,1024]{1,0:T(8,128)(2,1)} %tok.1) | copy-start | bytes 3145732
  134.3 5.2 %copy-start.2 = (bf16[2048,256]{1,0:T(8,128)(2,1)}, bf16[2048,256]{1,0:T(8,128)(2,1)S(1)}, u32[]{:S(2)}) copy-start(bf16[2048,256]{1,0:T(8,128)(2,1)S(1)} %get-tuple-element.53.q_ref) | copy-start | bytes 3145732
  134.3 5.2 %copy-start.3 = (bf16[2048,256]{1,0:T(8,128)(2,1)}, bf16[2048,256]{1,0:T(8,128)(2,1)S(1)}, u32[]{:S(2)}) copy-start(bf16[2048,256]{1,0:T(8,128)(2,1)S(1)} %get-tuple-element.54.k_ref) | copy-start | bytes 3145732
  134.4 5.2 %copy-start.4 = (bf16[2048,256]{1,0:T(8,128)(2,1)}, bf16[2048,256]{1,0:T(8,128)(2,1)S(1)}, u32[]{:S(2)}) copy-start(bf16[2048,256]{1,0:T(8,128)(2,1)S(1)} %get-tuple-element.55.v_ref) | copy-start | bytes 3145732
  134.4 5.2 %copy-start.5 = (f32[2048,1]{1,0:T(8,128)}, f32[2048,1]{1,0:T(8,128)S(1)}, u32[]{:S(2)}) copy-start(f32[2048,1]{1,0:T(8,128)S(1)} %get-tuple-element.59.tag_ref) | copy-start | bytes 24580
  134.4 5.2 %copy-start.6 = (bf16[2048,256]{1,0:T(8,128)(2,1)}, bf16[2048,256]{1,0:T(8,128)(2,1)S(1)}, u32[]{:S(2)}) copy-start(bf16[2048,256]{1,0:T(8,128)(2,1)S(1)} %get-tuple-element.56.o_ref) | copy-start | bytes 3145732
  134.4 5.1 %copy-start.7 = (f32[8,8,256]{2,1,0:T(8,128)}, f32[8,8,256]{2,1,0:T(8,128)S(1)}, u32[]{:S(2)}) copy-start(f32[8,8,256]{2,1,0:T(8,128)S(1)} %get-tuple-element.57.lse_ref) | copy-start | bytes 196612
  141.3 3.0 collective-permute-start
  141.3 3.0 copy-start.41
  156.6 3.1 copy-start.14
  156.6 4.4 copy-start.40
  169.2 4.5 copy-start.39
  176.4 14.3 %collective-permute-start.3 = (f32[512,1024]{1,0:T(8,128)}, f32[512,1024]{1,0:T(8,128)}, u32[]{:S(2)}, u32[]{:S(2)}) collective-permute-start(f32[512,1024]{1,0:T(8,128)} %slice.112), channel_id=1, source_target_pairs={{0,1},{1,0},{2,3},{3,2},{4,5},{5,4},{6,7},{7,6},{8,9},{9,8},{10,11... | collective-permute-start | bytes 6291464 | tf_op jit(solution)/shard_map/ppermute | solution.py:902
  184.0 9.9 %collective-permute-start.2 = (f32[512,1024]{1,0:T(8,128)}, f32[512,1024]{1,0:T(8,128)}, u32[]{:S(2)}, u32[]{:S(2)}) collective-permute-start(f32[512,1024]{1,0:T(8,128)} %slice.110), channel_id=1, source_target_pairs={{0,1},{1,0},{2,3},{3,2},{4,5},{5,4},{6,7},{7,6},{8,9},{9,8},{10,11... | collective-permute-start | bytes 6291464 | tf_op jit(solution)/shard_map/ppermute | solution.py:902
  186.1 7.8 %copy-start.16 = (f32[1024,1024]{1,0:T(8,128)S(1)}, f32[1024,1024]{1,0:T(8,128)}, u32[]{:S(2)}) copy-start(f32[1024,1024]{1,0:T(8,128)} %copy-done.15) | copy-start | bytes 12582916
  186.1 7.8 %copy-start.18 = (bf16[512,1024]{1,0:T(8,128)(2,1)S(1)}, bf16[512,1024]{1,0:T(8,128)(2,1)}, u32[]{:S(2)}) copy-start(bf16[512,1024]{1,0:T(8,128)(2,1)} %param.22) | copy-start | bytes 3145732
  186.1 51.3 %collective-permute-start.5 = (bf16[1024,1024]{1,0:T(8,128)(2,1)}, bf16[1024,1024]{1,0:T(8,128)(2,1)}, u32[]{:S(2)}, u32[]{:S(2)}) collective-permute-start(bf16[1024,1024]{1,0:T(8,128)(2,1)} %constant_dynamic-slice_fusion), channel_id=1, source_target_pairs={{0,2},{1,3},{2,0},{3,1},{4,6},{5,7},{6,4},{7,5},{8,10},{9,11},{10,... | collective-permute-start | bytes 6291464 | tf_op jit(solution)/shard_map/ppermute | solution.py:905
  193.9 3.4 copy-start.19
  197.3 3.7 copy-start.10
  200.8 41.1 %collective-permute-start.4 = (bf16[1024,512]{1,0:T(8,128)(2,1)S(1)}, bf16[1024,512]{1,0:T(8,128)(2,1)S(1)}, u32[]{:S(2)}, u32[]{:S(2)}) collective-permute-start(bf16[1024,512]{1,0:T(8,128)(2,1)S(1)} %dynamic-slice_convert_fusion), channel_id=1, source_target_pairs={{0,1},{1,0},{2,3},{3,2},{4,5},{5,4},{6,7},{7,6},{8,9},{9,8},{10,11... | collective-permute-start | bytes 3145736 | tf_op jit(solution)/shard_map/ppermute | solution.py:902
  204.6 43.9 %all-to-all-start = ((bf16[512,4,256]{2,0,1:T(8,128)(2,1)}), bf16[512,4,256]{2,0,1:T(8,128)(2,1)}, u32[]{:S(2)}, u32[]{:S(2)}) async-start(bf16[512,4,256]{2,0,1:T(8,128)(2,1)} %bitcast.63), calls=%async_computation | async-start | bytes 2097152 | tf_op jit(solution)/shard_map/all_to_all | solution.py:960
  218.7 23.3 %copy-start.9 = (f32[1024,1024]{1,0:T(8,128)S(1)}, f32[1024,1024]{1,0:T(8,128)}, u32[]{:S(2)}) copy-start(f32[1024,1024]{1,0:T(8,128)} %copy-done.8) | copy-start | bytes 12582916
  447.1 3.3 copy-start.23
  457.1 3.0 copy-start.20
  457.1 3.9 copy-start.21
  457.1 4.6 copy-start.22
  461.7 3.9 copy-start.1
  461.7 3.9 copy-start.31
  461.7 3.9 copy-start.32
  461.7 5.3 %copy-start.25 = (f32[128,4096]{1,0:T(8,128)S(1)}, f32[128,4096]{1,0:T(8,128)}, u32[]{:S(2)}) copy-start(f32[128,4096]{1,0:T(8,128)} %param.40) | copy-start | bytes 6291460
  461.7 5.3 %copy-start.26 = (f32[128,4096]{1,0:T(8,128)S(1)}, f32[128,4096]{1,0:T(8,128)}, u32[]{:S(2)}) copy-start(f32[128,4096]{1,0:T(8,128)} %param.35) | copy-start | bytes 6291460
  (17 other events, 34.3 us)

commit v7 on v6

--- a/solution.py
+++ b/solution.py
@@ -337,48 +337,54 @@
     qkv_near += [go.make(qkv_at(source(d)), qkv_at(source(d)), wide=near) for d in range(1, column)]
 
     at_step = [[] for _ in range(final + 2)]
+    soon = []
     out_cols = pl.ds(pl.multiple_of(side * out_half, out_half), out_half)
     out_at = lambda i: out_all.at[rows_at(i, wide_rows), out_cols]
     out_near = [go.make(out_own, out_at(w), wide=near)]
     out_starts = [go.make(out_own, out_at(w), narrow=mate)]
-    at_step[1].append((None, [out_near[0]]))
+    at_step[blocks + 6].append((None, [out_near[0]]))
+    out_late = []
     for d in range(1, column):
         out_starts.append(go.make(out_own, out_at(w), wide=target(d)))
         ref = out_at(source(d))
         out_near.append(go.make(ref, ref, wide=near))
-        at_step[5].append((out_starts[-1], [out_near[-1], go.make(ref, ref, narrow=mate)]))
+        out_late.append((out_starts[-1], [out_near[-1], go.make(ref, ref, narrow=mate)]))
     for d in range(column):
         ref = out_at(beside(d))
-        at_step[blocks + 2].append((out_near[d], [go.make(ref, ref, narrow=mate)]))
+        out_late.append((out_near[d], [go.make(ref, ref, narrow=mate)]))
 
     quarter = half // 4
     shared = pl.ds(pl.multiple_of(n // 2 * quarter, quarter), quarter)
     both = pl.ds(2 * quarter, 2 * quarter)
     own_out = [pltpu.make_async_copy(out_own, out_at(w), leave.at[0])]
 
-    def spread(own, result, steps, slot):
-        starts = []
-        for cols in (shared, both):
-            piece_at = lambda i: result.at[rows_at(i, wide_rows), cols]
-            passes = lambda i: [go.make(piece_at(i), piece_at(i), narrow=cross)] if cols is shared else []
-            nears = [go.make(own.at[:, cols], piece_at(w), wide=near)]
-            at_step[1].append((None, [nears[0]]))
-            if cols is shared:
-                starts.append(go.make(own.at[:, cols], piece_at(w), narrow=cross))
-            for d in range(1, column):
-                starts.append(go.make(own.at[:, cols], piece_at(w), wide=target(d)))
-                ref = piece_at(source(d))
-                nears.append(go.make(ref, ref, wide=near))
-                turn_at = steps[0] if cols is shared else steps[2] + (d - 1) * 2 // column
-                at_step[min(turn_at, final + 1)].append((starts[-1], [nears[-1]] + passes(source(d))))
-            if cols is shared:
-                for d in range(column):
-                    at_step[steps[1]].append((nears[d], passes(beside(d))))
-            own_out.append(pltpu.make_async_copy(own.at[:, cols], piece_at(w), leave.at[slot + (cols is both)]))
+    def spread(own, result, cols, steps, slot):
+        piece_at = lambda i: result.at[rows_at(i, wide_rows), cols]
+        over_x = cols is shared
+        passes = lambda i: [go.make(piece_at(i), piece_at(i), narrow=cross)] if over_x else []
+        nears = [go.make(own.at[:, cols], piece_at(w), wide=near)]
+        (soon if over_x else at_step[steps[0]]).append((None, nears[:1]))
+        starts = [go.make(own.at[:, cols], piece_at(w), narrow=cross)] if over_x else []
+        for d in range(1, column):
+            starts.append(go.make(own.at[:, cols], piece_at(w), wide=target(d)))
+            ref = piece_at(source(d))
+            nears.append(go.make(ref, ref, wide=near))
+            at_step[steps[1][(d - 1) * 3 // (column - 1)]].append((starts[-1], [nears[-1]] + passes(source(d))))
+        if over_x:
+            for d in range(column):
+                at_step[steps[2]].append((nears[d], passes(beside(d))))
+        own_out.append(pltpu.make_async_copy(own.at[:, cols], piece_at(w), leave.at[slot]))
         return starts
 
-    up_starts = spread(up_own, up_all, (blocks + 1, blocks + 3, blocks + 4), 1)
-    down_starts = spread(down_own, down_all, (final - 1, final + 1, final + 1), 3)
+    b = blocks
+    weight_starts = (
+        spread(up_own, up_all, shared, (0, (4, 4, 4), b + 2), 1)
+        + spread(down_own, down_all, shared, (0, (b + 2, b + 2, b + 2), b + 4), 2)
+        + spread(up_own, up_all, both, (1, (b + 3, b + 5, b + 6)), 3)
+        + spread(down_own, down_all, both, (b + 2, (b + 7, b + 8, b + 9)), 4)
+        + out_starts
+    )
+    at_step[final + 1] += out_late
 
     mine = pl.ds(pl.multiple_of(n * width, width), width)
 
@@ -413,15 +419,12 @@
             copy.wait()
         qkv_own[...] = stage_qkv[...].astype(BF)
         go.launch(*qkv_far, qkv_near[0], *to_mate)
-        for copy, stage, own, starts in zip(
-            loads[3:],
-            (stage_out, stage_up, stage_down),
-            (out_own, up_own, down_own),
-            (out_starts, up_starts, down_starts),
+        for copy, stage, own in zip(
+            loads[3:], (stage_out, stage_up, stage_down), (out_own, up_own, down_own)
         ):
             copy.wait()
             own[...] = stage[...].astype(BF)
-            go.launch(*starts)
+        go.launch(*weight_starts)
         tok_box[rows_at(n, group_rows), :] = tok[...]
         qkv_box[rows_at(w, wide_rows), :] = qkv_own[...]
         vec_box[pl.ds(w, 1)] = vec[...][None]
@@ -437,6 +440,9 @@
             if i < column - 1:
                 go.arrived(qkv_far[i])
                 go.launch(qkv_near[i + 1])
+            if i == 0:
+                for _, follow in soon:
+                    go.launch(*follow)
             if i < pieces:
                 go.arrived(over[i])
                 go.launch(passed[i])
@@ -609,42 +615,65 @@
 
 
 class Scatter:
-    def __init__(self, go, wide, narrow, part, near_in, own, far_out, far_in, box, local):
+    def __init__(self, go, wide, narrow, split, part, near_in, own, far_out, far_in, box, local, *extra):
         w, self.n = lax.axis_index("wide"), lax.axis_index("narrow")
-        self.go, self.column = go, wide // 2
+        self.go, self.column, self.split = go, wide // 2, split
         self.near_in, self.own, self.far_out, self.far_in, self.box = near_in, own, far_out, far_in, box
-        z, y = w // 2, lax.rem(w, 2)
+        z, y, x = w // 2, lax.rem(w, 2), self.n // 2
         near, mate, cross = w + 1 - 2 * y, self.n + 1 - 2 * lax.rem(self.n, 2), lax.rem(self.n + 2, narrow)
-        size = part.shape[0] // wide
+        size, cols = part.shape[0] // wide, box.shape[2]
         towards = [lax.rem(z + d, self.column) for d in range(1, self.column + 1)]
+        theirs, ours = [to * 2 + 1 - y for to in towards], [to * 2 + y for to in towards]
+        here = pl.ds(pl.multiple_of(x * cols, cols), cols) if split else pl.ds(0, cols)
+        self.loads = [
+            pltpu.make_async_copy(part.at[rows_at(i, size), here], own.at[k], local.at[k])
+            for k, i in enumerate(ours + theirs if split else ours)
+        ]
+        self.zero = []
+        if split:
+            self.cross_in, self.out = extra
+            there = pl.ds(pl.multiple_of((1 - x) * cols, cols), cols)
+            order = list(enumerate(ours + theirs))
+            order = order[self.column :] + order[: self.column]
+            self.zero = {
+                k: go.make(part.at[rows_at(i, size), there], self.cross_in.at[k], narrow=cross) for k, i in order
+            }
         self.first = [
-            go.make(part.at[rows_at(to * 2 + 1 - y, size)], near_in.at[k], wide=near) for k, to in enumerate(towards)
+            go.make(self.out.at[k] if split else part.at[rows_at(i, size)], near_in.at[k], wide=near)
+            for k, i in enumerate(theirs)
         ]
-        self.loads = [
-            pltpu.make_async_copy(part.at[rows_at(to * 2 + y, size)], own.at[k], local.at[k])
-            for k, to in enumerate(towards)
-        ]
-        self.second = [
-            go.make(far_out.at[k], far_in.at[k], wide=to * 2 + y) for k, to in enumerate(towards[:-1])
-        ]
+        self.second = [go.make(far_out.at[k], far_in.at[k], wide=i) for k, i in enumerate(ours[:-1])]
         self.over = go.make(box.at[self.n], box.at[self.n], narrow=cross)
         self.beside = go.make(box.at[self.n], box.at[self.n], narrow=mate)
         self.passed = go.make(box.at[cross], box.at[cross], narrow=mate)
 
-    def begin(self):
-        self.go.launch(*self.first)
+    def load(self):
         for copy in self.loads:
             copy.start()
+        if self.split:
+            self.go.launch(*self.zero.values())
+
+    def summed(self, k):
+        self.loads[k].wait()
+        value = self.own[k].astype(F32)
+        if self.split:
+            self.go.arrived(self.zero[k])
+            value = value + self.cross_in[k].astype(F32)
+        return value
+
+    def send(self, k):
+        if self.split:
+            self.out[k] = self.summed(self.column + k).astype(BF)
+        self.go.launch(self.first[k])
 
     def relay(self, k):
         self.go.arrived(self.first[k])
-        self.loads[k].wait()
         if k < self.column - 1:
-            self.far_out[k] = (self.own[k].astype(F32) + self.near_in[k].astype(F32)).astype(BF)
+            self.far_out[k] = (self.summed(k) + self.near_in[k].astype(F32)).astype(BF)
             self.go.launch(self.second[k])
 
     def total(self):
-        value = self.own[self.column - 1].astype(F32) + self.near_in[self.column - 1].astype(F32)
+        value = self.summed(self.column - 1) + self.near_in[self.column - 1].astype(F32)
         for k in range(self.column - 1):
             self.go.arrived(self.second[k])
             value = value + self.far_in[k].astype(F32)
@@ -656,14 +685,17 @@
         self.go.launch(self.passed)
 
     @staticmethod
-    def copies(wide):
-        return 2 * (wide // 2) - 1 + 3
+    def copies(wide, split):
+        return 2 * (wide // 2) - 1 + 3 + (wide if split else 0)
 
     @staticmethod
-    def scratch(wide, narrow, rows, cols):
+    def scratch(wide, narrow, rows, cols, split):
         column, size = wide // 2, rows // wide
-        sizes = [column, column, column - 1, column - 1, narrow]
-        return [pltpu.VMEM((count, size, cols), BF) for count in sizes] + [pltpu.SemaphoreType.DMA((column,))]
+        cols = cols // 2 if split else cols
+        many = wide if split else column
+        sizes = [column, many, column - 1, column - 1, narrow]
+        first = [pltpu.VMEM((count, size, cols), BF) for count in sizes] + [pltpu.SemaphoreType.DMA((many,))]
+        return first + ([pltpu.VMEM((count, size, cols), BF) for count in (wide, column)] if split else [])
 
 
 def square_sum(value):
@@ -684,9 +716,9 @@
     half = head_dim // 2
     go = Copies(send, recv)
     column = wide // 2
-    outs = Scatter(go, wide, narrow, part_out, *boxes[:6])
-    ups = Scatter(go, wide, narrow, part_up, *boxes[6:12])
-    downs = Scatter(go, wide, narrow, part_down, *boxes[12:])
+    outs = Scatter(go, wide, narrow, False, part_out, *boxes[:6])
+    ups = Scatter(go, wide, narrow, False, part_up, *boxes[6:12])
+    downs = Scatter(go, wide, narrow, True, part_down, *boxes[12:])
 
     @pl.when(step == 0)
     def _():
@@ -697,31 +729,38 @@
             + [{"wide": lax.rem(z + d, column) * 2 + y} for d in range(1, column)]
             + [{"narrow": n + 1 - 2 * lax.rem(n, 2)}, {"narrow": lax.rem(n + 2, narrow)}]
         )
-        outs.begin()
-        ups.begin()
-        downs.begin()
+        for k in range(column):
+            ups.send(k)
+        for scatter in (downs, ups, outs):
+            scatter.load()
 
     part = lambda i: range(column * i // 4, column * (i + 1) // 4)
-    plan = [
-        [],
-        [(outs.relay, range(column))],
-        [(ups.relay, part(0))],
-        [(ups.relay, part(1)), (outs.total, None)],
-        [(ups.relay, part(2)), (outs.share, None)],
-        [(ups.relay, part(3))],
-        [(downs.relay, part(0)), (ups.total, None)],
-    ]
-    actions = [[] for _ in range(last)]
-    for i, entries in enumerate(plan):
-        for action, ks in entries:
-            actions[min(i, last - 1)] += [action] if ks is None else [functools.partial(action, k) for k in ks]
-    for i in range(last):
-        if actions[i]:
-
-            @pl.when(step == i + 1)
+    plan = {
+        2: [(ups.relay, part(0))],
+        4: [(ups.relay, part(1))],
+        5: [(downs.send, range(column // 2))],
+        6: [(ups.relay, part(2))],
+        7: [(downs.send, range(column // 2, column))],
+        8: [(ups.relay, part(3)), (outs.send, range(column))],
+        10: [(downs.relay, part(0))],
+        11: [(downs.relay, part(1)), (ups.total, None)],
+        12: [(downs.relay, part(2))],
+        13: [(downs.relay, part(3)), (ups.share, None)],
+        14: [(outs.relay, range(column // 2))],
+        15: [(outs.relay, range(column // 2, column)), (downs.total, None)],
+    }
+
+    def act(i):
+        for action, ks in plan[i]:
+            for k in [None] if ks is None else ks:
+                action() if k is None else action(k)
+
+    for i in range(0, 2 * blocks, 2):
+        if i in plan:
+
+            @pl.when(step == i // 2)
             def _():
-                for action in actions[i]:
-                    action()
+                act(i)
 
     @pl.when(step == 0)
     def _():
@@ -756,6 +795,13 @@
     masked_key = [jnp.where(head_lanes(key.shape, h, head_dim), key, jnp.zeros_like(key)) for h in range(heads)]
 
     def body(i, carry):
+        for half_step in range(1, 2 * blocks, 2):
+            if half_step in plan:
+
+                @pl.when((step == half_step // 2) & (i == blocks // 2))
+                def _():
+                    act(half_step)
+
         grad_key, grad_value = carry
         at = pl.ds(pl.multiple_of(i * BLOCK, BLOCK), BLOCK)
         allowed = tag == seg_ref[pl.ds(i, 1), :]
@@ -786,9 +832,8 @@
 
     @pl.when(step == last)
     def _():
-        for k in range(column // 4, column):
-            downs.relay(k)
-        ups.share()
+        downs.share()
+        outs.total()
 
         def finish(i, carry):
             at = pl.ds(pl.multiple_of(i * BLOCK, BLOCK), BLOCK)
@@ -797,8 +842,7 @@
             return carry
 
         lax.fori_loop(0, blocks, finish, 0)
-        downs.total()
-        downs.share()
+        outs.share()
         go.finish()
         squares = jnp.zeros((1, 1), F32)
         for box in (outs.box, ups.box):
@@ -823,11 +867,11 @@
     results = [
         jax.ShapeDtypeStruct((rows, 3 * width), BF),
         jax.ShapeDtypeStruct((narrow, depth // wide, part_out.shape[1]), BF),
-        jax.ShapeDtypeStruct((narrow, depth // wide, part_down.shape[1]), BF),
+        jax.ShapeDtypeStruct((narrow, depth // wide, part_down.shape[1] // 2), BF),
         jax.ShapeDtypeStruct((narrow, depth // wide, part_up.shape[1]), BF),
         jax.ShapeDtypeStruct((8, 128), F32),
     ]
-    copies = 3 * Scatter.copies(wide)
+    copies = 2 * Scatter.copies(wide, False) + Scatter.copies(wide, True)
     return pl.pallas_call(
         functools.partial(backward_kernel, heads, head_dim, wide, narrow),
         grid=(blocks,),
@@ -846,9 +890,9 @@
             pltpu.SemaphoreType.DMA((copies,)),
             pltpu.SemaphoreType.DMA((copies,)),
         ]
-        + Scatter.scratch(wide, narrow, depth, part_out.shape[1])
-        + Scatter.scratch(wide, narrow, depth, part_up.shape[1])
-        + Scatter.scratch(wide, narrow, depth, part_down.shape[1]),
+        + Scatter.scratch(wide, narrow, depth, part_out.shape[1], False)
+        + Scatter.scratch(wide, narrow, depth, part_up.shape[1], False)
+        + Scatter.scratch(wide, narrow, depth, part_down.shape[1], True),
         compiler_params=pltpu.CompilerParams(
             collective_id=4, has_side_effects=True, vmem_limit_bytes=60 * 1024 * 1024
         ),
@@ -932,12 +976,6 @@
     act = (up_pre * erf_part).astype(BF)
     slope = erf_part + up_pre * (jnp.exp(-0.5 * up_pre * up_pre) * ((2.0 * jnp.pi) ** -0.5))
     part_down = dot(cot_pair, act, 0, 0).astype(BF)
-    far_side = me // 2
-    quarter_hidden = half_hidden // 2
-    leaving = take(part_down, (1 - far_side) * quarter_hidden, quarter_hidden)
-    act, leaving = lax.optimization_barrier((act, leaving))
-    came = across(leaving)
-    part_down = take(part_down, far_side * quarter_hidden, quarter_hidden)
     down_part = dot(act, down_w, 1, 1)
     down = down_part[:rows] + mate(down_part[rows:])
     layer_out = (resid + (down + vec[8])).astype(BF)
@@ -954,8 +992,6 @@
     own_out = take(part_out, side * (width // 2), width // 2)
     other_out = take(part_out, (1 - side) * (width // 2), width // 2)
     part_out = (own_out + mate(other_out.astype(BF)).astype(F32)).astype(BF)
-
-    part_down = (part_down.astype(F32) + came.astype(F32)).astype(BF)
 
     grad_mixed_mine = lax.all_to_all(grad_mixed, "narrow", 1, 0, tiled=True)
     grad_proj, shards_out, shards_down, shards_up, squares = backward_call(

time: 481 us -> 437 us (0.909)
  waiting for transfers between devices: 24.1 us -> 3.64 us
  Pallas kernels: 317 us -> 302 us
  matrix products: 54.4 us -> 59.5 us
  other arithmetic: 34.7 us -> 29.7 us
    pallas_call x1, Pallas kernels: 131 us -> 112 us  [backward_call(): pl.pallas_call(functools.partial(backward_kernel, heads, head_dim, wide,...]
    ppermute x1 -> x0, waiting for transfers between devices: 18.8 us -> none  [across(): return lax.ppermute(value, 'narrow', [(i, i ^ 2) for i in range(narrow)])]
    dot_general x10, matrix products: 54.4 us -> 59.5 us  [dot(): lax.dot_general(a, b, (((ca,), (cb,)), ((), ())), preferred_element_type=...]
    unnamed x88 -> x92, local copies, waits for them, and re-layouts: 15.4 us -> 13.2 us
  transfers between devices with their start and end apart: 7 -> 6, of which waited for: 3 -> 1; matrix products, arithmetic and copies ran while one was open for 10% -> 11% of each run, Pallas kernels for 28% -> 30%
where the time goes in v7:
time: 437 us; the launch traced here: 430 us
  Pallas kernels  302 us (69%)
  matrix products  59.5 us (14%)
  other arithmetic  29.7 us (7%)
  local copies, waits for them, and re-layouts  24.4 us (6%)
  starting transfers between devices  6.04 us (1%)
    pallas_call x1, Pallas kernels, forward_call(): pl.pallas_call(functools.partial(forward_kernel, heads, head_dim, wide, n...  131 us
    pallas_call x1, Pallas kernels, backward_call(): pl.pallas_call(functools.partial(backward_kernel, heads, head_dim, wide,...  112 us
    pallas_call x1, Pallas kernels, tail_call(): pl.pallas_call(functools.partial(tail_kernel, wide, narrow), in_specs=[vm...  60 us
    dot_general x10, matrix products, dot(): lax.dot_general(a, b, (((ca,), (cb,)), ((), ())), preferred_element_type=...  59.5 us
    unnamed x92, local copies, waits for them, and re-layouts  13.2 us
    sub x5, other arithmetic, adamw(): return (param - rate * (direction + decay * param), moment, square)  12.1 us
  transfers between devices with their start and end apart: 6, of which 1 were waited for; matrix products, arithmetic and copies ran while one was open for 11% of the time, Pallas kernels for 30%

profile of v7, /device:TPU:0, one launch (start us, length us, event | category | flops | bytes accessed | tf_op | source)
XLA Modules:
  0.0 429.7 jit_solution(15333116852742266519)
XLA Ops:
  4.2 130.7 %attention_forward.1 = (bf16[2048,256]{1,0:T(8,128)(2,1)S(1)}, bf16[2048,256]{1,0:T(8,128)(2,1)S(1)}, bf16[2048,256]{1,0:T(8,128)(2,1)S(1)}, f32[2048,256]{1,0:T...) custom-call(bf16[512,1024]{1,0:T(8,128)(2,1)} %tok.1, ...), custom_call_target="tpu_custom_call" | custom-call | flops 17179869184 | bytes 4194304 | tf_op jit(solution)/shard_map/attention_forward/pallas_call | solution.py:580
  135.0 5.1 %fusion.44 = (f32[512]{0:T(512)S(1)}, f32[512,1024]{1,0:T(8,128)S(1)}) fusion(f32[1024]{0:T(1024)S(1)} %bitcast.81, bf16[512,1024]{1,0:T(8,128)(2,1)} %get-tuple-element.44, bf16[1024,1024]{1,0:T(8,128)(2,1)} %get-tuple-element.45, bf16[512,1024]{1,0:T(8,128)(2,1)S(1)} %copy-done.12), kind=kOutput, calls=%fused_computation.128 | convolution fusion | flops 1075838464 | bytes 6297600 | tf_op jit(solution)/shard_map/dot_general | solution.py:18
  140.4 1.4 add_convert_fusion.1
  142.3 1.4 constant_dynamic-update-slice_fusion.1
  144.0 1.3 constant_dynamic-update-slice_fusion
  145.4 7.9 %multiply_convert_fusion = (bf16[1024,2048]{1,0:T(8,128)(2,1)S(1)}, f32[1024,2048]{1,0:T(8,128)S(1)}) fusion(f32[2048]{0:T(1024)S(1)} %bitcast.79, bf16[1024,2048]{1,0:T(8,128)(2,1)S(1)} %copy-done.43, bf16[512,1024]{1,0:T(8,128)(2,1)} %collective-permute-done, bf16[512,1024]{1,0:T(8,128)(2,1)} %add_convert_fusion.1), kind=kOutput, calls=%fused_computation.8 | convolution fusion | flops 4311744512 | bytes 18882560 | tf_op jit(solution)/shard_map/dot_general | solution.py:18
  153.4 8.0 %convert_reduce_fusion = (f32[2048]{0:T(1024)S(1)}, bf16[1024,2048]{1,0:T(8,128)(2,1)S(1)}) fusion(f32[1024,2048]{1,0:T(8,128)S(1)} %get-tuple-element.113, f32[2048]{0:T(1024)S(1)} %bitcast.80, bf16[1024,1024]{1,0:T(8,128)(2,1)S(1)} %constant_dynamic-update-slice_fusion, bf16[1024,2048]{1,0:T(8,128)(2,1)S(1)} %copy-done.42), kind=kOutput, calls=%fused_computation.7 | convolution fusion | flops 4322228224 | bytes 18890752 | tf_op jit(solution)/shard_map/dot_general | solution.py:18
  161.4 4.5 %fusion.46 = f32[1024,1024]{1,0:T(8,128)S(1)} fusion(bf16[1024,2048]{1,0:T(8,128)(2,1)S(1)} %get-tuple-element.115, bf16[1024,2048]{1,0:T(8,128)(2,1)S(1)} %copy-done.43), kind=kOutput, calls=%fused_computation.130 | convolution fusion | flops 4294967296 | bytes 12582912 | tf_op jit(solution)/shard_map/dot_general | solution.py:18
  166.0 1.7 slice.112
  168.6 4.5 %fusion.45 = f32[1024,1024]{1,0:T(8,128)S(1)} fusion(bf16[1024,2048]{1,0:T(8,128)(2,1)S(1)} %get-tuple-element.112, bf16[1024,2048]{1,0:T(8,128)(2,1)S(1)} %copy-done.42), kind=kOutput, calls=%fused_computation.129 | convolution fusion | flops 4294967296 | bytes 12582912 | tf_op jit(solution)/shard_map/dot_general | solution.py:18
  173.2 1.7 slice.110
  179.0 9.5 %convolution_convert_fusion.1.part_down = bf16[1024,2048]{1,0:T(8,128)(2,1)} fusion(bf16[1024,1024]{1,0:T(8,128)(2,1)} %copy-done.34, bf16[1024,2048]{1,0:T(8,128)(2,1)} %copy-done.40), kind=kOutput, calls=%fused_computation.12 | convolution fusion | flops 4297064448 | bytes 10485760 | tf_op jit(solution)/shard_map/dot_general | solution.py:18
  188.5 2.7 multiply_reduce_fusion
  191.6 3.4 convert_reduce_fusion.4
  195.0 1.3 fusion.35
  196.3 2.0 copy-done.8
  198.6 1.3 copy-done.39
  199.9 1.3 convolution_convert_fusion.3
  202.2 4.4 %all-to-all-start = ((bf16[512,4,256]{2,0,1:T(8,128)(2,1)}), bf16[512,4,256]{2,0,1:T(8,128)(2,1)}, u32[]{:S(2)}, u32[]{:S(2)}) async-start(bf16[512,4,256]{2,0,1:T(8,128)(2,1)} %bitcast.63), calls=%async_computation | async-start | bytes 2097152 | tf_op jit(solution)/shard_map/all_to_all | solution.py:996
  206.7 9.5 %convolution_convert_fusion.part_up = bf16[1024,2048]{1,0:T(8,128)(2,1)} fusion(bf16[1024,2048]{1,0:T(8,128)(2,1)} %copy-done.41, bf16[512,1024]{1,0:T(8,128)(2,1)} %collective-permute-done, bf16[512,1024]{1,0:T(8,128)(2,1)} %add_convert_fusion.1), kind=kOutput, calls=%fused_computation.11 | convolution fusion | flops 4301258752 | bytes 10485760 | tf_op jit(solution)/shard_map/dot_general | solution.py:18
  216.2 1.3 add_convert_fusion.part_out
  217.5 3.6 all-to-all-done
  221.2 111.5 %attention_backward.1 = (bf16[2048,768]{1,0:T(8,128)(2,1)}, bf16[4,128,512]{2,1,0:T(8,128)(2,1)}, bf16[4,128,1024]{2,1,0:T(8,128)(2,1)}, bf16[4,128,2048]{2,1,0:T(8,128)(2,1)}, f32[8,128]{1,0:T(8,128)}) custom-call(bf16[2048,256]{1,0:T(8,128)(2,1)} %copy-done.2, bf16[2048,256]{1,0:T(8,128)(2,1)} %copy-done.3, bf16[2048,256]{1,0:T(8,128)(2,1)} %copy-done.4, ...), custom_call_target="tpu_custom_call" | custom-call | flops 30064771072 | bytes 10485760 | tf_op jit(solution)/shard_map/attention_backward/pallas_call | solution.py:875
  332.7 2.4 convert_reduce_fusion.1
  335.1 7.8 %convolution_convert_fusion.2.part = bf16[1024,768]{1,0:T(8,128)(2,1)} fusion(bf16[2048,1024]{1,0:T(8,128)(2,1)} %get-tuple-element.49, bf16[2048,768]{1,0:T(8,128)(2,1)} %get-tuple-element.58.grad_proj), kind=kOutput, calls=%fused_computation.55 | convolution fusion | flops 3222011904 | bytes 8912896 | tf_op jit(solution)/shard_map/dot_general | solution.py:18
  344.2 60.0 %tail.1 = (f32[512,1024]{1,0:T(8,128)}, bf16[128,3072]{1,0:T(8,128)(2,1)}, f32[16,128]{1,0:T(8,128)}, f32[8,128]{1,0:T(8,128)}) custom-call(bf16[1024,768]{1,0:T(8,128)(2,1)} %convolution_convert_fusion.2.part, bf16[2048,768]{1,0:T(8,128)(2,1)} %get-tuple-element.58.grad_proj, bf16[1024,768]{1,0:T(8,128)(2,1)} %get-tuple-element.59.weight, ...), custom_call_target="tpu_custom_call" | custom-call | tf_op jit(solution)/shard_map/tail/pallas_call | solution.py:234
  404.2 1.3 slice.94
  411.4 1.7 fusion.14
  414.3 3.0 multiply_subtract_fusion.2
  418.9 3.9 multiply_subtract_fusion.1
  422.8 1.4 multiply_subtract_fusion.3
  425.1 3.2 multiply_subtract_fusion
  (140 shorter events, 20.4 us)
Async XLA Ops:
  0.7 143.4 %collective-permute-start.2 = (bf16[512,1024]{1,0:T(8,128)(2,1)}, bf16[512,1024]{1,0:T(8,128)(2,1)}, u32[]{:S(2)}, u32[]{:S(2)}) collective-permute-start(bf16[512,1024]{1,0:T(8,128)(2,1)} %param.22), channel_id=1, source_target_pairs={{0,1},{1,0},{2,3},{3,2},{4,5},{5,4},{6,7},{7,6},{8,9},{9,8},{10,11... | collective-permute-start | bytes 3145736 | tf_op jit(solution)/shard_map/ppermute | solution.py:946
  4.2 130.8 %copy-start.12 = (bf16[512,1024]{1,0:T(8,128)(2,1)S(1)}, bf16[512,1024]{1,0:T(8,128)(2,1)}, u32[]{:S(2)}) copy-start(bf16[512,1024]{1,0:T(8,128)(2,1)} %tok.1) | copy-start | bytes 3145732
  134.9 5.2 %copy-start.2 = (bf16[2048,256]{1,0:T(8,128)(2,1)}, bf16[2048,256]{1,0:T(8,128)(2,1)S(1)}, u32[]{:S(2)}) copy-start(bf16[2048,256]{1,0:T(8,128)(2,1)S(1)} %get-tuple-element.50.q_ref) | copy-start | bytes 3145732
  134.9 5.2 %copy-start.3 = (bf16[2048,256]{1,0:T(8,128)(2,1)}, bf16[2048,256]{1,0:T(8,128)(2,1)S(1)}, u32[]{:S(2)}) copy-start(bf16[2048,256]{1,0:T(8,128)(2,1)S(1)} %get-tuple-element.51.k_ref) | copy-start | bytes 3145732
  134.9 5.2 %copy-start.4 = (bf16[2048,256]{1,0:T(8,128)(2,1)}, bf16[2048,256]{1,0:T(8,128)(2,1)S(1)}, u32[]{:S(2)}) copy-start(bf16[2048,256]{1,0:T(8,128)(2,1)S(1)} %get-tuple-element.52.v_ref) | copy-start | bytes 3145732
  134.9 5.2 %copy-start.5 = (f32[2048,1]{1,0:T(8,128)}, f32[2048,1]{1,0:T(8,128)S(1)}, u32[]{:S(2)}) copy-start(f32[2048,1]{1,0:T(8,128)S(1)} %get-tuple-element.56.tag_ref) | copy-start | bytes 24580
  134.9 5.2 %copy-start.6 = (bf16[2048,256]{1,0:T(8,128)(2,1)}, bf16[2048,256]{1,0:T(8,128)(2,1)S(1)}, u32[]{:S(2)}) copy-start(bf16[2048,256]{1,0:T(8,128)(2,1)S(1)} %get-tuple-element.53.o_ref) | copy-start | bytes 3145732
  134.9 5.1 %copy-start.7 = (f32[8,8,256]{2,1,0:T(8,128)}, f32[8,8,256]{2,1,0:T(8,128)S(1)}, u32[]{:S(2)}) copy-start(f32[8,8,256]{2,1,0:T(8,128)S(1)} %get-tuple-element.54.lse_ref) | copy-start | bytes 196612
  141.8 3.5 collective-permute-start
  142.3 3.0 copy-start.43
  145.3 8.0 %copy-start.34 = (bf16[1024,1024]{1,0:T(8,128)(2,1)}, bf16[1024,1024]{1,0:T(8,128)(2,1)S(1)}, u32[]{:S(2)}) copy-start(bf16[1024,1024]{1,0:T(8,128)(2,1)S(1)} %constant_dynamic-update-slice_fusion) | copy-start | bytes 6291460
  145.4 8.0 %copy-start.42 = (bf16[1024,2048]{1,0:T(8,128)(2,1)S(1)}, bf16[1024,2048]{1,0:T(8,128)(2,1)}, u32[]{:S(2)}) copy-start(bf16[1024,2048]{1,0:T(8,128)(2,1)} %get-tuple-element.48) | copy-start | bytes 12582916
  153.3 15.3 %copy-start.40 = (bf16[1024,2048]{1,0:T(8,128)(2,1)}, bf16[1024,2048]{1,0:T(8,128)(2,1)S(1)}, u32[]{:S(2)}) copy-start(bf16[1024,2048]{1,0:T(8,128)(2,1)S(1)} %get-tuple-element.112) | copy-start | bytes 12582916
  161.4 4.5 %copy-start.41 = (bf16[1024,2048]{1,0:T(8,128)(2,1)}, bf16[1024,2048]{1,0:T(8,128)(2,1)S(1)}, u32[]{:S(2)}) copy-start(bf16[1024,2048]{1,0:T(8,128)(2,1)S(1)} %get-tuple-element.115) | copy-start | bytes 12582916
  168.6 19.9 %collective-permute-start.3 = (f32[512,1024]{1,0:T(8,128)}, f32[512,1024]{1,0:T(8,128)}, u32[]{:S(2)}, u32[]{:S(2)}) collective-permute-start(f32[512,1024]{1,0:T(8,128)} %slice.112), channel_id=1, source_target_pairs={{0,1},{1,0},{2,3},{3,2},{4,5},{5,4},{6,7},{7,6},{8,9},{9,8},{10,11... | collective-permute-start | bytes 6291464 | tf_op jit(solution)/shard_map/ppermute | solution.py:946
  175.8 15.4 %collective-permute-start.1 = (f32[512,1024]{1,0:T(8,128)}, f32[512,1024]{1,0:T(8,128)}, u32[]{:S(2)}, u32[]{:S(2)}) collective-permute-start(f32[512,1024]{1,0:T(8,128)} %slice.110), channel_id=1, source_target_pairs={{0,1},{1,0},{2,3},{3,2},{4,5},{5,4},{6,7},{7,6},{8,9},{9,8},{10,11... | collective-permute-start | bytes 6291464 | tf_op jit(solution)/shard_map/ppermute | solution.py:946
  179.0 9.5 %copy-start.17 = (f32[1024,1024]{1,0:T(8,128)S(1)}, f32[1024,1024]{1,0:T(8,128)}, u32[]{:S(2)}) copy-start(f32[1024,1024]{1,0:T(8,128)} %copy-done.16) | copy-start | bytes 12582916
  188.5 3.1 copy-start.18
  191.6 3.4 copy-start.19
  195.0 3.6 copy-start.10
  198.5 17.7 %collective-permute-start.4 = (bf16[1024,512]{1,0:T(8,128)(2,1)S(1)}, bf16[1024,512]{1,0:T(8,128)(2,1)S(1)}, u32[]{:S(2)}, u32[]{:S(2)}) collective-permute-start(bf16[1024,512]{1,0:T(8,128)(2,1)S(1)} %dynamic-slice_convert_fusion), channel_id=1, source_target_pairs={{0,1},{1,0},{2,3},{3,2},{4,5},{5,4},{6,7},{7,6},{8,9},{9,8},{10,11... | collective-permute-start | bytes 3145736 | tf_op jit(solution)/shard_map/ppermute | solution.py:946
  202.2 18.9 %all-to-all-start = ((bf16[512,4,256]{2,0,1:T(8,128)(2,1)}), bf16[512,4,256]{2,0,1:T(8,128)(2,1)}, u32[]{:S(2)}, u32[]{:S(2)}) async-start(bf16[512,4,256]{2,0,1:T(8,128)(2,1)} %bitcast.63), calls=%async_computation | async-start | bytes 2097152 | tf_op jit(solution)/shard_map/all_to_all | solution.py:996
  206.7 9.5 %copy-start.9 = (f32[1024,1024]{1,0:T(8,128)S(1)}, f32[1024,1024]{1,0:T(8,128)}, u32[]{:S(2)}) copy-start(f32[1024,1024]{1,0:T(8,128)} %copy-done.8) | copy-start | bytes 12582916
  404.2 3.4 copy-start.23
  414.3 3.0 copy-start.20
  414.3 3.9 copy-start.21
  414.3 4.6 %copy-start.22 = (f32[128,4096]{1,0:T(8,128)S(1)}, f32[128,4096]{1,0:T(8,128)}, u32[]{:S(2)}) copy-start(f32[128,4096]{1,0:T(8,128)} %param.34) | copy-start | bytes 6291460
  418.9 3.9 copy-start.1
  418.9 3.9 copy-start.31
  418.9 3.9 copy-start.32
  418.9 5.3 %copy-start.25 = (f32[128,4096]{1,0:T(8,128)S(1)}, f32[128,4096]{1,0:T(8,128)}, u32[]{:S(2)}) copy-start(f32[128,4096]{1,0:T(8,128)} %param.40) | copy-start | bytes 6291460
  418.9 5.3 %copy-start.26 = (f32[128,4096]{1,0:T(8,128)S(1)}, f32[128,4096]{1,0:T(8,128)}, u32[]{:S(2)}) copy-start(f32[128,4096]{1,0:T(8,128)} %param.35) | copy-start | bytes 6291460
  (18 other events, 37.1 us)

commit v8 on v7

--- a/solution.py
+++ b/solution.py
@@ -105,9 +105,9 @@
 
 
 def tail_kernel(
-    wide, narrow, part, grad_proj, weight, tok, vec_in, squares_in, normed_out, qkv_out, vec_out, square_out,
+    wide, narrow, normed, grad_proj, weight_in, tok_in, vec_in, squares_in, normed_out, qkv_out, vec_out, square_out,
     partial, mate_in, cross_out, cross_in, near_in, far_out, far_in, shards, vec_box, sums,
-    slices, slice_box, square_box, send, recv,
+    slices, slice_box, square_box, part, weight, tok, send, recv, local,
 ):
     w, n = lax.axis_index("wide"), lax.axis_index("narrow")
     column = wide // 2
@@ -116,11 +116,43 @@
     near, mate, cross = w + 1 - 2 * y, n + 1 - 2 * c, lax.rem(n + 2, narrow)
     wide_rows, group_rows = part.shape[0] // wide, normed_out.shape[0]
     towards = [lax.rem(z + d, column) for d in range(1, column + 1)]
+    loads = [
+        pltpu.make_async_copy(weight_in, weight, local.at[0]),
+        pltpu.make_async_copy(tok_in, tok, local.at[1]),
+    ]
+    for copy in loads:
+        copy.start()
     greet(others("wide", w, wide) + others("narrow", n, narrow))
     go = Copies(send, recv)
-    first = [
-        go.start(part.at[rows_at(towards[k] * 2 + 1 - y, wide_rows)], near_in.at[k], wide=near) for k in range(column)
-    ]
+    depth, chunk = part.shape[0], 128
+    sent = lambda k: go.make(part.at[rows_at(towards[k] * 2 + 1 - y, wide_rows)], near_in.at[k], wide=near)
+    first = [sent(k) for k in range(column)]
+    one_each = wide_rows == chunk
+
+    def rows_of(index):
+        at = rows_at(index, chunk)
+        part[at, :] = dot(normed[:, at], grad_proj[...], 0, 0).astype(BF)
+
+    if one_each:
+        for k in range(column):
+            rows_of(towards[k] * 2 + 1 - y)
+            go.launch(first[k])
+
+        def ours(k, carry):
+            rows_of(lax.rem(z + 1 + k, column) * 2 + y)
+            return carry
+
+        lax.fori_loop(0, column, ours, 0)
+    else:
+
+        def each(index, carry):
+            rows_of(index)
+            return carry
+
+        lax.fori_loop(0, depth // chunk, each, 0)
+        go.launch(*first)
+    for copy in loads:
+        copy.wait()
 
     seconds, kept = [], []
 
@@ -224,16 +256,17 @@
     square_out[...] = total
 
 
-def tail_call(part, grad_proj, weight, tok, vec_in, squares_in, wide, narrow):
-    depth, cols = part.shape
+def tail_call(normed, grad_proj, weight, tok, vec_in, squares_in, wide, narrow):
+    depth, cols = weight.shape
     rows = tok.shape[0] // narrow
     wide_rows = depth // wide
     column = wide // 2
     copies = 2 * column - 1 + 2 + (narrow - 1) + 2 + 3 + 2 * (wide - 1)
     vmem = pl.BlockSpec(memory_space=pltpu.VMEM)
+    anywhere = pl.BlockSpec(memory_space=pl.ANY)
     return pl.pallas_call(
         functools.partial(tail_kernel, wide, narrow),
-        in_specs=[vmem] * 6,
+        in_specs=[vmem, vmem, anywhere, anywhere, vmem, vmem],
         out_specs=[vmem] * 4,
         out_shape=[
             jax.ShapeDtypeStruct((rows, depth), F32),
@@ -255,14 +288,18 @@
             pltpu.VMEM((wide, 16, 128), F32),
             pltpu.VMEM((wide, 16, 128), F32),
             pltpu.VMEM((wide, 8, 128), F32),
+            pltpu.VMEM((depth, cols), BF),
+            pltpu.VMEM((depth, cols), BF),
+            pltpu.VMEM(tok.shape, BF),
             pltpu.SemaphoreType.DMA((copies,)),
             pltpu.SemaphoreType.DMA((copies,)),
+            pltpu.SemaphoreType.DMA((2,)),
         ],
         compiler_params=pltpu.CompilerParams(
             collective_id=1, has_side_effects=True, vmem_limit_bytes=56 * 1024 * 1024
         ),
         name="tail",
-    )(part, grad_proj, weight, tok, vec_in, squares_in)
+    )(normed, grad_proj, weight, tok, vec_in, squares_in)
 
 
 CLIP = 784
@@ -377,13 +414,11 @@
         return starts
 
     b = blocks
-    weight_starts = (
-        spread(up_own, up_all, shared, (0, (4, 4, 4), b + 2), 1)
-        + spread(down_own, down_all, shared, (0, (b + 2, b + 2, b + 2), b + 4), 2)
-        + spread(up_own, up_all, both, (1, (b + 3, b + 5, b + 6)), 3)
-        + spread(down_own, down_all, both, (b + 2, (b + 7, b + 8, b + 9)), 4)
-        + out_starts
-    )
+    weight_starts = spread(up_own, up_all, shared, (0, (4, 4, 4), b + 2), 1)
+    weight_starts += spread(down_own, down_all, shared, (0, (b + 2, b + 2, b + 2), b + 4), 2)
+    at_step[6].append((None, spread(up_own, up_all, both, (1, (b + 3, b + 5, b + 6)), 3)))
+    at_step[b + 3].append((None, spread(down_own, down_all, both, (b + 2, (b + 7, b + 8, b + 9)), 4)))
+    at_step[b + 6].append((None, out_starts))
     at_step[final + 1] += out_late
 
     mine = pl.ds(pl.multiple_of(n * width, width), width)
@@ -997,8 +1032,6 @@
     grad_proj, shards_out, shards_down, shards_up, squares = backward_call(
         query, keys, values, mixed_mine, grad_mixed_mine, lse, seg_rows[:, 0], tag_col, turns, part_out, part_down, part_up, head_dim, wide, narrow,
     )
-    part_qkv = dot(normed1_all, grad_proj, 0, 0).astype(BF)
-
     proj_sums = jnp.sum(grad_proj.astype(F32), axis=0).reshape(3, mine)
     proj_rows = lax.dynamic_update_slice(jnp.zeros((3, width), F32), proj_sums, (0, me * mine))
     up_sums = jnp.sum(grad_up_act.astype(F32), axis=0)
@@ -1017,7 +1050,7 @@
         axis=0,
     )
     grad_normed1, total_qkv, vector_total, square_total = tail_call(
-        part_qkv, grad_proj, qkv_w, tokens_all, vector_part, squares, wide, narrow
+        normed1_all, grad_proj, qkv_w, tokens_all, vector_part, squares, wide, narrow
     )
     grad_tokens = (grad_resid + norm_back(grad_normed1, vec[0], unit1, inverse1)).astype(BF)
 

time: 437 us -> 428 us (0.979)
  matrix products: 59.5 us -> 51.8 us
    pallas_call x1, Pallas kernels: 112 us -> 124 us  [backward_call(): pl.pallas_call(functools.partial(backward_kernel, heads, head_dim, wide,...]
    pallas_call x1, Pallas kernels: 131 us -> 120 us  [forward_call(): pl.pallas_call(functools.partial(forward_kernel, heads, head_dim, wide, n...]
    dot_general x10 -> x9, matrix products: 59.5 us -> 51.8 us  [dot(): lax.dot_general(a, b, (((ca,), (cb,)), ((), ())), preferred_element_type=...]
  transfers between devices with their start and end apart: 6 -> 6, of which waited for: 1 -> 1; matrix products, arithmetic and copies ran while one was open for 11% -> 11% of each run, Pallas kernels for 30% -> 29%
where the time goes in v8:
time: 428 us; the launch traced here: 421 us
  Pallas kernels  301 us (70%)
  matrix products  51.8 us (12%)
  other arithmetic  30.1 us (7%)
  local copies, waits for them, and re-layouts  24.2 us (6%)
  starting transfers between devices  6.03 us (1%)
    pallas_call x1, Pallas kernels, backward_call(): pl.pallas_call(functools.partial(backward_kernel, heads, head_dim, wide,...  124 us
    pallas_call x1, Pallas kernels, forward_call(): pl.pallas_call(functools.partial(forward_kernel, heads, head_dim, wide, n...  120 us
    pallas_call x1, Pallas kernels, tail_call(): pl.pallas_call(functools.partial(tail_kernel, wide, narrow), in_specs=[vm...  56.4 us
    dot_general x9, matrix products, dot(): lax.dot_general(a, b, (((ca,), (cb,)), ((), ())), preferred_element_type=...  51.8 us
    unnamed x92, local copies, waits for them, and re-layouts  13 us
    sub x5, other arithmetic, adamw(): return (param - rate * (direction + decay * param), moment, square)  12.2 us
  transfers between devices with their start and end apart: 6, of which 1 were waited for; matrix products, arithmetic and copies ran while one was open for 11% of the time, Pallas kernels for 29%

profile of v8, /device:TPU:0, one launch (start us, length us, event | category | flops | bytes accessed | tf_op | source)
XLA Modules:
  0.0 420.7 jit_solution(13816121755183969225)
XLA Ops:
  4.2 120.1 %attention_forward.1 = (bf16[2048,256]{1,0:T(8,128)(2,1)S(1)}, bf16[2048,256]{1,0:T(8,128)(2,1)S(1)}, bf16[2048,256]{1,0:T(8,128)(2,1)S(1)}, f32[2048,256]{1,0:T...) custom-call(bf16[512,1024]{1,0:T(8,128)(2,1)} %tok.1, ...), custom_call_target="tpu_custom_call" | custom-call | flops 17179869184 | bytes 4194304 | tf_op jit(solution)/shard_map/attention_forward/pallas_call | solution.py:615
  124.4 5.1 %fusion.44 = (f32[512]{0:T(512)S(1)}, f32[512,1024]{1,0:T(8,128)S(1)}) fusion(f32[1024]{0:T(1024)S(1)} %bitcast.79, bf16[512,1024]{1,0:T(8,128)(2,1)} %get-tuple-element.44, bf16[1024,1024]{1,0:T(8,128)(2,1)} %get-tuple-element.45, bf16[512,1024]{1,0:T(8,128)(2,1)S(1)} %copy-done.12), kind=kOutput, calls=%fused_computation.127 | convolution fusion | flops 1075838464 | bytes 6297600 | tf_op jit(solution)/shard_map/dot_general | solution.py:18
  129.9 1.4 add_convert_fusion.1
  131.8 1.4 constant_dynamic-update-slice_fusion.1
  133.5 1.3 constant_dynamic-update-slice_fusion
  134.8 8.0 %multiply_convert_fusion = (bf16[1024,2048]{1,0:T(8,128)(2,1)S(1)}, f32[1024,2048]{1,0:T(8,128)S(1)}) fusion(f32[2048]{0:T(1024)S(1)} %bitcast.77, bf16[1024,2048]{1,0:T(8,128)(2,1)S(1)} %copy-done.43, bf16[512,1024]{1,0:T(8,128)(2,1)} %collective-permute-done, bf16[512,1024]{1,0:T(8,128)(2,1)} %add_convert_fusion.1), kind=kOutput, calls=%fused_computation.8 | convolution fusion | flops 4311744512 | bytes 18882560 | tf_op jit(solution)/shard_map/dot_general | solution.py:18
  142.9 8.0 %convert_reduce_fusion = (f32[2048]{0:T(1024)S(1)}, bf16[1024,2048]{1,0:T(8,128)(2,1)S(1)}) fusion(f32[1024,2048]{1,0:T(8,128)S(1)} %get-tuple-element.113, f32[2048]{0:T(1024)S(1)} %bitcast.78, bf16[1024,1024]{1,0:T(8,128)(2,1)S(1)} %constant_dynamic-update-slice_fusion, bf16[1024,2048]{1,0:T(8,128)(2,1)S(1)} %copy-done.42), kind=kOutput, calls=%fused_computation.7 | convolution fusion | flops 4322228224 | bytes 18890752 | tf_op jit(solution)/shard_map/dot_general | solution.py:18
  150.9 4.5 %fusion.46 = f32[1024,1024]{1,0:T(8,128)S(1)} fusion(bf16[1024,2048]{1,0:T(8,128)(2,1)S(1)} %get-tuple-element.115, bf16[1024,2048]{1,0:T(8,128)(2,1)S(1)} %copy-done.43), kind=kOutput, calls=%fused_computation.129 | convolution fusion | flops 4294967296 | bytes 12582912 | tf_op jit(solution)/shard_map/dot_general | solution.py:18
  155.5 1.7 slice.112
  158.1 4.5 %fusion.45 = f32[1024,1024]{1,0:T(8,128)S(1)} fusion(bf16[1024,2048]{1,0:T(8,128)(2,1)S(1)} %get-tuple-element.112, bf16[1024,2048]{1,0:T(8,128)(2,1)S(1)} %copy-done.42), kind=kOutput, calls=%fused_computation.128 | convolution fusion | flops 4294967296 | bytes 12582912 | tf_op jit(solution)/shard_map/dot_general | solution.py:18
  162.7 1.7 slice.110
  168.5 9.5 %convolution_convert_fusion.1.part_down = bf16[1024,2048]{1,0:T(8,128)(2,1)} fusion(bf16[1024,1024]{1,0:T(8,128)(2,1)} %copy-done.34, bf16[1024,2048]{1,0:T(8,128)(2,1)} %copy-done.40), kind=kOutput, calls=%fused_computation.12 | convolution fusion | flops 4297064448 | bytes 10485760 | tf_op jit(solution)/shard_map/dot_general | solution.py:18
  178.0 2.9 multiply_reduce_fusion
  181.1 3.5 convert_reduce_fusion.4
  184.6 1.3 fusion.35
  185.9 2.0 copy-done.8
  188.2 1.3 copy-done.39
  189.5 1.3 convolution_convert_fusion.2
  191.9 4.4 %all-to-all-start = ((bf16[512,4,256]{2,0,1:T(8,128)(2,1)}), bf16[512,4,256]{2,0,1:T(8,128)(2,1)}, u32[]{:S(2)}, u32[]{:S(2)}) async-start(bf16[512,4,256]{2,0,1:T(8,128)(2,1)} %bitcast.61), calls=%async_computation | async-start | bytes 2097152 | tf_op jit(solution)/shard_map/all_to_all | solution.py:1031
  196.3 9.5 %convolution_convert_fusion.part_up = bf16[1024,2048]{1,0:T(8,128)(2,1)} fusion(bf16[1024,2048]{1,0:T(8,128)(2,1)} %copy-done.41, bf16[512,1024]{1,0:T(8,128)(2,1)} %collective-permute-done, bf16[512,1024]{1,0:T(8,128)(2,1)} %add_convert_fusion.1), kind=kOutput, calls=%fused_computation.11 | convolution fusion | flops 4301258752 | bytes 10485760 | tf_op jit(solution)/shard_map/dot_general | solution.py:18
  205.8 1.3 add_convert_fusion.part_out
  207.1 3.6 all-to-all-done
  210.8 124.2 %attention_backward.1 = (bf16[2048,768]{1,0:T(8,128)(2,1)}, bf16[4,128,512]{2,1,0:T(8,128)(2,1)}, bf16[4,128,1024]{2,1,0:T(8,128)(2,1)}, bf16[4,128,2048]{2,1,0:T(8,128)(2,1)}, f32[8,128]{1,0:T(8,128)}) custom-call(bf16[2048,256]{1,0:T(8,128)(2,1)} %copy-done.2, bf16[2048,256]{1,0:T(8,128)(2,1)} %copy-done.3, bf16[2048,256]{1,0:T(8,128)(2,1)} %copy-done.4, ...), custom_call_target="tpu_custom_call" | custom-call | flops 30064771072 | bytes 10485760 | tf_op jit(solution)/shard_map/attention_backward/pallas_call | solution.py:910
  335.0 2.4 convert_reduce_fusion.1
  337.5 1.3 concatenate.28.vec_in
  338.8 56.4 %tail.1 = (f32[512,1024]{1,0:T(8,128)}, bf16[128,3072]{1,0:T(8,128)(2,1)}, f32[16,128]{1,0:T(8,128)}, f32[8,128]{1,0:T(8,128)}) custom-call(bf16[2048,1024]{1,0:T(8,128)(2,1)} %get-tuple-element.49.normed, bf16[2048,768]{1,0:T(8,128)(2,1)} %get-tuple-element.58.grad_proj, bf16[1024,768]{1,0:T(8,128)(2,1)} %get-tuple-element.59.weight_in, ...), custom_call_target="tpu_custom_call" | custom-call | tf_op jit(solution)/shard_map/tail/pallas_call | solution.py:267
  395.2 1.3 slice.94
  402.3 1.7 fusion.14
  405.2 3.0 multiply_subtract_fusion.2
  409.8 4.0 multiply_subtract_fusion.1
  413.8 1.4 multiply_subtract_fusion.3
  416.1 3.2 multiply_subtract_fusion
  (139 shorter events, 18.9 us)
Async XLA Ops:
  0.7 132.8 %collective-permute-start.2 = (bf16[512,1024]{1,0:T(8,128)(2,1)}, bf16[512,1024]{1,0:T(8,128)(2,1)}, u32[]{:S(2)}, u32[]{:S(2)}) collective-permute-start(bf16[512,1024]{1,0:T(8,128)(2,1)} %param.22), channel_id=1, source_target_pairs={{0,1},{1,0},{2,3},{3,2},{4,5},{5,4},{6,7},{7,6},{8,9},{9,8},{10,11... | collective-permute-start | bytes 3145736 | tf_op jit(solution)/shard_map/ppermute | solution.py:981
  4.2 120.2 %copy-start.12 = (bf16[512,1024]{1,0:T(8,128)(2,1)S(1)}, bf16[512,1024]{1,0:T(8,128)(2,1)}, u32[]{:S(2)}) copy-start(bf16[512,1024]{1,0:T(8,128)(2,1)} %tok.1) | copy-start | bytes 3145732
  124.3 5.2 %copy-start.2 = (bf16[2048,256]{1,0:T(8,128)(2,1)}, bf16[2048,256]{1,0:T(8,128)(2,1)S(1)}, u32[]{:S(2)}) copy-start(bf16[2048,256]{1,0:T(8,128)(2,1)S(1)} %get-tuple-element.50.q_ref) | copy-start | bytes 3145732
  124.3 5.2 %copy-start.3 = (bf16[2048,256]{1,0:T(8,128)(2,1)}, bf16[2048,256]{1,0:T(8,128)(2,1)S(1)}, u32[]{:S(2)}) copy-start(bf16[2048,256]{1,0:T(8,128)(2,1)S(1)} %get-tuple-element.51.k_ref) | copy-start | bytes 3145732
  124.3 5.2 %copy-start.4 = (bf16[2048,256]{1,0:T(8,128)(2,1)}, bf16[2048,256]{1,0:T(8,128)(2,1)S(1)}, u32[]{:S(2)}) copy-start(bf16[2048,256]{1,0:T(8,128)(2,1)S(1)} %get-tuple-element.52.v_ref) | copy-start | bytes 3145732
  124.3 5.2 %copy-start.5 = (f32[2048,1]{1,0:T(8,128)}, f32[2048,1]{1,0:T(8,128)S(1)}, u32[]{:S(2)}) copy-start(f32[2048,1]{1,0:T(8,128)S(1)} %get-tuple-element.56.tag_ref) | copy-start | bytes 24580
  124.3 5.2 %copy-start.6 = (bf16[2048,256]{1,0:T(8,128)(2,1)}, bf16[2048,256]{1,0:T(8,128)(2,1)S(1)}, u32[]{:S(2)}) copy-start(bf16[2048,256]{1,0:T(8,128)(2,1)S(1)} %get-tuple-element.53.o_ref) | copy-start | bytes 3145732
  124.3 5.1 %copy-start.7 = (f32[8,8,256]{2,1,0:T(8,128)}, f32[8,8,256]{2,1,0:T(8,128)S(1)}, u32[]{:S(2)}) copy-start(f32[8,8,256]{2,1,0:T(8,128)S(1)} %get-tuple-element.54.lse_ref) | copy-start | bytes 196612
  131.3 3.5 collective-permute-start
  131.8 3.0 copy-start.43
  134.8 8.1 %copy-start.34 = (bf16[1024,1024]{1,0:T(8,128)(2,1)}, bf16[1024,1024]{1,0:T(8,128)(2,1)S(1)}, u32[]{:S(2)}) copy-start(bf16[1024,1024]{1,0:T(8,128)(2,1)S(1)} %constant_dynamic-update-slice_fusion) | copy-start | bytes 6291460
  134.8 8.1 %copy-start.42 = (bf16[1024,2048]{1,0:T(8,128)(2,1)S(1)}, bf16[1024,2048]{1,0:T(8,128)(2,1)}, u32[]{:S(2)}) copy-start(bf16[1024,2048]{1,0:T(8,128)(2,1)} %get-tuple-element.48) | copy-start | bytes 12582916
  142.8 15.3 %copy-start.40 = (bf16[1024,2048]{1,0:T(8,128)(2,1)}, bf16[1024,2048]{1,0:T(8,128)(2,1)S(1)}, u32[]{:S(2)}) copy-start(bf16[1024,2048]{1,0:T(8,128)(2,1)S(1)} %get-tuple-element.112) | copy-start | bytes 12582916
  150.9 4.5 %copy-start.41 = (bf16[1024,2048]{1,0:T(8,128)(2,1)}, bf16[1024,2048]{1,0:T(8,128)(2,1)S(1)}, u32[]{:S(2)}) copy-start(bf16[1024,2048]{1,0:T(8,128)(2,1)S(1)} %get-tuple-element.115) | copy-start | bytes 12582916
  158.1 19.9 %collective-permute-start.3 = (f32[512,1024]{1,0:T(8,128)}, f32[512,1024]{1,0:T(8,128)}, u32[]{:S(2)}, u32[]{:S(2)}) collective-permute-start(f32[512,1024]{1,0:T(8,128)} %slice.112), channel_id=1, source_target_pairs={{0,1},{1,0},{2,3},{3,2},{4,5},{5,4},{6,7},{7,6},{8,9},{9,8},{10,11... | collective-permute-start | bytes 6291464 | tf_op jit(solution)/shard_map/ppermute | solution.py:981
  165.3 15.6 %collective-permute-start.1 = (f32[512,1024]{1,0:T(8,128)}, f32[512,1024]{1,0:T(8,128)}, u32[]{:S(2)}, u32[]{:S(2)}) collective-permute-start(f32[512,1024]{1,0:T(8,128)} %slice.110), channel_id=1, source_target_pairs={{0,1},{1,0},{2,3},{3,2},{4,5},{5,4},{6,7},{7,6},{8,9},{9,8},{10,11... | collective-permute-start | bytes 6291464 | tf_op jit(solution)/shard_map/ppermute | solution.py:981
  168.5 9.5 %copy-start.17 = (f32[1024,1024]{1,0:T(8,128)S(1)}, f32[1024,1024]{1,0:T(8,128)}, u32[]{:S(2)}) copy-start(f32[1024,1024]{1,0:T(8,128)} %copy-done.16) | copy-start | bytes 12582916
  178.0 3.1 copy-start.18
  181.1 3.5 copy-start.19
  184.6 3.6 copy-start.10
  188.1 17.7 %collective-permute-start.4 = (bf16[1024,512]{1,0:T(8,128)(2,1)S(1)}, bf16[1024,512]{1,0:T(8,128)(2,1)S(1)}, u32[]{:S(2)}, u32[]{:S(2)}) collective-permute-start(bf16[1024,512]{1,0:T(8,128)(2,1)S(1)} %dynamic-slice_convert_fusion), channel_id=1, source_target_pairs={{0,1},{1,0},{2,3},{3,2},{4,5},{5,4},{6,7},{7,6},{8,9},{9,8},{10,11... | collective-permute-start | bytes 3145736 | tf_op jit(solution)/shard_map/ppermute | solution.py:981
  191.9 18.9 %all-to-all-start = ((bf16[512,4,256]{2,0,1:T(8,128)(2,1)}), bf16[512,4,256]{2,0,1:T(8,128)(2,1)}, u32[]{:S(2)}, u32[]{:S(2)}) async-start(bf16[512,4,256]{2,0,1:T(8,128)(2,1)} %bitcast.61), calls=%async_computation | async-start | bytes 2097152 | tf_op jit(solution)/shard_map/all_to_all | solution.py:1031
  196.3 9.5 %copy-start.9 = (f32[1024,1024]{1,0:T(8,128)S(1)}, f32[1024,1024]{1,0:T(8,128)}, u32[]{:S(2)}) copy-start(f32[1024,1024]{1,0:T(8,128)} %copy-done.8) | copy-start | bytes 12582916
  395.2 3.3 copy-start.23
  405.2 3.0 copy-start.20
  405.2 3.9 copy-start.21
  405.2 4.6 %copy-start.22 = (f32[128,4096]{1,0:T(8,128)S(1)}, f32[128,4096]{1,0:T(8,128)}, u32[]{:S(2)}) copy-start(f32[128,4096]{1,0:T(8,128)} %param.34) | copy-start | bytes 6291460
  409.8 4.0 copy-start.1
  409.8 4.0 copy-start.31
  409.8 4.0 copy-start.32
  409.8 5.4 %copy-start.25 = (f32[128,4096]{1,0:T(8,128)S(1)}, f32[128,4096]{1,0:T(8,128)}, u32[]{:S(2)}) copy-start(f32[128,4096]{1,0:T(8,128)} %param.40) | copy-start | bytes 6291460
  409.8 5.4 %copy-start.26 = (f32[128,4096]{1,0:T(8,128)S(1)}, f32[128,4096]{1,0:T(8,128)}, u32[]{:S(2)}) copy-start(f32[128,4096]{1,0:T(8,128)} %param.35) | copy-start | bytes 6291460
  (18 other events, 37.3 us)

commit v9 on v8

--- a/solution.py
+++ b/solution.py
@@ -100,6 +100,11 @@
             copy.wait_send()
 
 
+def across_column(z, d):
+    bits = [1 << b for b in range(d.bit_length()) if d >> b & 1]
+    return z + sum(bit * (1 - 2 * lax.rem(z // bit, 2)) for bit in bits)
+
+
 def rows_at(index, size):
     return pl.ds(pl.multiple_of(index * size, size), size)
 
@@ -115,7 +120,7 @@
     x, c = n // 2, lax.rem(n, 2)
     near, mate, cross = w + 1 - 2 * y, n + 1 - 2 * c, lax.rem(n + 2, narrow)
     wide_rows, group_rows = part.shape[0] // wide, normed_out.shape[0]
-    towards = [lax.rem(z + d, column) for d in range(1, column + 1)]
+    towards = [across_column(z, d) for d in range(column - 1, -1, -1)]
     loads = [
         pltpu.make_async_copy(weight_in, weight, local.at[0]),
         pltpu.make_async_copy(tok_in, tok, local.at[1]),
@@ -335,9 +340,8 @@
     column = wide // 2
     z, y, side = w // 2, lax.rem(w, 2), lax.rem(n, 2)
     near, mate, cross = w + 1 - 2 * y, n + 1 - 2 * side, lax.rem(n + 2, narrow)
-    source = lambda d: lax.rem(z - d + column, column) * 2 + y
-    target = lambda d: lax.rem(z + d, column) * 2 + y
-    beside = lambda d: lax.rem(z - d + column, column) * 2 + 1 - y
+    source = target = lambda d: across_column(z, d) * 2 + y
+    beside = lambda d: across_column(z, d) * 2 + 1 - y
     wide_rows, out_half = out_own.shape
     half = up_own.shape[1]
     group_rows = tok.shape[0]
@@ -657,7 +661,7 @@
         z, y, x = w // 2, lax.rem(w, 2), self.n // 2
         near, mate, cross = w + 1 - 2 * y, self.n + 1 - 2 * lax.rem(self.n, 2), lax.rem(self.n + 2, narrow)
         size, cols = part.shape[0] // wide, box.shape[2]
-        towards = [lax.rem(z + d, self.column) for d in range(1, self.column + 1)]
+        towards = [across_column(z, d) for d in range(self.column - 1, -1, -1)]
         theirs, ours = [to * 2 + 1 - y for to in towards], [to * 2 + y for to in towards]
         here = pl.ds(pl.multiple_of(x * cols, cols), cols) if split else pl.ds(0, cols)
         self.loads = [
@@ -761,7 +765,7 @@
         z, y = w // 2, lax.rem(w, 2)
         greet(
             [{"wide": w + 1 - 2 * y}]
-            + [{"wide": lax.rem(z + d, column) * 2 + y} for d in range(1, column)]
+            + [{"wide": across_column(z, d) * 2 + y} for d in range(1, column)]
             + [{"narrow": n + 1 - 2 * lax.rem(n, 2)}, {"narrow": lax.rem(n + 2, narrow)}]
         )
         for k in range(column):

time: 428 us -> 415 us (0.970)
  Pallas kernels: 301 us -> 288 us
    pallas_call x1, Pallas kernels: 124 us -> 109 us  [backward_call(): pl.pallas_call(functools.partial(backward_kernel, heads, head_dim, wide,...]
  transfers between devices with their start and end apart: 6 -> 6, of which waited for: 1 -> 1; matrix products, arithmetic and copies ran while one was open for 11% -> 11% of each run, Pallas kernels for 29% -> 30%
where the time goes in v9:
time: 415 us; the launch traced here: 408 us
  Pallas kernels  288 us (69%)
  matrix products  51.8 us (12%)
  other arithmetic  30.1 us (7%)
  local copies, waits for them, and re-layouts  24.2 us (6%)
  starting transfers between devices  6.04 us (1%)
  between operations  4.27 us (1%)
    pallas_call x1, Pallas kernels, forward_call(): pl.pallas_call(functools.partial(forward_kernel, heads, head_dim, wide, n...  123 us
    pallas_call x1, Pallas kernels, backward_call(): pl.pallas_call(functools.partial(backward_kernel, heads, head_dim, wide,...  109 us
    pallas_call x1, Pallas kernels, tail_call(): pl.pallas_call(functools.partial(tail_kernel, wide, narrow), in_specs=[vm...  55.6 us
    dot_general x9, matrix products, dot(): lax.dot_general(a, b, (((ca,), (cb,)), ((), ())), preferred_element_type=...  51.8 us
    unnamed x92, local copies, waits for them, and re-layouts  13 us
    sub x5, other arithmetic, adamw(): return (param - rate * (direction + decay * param), moment, square)  12.2 us
  transfers between devices with their start and end apart: 6, of which 1 were waited for; matrix products, arithmetic and copies ran while one was open for 11% of the time, Pallas kernels for 30%

profile of v9, /device:TPU:0, one launch (start us, length us, event | category | flops | bytes accessed | tf_op | source)
XLA Modules:
  0.0 407.7 jit_solution(10732376213527947875)
XLA Ops:
  4.2 122.7 %attention_forward.1 = (bf16[2048,256]{1,0:T(8,128)(2,1)S(1)}, bf16[2048,256]{1,0:T(8,128)(2,1)S(1)}, bf16[2048,256]{1,0:T(8,128)(2,1)S(1)}, f32[2048,256]{1,0:T...) custom-call(bf16[512,1024]{1,0:T(8,128)(2,1)} %tok.1, ...), custom_call_target="tpu_custom_call" | custom-call | flops 17179869184 | bytes 4194304 | tf_op jit(solution)/shard_map/attention_forward/pallas_call | solution.py:619
  127.0 5.1 %fusion.44 = (f32[512]{0:T(512)S(1)}, f32[512,1024]{1,0:T(8,128)S(1)}) fusion(f32[1024]{0:T(1024)S(1)} %bitcast.79, bf16[512,1024]{1,0:T(8,128)(2,1)} %get-tuple-element.44, bf16[1024,1024]{1,0:T(8,128)(2,1)} %get-tuple-element.45, bf16[512,1024]{1,0:T(8,128)(2,1)S(1)} %copy-done.12), kind=kOutput, calls=%fused_computation.127 | convolution fusion | flops 1075838464 | bytes 6297600 | tf_op jit(solution)/shard_map/dot_general | solution.py:18
  132.4 1.4 add_convert_fusion.1
  134.3 1.4 constant_dynamic-update-slice_fusion.1
  136.0 1.3 constant_dynamic-update-slice_fusion
  137.4 8.0 %multiply_convert_fusion = (bf16[1024,2048]{1,0:T(8,128)(2,1)S(1)}, f32[1024,2048]{1,0:T(8,128)S(1)}) fusion(f32[2048]{0:T(1024)S(1)} %bitcast.77, bf16[1024,2048]{1,0:T(8,128)(2,1)S(1)} %copy-done.43, bf16[512,1024]{1,0:T(8,128)(2,1)} %collective-permute-done, bf16[512,1024]{1,0:T(8,128)(2,1)} %add_convert_fusion.1), kind=kOutput, calls=%fused_computation.8 | convolution fusion | flops 4311744512 | bytes 18882560 | tf_op jit(solution)/shard_map/dot_general | solution.py:18
  145.4 8.0 %convert_reduce_fusion = (f32[2048]{0:T(1024)S(1)}, bf16[1024,2048]{1,0:T(8,128)(2,1)S(1)}) fusion(f32[1024,2048]{1,0:T(8,128)S(1)} %get-tuple-element.113, f32[2048]{0:T(1024)S(1)} %bitcast.78, bf16[1024,1024]{1,0:T(8,128)(2,1)S(1)} %constant_dynamic-update-slice_fusion, bf16[1024,2048]{1,0:T(8,128)(2,1)S(1)} %copy-done.42), kind=kOutput, calls=%fused_computation.7 | convolution fusion | flops 4322228224 | bytes 18890752 | tf_op jit(solution)/shard_map/dot_general | solution.py:18
  153.5 4.5 %fusion.46 = f32[1024,1024]{1,0:T(8,128)S(1)} fusion(bf16[1024,2048]{1,0:T(8,128)(2,1)S(1)} %get-tuple-element.115, bf16[1024,2048]{1,0:T(8,128)(2,1)S(1)} %copy-done.43), kind=kOutput, calls=%fused_computation.129 | convolution fusion | flops 4294967296 | bytes 12582912 | tf_op jit(solution)/shard_map/dot_general | solution.py:18
  158.0 1.7 slice.112
  160.7 4.5 %fusion.45 = f32[1024,1024]{1,0:T(8,128)S(1)} fusion(bf16[1024,2048]{1,0:T(8,128)(2,1)S(1)} %get-tuple-element.112, bf16[1024,2048]{1,0:T(8,128)(2,1)S(1)} %copy-done.42), kind=kOutput, calls=%fused_computation.128 | convolution fusion | flops 4294967296 | bytes 12582912 | tf_op jit(solution)/shard_map/dot_general | solution.py:18
  165.3 1.7 slice.110
  171.0 9.5 %convolution_convert_fusion.1.part_down = bf16[1024,2048]{1,0:T(8,128)(2,1)} fusion(bf16[1024,1024]{1,0:T(8,128)(2,1)} %copy-done.34, bf16[1024,2048]{1,0:T(8,128)(2,1)} %copy-done.40), kind=kOutput, calls=%fused_computation.12 | convolution fusion | flops 4297064448 | bytes 10485760 | tf_op jit(solution)/shard_map/dot_general | solution.py:18
  180.6 2.9 multiply_reduce_fusion
  183.7 3.5 convert_reduce_fusion.4
  187.2 1.3 fusion.35
  188.5 2.0 copy-done.8
  190.8 1.3 copy-done.39
  192.1 1.3 convolution_convert_fusion.2
  194.4 4.4 %all-to-all-start = ((bf16[512,4,256]{2,0,1:T(8,128)(2,1)}), bf16[512,4,256]{2,0,1:T(8,128)(2,1)}, u32[]{:S(2)}, u32[]{:S(2)}) async-start(bf16[512,4,256]{2,0,1:T(8,128)(2,1)} %bitcast.61), calls=%async_computation | async-start | bytes 2097152 | tf_op jit(solution)/shard_map/all_to_all | solution.py:1035
  198.9 9.5 %convolution_convert_fusion.part_up = bf16[1024,2048]{1,0:T(8,128)(2,1)} fusion(bf16[1024,2048]{1,0:T(8,128)(2,1)} %copy-done.41, bf16[512,1024]{1,0:T(8,128)(2,1)} %collective-permute-done, bf16[512,1024]{1,0:T(8,128)(2,1)} %add_convert_fusion.1), kind=kOutput, calls=%fused_computation.11 | convolution fusion | flops 4301258752 | bytes 10485760 | tf_op jit(solution)/shard_map/dot_general | solution.py:18
  208.4 1.3 add_convert_fusion.part_out
  209.7 3.6 all-to-all-done
  213.3 109.4 %attention_backward.1 = (bf16[2048,768]{1,0:T(8,128)(2,1)}, bf16[4,128,512]{2,1,0:T(8,128)(2,1)}, bf16[4,128,1024]{2,1,0:T(8,128)(2,1)}, bf16[4,128,2048]{2,1,0:T(8,128)(2,1)}, f32[8,128]{1,0:T(8,128)}) custom-call(bf16[2048,256]{1,0:T(8,128)(2,1)} %copy-done.2, bf16[2048,256]{1,0:T(8,128)(2,1)} %copy-done.3, bf16[2048,256]{1,0:T(8,128)(2,1)} %copy-done.4, ...), custom_call_target="tpu_custom_call" | custom-call | flops 30064771072 | bytes 10485760 | tf_op jit(solution)/shard_map/attention_backward/pallas_call | solution.py:914
  322.8 2.4 convert_reduce_fusion.1
  325.3 1.3 concatenate.28.vec_in
  326.6 55.6 %tail.1 = (f32[512,1024]{1,0:T(8,128)}, bf16[128,3072]{1,0:T(8,128)(2,1)}, f32[16,128]{1,0:T(8,128)}, f32[8,128]{1,0:T(8,128)}) custom-call(bf16[2048,1024]{1,0:T(8,128)(2,1)} %get-tuple-element.49.normed, bf16[2048,768]{1,0:T(8,128)(2,1)} %get-tuple-element.58.grad_proj, bf16[1024,768]{1,0:T(8,128)(2,1)} %get-tuple-element.59.weight_in, ...), custom_call_target="tpu_custom_call" | custom-call | tf_op jit(solution)/shard_map/tail/pallas_call | solution.py:272
  382.2 1.3 slice.94
  389.3 1.7 fusion.14
  392.3 3.0 multiply_subtract_fusion.2
  396.8 4.0 multiply_subtract_fusion.1
  400.8 1.4 multiply_subtract_fusion.3
  403.1 3.2 multiply_subtract_fusion
  (139 shorter events, 18.9 us)
Async XLA Ops:
  0.7 135.4 %collective-permute-start.2 = (bf16[512,1024]{1,0:T(8,128)(2,1)}, bf16[512,1024]{1,0:T(8,128)(2,1)}, u32[]{:S(2)}, u32[]{:S(2)}) collective-permute-start(bf16[512,1024]{1,0:T(8,128)(2,1)} %param.22), channel_id=1, source_target_pairs={{0,1},{1,0},{2,3},{3,2},{4,5},{5,4},{6,7},{7,6},{8,9},{9,8},{10,11... | collective-permute-start | bytes 3145736 | tf_op jit(solution)/shard_map/ppermute | solution.py:985
  4.2 122.8 %copy-start.12 = (bf16[512,1024]{1,0:T(8,128)(2,1)S(1)}, bf16[512,1024]{1,0:T(8,128)(2,1)}, u32[]{:S(2)}) copy-start(bf16[512,1024]{1,0:T(8,128)(2,1)} %tok.1) | copy-start | bytes 3145732
  126.9 5.2 %copy-start.2 = (bf16[2048,256]{1,0:T(8,128)(2,1)}, bf16[2048,256]{1,0:T(8,128)(2,1)S(1)}, u32[]{:S(2)}) copy-start(bf16[2048,256]{1,0:T(8,128)(2,1)S(1)} %get-tuple-element.50.q_ref) | copy-start | bytes 3145732
  126.9 5.2 %copy-start.3 = (bf16[2048,256]{1,0:T(8,128)(2,1)}, bf16[2048,256]{1,0:T(8,128)(2,1)S(1)}, u32[]{:S(2)}) copy-start(bf16[2048,256]{1,0:T(8,128)(2,1)S(1)} %get-tuple-element.51.k_ref) | copy-start | bytes 3145732
  126.9 5.2 %copy-start.4 = (bf16[2048,256]{1,0:T(8,128)(2,1)}, bf16[2048,256]{1,0:T(8,128)(2,1)S(1)}, u32[]{:S(2)}) copy-start(bf16[2048,256]{1,0:T(8,128)(2,1)S(1)} %get-tuple-element.52.v_ref) | copy-start | bytes 3145732
  126.9 5.2 %copy-start.5 = (f32[2048,1]{1,0:T(8,128)}, f32[2048,1]{1,0:T(8,128)S(1)}, u32[]{:S(2)}) copy-start(f32[2048,1]{1,0:T(8,128)S(1)} %get-tuple-element.56.tag_ref) | copy-start | bytes 24580
  126.9 5.2 %copy-start.6 = (bf16[2048,256]{1,0:T(8,128)(2,1)}, bf16[2048,256]{1,0:T(8,128)(2,1)S(1)}, u32[]{:S(2)}) copy-start(bf16[2048,256]{1,0:T(8,128)(2,1)S(1)} %get-tuple-element.53.o_ref) | copy-start | bytes 3145732
  126.9 5.1 %copy-start.7 = (f32[8,8,256]{2,1,0:T(8,128)}, f32[8,8,256]{2,1,0:T(8,128)S(1)}, u32[]{:S(2)}) copy-start(f32[8,8,256]{2,1,0:T(8,128)S(1)} %get-tuple-element.54.lse_ref) | copy-start | bytes 196612
  133.8 3.5 collective-permute-start
  134.3 3.0 copy-start.43
  137.3 8.1 %copy-start.34 = (bf16[1024,1024]{1,0:T(8,128)(2,1)}, bf16[1024,1024]{1,0:T(8,128)(2,1)S(1)}, u32[]{:S(2)}) copy-start(bf16[1024,1024]{1,0:T(8,128)(2,1)S(1)} %constant_dynamic-update-slice_fusion) | copy-start | bytes 6291460
  137.4 8.1 %copy-start.42 = (bf16[1024,2048]{1,0:T(8,128)(2,1)S(1)}, bf16[1024,2048]{1,0:T(8,128)(2,1)}, u32[]{:S(2)}) copy-start(bf16[1024,2048]{1,0:T(8,128)(2,1)} %get-tuple-element.48) | copy-start | bytes 12582916
  145.4 15.3 %copy-start.40 = (bf16[1024,2048]{1,0:T(8,128)(2,1)}, bf16[1024,2048]{1,0:T(8,128)(2,1)S(1)}, u32[]{:S(2)}) copy-start(bf16[1024,2048]{1,0:T(8,128)(2,1)S(1)} %get-tuple-element.112) | copy-start | bytes 12582916
  153.5 4.5 %copy-start.41 = (bf16[1024,2048]{1,0:T(8,128)(2,1)}, bf16[1024,2048]{1,0:T(8,128)(2,1)S(1)}, u32[]{:S(2)}) copy-start(bf16[1024,2048]{1,0:T(8,128)(2,1)S(1)} %get-tuple-element.115) | copy-start | bytes 12582916
  160.7 19.9 %collective-permute-start.3 = (f32[512,1024]{1,0:T(8,128)}, f32[512,1024]{1,0:T(8,128)}, u32[]{:S(2)}, u32[]{:S(2)}) collective-permute-start(f32[512,1024]{1,0:T(8,128)} %slice.112), channel_id=1, source_target_pairs={{0,1},{1,0},{2,3},{3,2},{4,5},{5,4},{6,7},{7,6},{8,9},{9,8},{10,11... | collective-permute-start | bytes 6291464 | tf_op jit(solution)/shard_map/ppermute | solution.py:985
  167.9 15.6 %collective-permute-start.1 = (f32[512,1024]{1,0:T(8,128)}, f32[512,1024]{1,0:T(8,128)}, u32[]{:S(2)}, u32[]{:S(2)}) collective-permute-start(f32[512,1024]{1,0:T(8,128)} %slice.110), channel_id=1, source_target_pairs={{0,1},{1,0},{2,3},{3,2},{4,5},{5,4},{6,7},{7,6},{8,9},{9,8},{10,11... | collective-permute-start | bytes 6291464 | tf_op jit(solution)/shard_map/ppermute | solution.py:985
  171.0 9.5 %copy-start.17 = (f32[1024,1024]{1,0:T(8,128)S(1)}, f32[1024,1024]{1,0:T(8,128)}, u32[]{:S(2)}) copy-start(f32[1024,1024]{1,0:T(8,128)} %copy-done.16) | copy-start | bytes 12582916
  180.5 3.1 copy-start.18
  183.7 3.5 copy-start.19
  187.2 3.6 copy-start.10
  190.7 17.7 %collective-permute-start.4 = (bf16[1024,512]{1,0:T(8,128)(2,1)S(1)}, bf16[1024,512]{1,0:T(8,128)(2,1)S(1)}, u32[]{:S(2)}, u32[]{:S(2)}) collective-permute-start(bf16[1024,512]{1,0:T(8,128)(2,1)S(1)} %dynamic-slice_convert_fusion), channel_id=1, source_target_pairs={{0,1},{1,0},{2,3},{3,2},{4,5},{5,4},{6,7},{7,6},{8,9},{9,8},{10,11... | collective-permute-start | bytes 3145736 | tf_op jit(solution)/shard_map/ppermute | solution.py:985
  194.4 18.9 %all-to-all-start = ((bf16[512,4,256]{2,0,1:T(8,128)(2,1)}), bf16[512,4,256]{2,0,1:T(8,128)(2,1)}, u32[]{:S(2)}, u32[]{:S(2)}) async-start(bf16[512,4,256]{2,0,1:T(8,128)(2,1)} %bitcast.61), calls=%async_computation | async-start | bytes 2097152 | tf_op jit(solution)/shard_map/all_to_all | solution.py:1035
  198.9 9.5 %copy-start.9 = (f32[1024,1024]{1,0:T(8,128)S(1)}, f32[1024,1024]{1,0:T(8,128)}, u32[]{:S(2)}) copy-start(f32[1024,1024]{1,0:T(8,128)} %copy-done.8) | copy-start | bytes 12582916
  382.2 3.3 copy-start.23
  392.2 3.0 copy-start.20
  392.2 3.9 copy-start.21
  392.2 4.6 %copy-start.22 = (f32[128,4096]{1,0:T(8,128)S(1)}, f32[128,4096]{1,0:T(8,128)}, u32[]{:S(2)}) copy-start(f32[128,4096]{1,0:T(8,128)} %param.34) | copy-start | bytes 6291460
  396.8 4.0 copy-start.1
  396.8 4.0 copy-start.31
  396.8 4.0 copy-start.32
  396.8 5.4 %copy-start.25 = (f32[128,4096]{1,0:T(8,128)S(1)}, f32[128,4096]{1,0:T(8,128)}, u32[]{:S(2)}) copy-start(f32[128,4096]{1,0:T(8,128)} %param.40) | copy-start | bytes 6291460
  396.8 5.4 %copy-start.26 = (f32[128,4096]{1,0:T(8,128)S(1)}, f32[128,4096]{1,0:T(8,128)}, u32[]{:S(2)}) copy-start(f32[128,4096]{1,0:T(8,128)} %param.35) | copy-start | bytes 6291460
  (18 other events, 37.3 us)

commit v10 on v9

--- a/solution.py
+++ b/solution.py
@@ -1015,14 +1015,14 @@
     act = (up_pre * erf_part).astype(BF)
     slope = erf_part + up_pre * (jnp.exp(-0.5 * up_pre * up_pre) * ((2.0 * jnp.pi) ** -0.5))
     part_down = dot(cot_pair, act, 0, 0).astype(BF)
-    down_part = dot(act, down_w, 1, 1)
-    down = down_part[:rows] + mate(down_part[rows:])
+    down_theirs = mate(dot(act[rows:], down_w, 1, 1))
+    down = dot(act[:rows], down_w, 1, 1) + down_theirs
     layer_out = (resid + (down + vec[8])).astype(BF)
 
     grad_up_act = (dot(cot_pair, down_w, 1, 0) * slope).astype(BF)
     part_up = dot(normed2_pair, grad_up_act, 0, 0).astype(BF)
-    grad_normed2_part = dot(grad_up_act, up_w, 1, 1)
-    grad_normed2 = grad_normed2_part[:rows] + mate(grad_normed2_part[rows:])
+    grad_theirs = mate(dot(grad_up_act[rows:], up_w, 1, 1))
+    grad_normed2 = dot(grad_up_act[:rows], up_w, 1, 1) + grad_theirs
     cot = cotangent.astype(F32)
     grad_resid = cot + norm_back(grad_normed2, vec[6], unit2, inverse2)
     grad_branch = grad_resid.astype(BF)

time: 415 us -> 428 us (1.031)
  matrix products: 51.8 us -> 70.8 us
    dot_general x9 -> x11, matrix products: 51.8 us -> 70.8 us  [dot(): lax.dot_general(a, b, (((ca,), (cb,)), ((), ())), preferred_element_type=...]
    unnamed x92 -> x88, local copies, waits for them, and re-layouts: 13 us -> 11.2 us
  transfers between devices with their start and end apart: 6 -> 6, of which waited for: 1 -> 1; matrix products, arithmetic and copies ran while one was open for 11% -> 11% of each run, Pallas kernels for 30% -> 0%
where the time goes in v10:
time: 428 us; the launch traced here: 425 us
  Pallas kernels  291 us (68%)
  matrix products  70.8 us (17%)
  other arithmetic  27.8 us (6%)
  local copies, waits for them, and re-layouts  20.3 us (5%)
  starting transfers between devices  6.34 us (1%)
  waiting for transfers between devices  4.34 us (1%)
    pallas_call x1, Pallas kernels, forward_call(): pl.pallas_call(functools.partial(forward_kernel, heads, head_dim, wide, n...  123 us
    pallas_call x1, Pallas kernels, backward_call(): pl.pallas_call(functools.partial(backward_kernel, heads, head_dim, wide,...  110 us
    dot_general x11, matrix products, dot(): lax.dot_general(a, b, (((ca,), (cb,)), ((), ())), preferred_element_type=...  70.8 us
    pallas_call x1, Pallas kernels, tail_call(): pl.pallas_call(functools.partial(tail_kernel, wide, narrow), in_specs=[vm...  58.7 us
    sub x5, other arithmetic, adamw(): return (param - rate * (direction + decay * param), moment, square)  12.1 us
    unnamed x88, local copies, waits for them, and re-layouts  11.2 us
  transfers between devices with their start and end apart: 6, of which 1 were waited for; matrix products, arithmetic and copies ran while one was open for 11% of the time, Pallas kernels for 0%

profile of v10, /device:TPU:0, one launch (start us, length us, event | category | flops | bytes accessed | tf_op | source)
XLA Modules:
  0.0 425.0 jit_solution(3036333006174400851)
XLA Ops:
  3.6 122.6 %attention_forward.1 = (bf16[2048,256]{1,0:T(8,128)(2,1)S(1)}, bf16[2048,256]{1,0:T(8,128)(2,1)S(1)}, bf16[2048,256]{1,0:T(8,128)(2,1)S(1)}, f32[2048,256]{1,0:T...) custom-call(bf16[512,1024]{1,0:T(8,128)(2,1)} %tok.1, ...), custom_call_target="tpu_custom_call" | custom-call | flops 17179869184 | bytes 4194304 | tf_op jit(solution)/shard_map/attention_forward/pallas_call | solution.py:619
  126.3 5.1 %fusion.54 = (f32[512]{0:T(512)S(1)}, f32[512,1024]{1,0:T(8,128)S(1)}) fusion(f32[1024]{0:T(1024)S(1)} %bitcast.80, bf16[512,1024]{1,0:T(8,128)(2,1)} %get-tuple-element.44, bf16[1024,1024]{1,0:T(8,128)(2,1)} %get-tuple-element.45, bf16[512,1024]{1,0:T(8,128)(2,1)S(1)} %copy-done.11), kind=kOutput, calls=%fused_computation.132 | convolution fusion | flops 1075838464 | bytes 6297600 | tf_op jit(solution)/shard_map/dot_general | solution.py:18
  131.8 1.4 add_convert_fusion.2
  133.9 2.3 constant_dynamic-update-slice_fusion.1
  138.1 2.3 constant_dynamic-update-slice_fusion
  140.4 8.1 %multiply_convert_fusion = (bf16[1024,2048]{1,0:T(8,128)(2,1)S(1)}, f32[1024,2048]{1,0:T(8,128)S(1)}) fusion(f32[2048]{0:T(1024)S(1)} %bitcast.75, bf16[1024,2048]{1,0:T(8,128)(2,1)} %get-tuple-element.47, bf16[512,1024]{1,0:T(8,128)(2,1)} %collective-permute-done, bf16[512,1024]{1,0:T(8,128)(2,1)} %add_convert_fusion.2), kind=kOutput, calls=%fused_computation.8 | convolution fusion | flops 4311744512 | bytes 18882560 | tf_op jit(solution)/shard_map/dot_general | solution.py:18
  148.5 19.7 %convert_reduce_fusion = (f32[2048]{0:T(1024)S(1)}, bf16[1024,2048]{1,0:T(8,128)(2,1)S(1)}) fusion(f32[1024,2048]{1,0:T(8,128)S(1)} %get-tuple-element.111, f32[2048]{0:T(1024)S(1)} %bitcast.76, bf16[1024,1024]{1,0:T(8,128)(2,1)S(1)} %copy-done.28, bf16[1024,2048]{1,0:T(8,128)(2,1)S(1)} %copy-done.37), kind=kOutput, calls=%fused_computation.7 | convolution fusion | flops 4322228224 | bytes 18890752 | tf_op jit(solution)/shard_map/dot_general | solution.py:18
  168.2 3.7 fusion.18
  172.4 3.7 fusion.22
  176.4 9.5 %convolution_convert_fusion.part_up = bf16[1024,2048]{1,0:T(8,128)(2,1)} fusion(bf16[1024,2048]{1,0:T(8,128)(2,1)} %copy-done.40, bf16[512,1024]{1,0:T(8,128)(2,1)} %collective-permute-done, bf16[512,1024]{1,0:T(8,128)(2,1)} %add_convert_fusion.2), kind=kOutput, calls=%fused_computation.11 | convolution fusion | flops 4301258752 | bytes 10485760 | tf_op jit(solution)/shard_map/dot_general | solution.py:18
  185.9 6.3 %convolution_convert_fusion.1.part_down = bf16[1024,2048]{1,0:T(8,128)(2,1)} fusion(bf16[1024,1024]{1,0:T(8,128)(2,1)S(1)} %copy-done.29, bf16[1024,2048]{1,0:T(8,128)(2,1)S(1)} %copy-done.36), kind=kOutput, calls=%fused_computation.12 | convolution fusion | flops 4297064448 | bytes 10485760 | tf_op jit(solution)/shard_map/dot_general | solution.py:18
  192.2 4.6 %multiply_reduce_fusion = (f32[1024]{0:T(1024)S(1)}, f32[512]{0:T(512)S(1)}, f32[512]{0:T(512)S(1)}, f32[1024]{0:T(1024)S(1)}, f32[512,1024]{1,0:T(8,128)S(1)}) fusion(f32[512,1024]{1,0:T(8,128)S(1)} %get-tuple-element.109, f32[512]{0:T(512)S(1)} %add_rsqrt_fusion.1, f32[512]{0:T(512)S(1)} %broadcast_multiply_fusion.5, f32[1024]{0:T(1024)S(1)} %bitcast.66, ...), kind=kOutput, calls=%fused_computation.48 | convolution fusion | flops 2152723456 | bytes 12603392 | tf_op jit(solution)/shard_map/dot_general | solution.py:18
  196.8 3.0 convert_reduce_fusion.4
  199.8 1.3 fusion.45
  201.2 1.9 copy-done.8
  203.1 1.1 dynamic-slice_convert_fusion
  205.1 1.3 convolution_convert_fusion.2
  207.4 4.7 %all-to-all-start = ((bf16[512,4,256]{2,0,1:T(8,128)(2,1)}), bf16[512,4,256]{2,0,1:T(8,128)(2,1)}, u32[]{:S(2)}, u32[]{:S(2)}) async-start(bf16[512,4,256]{2,0,1:T(8,128)(2,1)} %bitcast.63), calls=%async_computation | async-start | bytes 2097152 | tf_op jit(solution)/shard_map/all_to_all | solution.py:1035
  212.1 7.6 %add_convert_fusion.1 = bf16[512,1024]{1,0:T(8,128)(2,1)} fusion(f32[512,1024]{1,0:T(8,128)} %copy-done.10, f32[512,1024]{1,0:T(8,128)} %collective-permute-done.1, bf16[1024,2048]{1,0:T(8,128)(2,1)} %get-tuple-element.48, bf16[1024,2048]{1,0:T(8,128)(2,1)} %copy-done.35, f32[1024]{0:T(1024)S(1)} %bitcast.77), kind=kOutput, calls=%fused_computation.53 | convolution fusion | flops 2149580800 | bytes 11538432 | tf_op jit(solution)/shard_map/dot_general | solution.py:18
  219.7 2.6 add_convert_fusion.part_out
  222.3 4.3 %all-to-all-done = bf16[512,4,256]{2,0,1:T(8,128)(2,1)} async-done(((bf16[512,4,256]{2,0,1:T(8,128)(2,1)}), bf16[512,4,256]{2,0,1:T(8,128)(2,1)}, u32[]{:S(2)}, u32[]{:S(2)}) %all-to-all-start) | async-done | bytes 1048608 | tf_op jit(solution)/shard_map/all_to_all | solution.py:1035
  226.6 110.1 %attention_backward.1 = (bf16[2048,768]{1,0:T(8,128)(2,1)}, bf16[4,128,512]{2,1,0:T(8,128)(2,1)}, bf16[4,128,1024]{2,1,0:T(8,128)(2,1)}, bf16[4,128,2048]{2,1,0:T(8,128)(2,1)}, f32[8,128]{1,0:T(8,128)}) custom-call(bf16[2048,256]{1,0:T(8,128)(2,1)} %copy-done.2, bf16[2048,256]{1,0:T(8,128)(2,1)} %copy-done.3, bf16[2048,256]{1,0:T(8,128)(2,1)} %copy-done.4, ...), custom_call_target="tpu_custom_call" | custom-call | flops 30064771072 | bytes 10485760 | tf_op jit(solution)/shard_map/attention_backward/pallas_call | solution.py:914
  336.7 2.4 convert_reduce_fusion.1
  339.1 1.3 concatenate.28.vec_in
  340.4 58.7 %tail.1 = (f32[512,1024]{1,0:T(8,128)}, bf16[128,3072]{1,0:T(8,128)(2,1)}, f32[16,128]{1,0:T(8,128)}, f32[8,128]{1,0:T(8,128)}) custom-call(bf16[2048,1024]{1,0:T(8,128)(2,1)} %get-tuple-element.49.normed, bf16[2048,768]{1,0:T(8,128)(2,1)} %get-tuple-element.58.grad_proj, bf16[1024,768]{1,0:T(8,128)(2,1)} %get-tuple-element.59.weight_in, ...), custom_call_target="tpu_custom_call" | custom-call | tf_op jit(solution)/shard_map/tail/pallas_call | solution.py:272
  399.1 1.2 slice.94
  401.1 1.4 slice_bitcast_fusion.3
  406.7 1.7 fusion.14
  409.7 3.0 multiply_subtract_fusion.2
  414.3 3.9 multiply_subtract_fusion.1
  418.2 1.4 multiply_subtract_fusion.3
  420.5 3.2 multiply_subtract_fusion
  (134 shorter events, 15.7 us)
Async XLA Ops:
  3.6 122.7 %copy-start.11 = (bf16[512,1024]{1,0:T(8,128)(2,1)S(1)}, bf16[512,1024]{1,0:T(8,128)(2,1)}, u32[]{:S(2)}) copy-start(bf16[512,1024]{1,0:T(8,128)(2,1)} %tok.1) | copy-start | bytes 3145732
  126.2 5.2 %copy-start.2 = (bf16[2048,256]{1,0:T(8,128)(2,1)}, bf16[2048,256]{1,0:T(8,128)(2,1)S(1)}, u32[]{:S(2)}) copy-start(bf16[2048,256]{1,0:T(8,128)(2,1)S(1)} %get-tuple-element.50.q_ref) | copy-start | bytes 3145732
  126.2 5.2 %copy-start.3 = (bf16[2048,256]{1,0:T(8,128)(2,1)}, bf16[2048,256]{1,0:T(8,128)(2,1)S(1)}, u32[]{:S(2)}) copy-start(bf16[2048,256]{1,0:T(8,128)(2,1)S(1)} %get-tuple-element.51.k_ref) | copy-start | bytes 3145732
  126.2 5.2 %copy-start.4 = (bf16[2048,256]{1,0:T(8,128)(2,1)}, bf16[2048,256]{1,0:T(8,128)(2,1)S(1)}, u32[]{:S(2)}) copy-start(bf16[2048,256]{1,0:T(8,128)(2,1)S(1)} %get-tuple-element.52.v_ref) | copy-start | bytes 3145732
  126.3 5.2 %copy-start.5 = (f32[2048,1]{1,0:T(8,128)}, f32[2048,1]{1,0:T(8,128)S(1)}, u32[]{:S(2)}) copy-start(f32[2048,1]{1,0:T(8,128)S(1)} %get-tuple-element.56.tag_ref) | copy-start | bytes 24580
  126.3 5.2 %copy-start.6 = (bf16[2048,256]{1,0:T(8,128)(2,1)}, bf16[2048,256]{1,0:T(8,128)(2,1)S(1)}, u32[]{:S(2)}) copy-start(bf16[2048,256]{1,0:T(8,128)(2,1)S(1)} %get-tuple-element.53.o_ref) | copy-start | bytes 3145732
  126.3 5.2 %copy-start.7 = (f32[8,8,256]{2,1,0:T(8,128)}, f32[8,8,256]{2,1,0:T(8,128)S(1)}, u32[]{:S(2)}) copy-start(f32[8,8,256]{2,1,0:T(8,128)S(1)} %get-tuple-element.54.lse_ref) | copy-start | bytes 196612
  131.4 60.8 %copy-start.10 = (f32[512,1024]{1,0:T(8,128)}, f32[512,1024]{1,0:T(8,128)S(1)}, u32[]{:S(2)}) copy-start(f32[512,1024]{1,0:T(8,128)S(1)} %get-tuple-element.109) | copy-start | bytes 6291460
  133.2 7.1 %collective-permute-start = (bf16[512,1024]{1,0:T(8,128)(2,1)}, bf16[512,1024]{1,0:T(8,128)(2,1)}, u32[]{:S(2)}, u32[]{:S(2)}) collective-permute-start(bf16[512,1024]{1,0:T(8,128)(2,1)} %add_convert_fusion.2), channel_id=1, source_target_pairs={{0,1},{1,0},{2,3},{3,2},{4,5},{5,4},{6,7},{7,6},{8,9},{9,8},{10,11... | collective-permute-start | bytes 3145736 | tf_op jit(solution)/shard_map/ppermute | solution.py:985
  133.7 4.4 %collective-permute-start.2 = (bf16[512,1024]{1,0:T(8,128)(2,1)}, bf16[512,1024]{1,0:T(8,128)(2,1)}, u32[]{:S(2)}, u32[]{:S(2)}) collective-permute-start(bf16[512,1024]{1,0:T(8,128)(2,1)} %param.22), channel_id=1, source_target_pairs={{0,1},{1,0},{2,3},{3,2},{4,5},{5,4},{6,7},{7,6},{8,9},{9,8},{10,11... | collective-permute-start | bytes 3145736 | tf_op jit(solution)/shard_map/ppermute | solution.py:985
  140.3 8.1 %copy-start.28 = (bf16[1024,1024]{1,0:T(8,128)(2,1)S(1)}, bf16[1024,1024]{1,0:T(8,128)(2,1)}, u32[]{:S(2)}) copy-start(bf16[1024,1024]{1,0:T(8,128)(2,1)} %constant_dynamic-update-slice_fusion) | copy-start | bytes 6291460
  140.3 8.1 %copy-start.37 = (bf16[1024,2048]{1,0:T(8,128)(2,1)S(1)}, bf16[1024,2048]{1,0:T(8,128)(2,1)}, u32[]{:S(2)}) copy-start(bf16[1024,2048]{1,0:T(8,128)(2,1)} %get-tuple-element.48) | copy-start | bytes 12582916
  148.4 23.9 %copy-start.35 = (bf16[1024,2048]{1,0:T(8,128)(2,1)}, bf16[1024,2048]{1,0:T(8,128)(2,1)S(1)}, u32[]{:S(2)}) copy-start(bf16[1024,2048]{1,0:T(8,128)(2,1)S(1)} %get-tuple-element.110) | copy-start | bytes 12582916
  148.5 19.7 %copy-start.38 = (bf16[1024,2048]{1,0:T(8,128)(2,1)S(1)}, bf16[1024,2048]{1,0:T(8,128)(2,1)}, u32[]{:S(2)}) copy-start(bf16[1024,2048]{1,0:T(8,128)(2,1)} %get-tuple-element.47) | copy-start | bytes 12582916
  168.2 3.7 copy-start.40
  171.9 20.3 %collective-permute-start.3 = (f32[512,1024]{1,0:T(8,128)}, f32[512,1024]{1,0:T(8,128)}, u32[]{:S(2)}, u32[]{:S(2)}) collective-permute-start(f32[512,1024]{1,0:T(8,128)} %fusion.18), channel_id=1, source_target_pairs={{0,1},{1,0},{2,3},{3,2},{4,5},{5,4},{6,7},{7,6},{8,9},{9,8},{10,11... | collective-permute-start | bytes 6291464 | tf_op jit(solution)/shard_map/ppermute | solution.py:985
  176.3 9.6 %copy-start.29 = (bf16[1024,1024]{1,0:T(8,128)(2,1)S(1)}, bf16[1024,1024]{1,0:T(8,128)(2,1)}, u32[]{:S(2)}) copy-start(bf16[1024,1024]{1,0:T(8,128)(2,1)} %constant_dynamic-update-slice_fusion) | copy-start | bytes 6291460
  176.3 9.6 %copy-start.36 = (bf16[1024,2048]{1,0:T(8,128)(2,1)S(1)}, bf16[1024,2048]{1,0:T(8,128)(2,1)}, u32[]{:S(2)}) copy-start(bf16[1024,2048]{1,0:T(8,128)(2,1)} %copy-done.35) | copy-start | bytes 12582916
  176.3 35.8 %collective-permute-start.1 = (f32[512,1024]{1,0:T(8,128)}, f32[512,1024]{1,0:T(8,128)}, u32[]{:S(2)}, u32[]{:S(2)}) collective-permute-start(f32[512,1024]{1,0:T(8,128)} %fusion.22), channel_id=1, source_target_pairs={{0,1},{1,0},{2,3},{3,2},{4,5},{5,4},{6,7},{7,6},{8,9},{9,8},{10,11... | collective-permute-start | bytes 6291464 | tf_op jit(solution)/shard_map/ppermute | solution.py:985
  185.9 6.4 %copy-start.39 = (bf16[1024,2048]{1,0:T(8,128)(2,1)S(1)}, bf16[1024,2048]{1,0:T(8,128)(2,1)}, u32[]{:S(2)}) copy-start(bf16[1024,2048]{1,0:T(8,128)(2,1)} %get-tuple-element.47) | copy-start | bytes 12582916
  185.9 6.4 %copy-start.41 = (bf16[1024,2048]{1,0:T(8,128)(2,1)S(1)}, bf16[1024,2048]{1,0:T(8,128)(2,1)}, u32[]{:S(2)}) copy-start(bf16[1024,2048]{1,0:T(8,128)(2,1)} %copy-done.40) | copy-start | bytes 12582916
  204.2 15.5 %collective-permute-start.4 = (bf16[1024,512]{1,0:T(8,128)(2,1)}, bf16[1024,512]{1,0:T(8,128)(2,1)}, u32[]{:S(2)}, u32[]{:S(2)}) collective-permute-start(bf16[1024,512]{1,0:T(8,128)(2,1)} %dynamic-slice_convert_fusion), channel_id=1, source_target_pairs={{0,1},{1,0},{2,3},{3,2},{4,5},{5,4},{6,7},{7,6},{8,9},{9,8},{10,11... | collective-permute-start | bytes 3145736 | tf_op jit(solution)/shard_map/ppermute | solution.py:985
  207.4 19.2 %all-to-all-start = ((bf16[512,4,256]{2,0,1:T(8,128)(2,1)}), bf16[512,4,256]{2,0,1:T(8,128)(2,1)}, u32[]{:S(2)}, u32[]{:S(2)}) async-start(bf16[512,4,256]{2,0,1:T(8,128)(2,1)} %bitcast.63), calls=%async_computation | async-start | bytes 2097152 | tf_op jit(solution)/shard_map/all_to_all | solution.py:1035
  212.1 7.6 %copy-start.9 = (f32[1024,1024]{1,0:T(8,128)S(1)}, f32[1024,1024]{1,0:T(8,128)}, u32[]{:S(2)}) copy-start(f32[1024,1024]{1,0:T(8,128)} %copy-done.8) | copy-start | bytes 12582916
  409.7 3.0 copy-start.14
  409.7 3.9 copy-start.15
  409.7 4.6 %copy-start.16 = (f32[128,4096]{1,0:T(8,128)S(1)}, f32[128,4096]{1,0:T(8,128)}, u32[]{:S(2)}) copy-start(f32[128,4096]{1,0:T(8,128)} %param.34) | copy-start | bytes 6291460
  414.3 3.9 copy-start.1
  414.3 3.9 copy-start.25
  414.3 3.9 copy-start.26
  414.3 5.3 %copy-start.19 = (f32[128,4096]{1,0:T(8,128)S(1)}, f32[128,4096]{1,0:T(8,128)}, u32[]{:S(2)}) copy-start(f32[128,4096]{1,0:T(8,128)} %param.40) | copy-start | bytes 6291460
  414.3 5.3 %copy-start.20 = (f32[128,4096]{1,0:T(8,128)S(1)}, f32[128,4096]{1,0:T(8,128)}, u32[]{:S(2)}) copy-start(f32[128,4096]{1,0:T(8,128)} %param.35) | copy-start | bytes 6291460
  (16 other events, 32.2 us)
